TPU v7x, 32 devices: a whole 2x2x4 slice. The times are simulated.
32 devices in a mesh: dom: 16 (over z, y, x), edge: 2 (over core).
Axes of the slice: x: 2, y: 2, z: 4, core: 2. Of those that a mesh axis runs over, the one named last changes fastest.
Arguments:
- node_lat: bfloat16 [8192, 256], P(('dom', 'edge')), may hold values from -6 to 6
- edge_lat: bfloat16 [98304, 256], P(('dom', 'edge')), may hold values from -6 to 6
- senders: int32 [98304], P(('dom', 'edge')), may hold values from 0 to 1535
- receivers: int32 [98304], P(('dom', 'edge')), may hold values from 0 to 511
- live_edges: int32 [16, 2], P('dom', 'edge'), may hold values from 768 to 3072, as said below
- send_rows: int32 [32, 4, 128], P(('dom', 'edge')), may hold values from 0 to 255, as said below
- edge_w1: bfloat16 [2, 768, 256], replicated, may hold values from -0.21875 to 0.21875
- edge_b1: float32 [2, 256], replicated, may hold values from -3 to 3
- edge_w2: bfloat16 [2, 256, 256], replicated, may hold values from -0.375 to 0.375
- edge_gain: float32 [2, 256], replicated, may hold values from 0.1 to 1.9
- node_w1: bfloat16 [2, 512, 256], replicated, may hold values from -0.25 to 0.25
- node_b1: float32 [2, 256], replicated, may hold values from -3 to 3
- node_w2: bfloat16 [2, 256, 256], replicated, may hold values from -0.375 to 0.375
- node_gain: float32 [2, 256], replicated, may hold values from 0.1 to 1.9
Outputs:
- node_out: bfloat16 [8192, 256], P(('dom', 'edge'))
- edge_out: bfloat16 [98304, 256], P(('dom', 'edge'))
Inputs may be any that keep to these rules, and one draw needn't show every extreme that they name: `send_rows`: for each device and face, 128 distinct rows of the device's own 256 nodes. `live_edges`: a multiple of 128 for every device; some device is full in every draw. `senders`: rows of the domain's node table. `receivers`: nodes of the edge's own domain.
All inputs are finite; a program needn't handle non-finite values.
Results may differ from a plain program's by a relative error of at most 0.014.
Values may be sent and summed in bfloat16 or wider, within the bound.
No kernel may reach another device: no remote copies, remote signals or barrier semaphores. Data moves between devices by JAX's collectives and lax.ppermute only.
A program may use at most 64 MiB of HBM per device.

v0:
```python
import jax
import jax.numpy as jnp
from jax import lax
from jax.sharding import PartitionSpec as P

LAYERS = 2


eps_norm = 1e-05


def passed_along(value, axis, steps):
    count = lax.axis_size(axis)
    pairs = [(source, (source + steps) % count) for source in range(count)]
    return lax.ppermute(value, axis, pairs)


def layer_norm(values, norm_gain):
    center = values - jnp.mean(values, axis=-1, keepdims=True)
    spread = jnp.mean(center * center, axis=-1, keepdims=True)
    return center * lax.rsqrt(spread + eps_norm) * norm_gain


def edge_update(
    edge_rows, sender_rows, receiver_rows, weight_in, bias_in, weight_out, norm_gain, live_rows
):
    feature_width = edge_rows.shape[1]
    pre_act = jnp.dot(edge_rows, weight_in[:feature_width], preferred_element_type=jnp.float32)
    pre_act = pre_act + jnp.dot(
        sender_rows,
        weight_in[feature_width : 2 * feature_width],
        preferred_element_type=jnp.float32,
    )
    pre_act = pre_act + jnp.dot(
        receiver_rows, weight_in[2 * feature_width :], preferred_element_type=jnp.float32
    )
    hidden_rows = jax.nn.relu(pre_act + bias_in).astype(jnp.bfloat16)
    messages = layer_norm(
        jnp.dot(hidden_rows, weight_out, preferred_element_type=jnp.float32), norm_gain
    )
    messages = jnp.where(live_rows[:, None], messages, jnp.float32(0.0))
    return ((edge_rows.astype(jnp.float32) + messages).astype(jnp.bfloat16), messages)


def node_update(node_rows, aggregate, weight_in, bias_in, weight_out, norm_gain):
    feature_width = node_rows.shape[1]
    pre_act = jnp.dot(node_rows, weight_in[:feature_width], preferred_element_type=jnp.float32)
    pre_act = pre_act + jnp.dot(
        aggregate, weight_in[feature_width:], preferred_element_type=jnp.float32
    )
    hidden_rows = jax.nn.relu(pre_act + bias_in).astype(jnp.bfloat16)
    update = layer_norm(
        jnp.dot(hidden_rows, weight_out, preferred_element_type=jnp.float32), norm_gain
    )
    return (node_rows.astype(jnp.float32) + update).astype(jnp.bfloat16)


def shards(
    node_lat,
    edge_lat,
    senders,
    receivers,
    live_edges,
    send_rows,
    edge_w1,
    edge_b1,
    edge_w2,
    edge_gain,
    node_w1,
    node_b1,
    node_w2,
    node_gain,
):
    rank_count = lax.axis_size("edge")
    domains = lax.axis_size("dom")
    stride = domains // 4
    offsets = (1, -1, stride, -stride)
    node_count = node_lat.shape[0]
    face_count = send_rows.shape[1]
    latent = node_lat.shape[1]
    live_rows = lax.broadcasted_iota(jnp.int32, (edge_lat.shape[0],), 0) < live_edges[0, 0]
    lists_all = None
    lists_all = lax.all_gather(send_rows, "edge", axis=0, tiled=True)
    lists_all = lists_all + (jnp.arange(rank_count, dtype=jnp.int32) * node_count)[:, None, None]
    owned_rows = node_lat
    edge_rows = edge_lat
    for layer_index in range(LAYERS):
        received = []
        domain_rows = lax.all_gather(owned_rows, "edge", axis=0, tiled=True)
        face_rows = jnp.take(domain_rows, lists_all, axis=0)
        for face_index in range(face_count):
            received.append(passed_along(face_rows[:, face_index], "dom", offsets[face_index]))
        halo_all = jnp.stack(received, axis=1).reshape(-1, latent)
        node_table = jnp.concatenate([domain_rows, halo_all], axis=0)
        sender_rows = jnp.take(node_table, senders, axis=0)
        receiver_rows = jnp.take(domain_rows, receivers, axis=0)
        edge_rows, messages = edge_update(
            edge_rows,
            sender_rows,
            receiver_rows,
            edge_w1[layer_index],
            edge_b1[layer_index],
            edge_w2[layer_index],
            edge_gain[layer_index],
            live_rows,
        )
        summed = lax.psum_scatter(
            jax.ops.segment_sum(
                messages, receivers, num_segments=lax.axis_size("edge") * node_count
            ).astype(jnp.bfloat16),
            "edge",
            scatter_dimension=0,
            tiled=True,
        )
        owned_rows = node_update(
            owned_rows,
            summed,
            node_w1[layer_index],
            node_b1[layer_index],
            node_w2[layer_index],
            node_gain[layer_index],
        )
    return (owned_rows, edge_rows)


def solution(mesh):
    in_specs = (
        P(("dom", "edge"), None),
        P(("dom", "edge"), None),
        P(("dom", "edge")),
        P(("dom", "edge")),
        P("dom", "edge"),
        P(("dom", "edge"), None, None),
        P(),
        P(),
        P(),
        P(),
        P(),
        P(),
        P(),
        P(),
    )
    out_specs = (P(("dom", "edge"), None), P(("dom", "edge"), None))
    return jax.shard_map(shards, mesh=mesh, in_specs=in_specs, out_specs=out_specs, check_vma=False)
```

profile of v0, /device:TPU:0, one launch (start us, length us, event | category | flops | bytes accessed | tf_op | source)
XLA Modules:
  0.0 206.5 jit_solution(2417402973483310563)
XLA Ops:
  7.2 2.3 %all_gather.9 = bf16[512,256]{1,0:T(8,128)(2,1)S(1)} all-gather(bf16[256,256]{1,0:T(8,128)(2,1)} %param.20), channel_id=1, replica_groups=mesh['dom'=16,'edge'=2] {'edge'}, dimensions={0}, use_global_device_ids=true | all-gather | bytes 393216 | tf_op jit(solution)/shard_map/all_gather | solution.py:89
  9.6 2.0 all_gather.10
  11.7 3.9 %gather_fusion = bf16[1024,256]{1,0:T(8,128)(2,1)S(1)} fusion(bf16[512,256]{1,0:T(8,128)(2,1)S(1)} %all_gather.9, s32[1024]{0:T(1024)S(1)} %broadcast_clamp_fusion), kind=kCustom, calls=%fused_computation.clone | custom fusion | bytes 1052672 | tf_op jit(solution)/shard_map/jit(_take)/gather | solution.py:90
  16.0 3.0 %collective-permute-start.2 = (bf16[2,128,256]{2,1,0:T(8,128)(2,1)S(1)}, bf16[2,128,256]{2,1,0:T(8,128)(2,1)S(1)}, u32[]{:S(2)}, u32[]{:S(2)}) collective-permute-start(bf16[2,128,256]{2,1,0:T(8,128)(2,1)S(1)} %get-tuple-element.20), channel_id=1, source_target_pairs={{0,8},{2,10},{4,12},{6,14},{8,16},{10,18},{12,20},{14,22},{16,24},... | collective-permute-start | bytes 393224 | tf_op jit(solution)/shard_map/ppermute | solution.py:15
  18.9 2.1 %collective-permute-start.3 = (bf16[2,128,256]{2,1,0:T(8,128)(2,1)S(1)}, bf16[2,128,256]{2,1,0:T(8,128)(2,1)S(1)}, u32[]{:S(2)}, u32[]{:S(2)}) collective-permute-start(bf16[2,128,256]{2,1,0:T(8,128)(2,1)S(1)} %get-tuple-element.19), channel_id=1, source_target_pairs={{0,24},{2,26},{4,28},{6,30},{8,0},{10,2},{12,4},{14,6},{16,8},{18,... | collective-permute-start | bytes 393224 | tf_op jit(solution)/shard_map/ppermute | solution.py:15
  21.0 1.6 collective-permute-start
  22.6 4.0 %collective-permute-start.1 = (bf16[2,128,256]{2,1,0:T(8,128)(2,1)S(1)}, bf16[2,128,256]{2,1,0:T(8,128)(2,1)S(1)}, u32[]{:S(2)}, u32[]{:S(2)}) collective-permute-start(bf16[2,128,256]{2,1,0:T(8,128)(2,1)S(1)} %get-tuple-element.18), channel_id=1, source_target_pairs={{0,30},{2,0},{4,2},{6,4},{8,6},{10,8},{12,10},{14,12},{16,14},{18,... | collective-permute-start | bytes 393224 | tf_op jit(solution)/shard_map/ppermute | solution.py:15
  26.7 0.6 fusion.113
  27.3 0.6 fusion.112
  27.9 0.6 fusion.111
  28.5 1.1 fusion.74
  29.6 3.1 %fusion.72 = f32[3072,256]{1,0:T(8,128)} fusion(bf16[3072,256]{1,0:T(8,128)(2,1)S(1)} %copy-done.1, bf16[2,768,256]{2,1,0:T(8,128)(2,1)} %param.26), kind=kOutput, calls=%fused_computation.98 | convolution fusion | flops 402653184 | bytes 4849664 | tf_op jit(solution)/shard_map/dot_general | solution.py:28
  32.7 0.6 fusion.110
  33.4 13.0 %gather_fusion.2 = bf16[3072,256]{1,0:T(8,128)(2,1)} fusion(bf16[512,256]{1,0:T(8,128)(2,1)S(1)} %all_gather.9, s32[3072]{0:T(1024)S(1)} %fusion.99), kind=kCustom, calls=%fused_computation.2.clone | custom fusion | bytes 3158016 | tf_op jit(solution)/shard_map/jit(_take)/gather | solution.py:96
  47.3 13.0 %gather_fusion.1 = bf16[3072,256]{1,0:T(8,128)(2,1)} fusion(bf16[1536,256]{1,0:T(8,128)(2,1)S(1)} %pad_maximum_fusion, s32[3072]{0:T(1024)S(1)} %fusion.98), kind=kCustom, calls=%fused_computation.1.clone | custom fusion | bytes 3158016 | tf_op jit(solution)/shard_map/jit(_take)/gather | solution.py:95
  60.4 3.1 %convolution_add_fusion.3 = f32[3072,256]{1,0:T(8,128)S(1)} fusion(f32[3072,256]{1,0:T(8,128)} %fusion.72, bf16[3072,256]{1,0:T(8,128)(2,1)} %gather_fusion.1, pred[3072]{0:T(1024)(128)(4,1)S(1)} %compare_and_fusion.1, bf16[2,768,256]{2,1,0:T(8,128)(2,1)} %param.26), kind=kOutput, calls=%fused_computation.15 | convolution fusion | flops 404226048 | bytes 7998464 | tf_op jit(solution)/shard_map/dot_general | solution.py:29
  63.4 4.9 %fusion.114 = (f32[3072]{0:T(1024)}, f32[3072,256]{0,1:T(8,128)}) fusion(bf16[2,256,256]{2,1,0:T(8,128)(2,1)} %param.28, f32[3072,256]{1,0:T(8,128)S(1)} %convolution_add_fusion.3, bf16[3072,256]{1,0:T(8,128)(2,1)} %gather_fusion.2, f32[256]{0:T(256)S(1)} %bitcast.142, pred[3072]{0:T(1024)(128)(4,1)S(1)} %compare_and_fusion, bf16[2,768,256]{2,1,0:T(8,128)(2,1)} %param.26), kind=kOutput, calls=%fused_computation.151 | convolution fusion | flops 810021888 | bytes 8142848 | tf_op jit(solution)/shard_map/dot_general | solution.py:39
  68.4 2.4 %copy.53 = f32[3072,256]{1,0:T(8,128)S(1)} copy(f32[3072,256]{0,1:T(8,128)} %get-tuple-element.30) | data formatting | bytes 6291456 | tf_op jit(solution)/shard_map/dot_general | solution.py:39
  70.8 0.7 broadcast_multiply_fusion.1
  71.5 0.9 multiply_reduce_fusion.1
  72.4 0.6 add_rsqrt_fusion.1
  73.0 21.1 %scatter_custom_fusion = f32[512,256]{1,0:T(8,128)} fusion(s32[3072]{0:T(1024)} %param.23, f32[3072,256]{1,0:T(8,128)S(1)} %copy.53, f32[256]{0:T(256)} %bitcast.135, f32[3072]{0:T(1024)} %add_rsqrt_fusion.1, f32[3072]{0:T(1024)S(1)} %broadcast_multiply_fusion.1, f32[]{:T(128)} %constant.36.clone.1, pred[3072]{0:T(1024)(128)(4,1)S(1)} %iota_compare_fusion), kind=kCustom, calls=%fused_computation.24 | custom fusion | flops 3932160 | bytes 3699712 | tf_op jit(solution)/shard_map/scatter-add | solution.py:108
  94.1 1.8 convert_element_type.44
  96.0 4.4 %add_convert_fusion.1 = bf16[3072,256]{1,0:T(8,128)(2,1)S(1)} fusion(bf16[3072,256]{1,0:T(8,128)(2,1)} %param.21, f32[3072,256]{1,0:T(8,128)S(1)} %copy.53, f32[256]{0:T(256)} %bitcast.136, f32[3072]{0:T(1024)} %add_rsqrt_fusion.1, f32[3072]{0:T(1024)S(1)} %broadcast_multiply_fusion.1, pred[3072]{0:T(1024)(128)(4,1)S(1)} %iota_compare_fusion), kind=kLoop, calls=%fused_computation.21 | loop fusion | flops 5505024 | bytes 6320128 | tf_op jit(solution)/shard_map/convert_element_type | solution.py:42
  100.4 1.1 copy-done
  101.6 3.2 %fusion.61 = f32[3072,256]{1,0:T(8,128)} fusion(bf16[3072,256]{1,0:T(8,128)(2,1)S(1)} %add_convert_fusion.1, bf16[2,768,256]{2,1,0:T(8,128)(2,1)} %param.26), kind=kOutput, calls=%fused_computation.89 | convolution fusion | flops 402653184 | bytes 4849664 | tf_op jit(solution)/shard_map/dot_general | solution.py:28
  104.8 1.3 fusion.119
  106.3 2.2 %all_gather.11 = bf16[512,256]{0,1:T(8,128)(2,1)S(1)} all-gather(bf16[256,256]{0,1:T(8,128)(2,1)S(1)} %add_convert_fusion.3), channel_id=1, replica_groups=mesh['dom'=16,'edge'=2] {'edge'}, dimensions={0}, use_global_device_ids=true | all-gather | bytes 393216 | tf_op jit(solution)/shard_map/all_gather | solution.py:89
  108.6 3.9 %gather_fusion.3 = bf16[1024,256]{1,0:T(8,128)(2,1)S(1)} fusion(bf16[512,256]{1,0:T(8,128)(2,1)S(1)} %copy.59, s32[1024]{0:T(1024)S(1)} %copy-done.12), kind=kCustom, calls=%fused_computation.3.clone | custom fusion | bytes 1052672 | tf_op jit(solution)/shard_map/jit(_take)/gather | solution.py:90
  112.6 12.9 %gather_fusion.5 = bf16[3072,256]{1,0:T(8,128)(2,1)} fusion(bf16[512,256]{1,0:T(8,128)(2,1)S(1)} %copy.59, s32[3072]{0:T(1024)S(1)} %copy-done.8), kind=kCustom, calls=%fused_computation.5.clone | custom fusion | bytes 3158016 | tf_op jit(solution)/shard_map/jit(_take)/gather | solution.py:96
  125.9 5.6 %collective-permute-start.5 = (bf16[2,128,256]{2,1,0:T(8,128)(2,1)S(1)}, bf16[2,128,256]{2,1,0:T(8,128)(2,1)S(1)}, u32[]{:S(2)}, u32[]{:S(2)}) collective-permute-start(bf16[2,128,256]{2,1,0:T(8,128)(2,1)S(1)} %get-tuple-element.14), channel_id=1, source_target_pairs={{0,30},{2,0},{4,2},{6,4},{8,6},{10,8},{12,10},{14,12},{16,14},{18,... | collective-permute-start | bytes 393224 | tf_op jit(solution)/shard_map/ppermute | solution.py:15
  131.5 3.8 %collective-permute-start.7 = (bf16[2,128,256]{2,1,0:T(8,128)(2,1)S(1)}, bf16[2,128,256]{2,1,0:T(8,128)(2,1)S(1)}, u32[]{:S(2)}, u32[]{:S(2)}) collective-permute-start(bf16[2,128,256]{2,1,0:T(8,128)(2,1)S(1)} %get-tuple-element.15), channel_id=1, source_target_pairs={{0,24},{2,26},{4,28},{6,30},{8,0},{10,2},{12,4},{14,6},{16,8},{18,... | collective-permute-start | bytes 393224 | tf_op jit(solution)/shard_map/ppermute | solution.py:15
  135.5 0.4 collective-permute-done.4
  135.9 3.7 %collective-permute-done.6 = bf16[2,128,256]{2,1,0:T(8,128)(2,1)S(1)} collective-permute-done((bf16[2,128,256]{2,1,0:T(8,128)(2,1)S(1)}, bf16[2,128,256]{2,1,0:T(8,128)(2,1)S(1)}, u32[]{:S(2)}, u32[]{:S(2)}) %collective-permute-start.6) | collective-permute-done | bytes 131104 | tf_op jit(solution)/shard_map/ppermute | solution.py:15
  140.1 13.0 %gather_fusion.4 = bf16[3072,256]{1,0:T(8,128)(2,1)} fusion(bf16[1536,256]{1,0:T(8,128)(2,1)S(1)} %pad_maximum_fusion.1, s32[3072]{0:T(1024)S(1)} %copy-done.6), kind=kCustom, calls=%fused_computation.4.clone | custom fusion | bytes 3158016 | tf_op jit(solution)/shard_map/jit(_take)/gather | solution.py:95
  153.1 3.1 %convolution_add_fusion.1 = f32[3072,256]{1,0:T(8,128)S(1)} fusion(f32[3072,256]{1,0:T(8,128)} %fusion.61, bf16[3072,256]{1,0:T(8,128)(2,1)} %gather_fusion.4, pred[3072]{0:T(1024)(128)(4,1)S(1)} %copy-done.14, bf16[2,768,256]{2,1,0:T(8,128)(2,1)} %param.26), kind=kOutput, calls=%fused_computation.11 | convolution fusion | flops 404226048 | bytes 7998464 | tf_op jit(solution)/shard_map/dot_general | solution.py:29
  156.2 4.9 %fusion.122 = (f32[3072]{0:T(1024)}, f32[3072,256]{0,1:T(8,128)}) fusion(bf16[2,256,256]{2,1,0:T(8,128)(2,1)} %param.28, f32[3072,256]{1,0:T(8,128)S(1)} %convolution_add_fusion.1, bf16[3072,256]{1,0:T(8,128)(2,1)} %gather_fusion.5, f32[256]{0:T(256)S(1)} %bitcast.139, pred[3072]{0:T(1024)(128)(4,1)S(1)} %copy-done.16, bf16[2,768,256]{2,1,0:T(8,128)(2,1)} %param.26), kind=kOutput, calls=%fused_computation.153 | convolution fusion | flops 810021888 | bytes 8142848 | tf_op jit(solution)/shard_map/dot_general | solution.py:39
  161.2 2.4 %copy.61 = f32[3072,256]{1,0:T(8,128)S(1)} copy(f32[3072,256]{0,1:T(8,128)} %get-tuple-element.34) | data formatting | bytes 6291456 | tf_op jit(solution)/shard_map/dot_general | solution.py:39
  163.5 0.7 broadcast_multiply_fusion
  164.2 0.9 multiply_reduce_fusion
  165.2 0.6 add_rsqrt_fusion
  165.8 21.1 %scatter_custom_fusion.1 = f32[512,256]{1,0:T(8,128)} fusion(s32[3072]{0:T(1024)} %param.23, f32[3072,256]{1,0:T(8,128)S(1)} %copy.61, f32[256]{0:T(256)} %bitcast.133, f32[3072]{0:T(1024)} %add_rsqrt_fusion, f32[3072]{0:T(1024)S(1)} %broadcast_multiply_fusion, f32[]{:T(128)} %constant.36.clone.1, pred[3072]{0:T(1024)(128)(4,1)S(1)} %iota_compare_fusion), kind=kCustom, calls=%fused_computation.25 | custom fusion | flops 3932160 | bytes 3699712 | tf_op jit(solution)/shard_map/scatter-add | solution.py:108
  186.9 1.8 convert_element_type.51
  188.7 5.3 %add_convert_fusion = bf16[3072,256]{1,0:T(8,128)(2,1)} fusion(bf16[3072,256]{1,0:T(8,128)(2,1)} %copy-done, f32[3072,256]{1,0:T(8,128)S(1)} %copy.61, f32[256]{0:T(256)} %bitcast.134, f32[3072]{0:T(1024)} %add_rsqrt_fusion, f32[3072]{0:T(1024)S(1)} %broadcast_multiply_fusion, pred[3072]{0:T(1024)(128)(4,1)S(1)} %iota_compare_fusion), kind=kLoop, calls=%fused_computation.18 | loop fusion | flops 5505024 | bytes 6320128 | tf_op jit(solution)/shard_map/convert_element_type | solution.py:42
  194.0 2.7 %reduce-scatter.5.cloned.1.call-done = bf16[256,256]{1,0:T(8,128)(2,1)} async-done(((bf16[512,256]{1,0:T(8,128)(2,1)}), bf16[256,256]{1,0:T(8,128)(2,1)}) %reduce-scatter.5.cloned.1.call-update) | async-done | bytes 131088 | tf_op jit(solution)/shard_map/reduce_scatter | solution.py:107
  196.6 1.4 fusion.127
  198.2 0.7 add_convert_fusion.2
  198.9 0.8 copy.62
  (92 shorter events, 2.2 us)
Async XLA Ops:
  7.2 97.6 %reduce-scatter.3.cloned.1.call-start = ((), (), s32[]{:S(2)}) async-start(), calls=%async_computation.2 | async-start | bytes 393216 | tf_op jit(solution)/shard_map/reduce_scatter | solution.py:107
  11.6 4.1 %copy-start.17 = (pred[2,4,128]{2,1,0:T(4,128)(4,1)}, pred[2,4,128]{2,1,0:T(4,128)(4,1)S(1)}, u32[]{:S(2)}) copy-start(pred[2,4,128]{2,1,0:T(4,128)(4,1)S(1)} %get-tuple-element.11) | copy-start | bytes 3076
  11.6 4.1 %copy-start.11 = (s32[1024]{0:T(1024)}, s32[1024]{0:T(1024)S(1)}, u32[]{:S(2)}) copy-start(s32[1024]{0:T(1024)S(1)} %broadcast_clamp_fusion) | copy-start | bytes 12292
  11.6 15.0 %copy-start.9 = (s32[3072]{0:T(1024)S(1)}, s32[3072]{0:T(1024)}, u32[]{:S(2)}) copy-start(s32[3072]{0:T(1024)} %param.22) | copy-start | bytes 36868
  11.7 15.0 %copy-start.10 = (s32[3072]{0:T(1024)S(1)}, s32[3072]{0:T(1024)}, u32[]{:S(2)}) copy-start(s32[3072]{0:T(1024)} %param.23) | copy-start | bytes 36868
  11.7 15.1 %copy-start.22 = (f32[2,256]{1,0:T(2,128)S(1)}, f32[2,256]{1,0:T(2,128)}, u32[]{:S(2)}) copy-start(f32[2,256]{1,0:T(2,128)} %param.27) | copy-start | bytes 6148
  11.7 15.7 %copy-start.23 = (f32[2,256]{1,0:T(2,128)S(1)}, f32[2,256]{1,0:T(2,128)}, u32[]{:S(2)}) copy-start(f32[2,256]{1,0:T(2,128)} %param.29) | copy-start | bytes 6148
  11.7 16.2 %copy-start.24 = (f32[2,256]{1,0:T(2,128)S(1)}, f32[2,256]{1,0:T(2,128)}, u32[]{:S(2)}) copy-start(f32[2,256]{1,0:T(2,128)} %param.31) | copy-start | bytes 6148
  11.7 16.8 %copy-start.2 = (bf16[256,256]{1,0:T(8,128)(2,1)S(1)}, bf16[256,256]{1,0:T(8,128)(2,1)}, u32[]{:S(2)}) copy-start(bf16[256,256]{1,0:T(8,128)(2,1)} %param.20) | copy-start | bytes 393220
  11.7 17.9 %copy-start.1 = (bf16[3072,256]{1,0:T(8,128)(2,1)S(1)}, bf16[3072,256]{1,0:T(8,128)(2,1)}, u32[]{:S(2)}) copy-start(bf16[3072,256]{1,0:T(8,128)(2,1)} %param.21) | copy-start | bytes 4718596
  16.0 31.1 %collective-permute-start.2 = (bf16[2,128,256]{2,1,0:T(8,128)(2,1)S(1)}, bf16[2,128,256]{2,1,0:T(8,128)(2,1)S(1)}, u32[]{:S(2)}, u32[]{:S(2)}) collective-permute-start(bf16[2,128,256]{2,1,0:T(8,128)(2,1)S(1)} %get-tuple-element.20), channel_id=1, source_target_pairs={{0,8},{2,10},{4,12},{6,14},{8,16},{10,18},{12,20},{14,22},{16,24},... | collective-permute-start | bytes 393224 | tf_op jit(solution)/shard_map/ppermute | solution.py:15
  18.9 28.2 %collective-permute-start.3 = (bf16[2,128,256]{2,1,0:T(8,128)(2,1)S(1)}, bf16[2,128,256]{2,1,0:T(8,128)(2,1)S(1)}, u32[]{:S(2)}, u32[]{:S(2)}) collective-permute-start(bf16[2,128,256]{2,1,0:T(8,128)(2,1)S(1)} %get-tuple-element.19), channel_id=1, source_target_pairs={{0,24},{2,26},{4,28},{6,30},{8,0},{10,2},{12,4},{14,6},{16,8},{18,... | collective-permute-start | bytes 393224 | tf_op jit(solution)/shard_map/ppermute | solution.py:15
  21.0 26.1 %collective-permute-start = (bf16[2,128,256]{2,1,0:T(8,128)(2,1)S(1)}, bf16[2,128,256]{2,1,0:T(8,128)(2,1)S(1)}, u32[]{:S(2)}, u32[]{:S(2)}) collective-permute-start(bf16[2,128,256]{2,1,0:T(8,128)(2,1)S(1)} %get-tuple-element.17), channel_id=1, source_target_pairs={{0,2},{2,4},{4,6},{6,8},{8,10},{10,12},{12,14},{14,16},{16,18},{18... | collective-permute-start | bytes 393224 | tf_op jit(solution)/shard_map/ppermute | solution.py:15
  22.6 24.5 %collective-permute-start.1 = (bf16[2,128,256]{2,1,0:T(8,128)(2,1)S(1)}, bf16[2,128,256]{2,1,0:T(8,128)(2,1)S(1)}, u32[]{:S(2)}, u32[]{:S(2)}) collective-permute-start(bf16[2,128,256]{2,1,0:T(8,128)(2,1)S(1)} %get-tuple-element.18), channel_id=1, source_target_pairs={{0,30},{2,0},{4,2},{6,4},{8,6},{10,8},{12,10},{14,12},{16,14},{18,... | collective-permute-start | bytes 393224 | tf_op jit(solution)/shard_map/ppermute | solution.py:15
  26.6 20.7 %copy-start.5 = (s32[3072]{0:T(1024)}, s32[3072]{0:T(1024)S(1)}, u32[]{:S(2)}) copy-start(s32[3072]{0:T(1024)S(1)} %fusion.98) | copy-start | bytes 36868
  26.7 33.7 %copy-start.13 = (pred[3072]{0:T(1024)(128)(4,1)}, pred[3072]{0:T(1024)(128)(4,1)S(1)}, u32[]{:S(2)}) copy-start(pred[3072]{0:T(1024)(128)(4,1)S(1)} %compare_and_fusion.1) | copy-start | bytes 9220
  26.7 6.7 %copy-start.7 = (s32[3072]{0:T(1024)}, s32[3072]{0:T(1024)S(1)}, u32[]{:S(2)}) copy-start(s32[3072]{0:T(1024)S(1)} %fusion.99) | copy-start | bytes 36868
  26.7 36.7 %copy-start.15 = (pred[3072]{0:T(1024)(128)(4,1)}, pred[3072]{0:T(1024)(128)(4,1)S(1)}, u32[]{:S(2)}) copy-start(pred[3072]{0:T(1024)(128)(4,1)S(1)} %compare_and_fusion) | copy-start | bytes 9220
  29.6 3.1 %copy-start.25 = (f32[2,256]{1,0:T(2,128)S(1)}, f32[2,256]{1,0:T(2,128)}, u32[]{:S(2)}) copy-start(f32[2,256]{1,0:T(2,128)} %param.33) | copy-start | bytes 6148
  95.9 100.7 %reduce-scatter.5.cloned.1.call-start = ((), (), s32[]{:S(2)}) async-start(), calls=%async_computation.3 | async-start | bytes 393216 | tf_op jit(solution)/shard_map/reduce_scatter | solution.py:107
  100.4 1.1 copy-start
  101.5 3.2 %copy-start.3 = (bf16[2,512,256]{2,1,0:T(8,128)(2,1)S(1)}, bf16[2,512,256]{2,1,0:T(8,128)(2,1)}, u32[]{:S(2)}) copy-start(bf16[2,512,256]{2,1,0:T(8,128)(2,1)} %param.30) | copy-start | bytes 1572868
  101.5 3.2 %copy-start.4 = (bf16[2,256,256]{2,1,0:T(8,128)(2,1)S(1)}, bf16[2,256,256]{2,1,0:T(8,128)(2,1)}, u32[]{:S(2)}) copy-start(bf16[2,256,256]{2,1,0:T(8,128)(2,1)} %param.32) | copy-start | bytes 786436
  101.5 3.2 %copy-start.21 = (f32[1,256]{1,0:T(1,128)S(1)}, f32[1,256]{1,0:T(1,128)}, u32[]{:S(2)}) copy-start(f32[1,256]{1,0:T(1,128)} %get-tuple-element.24) | copy-start | bytes 3076
  101.5 4.6 %copy-start.20 = (f32[1,256]{1,0:T(1,128)S(1)}, f32[1,256]{1,0:T(1,128)}, u32[]{:S(2)}) copy-start(f32[1,256]{1,0:T(1,128)} %get-tuple-element.22) | copy-start | bytes 3076
  101.5 7.1 %copy-start.12 = (s32[1024]{0:T(1024)S(1)}, s32[1024]{0:T(1024)}, u32[]{:S(2)}) copy-start(s32[1024]{0:T(1024)} %copy-done.11) | copy-start | bytes 12292
  106.1 6.4 %copy-start.8 = (s32[3072]{0:T(1024)S(1)}, s32[3072]{0:T(1024)}, u32[]{:S(2)}) copy-start(s32[3072]{0:T(1024)} %copy-done.7) | copy-start | bytes 36868
  112.6 13.0 %copy-start.18 = (pred[2,4,128]{2,1,0:T(4,128)(4,1)S(1)}, pred[2,4,128]{2,1,0:T(4,128)(4,1)}, u32[]{:S(2)}) copy-start(pred[2,4,128]{2,1,0:T(4,128)(4,1)} %copy-done.17) | copy-start | bytes 3076
  125.5 14.5 %copy-start.6 = (s32[3072]{0:T(1024)S(1)}, s32[3072]{0:T(1024)}, u32[]{:S(2)}) copy-start(s32[3072]{0:T(1024)} %copy-done.5) | copy-start | bytes 36868
  125.8 10.1 %collective-permute-start.4 = (bf16[2,128,256]{2,1,0:T(8,128)(2,1)S(1)}, bf16[2,128,256]{2,1,0:T(8,128)(2,1)S(1)}, u32[]{:S(2)}, u32[]{:S(2)}) collective-permute-start(bf16[2,128,256]{2,1,0:T(8,128)(2,1)S(1)} %get-tuple-element.13), channel_id=1, source_target_pairs={{0,2},{2,4},{4,6},{6,8},{8,10},{10,12},{12,14},{14,16},{16,18},{18... | collective-permute-start | bytes 393224 | tf_op jit(solution)/shard_map/ppermute | solution.py:15
  125.9 10.1 %collective-permute-start.5 = (bf16[2,128,256]{2,1,0:T(8,128)(2,1)S(1)}, bf16[2,128,256]{2,1,0:T(8,128)(2,1)S(1)}, u32[]{:S(2)}, u32[]{:S(2)}) collective-permute-start(bf16[2,128,256]{2,1,0:T(8,128)(2,1)S(1)} %get-tuple-element.14), channel_id=1, source_target_pairs={{0,30},{2,0},{4,2},{6,4},{8,6},{10,8},{12,10},{14,12},{16,14},{18,... | collective-permute-start | bytes 393224 | tf_op jit(solution)/shard_map/ppermute | solution.py:15
  131.5 8.2 %collective-permute-start.6 = (bf16[2,128,256]{2,1,0:T(8,128)(2,1)S(1)}, bf16[2,128,256]{2,1,0:T(8,128)(2,1)S(1)}, u32[]{:S(2)}, u32[]{:S(2)}) collective-permute-start(bf16[2,128,256]{2,1,0:T(8,128)(2,1)S(1)} %get-tuple-element.16), channel_id=1, source_target_pairs={{0,8},{2,10},{4,12},{6,14},{8,16},{10,18},{12,20},{14,22},{16,24},... | collective-permute-start | bytes 393224 | tf_op jit(solution)/shard_map/ppermute | solution.py:15
  131.5 8.4 %collective-permute-start.7 = (bf16[2,128,256]{2,1,0:T(8,128)(2,1)S(1)}, bf16[2,128,256]{2,1,0:T(8,128)(2,1)S(1)}, u32[]{:S(2)}, u32[]{:S(2)}) collective-permute-start(bf16[2,128,256]{2,1,0:T(8,128)(2,1)S(1)} %get-tuple-element.15), channel_id=1, source_target_pairs={{0,24},{2,26},{4,28},{6,30},{8,0},{10,2},{12,4},{14,6},{16,8},{18,... | collective-permute-start | bytes 393224 | tf_op jit(solution)/shard_map/ppermute | solution.py:15
  140.1 13.1 %copy-start.14 = (pred[3072]{0:T(1024)(128)(4,1)S(1)}, pred[3072]{0:T(1024)(128)(4,1)}, u32[]{:S(2)}) copy-start(pred[3072]{0:T(1024)(128)(4,1)} %copy-done.13) | copy-start | bytes 9220
  153.1 3.1 %copy-start.16 = (pred[3072]{0:T(1024)(128)(4,1)S(1)}, pred[3072]{0:T(1024)(128)(4,1)}, u32[]{:S(2)}) copy-start(pred[3072]{0:T(1024)(128)(4,1)} %copy-done.15) | copy-start | bytes 9220
  153.1 3.1 %copy-start.19 = (f32[1,256]{1,0:T(1,128)S(1)}, f32[1,256]{1,0:T(1,128)}, u32[]{:S(2)}) copy-start(f32[1,256]{1,0:T(1,128)} %get-tuple-element.27) | copy-start | bytes 3076
Sparse Core Ops, SparseCore 0:
  96.0 3.7 reduce-scatter.2
  188.8 7.7 reduce-scatter.4
where the time goes:
time: 207 us
  local copies, waits for them, and re-layouts  69.4 us (34%)
  other arithmetic  61.7 us (30%)
  matrix products  26.4 us (13%)
  starting transfers between devices  20.2 us (10%)
  between operations  15.3 us (7%)
  waiting for transfers between devices  7.07 us (3%)
  blocking collectives  6.49 us (3%)
    scatter-add x2, other arithmetic, shards(): jax.ops.segment_sum(messages, receivers, num_segments=lax.axis_size('edge...  42.2 us
    gather x2, local copies, waits for them, and re-layouts, shards(): sender_rows = jnp.take(node_table, senders, axis=0)  26.1 us
    gather x2, local copies, waits for them, and re-layouts, shards(): receiver_rows = jnp.take(domain_rows, receivers, axis=0)  25.9 us
    ppermute x8, starting transfers between devices, passed_along(): return lax.ppermute(value, axis, pairs)  20.2 us
    dot_general x2, matrix products, edge_update(): jnp.dot(hidden_rows, weight_out, preferred_element_type=jnp.float32)  9.85 us
    convert_element_type x2, other arithmetic, edge_update(): (edge_rows.astype(jnp.float32) + messages).astype(jnp.bfloat16)  9.69 us
    gather x2, local copies, waits for them, and re-layouts, shards(): face_rows = jnp.take(domain_rows, lists_all, axis=0)  7.88 us
    dot_general x2, matrix products, edge_update(): jnp.dot(edge_rows, weight_in[:feature_width], preferred_element_type=jnp....  6.32 us
  transfers between devices with their start and end apart: 10, of which 4 were waited for; matrix products, arithmetic and copies ran while one was open for 16% of the time, Pallas kernels for 0%

commit v1 on v0

--- a/solution.py
+++ b/solution.py
@@ -1,6 +1,10 @@
+import functools
+
 import jax
 import jax.numpy as jnp
 from jax import lax
+from jax.experimental import pallas as pl
+from jax.experimental.pallas import tpu as pltpu
 from jax.sharding import PartitionSpec as P
 
 LAYERS = 2
@@ -55,7 +59,409 @@
     return (node_rows.astype(jnp.float32) + update).astype(jnp.bfloat16)
 
 
-def shards(
+F32 = jnp.float32
+BF16 = jnp.bfloat16
+TILE = 256
+HALF = 128
+ROWS = 512
+IN_VMEM = pl.BlockSpec(memory_space=pltpu.VMEM)
+IN_SMEM = pl.BlockSpec(memory_space=pltpu.SMEM)
+
+
+def shaped(shape, dtype):
+    return jax.ShapeDtypeStruct(shape, dtype)
+
+
+def call(kernel, outs, args, scratch=(), smem=(), flops=0, limit=24, name=None):
+    nbytes = sum(a.size * a.dtype.itemsize for a in args)
+    return pl.pallas_call(
+        kernel,
+        out_shape=outs,
+        in_specs=[IN_SMEM if k in smem else IN_VMEM for k in range(len(args))],
+        out_specs=jax.tree.map(lambda _: IN_VMEM, outs),
+        scratch_shapes=scratch,
+        compiler_params=pltpu.CompilerParams(vmem_limit_bytes=limit << 20),
+        cost_estimate=pl.CostEstimate(flops=flops, transcendentals=0, bytes_accessed=nbytes),
+        name=name,
+    )(*args)
+
+
+def place(stride):
+    dom = lax.axis_index("dom")
+    core = lax.axis_index("edge")
+    return core, lax.rem(dom, 2), lax.rem(lax.div(dom, stride), 2)
+
+
+def mm(a, b):
+    return jnp.dot(a, b, preferred_element_type=F32)
+
+
+def column(row):
+    return jnp.transpose(jnp.broadcast_to(row.astype(F32), (HALF, HALF)))
+
+
+def one_hot_rows(row):
+    col = column(row)
+    lane = lax.broadcasted_iota(jnp.int32, (HALF, HALF), 1).astype(F32)
+    parts = [jnp.where(col == lane + float(k), 1.0, 0.0) for k in (0, HALF)]
+    return jnp.concatenate(parts, axis=1).astype(BF16)
+
+
+def dyn(start, size):
+    return pl.ds(pl.multiple_of(start, size), size)
+
+
+def pick_kernel(stride, nodes_ref, lists_ref, far_d, far_s, near_d, near_s):
+    _, par_d, par_s = place(stride)
+    nodes = nodes_ref[...]
+    for face, out in (
+        (1 - par_d, far_d),
+        (3 - par_s, far_s),
+        (par_d, near_d),
+        (2 + par_s, near_s),
+    ):
+        out[...] = mm(one_hot_rows(lists_ref[0, pl.ds(face, 1), :]), nodes).astype(BF16)
+
+
+def index_kernel(stride, edges, send_ref, recv_ref, live_ref, cols, rows):
+    _, par_d, par_s = place(stride)
+    live = live_ref[0, 0]
+    lane = lax.broadcasted_iota(jnp.int32, (1, HALF), 1)
+    for k in range(edges // HALF):
+        at = pl.ds(k * HALF, HALF)
+        v = send_ref[:, at]
+        j = v - 2 * TILE
+        owner = lax.shift_right_arithmetic(j, 9)
+        face = lax.shift_right_arithmetic(j, 7) & 3
+        core = lax.shift_right_arithmetic(face, 1)
+        par = jnp.where(core == 0, par_d, par_s)
+        near = (face & 1) != par
+        tile = jnp.where(near, 2, 4) + core
+        at_tile = ((owner ^ core) & 1) * HALF + (j & (HALF - 1))
+        local = v < 2 * TILE
+        hi = jnp.where(local, lax.shift_right_arithmetic(v, 8), tile)
+        lo = jnp.where(local, v & (TILE - 1), at_tile)
+        cols[0, at, :] = column(hi).astype(BF16)
+        cols[1, at, :] = column(lo).astype(BF16)
+        v = recv_ref[:, at]
+        hi = lax.shift_right_arithmetic(v, 8)
+        lo = v & (TILE - 1)
+        cols[2, at, :] = column(hi).astype(BF16)
+        cols[3, at, :] = column(lo).astype(BF16)
+        rows[0:1, at] = jnp.where(lane + k * HALF < live, hi, -1).astype(F32)
+        rows[1:2, at] = lo.astype(F32)
+
+
+def lane_iota(rows):
+    lane = lax.broadcasted_iota(jnp.int32, (rows, HALF), 1).astype(F32)
+    return lane.astype(BF16), (lane + float(HALF)).astype(BF16)
+
+
+def hits(hi, lo, tile, lanes):
+    at = jnp.where(hi == tile, lo, jnp.asarray(-1, BF16))
+    one = jnp.ones(at.shape, BF16)
+    zero = jnp.zeros(at.shape, BF16)
+    return jnp.concatenate([jnp.where(at == lane, one, zero) for lane in lanes], axis=1)
+
+
+def local_kernel(layer, stacked, edge_ref, cols, *refs):
+    if stacked:
+        dom_ref, w1_ref, b1_ref, pre_ref, t_s, t_r = refs
+        dom = dom_ref[...]
+        t_s[...] = mm(dom, w1_ref[layer, TILE : 2 * TILE, :]).astype(BF16)
+        t_r[...] = mm(dom, w1_ref[layer, 2 * TILE :, :]).astype(BF16)
+    else:
+        own_ref, peer_ref, w1_ref, b1_ref, pre_ref, t_s, t_r = refs
+        core = lax.axis_index("edge")
+        for owner, ref in ((core, own_ref), (1 - core, peer_ref)):
+            at = dyn(owner * TILE, TILE)
+            t_s[at, :] = mm(ref[...], w1_ref[layer, TILE : 2 * TILE, :]).astype(BF16)
+            t_r[at, :] = mm(ref[...], w1_ref[layer, 2 * TILE :, :]).astype(BF16)
+    lanes = lane_iota(ROWS)
+    bias = b1_ref[layer : layer + 1, :]
+    w_e = w1_ref[layer, 0:TILE, :]
+
+    def step(k, carry):
+        at = dyn(k * ROWS, ROWS)
+        acc = mm(edge_ref[at, :], w_e)
+        for base, table in ((0, t_s), (2, t_r)):
+            hi = cols[base, at, :]
+            lo = cols[base + 1, at, :]
+            for tile in range(2):
+                acc = acc + mm(
+                    hits(hi, lo, jnp.asarray(tile, BF16), lanes),
+                    table[tile * TILE : (tile + 1) * TILE, :],
+                )
+        pre_ref[at, :] = acc + bias
+        return carry
+
+    lax.fori_loop(0, edge_ref.shape[0] // ROWS, step, 0)
+
+
+def halo_tables(layer, first, halves, w1_ref, refs, table):
+    core = lax.axis_index("edge")
+    w_s = w1_ref[layer, TILE : 2 * TILE, :]
+    if halves:
+        own_d, own_s, peer_d, peer_s = refs
+        for axis, owner, ref in (
+            (0, core, own_d),
+            (1, core, own_s),
+            (0, 1 - core, peer_d),
+            (1, 1 - core, peer_s),
+        ):
+            row = axis * TILE + lax.rem(owner + axis, 2) * HALF
+            table[dyn(row, HALF), :] = mm(ref[...], w_s).astype(BF16)
+    else:
+        own, peer = refs
+        for axis, ref in ((core, own), (1 - core, peer)):
+            table[dyn(axis * TILE, TILE), :] = mm(ref[...], w_s).astype(BF16)
+    return first, first + 1
+
+
+def near_kernel(layer, halves, pre_ref, cols, w1_ref, *refs):
+    refs, (out_ref, table) = refs[:-2], refs[-2:]
+    tiles = halo_tables(layer, 2, halves, w1_ref, refs, table)
+    lanes = lane_iota(ROWS)
+
+    def step(k, carry):
+        at = dyn(k * ROWS, ROWS)
+        hi = cols[0, at, :]
+        lo = cols[1, at, :]
+        acc = pre_ref[at, :]
+        for n, tile in enumerate(tiles):
+            acc = acc + mm(
+                hits(hi, lo, jnp.asarray(tile, BF16), lanes), table[n * TILE : (n + 1) * TILE, :]
+            )
+        out_ref[at, :] = acc
+        return carry
+
+    lax.fori_loop(0, pre_ref.shape[0] // ROWS, step, 0)
+
+
+def edge_kernel(layer, halves, split, live_ref, pre_ref, cols, rows, edge_ref, w1_ref, w2_ref, gain_ref, *refs):
+    if split:
+        refs, (out_ref, keep_ref, give_ref, table, msgs) = refs[:-5], refs[-5:]
+    else:
+        refs, (out_ref, part_ref, table, msgs) = refs[:-4], refs[-4:]
+    tiles = halo_tables(layer, 4, halves, w1_ref, refs, table)
+    lanes = lane_iota(ROWS)
+    live = live_ref[0, 0]
+    gain = gain_ref[layer : layer + 1, :]
+    w2 = w2_ref[layer]
+    place_in = lax.broadcasted_iota(jnp.int32, (ROWS, TILE), 0)
+
+    def step(k, carry):
+        at = dyn(k * ROWS, ROWS)
+        hi = cols[0, at, :]
+        lo = cols[1, at, :]
+        acc = pre_ref[at, :]
+        for n, tile in enumerate(tiles):
+            acc = acc + mm(
+                hits(hi, lo, jnp.asarray(tile, BF16), lanes), table[n * TILE : (n + 1) * TILE, :]
+            )
+        hidden = jnp.maximum(acc, 0.0).astype(BF16)
+        message = layer_norm(mm(hidden, w2), gain)
+        msgs[at, :] = message.astype(BF16)
+        message = jnp.where(place_in + k * ROWS < live, message, 0.0)
+        out_ref[at, :] = (edge_ref[at, :].astype(F32) + message).astype(BF16)
+        return carry
+
+    count = edge_ref.shape[0] // ROWS
+    lax.fori_loop(0, count, step, 0)
+    spot = lax.broadcasted_iota(jnp.int32, (TILE, ROWS), 0).astype(F32).astype(BF16)
+    one = jnp.ones((TILE, ROWS), BF16)
+    zero = jnp.zeros((TILE, ROWS), BF16)
+    sums = [None, None]
+    for k in range(count):
+        at = pl.ds(k * ROWS, ROWS)
+        hi = rows[0:1, at]
+        lo = rows[1:2, at]
+        msg = msgs[at, :]
+        for n in range(2):
+            here = jnp.where(hi == float(n), lo, -1.0).astype(BF16)
+            hot = jnp.where(jnp.broadcast_to(here, (TILE, ROWS)) == spot, one, zero)
+            part = mm(hot, msg)
+            sums[n] = part if sums[n] is None else sums[n] + part
+    if split:
+        core = lax.axis_index("edge")
+        mine = core == 0
+        keep_ref[...] = jnp.where(mine, sums[0], sums[1]).astype(BF16)
+        give_ref[...] = jnp.where(mine, sums[1], sums[0]).astype(BF16)
+    else:
+        for n in range(2):
+            part_ref[n * TILE : (n + 1) * TILE, :] = sums[n].astype(BF16)
+
+
+def updated(layer, nodes, first, second, w1_ref, b1_ref, w2_ref, gain_ref):
+    total = (first.astype(F32) + second.astype(F32)).astype(BF16)
+    pre = mm(nodes, w1_ref[layer, 0:TILE, :]) + mm(total, w1_ref[layer, TILE:, :])
+    hidden = jnp.maximum(pre + b1_ref[layer : layer + 1, :], 0.0).astype(BF16)
+    step = layer_norm(mm(hidden, w2_ref[layer]), gain_ref[layer : layer + 1, :])
+    return (nodes.astype(F32) + step).astype(BF16)
+
+
+def node_kernel(
+    stride, layer, own_ref, peer_ref, first, second, list_own, list_peer, w1, b1, w2, gain, out, far, near
+):
+    core, par_d, par_s = place(stride)
+    for owner, ref in ((core, own_ref), (1 - core, peer_ref)):
+        at = dyn(owner * TILE, TILE)
+        out[at, :] = updated(layer, ref[...], first[at, :], second[at, :], w1, b1, w2, gain)
+    par = jnp.where(core == 0, par_d, par_s)
+    for face, ref in ((2 * core + 1 - par, far), (2 * core + par, near)):
+        for n, (owner, lists) in enumerate(((core, list_own), (1 - core, list_peer))):
+            hot = one_hot_rows(lists[0, pl.ds(face, 1), :])
+            ref[n * HALF : (n + 1) * HALF, :] = mm(hot, out[dyn(owner * TILE, TILE), :]).astype(BF16)
+
+
+def last_kernel(layer, nodes_ref, first, second, w1, b1, w2, gain, out):
+    core = lax.axis_index("edge")
+    nodes = nodes_ref[dyn(core * TILE, TILE), :]
+    out[...] = updated(layer, nodes, first[...], second[...], w1, b1, w2, gain)
+
+
+def met(count, stride, odd):
+    pairs = []
+    for dom in range(count):
+        ahead = (dom // stride) % 2 == odd
+        pairs.append((dom + (stride if ahead else -stride)) % count)
+    return pairs
+
+
+def swapped(value):
+    return lax.ppermute(value, "edge", [(0, 1), (1, 0)])
+
+
+def fast_shards(
+    node_lat,
+    edge_lat,
+    senders,
+    receivers,
+    live_edges,
+    send_rows,
+    edge_w1,
+    edge_b1,
+    edge_w2,
+    edge_gain,
+    node_w1,
+    node_b1,
+    node_w2,
+    node_gain,
+):
+    domains = lax.axis_size("dom")
+    stride = domains // 4
+    edges, width = edge_lat.shape
+    nodes = node_lat.shape[0]
+    near_d, far_d = met(domains, 1, 0), met(domains, 1, 1)
+    near_s, far_s = met(domains, stride, 0), met(domains, stride, 1)
+
+    def sent(value, partner):
+        return lax.ppermute(value, "dom", list(enumerate(partner)))
+
+    def sent_by_core(value, partner_d, partner_s):
+        pairs = [(2 * d, 2 * p) for d, p in enumerate(partner_d)]
+        pairs += [(2 * d + 1, 2 * p + 1) for d, p in enumerate(partner_s)]
+        return lax.ppermute(value, ("dom", "edge"), pairs)
+
+    face = shaped((HALF, width), BF16)
+    table = pltpu.VMEM((2 * TILE, width), BF16)
+    messages = pltpu.VMEM((edges, width), BF16)
+    pre_shape = shaped((edges, width), F32)
+    pass_flops = 2 * edges * TILE * width
+
+    picked = call(
+        functools.partial(pick_kernel, stride), [face] * 4, (node_lat, send_rows), name="pick"
+    )
+    halo = [
+        sent(value, partner) for value, partner in zip(picked, (far_d, far_s, near_d, near_s))
+    ]
+    peer_nodes = swapped(node_lat)
+    peer_lists = swapped(send_rows)
+    cols, rows = call(
+        functools.partial(index_kernel, stride, edges),
+        [shaped((4, edges, HALF), BF16), shaped((2, edges), F32)],
+        (senders[None], receivers[None], live_edges),
+        smem=(2,),
+        name="index",
+    )
+    own_nodes = node_lat
+    edge_rows = edge_lat
+    for layer in range(LAYERS):
+        last = layer == LAYERS - 1
+        if layer == 0:
+            node_args = (node_lat, peer_nodes)
+            far = (halo[0], halo[1], swapped(halo[0]), swapped(halo[1]))
+            near = (halo[2], halo[3], swapped(halo[2]), swapped(halo[3]))
+        else:
+            node_args = (all_nodes,)
+            far = sent_by_core(far_rows, far_d, far_s)
+            near = sent_by_core(near_rows, near_d, near_s)
+            far = (far, swapped(far))
+            near = (near, swapped(near))
+        pre = call(
+            functools.partial(local_kernel, layer, layer > 0),
+            pre_shape,
+            (edge_rows, cols, *node_args, edge_w1, edge_b1),
+            scratch=[table, table],
+            flops=5 * pass_flops,
+            name="local",
+        )
+        pre = call(
+            functools.partial(near_kernel, layer, layer == 0),
+            pre_shape,
+            (pre, cols, edge_w1, *near),
+            scratch=[table],
+            flops=2 * pass_flops,
+            name="near",
+        )
+        if last:
+            outs = [shaped((nodes, width), BF16)] * 2
+        else:
+            outs = [shaped((2 * nodes, width), BF16)]
+        edge_rows, *partial = call(
+            functools.partial(edge_kernel, layer, layer == 0, last),
+            [shaped((edges, width), BF16)] + outs,
+            (live_edges, pre, cols, rows, edge_rows, edge_w1, edge_w2, edge_gain, *far),
+            scratch=[table, messages],
+            smem=(0,),
+            flops=5 * pass_flops,
+            name="far",
+        )
+        other = swapped(partial[-1])
+        weights = (node_w1, node_b1, node_w2, node_gain)
+        if last:
+            out = call(
+                functools.partial(last_kernel, layer),
+                shaped((nodes, width), BF16),
+                (all_nodes, partial[0], other, *weights),
+                name="last",
+            )
+        else:
+            rows_out = shaped((TILE, width), BF16)
+            all_nodes, far_rows, near_rows = call(
+                functools.partial(node_kernel, stride, layer),
+                [shaped((2 * nodes, width), BF16), rows_out, rows_out],
+                (*node_args, partial[0], other, send_rows, peer_lists, *weights),
+                name="nodes",
+            )
+    return out, edge_rows
+
+
+def shards(*args):
+    node_lat, edge_lat, _, _, _, send_rows = args[:6]
+    domains = lax.axis_size("dom")
+    fits = (
+        lax.axis_size("edge") == 2
+        and domains % 8 == 0
+        and node_lat.shape == (TILE, TILE)
+        and edge_lat.shape[0] % ROWS == 0
+        and send_rows.shape[1:] == (4, HALF)
+        and args[6].shape == (LAYERS, 3 * TILE, TILE)
+    )
+    return (fast_shards if fits else general_shards)(*args)
+
+
+def general_shards(
     node_lat,
     edge_lat,
     senders,

time: 207 us -> 57.8 us (0.28)
  local copies, waits for them, and re-layouts: 69.4 us -> 7.17 us
  other arithmetic: 61.7 us -> 0 us
  matrix products: 26.4 us -> 0 us
  Pallas kernels: 0 us -> 25.4 us
  between operations: 15.3 us -> 1.57 us
  blocking collectives: 6.49 us -> 0 us
  starting transfers between devices: 20.2 us -> 14.4 us
    gather x6 -> x0, local copies, waits for them, and re-layouts: 59.9 us -> none  [the longest x2 26.1 us: shards(): sender_rows = jnp.take(node_table, senders, axis=0)]
    scatter-add x2 -> x0, other arithmetic: 42.2 us -> none  [shards(): jax.ops.segment_sum(messages, receivers, num_segments=lax.axis_size('edge...]
    dot_general x10 -> x0, matrix products: 26.4 us -> none  [the longest x2 9.85 us: edge_update(): jnp.dot(hidden_rows, weight_out, preferred_element_type=jnp.float32)]
    pallas_call x0 -> x10, Pallas kernels: none -> 25.4 us  [call(): pl.pallas_call(kernel, out_shape=outs, in_specs=[IN_SMEM if k in smem els...]
    convert_element_type x6 -> x0, other arithmetic: 14.1 us -> none  [the longest x2 9.69 us: edge_update(): (edge_rows.astype(jnp.float32) + messages).astype(jnp.bfloat16)]
    all_gather x3 -> x0, blocking collectives: 6.49 us -> none  [the longest x2 4.51 us: shards(): domain_rows = lax.all_gather(owned_rows, 'edge', axis=0, tiled=True)]
    ppermute x8 -> x16, starting transfers between devices: 20.2 us -> 14.4 us  [the longest x4 9.11 us: sent(): return lax.ppermute(value, 'dom', list(enumerate(partner)))]
    unnamed x54 -> x34, local copies, waits for them, and re-layouts: 2.12 us -> 7.17 us
  transfers between devices with their start and end apart: 10 -> 16, of which waited for: 4 -> 5; matrix products, arithmetic and copies ran while one was open for 16% -> 0% of each run, Pallas kernels for 0% -> 22%
where the time goes in v1:
time: 57.8 us; the launch traced here: 57.4 us
  Pallas kernels  25.4 us (44%)
  starting transfers between devices  14.4 us (25%)
  waiting for transfers between devices  8.87 us (15%)
  local copies, waits for them, and re-layouts  7.17 us (12%)
  between operations  1.57 us (3%)
    pallas_call x10, Pallas kernels, call(): pl.pallas_call(kernel, out_shape=outs, in_specs=[IN_SMEM if k in smem els...  25.4 us
    ppermute x4, starting transfers between devices, sent(): return lax.ppermute(value, 'dom', list(enumerate(partner)))  9.11 us
    unnamed x34, local copies, waits for them, and re-layouts  7.17 us
    ppermute x2, waiting for transfers between devices, sent_by_core(): return lax.ppermute(value, ('dom', 'edge'), pairs)  5.93 us
    ppermute x2, starting transfers between devices, sent_by_core(): return lax.ppermute(value, ('dom', 'edge'), pairs)  2.75 us
    ppermute x10, starting transfers between devices, swapped(): return lax.ppermute(value, 'edge', [(0, 1), (1, 0)])  2.5 us
    ppermute x10, waiting for transfers between devices, swapped(): return lax.ppermute(value, 'edge', [(0, 1), (1, 0)])  2.08 us
  transfers between devices with their start and end apart: 16, of which 5 were waited for; matrix products, arithmetic and copies ran while one was open for 0% of the time, Pallas kernels for 22%

profile of v1, /device:TPU:0, one launch (start us, length us, event | category | flops | bytes accessed | tf_op | source)
XLA Modules:
  0.0 57.4 jit_solution(6124921947523772744)
XLA Ops:
  0.6 0.6 collective-permute-start
  1.2 0.9 %copy-done.5 = bf16[256,256]{1,0:T(8,128)(2,1)S(1)} copy-done((bf16[256,256]{1,0:T(8,128)(2,1)S(1)}, bf16[256,256]{1,0:T(8,128)(2,1)}, u32[]{:S(2)}) %copy-start.5) | copy-done | bytes 131096
  2.1 0.7 %copy-done.11 = s32[1,4,128]{2,1,0:T(4,128)S(1)} copy-done((s32[1,4,128]{2,1,0:T(4,128)S(1)}, s32[1,4,128]{2,1,0:T(4,128)}, u32[]{:S(2)}) %copy-start.11) | copy-done | bytes 2072
  2.8 0.3 pick.1
  3.1 2.6 %collective-permute-start.1 = (bf16[128,256]{1,0:T(8,128)(2,1)S(1)}, bf16[128,256]{1,0:T(8,128)(2,1)S(1)}, u32[]{:S(2)}, u32[]{:S(2)}) collective-permute-start(bf16[128,256]{1,0:T(8,128)(2,1)S(1)} %get-tuple-element.17), channel_id=1, source_target_pairs={{0,2},{2,0},{4,6},{6,4},{8,10},{10,8},{12,14},{14,12},{16,18},{18,... | collective-permute-start | bytes 196616 | tf_op jit(solution)/shard_map/ppermute | solution.py:359
  5.6 1.6 %collective-permute-start.2 = (bf16[128,256]{1,0:T(8,128)(2,1)S(1)}, bf16[128,256]{1,0:T(8,128)(2,1)S(1)}, u32[]{:S(2)}, u32[]{:S(2)}) collective-permute-start(bf16[128,256]{1,0:T(8,128)(2,1)S(1)} %get-tuple-element.18), channel_id=1, source_target_pairs={{0,8},{2,10},{4,12},{6,14},{8,0},{10,2},{12,4},{14,6},{16,24},{18,... | collective-permute-start | bytes 196616 | tf_op jit(solution)/shard_map/ppermute | solution.py:359
  7.2 3.4 %collective-permute-start.5 = (bf16[128,256]{1,0:T(8,128)(2,1)S(1)}, bf16[128,256]{1,0:T(8,128)(2,1)S(1)}, u32[]{:S(2)}, u32[]{:S(2)}) collective-permute-start(bf16[128,256]{1,0:T(8,128)(2,1)S(1)} %get-tuple-element.20), channel_id=1, source_target_pairs={{0,30},{2,4},{4,2},{6,8},{8,6},{10,12},{12,10},{14,16},{16,14},{18... | collective-permute-start | bytes 196616 | tf_op jit(solution)/shard_map/ppermute | solution.py:359
  10.6 1.6 %collective-permute-start.6 = (bf16[128,256]{1,0:T(8,128)(2,1)S(1)}, bf16[128,256]{1,0:T(8,128)(2,1)S(1)}, u32[]{:S(2)}, u32[]{:S(2)}) collective-permute-start(bf16[128,256]{1,0:T(8,128)(2,1)S(1)} %get-tuple-element.21), channel_id=1, source_target_pairs={{0,24},{2,26},{4,28},{6,30},{8,16},{10,18},{12,20},{14,22},{16,8},... | collective-permute-start | bytes 196616 | tf_op jit(solution)/shard_map/ppermute | solution.py:359
  12.8 0.0 copy-start.9
  12.8 0.7 %copy-done.9 = s32[3072]{0:T(1024)S(1)} copy-done((s32[3072]{0:T(1024)S(1)}, s32[3072]{0:T(1024)}, u32[]{:S(2)}) %copy-start.9) | copy-done | bytes 12312
  13.5 0.7 %copy-done.10 = s32[3072]{0:T(1024)S(1)} copy-done((s32[3072]{0:T(1024)S(1)}, s32[3072]{0:T(1024)}, u32[]{:S(2)}) %copy-start.10) | copy-done | bytes 12312
  14.3 0.9 %index.1 = (bf16[4,3072,128]{2,1,0:T(8,128)(2,1)S(1)}, f32[2,3072]{1,0:T(2,128)S(1)}) custom-call(s32[1,3072]{1,0:T(1,128)S(1)} %bitcast.2, s32[1,3072]{1,0:T(1,128)S(1)} %bitcast.3, s32[1,1]{1,0:T(1,128)S(6)} %copy.16.live_ref), custom_call_target="tpu_custom_call" | custom-call | bytes 24580 | tf_op jit(solution)/shard_map/index/pallas_call | solution.py:77
  15.2 0.1 collective-permute-start.3
  15.2 0.0 collective-permute-done.2.refs_1_
  15.2 0.5 collective-permute-start.4
  15.7 0.0 collective-permute-done.5.refs_0_
  15.7 0.1 collective-permute-start.7
  15.8 0.8 %collective-permute-done.6.refs_1_ = bf16[128,256]{1,0:T(8,128)(2,1)S(1)} collective-permute-done((bf16[128,256]{1,0:T(8,128)(2,1)S(1)}, bf16[128,256]{1,0:T(8,128)(2,1)S(1)}, u32[]{:S(2)}, u32[]{:S(2)}) %collective-permute-start.6) | collective-permute-done | bytes 65568 | tf_op jit(solution)/shard_map/ppermute | solution.py:359
  16.7 1.1 %copy-done = bf16[2,768,256]{2,1,0:T(8,128)(2,1)S(1)} copy-done((bf16[2,768,256]{2,1,0:T(8,128)(2,1)S(1)}, bf16[2,768,256]{2,1,0:T(8,128)(2,1)}, u32[]{:S(2)}) %copy-start) | copy-done | bytes 786456
  17.8 1.4 %copy-done.2 = bf16[3072,256]{1,0:T(8,128)(2,1)S(1)} copy-done((bf16[3072,256]{1,0:T(8,128)(2,1)S(1)}, bf16[3072,256]{1,0:T(8,128)(2,1)}, u32[]{:S(2)}) %copy-start.2) | copy-done | bytes 1572888
  19.2 0.9 %copy-done.6 = bf16[256,256]{1,0:T(8,128)(2,1)S(1)} copy-done((bf16[256,256]{1,0:T(8,128)(2,1)S(1)}, bf16[256,256]{1,0:T(8,128)(2,1)}, u32[]{:S(2)}) %copy-start.6) | copy-done | bytes 131096
  20.1 0.7 %copy-done.13 = f32[2,256]{1,0:T(2,128)S(1)} copy-done((f32[2,256]{1,0:T(2,128)S(1)}, f32[2,256]{1,0:T(2,128)}, u32[]{:S(2)}) %copy-start.13) | copy-done | bytes 2072
  20.8 3.5 %local.2.pre_ref = f32[3072,256]{1,0:T(8,128)S(1)} custom-call(bf16[3072,256]{1,0:T(8,128)(2,1)S(1)} %copy-done.2, bf16[4,3072,128]{2,1,0:T(8,128)(2,1)S(1)} %get-tuple-element.16.cols, bf16[256,256]{1,0:T(8,128)(2,1)S(1)} %copy-done.6, bf16[256,256]{1,0:T(8,128)(2,1)S(1)} %collective-permute-done.refs_1_.peer_ref, bf16[2,768,256]{2,1,0:T(8,128)(2,1)S(1)} %copy-done, ...), custom_call_target="tpu_custom_call" | custom-call | flops 2013265920 | bytes 5769216 | tf_op jit(solution)/shard_map/local/pallas_call | solution.py:77
  24.3 0.0 copy-start.3
  24.3 0.0 copy-start.7
  24.3 0.0 copy-start.14
  24.4 2.1 %near.2.pre_ref = f32[3072,256]{1,0:T(8,128)S(1)} custom-call(f32[3072,256]{1,0:T(8,128)S(1)} %local.2.pre_ref, bf16[4,3072,128]{2,1,0:T(8,128)(2,1)S(1)} %get-tuple-element.16.cols, bf16[2,768,256]{2,1,0:T(8,128)(2,1)S(1)} %copy-done.1, bf16[128,256]{1,0:T(8,128)(2,1)S(1)} %collective-permute-done.1.refs_0_, ...), custom_call_target="tpu_custom_call" | custom-call | flops 805306368 | bytes 7340032 | tf_op jit(solution)/shard_map/near/pallas_call | solution.py:77
  26.5 0.0 copy-start.12
  26.5 0.0 copy-start.4
  26.6 0.0 copy-start.8
  26.6 0.0 copy-start.15
  26.6 0.0 copy-start.16
  26.6 5.3 %far.2 = (bf16[3072,256]{1,0:T(8,128)(2,1)S(1)}, bf16[512,256]{1,0:T(8,128)(2,1)S(1)}) custom-call(s32[1,1]{1,0:T(1,128)S(6)} %copy.16.live_ref, f32[3072,256]{1,0:T(8,128)S(1)} %near.2.pre_ref, bf16[4,3072,128]{2,1,0:T(8,128)(2,1)S(1)} %get-tuple-element.16.cols, f32[2,3072]{1,0:T(2,128)S(1)} %get-tuple-element.19.rows, bf16[3072,256]{1,0:T(8,128)(2,1)S(1)} %copy-done.3, ...), custom_call_target="tpu_custom_call" | custom-call | flops 2013265920 | bytes 9201668 | tf_op jit(solution)/shard_map/far/pallas_call | solution.py:77
  31.9 0.6 %collective-permute-start.9 = (bf16[512,256]{1,0:T(8,128)(2,1)S(1)}, bf16[512,256]{1,0:T(8,128)(2,1)S(1)}, u32[]{:S(2)}, u32[]{:S(2)}) collective-permute-start(bf16[512,256]{1,0:T(8,128)(2,1)S(1)} %get-tuple-element.22.first), channel_id=1, source_target_pairs={{0,1},{1,0},{2,3},{3,2},{4,5},{5,4},{6,7},{7,6},{8,9},{9,8},{10,11... | collective-permute-start | bytes 786440 | tf_op jit(solution)/shard_map/ppermute | solution.py:332
  32.5 0.1 collective-permute-start.10
  32.6 1.1 %collective-permute-done.10.list_peer = s32[1,4,128]{2,1,0:T(4,128)S(1)} collective-permute-done((s32[1,4,128]{2,1,0:T(4,128)S(1)}, s32[1,4,128]{2,1,0:T(4,128)S(1)}, u32[]{:S(2)}, u32[]{:S(2)}) %collective-permute-start.10) | collective-permute-done | bytes 2080 | tf_op jit(solution)/shard_map/ppermute | solution.py:332
  33.7 1.1 %nodes.1 = (bf16[512,256]{1,0:T(8,128)(2,1)S(1)}, bf16[256,256]{1,0:T(8,128)(2,1)S(1)}, bf16[256,256]{1,0:T(8,128)(2,1)S(1)}) custom-call(bf16[256,256]{1,0:T(8,128)(2,1)S(1)} %copy-done.6, bf16[256,256]{1,0:T(8,128)(2,1)S(1)} %collective-permute-done.refs_1_.peer_ref, bf16[512,256]{1,0:T(8,128)(2,1)S(1)} %get-tuple-element.22.first, ...), custom_call_target="tpu_custom_call" | custom-call | bytes 1581056 | tf_op jit(solution)/shard_map/nodes/pallas_call | solution.py:77
  34.7 0.1 collective-permute-start.11
  34.8 2.7 %collective-permute-start.13 = (bf16[256,256]{1,0:T(8,128)(2,1)S(1)}, bf16[256,256]{1,0:T(8,128)(2,1)S(1)}, u32[]{:S(2)}, u32[]{:S(2)}) collective-permute-start(bf16[256,256]{1,0:T(8,128)(2,1)S(1)} %get-tuple-element.26), channel_id=1, source_target_pairs={{0,30},{2,4},{4,2},{6,8},{8,6},{10,12},{12,10},{14,16},{16,14},{18... | collective-permute-start | bytes 393224 | tf_op jit(solution)/shard_map/ppermute | solution.py:364
  37.5 2.3 %collective-permute-done.11.refs_0_ = bf16[256,256]{1,0:T(8,128)(2,1)S(1)} collective-permute-done((bf16[256,256]{1,0:T(8,128)(2,1)S(1)}, bf16[256,256]{1,0:T(8,128)(2,1)S(1)}, u32[]{:S(2)}, u32[]{:S(2)}) %collective-permute-start.11) | collective-permute-done | bytes 131104 | tf_op jit(solution)/shard_map/ppermute | solution.py:364
  39.8 0.1 collective-permute-start.12
  39.9 3.7 %collective-permute-done.13.refs_0_ = bf16[256,256]{1,0:T(8,128)(2,1)S(1)} collective-permute-done((bf16[256,256]{1,0:T(8,128)(2,1)S(1)}, bf16[256,256]{1,0:T(8,128)(2,1)S(1)}, u32[]{:S(2)}, u32[]{:S(2)}) %collective-permute-start.13) | collective-permute-done | bytes 131104 | tf_op jit(solution)/shard_map/ppermute | solution.py:364
  43.6 3.5 %local.3.pre_ref = f32[3072,256]{1,0:T(8,128)S(1)} custom-call(bf16[3072,256]{1,0:T(8,128)(2,1)S(1)} %get-tuple-element.24.edge_ref, bf16[4,3072,128]{2,1,0:T(8,128)(2,1)S(1)} %get-tuple-element.16.cols, bf16[512,256]{1,0:T(8,128)(2,1)S(1)} %get-tuple-element.23.refs_0_.nodes_ref, bf16[2,768,256]{2,1,0:T(8,128)(2,1)S(1)} %copy-done.1, f32[2,256]{1,0:T(2,128)S(1)} %copy-done.13), custom_call_target="tpu_custom_call" | custom-call | flops 2013265920 | bytes 5769216 | tf_op jit(solution)/shard_map/local/pallas_call | solution.py:77
  47.0 2.1 %near.3.pre_ref = f32[3072,256]{1,0:T(8,128)S(1)} custom-call(f32[3072,256]{1,0:T(8,128)S(1)} %local.3.pre_ref, bf16[4,3072,128]{2,1,0:T(8,128)(2,1)S(1)} %get-tuple-element.16.cols, bf16[2,768,256]{2,1,0:T(8,128)(2,1)S(1)} %copy-done.1, bf16[256,256]{1,0:T(8,128)(2,1)S(1)} %collective-permute-done.11.refs_0_, ...), custom_call_target="tpu_custom_call" | custom-call | flops 805306368 | bytes 7340032 | tf_op jit(solution)/shard_map/near/pallas_call | solution.py:77
  49.2 5.5 %far.3 = (bf16[3072,256]{1,0:T(8,128)(2,1)}, bf16[256,256]{1,0:T(8,128)(2,1)S(1)}, bf16[256,256]{1,0:T(8,128)(2,1)S(1)}) custom-call(s32[1,1]{1,0:T(1,128)S(6)} %copy.16.live_ref, f32[3072,256]{1,0:T(8,128)S(1)} %near.3.pre_ref, bf16[4,3072,128]{2,1,0:T(8,128)(2,1)S(1)} %get-tuple-element.16.cols, f32[2,3072]{1,0:T(2,128)S(1)} %get-tuple-element.19.rows, ...), custom_call_target="tpu_custom_call" | custom-call | flops 2013265920 | bytes 9201668 | tf_op jit(solution)/shard_map/far/pallas_call | solution.py:77
  54.6 0.5 collective-permute-start.15
  55.2 1.0 %collective-permute-done.15.second = bf16[256,256]{1,0:T(8,128)(2,1)S(1)} collective-permute-done((bf16[256,256]{1,0:T(8,128)(2,1)S(1)}, bf16[256,256]{1,0:T(8,128)(2,1)S(1)}, u32[]{:S(2)}, u32[]{:S(2)}) %collective-permute-start.15) | collective-permute-done | bytes 131104 | tf_op jit(solution)/shard_map/ppermute | solution.py:332
  56.2 1.2 %last.1 = bf16[256,256]{1,0:T(8,128)(2,1)} custom-call(bf16[512,256]{1,0:T(8,128)(2,1)S(1)} %get-tuple-element.23.refs_0_.nodes_ref, bf16[256,256]{1,0:T(8,128)(2,1)S(1)} %get-tuple-element.27.first, bf16[256,256]{1,0:T(8,128)(2,1)S(1)} %collective-permute-done.15.second, bf16[2,512,256]{2,1,0:T(8,128)(2,1)S(1)} %copy-done.4, f32[2,256]{1,0:T(2,128)S(1)} %copy-done.15, ...), custom_call_target="tpu_custom_call" | custom-call | bytes 1314816 | tf_op jit(solution)/shard_map/last/pallas_call | solution.py:77
  (28 shorter events, 0.1 us)
Async XLA Ops:
  0.6 16.0 %collective-permute-start = (bf16[256,256]{1,0:T(8,128)(2,1)}, bf16[256,256]{1,0:T(8,128)(2,1)S(1)}, u32[]{:S(2)}, u32[]{:S(2)}) collective-permute-start(bf16[256,256]{1,0:T(8,128)(2,1)} %own_ref.1), channel_id=1, source_target_pairs={{0,1},{1,0},{2,3},{3,2},{4,5},{5,4},{6,7},{7,6},{8,9},{9,8},{10,11... | collective-permute-start | bytes 393224 | tf_op jit(solution)/shard_map/ppermute | solution.py:332
  1.2 0.9 %copy-start.5 = (bf16[256,256]{1,0:T(8,128)(2,1)S(1)}, bf16[256,256]{1,0:T(8,128)(2,1)}, u32[]{:S(2)}) copy-start(bf16[256,256]{1,0:T(8,128)(2,1)} %own_ref.1) | copy-start | bytes 393220
  2.1 0.7 %copy-start.11 = (s32[1,4,128]{2,1,0:T(4,128)S(1)}, s32[1,4,128]{2,1,0:T(4,128)}, u32[]{:S(2)}) copy-start(s32[1,4,128]{2,1,0:T(4,128)} %list_own.1) | copy-start | bytes 6148
  3.1 12.1 %collective-permute-start.1 = (bf16[128,256]{1,0:T(8,128)(2,1)S(1)}, bf16[128,256]{1,0:T(8,128)(2,1)S(1)}, u32[]{:S(2)}, u32[]{:S(2)}) collective-permute-start(bf16[128,256]{1,0:T(8,128)(2,1)S(1)} %get-tuple-element.17), channel_id=1, source_target_pairs={{0,2},{2,0},{4,6},{6,4},{8,10},{10,8},{12,14},{14,12},{16,18},{18,... | collective-permute-start | bytes 196616 | tf_op jit(solution)/shard_map/ppermute | solution.py:359
  5.6 9.6 %collective-permute-start.2 = (bf16[128,256]{1,0:T(8,128)(2,1)S(1)}, bf16[128,256]{1,0:T(8,128)(2,1)S(1)}, u32[]{:S(2)}, u32[]{:S(2)}) collective-permute-start(bf16[128,256]{1,0:T(8,128)(2,1)S(1)} %get-tuple-element.18), channel_id=1, source_target_pairs={{0,8},{2,10},{4,12},{6,14},{8,0},{10,2},{12,4},{14,6},{16,24},{18,... | collective-permute-start | bytes 196616 | tf_op jit(solution)/shard_map/ppermute | solution.py:359
  7.2 8.5 %collective-permute-start.5 = (bf16[128,256]{1,0:T(8,128)(2,1)S(1)}, bf16[128,256]{1,0:T(8,128)(2,1)S(1)}, u32[]{:S(2)}, u32[]{:S(2)}) collective-permute-start(bf16[128,256]{1,0:T(8,128)(2,1)S(1)} %get-tuple-element.20), channel_id=1, source_target_pairs={{0,30},{2,4},{4,2},{6,8},{8,6},{10,12},{12,10},{14,16},{16,14},{18... | collective-permute-start | bytes 196616 | tf_op jit(solution)/shard_map/ppermute | solution.py:359
  10.6 6.1 %collective-permute-start.6 = (bf16[128,256]{1,0:T(8,128)(2,1)S(1)}, bf16[128,256]{1,0:T(8,128)(2,1)S(1)}, u32[]{:S(2)}, u32[]{:S(2)}) collective-permute-start(bf16[128,256]{1,0:T(8,128)(2,1)S(1)} %get-tuple-element.21), channel_id=1, source_target_pairs={{0,24},{2,26},{4,28},{6,30},{8,16},{10,18},{12,20},{14,22},{16,8},... | collective-permute-start | bytes 196616 | tf_op jit(solution)/shard_map/ppermute | solution.py:359
  12.8 0.7 %copy-start.9 = (s32[3072]{0:T(1024)S(1)}, s32[3072]{0:T(1024)}, u32[]{:S(2)}) copy-start(s32[3072]{0:T(1024)} %param.16) | copy-start | bytes 36868
  13.5 0.7 %copy-start.10 = (s32[3072]{0:T(1024)S(1)}, s32[3072]{0:T(1024)}, u32[]{:S(2)}) copy-start(s32[3072]{0:T(1024)} %param.17) | copy-start | bytes 36868
  15.2 9.2 %collective-permute-start.3 = (bf16[128,256]{1,0:T(8,128)(2,1)S(1)}, bf16[128,256]{1,0:T(8,128)(2,1)S(1)}, u32[]{:S(2)}, u32[]{:S(2)}) collective-permute-start(bf16[128,256]{1,0:T(8,128)(2,1)S(1)} %collective-permute-done.1.refs_0_), channel_id=1, source_target_pairs={{0,1},{1,0},{2,3},{3,2},{4,5},{5,4},{6,7},{7,6},{8,9},{9,8},{10,11... | collective-permute-start | bytes 196616 | tf_op jit(solution)/shard_map/ppermute | solution.py:332
  15.2 9.1 %collective-permute-start.4 = (bf16[128,256]{1,0:T(8,128)(2,1)S(1)}, bf16[128,256]{1,0:T(8,128)(2,1)S(1)}, u32[]{:S(2)}, u32[]{:S(2)}) collective-permute-start(bf16[128,256]{1,0:T(8,128)(2,1)S(1)} %collective-permute-done.2.refs_1_), channel_id=1, source_target_pairs={{0,1},{1,0},{2,3},{3,2},{4,5},{5,4},{6,7},{7,6},{8,9},{9,8},{10,11... | collective-permute-start | bytes 196616 | tf_op jit(solution)/shard_map/ppermute | solution.py:332
  15.7 10.7 %collective-permute-start.7 = (bf16[128,256]{1,0:T(8,128)(2,1)S(1)}, bf16[128,256]{1,0:T(8,128)(2,1)S(1)}, u32[]{:S(2)}, u32[]{:S(2)}) collective-permute-start(bf16[128,256]{1,0:T(8,128)(2,1)S(1)} %collective-permute-done.5.refs_0_), channel_id=1, source_target_pairs={{0,1},{1,0},{2,3},{3,2},{4,5},{5,4},{6,7},{7,6},{8,9},{9,8},{10,11... | collective-permute-start | bytes 196616 | tf_op jit(solution)/shard_map/ppermute | solution.py:332
  16.7 9.8 %collective-permute-start.8 = (bf16[128,256]{1,0:T(8,128)(2,1)S(1)}, bf16[128,256]{1,0:T(8,128)(2,1)S(1)}, u32[]{:S(2)}, u32[]{:S(2)}) collective-permute-start(bf16[128,256]{1,0:T(8,128)(2,1)S(1)} %collective-permute-done.6.refs_1_), channel_id=1, source_target_pairs={{0,1},{1,0},{2,3},{3,2},{4,5},{5,4},{6,7},{7,6},{8,9},{9,8},{10,11... | collective-permute-start | bytes 196616 | tf_op jit(solution)/shard_map/ppermute | solution.py:332
  16.7 1.1 %copy-start = (bf16[2,768,256]{2,1,0:T(8,128)(2,1)S(1)}, bf16[2,768,256]{2,1,0:T(8,128)(2,1)}, u32[]{:S(2)}) copy-start(bf16[2,768,256]{2,1,0:T(8,128)(2,1)} %w1_ref.7) | copy-start | bytes 2359300
  17.8 1.4 %copy-start.2 = (bf16[3072,256]{1,0:T(8,128)(2,1)S(1)}, bf16[3072,256]{1,0:T(8,128)(2,1)}, u32[]{:S(2)}) copy-start(bf16[3072,256]{1,0:T(8,128)(2,1)} %edge_ref.3) | copy-start | bytes 4718596
  19.2 0.9 %copy-start.6 = (bf16[256,256]{1,0:T(8,128)(2,1)S(1)}, bf16[256,256]{1,0:T(8,128)(2,1)}, u32[]{:S(2)}) copy-start(bf16[256,256]{1,0:T(8,128)(2,1)} %own_ref.1) | copy-start | bytes 393220
  20.1 0.7 %copy-start.13 = (f32[2,256]{1,0:T(2,128)S(1)}, f32[2,256]{1,0:T(2,128)}, u32[]{:S(2)}) copy-start(f32[2,256]{1,0:T(2,128)} %refs_2_.3) | copy-start | bytes 6148
  20.8 3.6 %copy-start.1 = (bf16[2,768,256]{2,1,0:T(8,128)(2,1)S(1)}, bf16[2,768,256]{2,1,0:T(8,128)(2,1)}, u32[]{:S(2)}) copy-start(bf16[2,768,256]{2,1,0:T(8,128)(2,1)} %w1_ref.7) | copy-start | bytes 2359300
  24.3 2.2 %copy-start.3 = (bf16[3072,256]{1,0:T(8,128)(2,1)S(1)}, bf16[3072,256]{1,0:T(8,128)(2,1)}, u32[]{:S(2)}) copy-start(bf16[3072,256]{1,0:T(8,128)(2,1)} %edge_ref.3) | copy-start | bytes 4718596
  24.3 2.2 %copy-start.7 = (bf16[2,256,256]{2,1,0:T(8,128)(2,1)S(1)}, bf16[2,256,256]{2,1,0:T(8,128)(2,1)}, u32[]{:S(2)}) copy-start(bf16[2,256,256]{2,1,0:T(8,128)(2,1)} %w2_ref.3) | copy-start | bytes 786436
  24.3 2.2 %copy-start.14 = (f32[2,256]{1,0:T(2,128)S(1)}, f32[2,256]{1,0:T(2,128)}, u32[]{:S(2)}) copy-start(f32[2,256]{1,0:T(2,128)} %gain_ref.3) | copy-start | bytes 6148
  26.5 6.0 %copy-start.12 = (s32[1,4,128]{2,1,0:T(4,128)S(1)}, s32[1,4,128]{2,1,0:T(4,128)}, u32[]{:S(2)}) copy-start(s32[1,4,128]{2,1,0:T(4,128)} %list_own.1) | copy-start | bytes 6148
  26.5 7.1 %copy-start.4 = (bf16[2,512,256]{2,1,0:T(8,128)(2,1)S(1)}, bf16[2,512,256]{2,1,0:T(8,128)(2,1)}, u32[]{:S(2)}) copy-start(bf16[2,512,256]{2,1,0:T(8,128)(2,1)} %w1.3) | copy-start | bytes 1572868
  26.6 7.1 %copy-start.8 = (bf16[2,256,256]{2,1,0:T(8,128)(2,1)S(1)}, bf16[2,256,256]{2,1,0:T(8,128)(2,1)}, u32[]{:S(2)}) copy-start(bf16[2,256,256]{2,1,0:T(8,128)(2,1)} %w2.3) | copy-start | bytes 786436
  26.6 7.1 %copy-start.15 = (f32[2,256]{1,0:T(2,128)S(1)}, f32[2,256]{1,0:T(2,128)}, u32[]{:S(2)}) copy-start(f32[2,256]{1,0:T(2,128)} %b1.3) | copy-start | bytes 6148
  26.6 7.1 %copy-start.16 = (f32[2,256]{1,0:T(2,128)S(1)}, f32[2,256]{1,0:T(2,128)}, u32[]{:S(2)}) copy-start(f32[2,256]{1,0:T(2,128)} %gain.3) | copy-start | bytes 6148
  31.9 1.7 %collective-permute-start.9 = (bf16[512,256]{1,0:T(8,128)(2,1)S(1)}, bf16[512,256]{1,0:T(8,128)(2,1)S(1)}, u32[]{:S(2)}, u32[]{:S(2)}) collective-permute-start(bf16[512,256]{1,0:T(8,128)(2,1)S(1)} %get-tuple-element.22.first), channel_id=1, source_target_pairs={{0,1},{1,0},{2,3},{3,2},{4,5},{5,4},{6,7},{7,6},{8,9},{9,8},{10,11... | collective-permute-start | bytes 786440 | tf_op jit(solution)/shard_map/ppermute | solution.py:332
  32.5 1.2 %collective-permute-start.10 = (s32[1,4,128]{2,1,0:T(4,128)S(1)}, s32[1,4,128]{2,1,0:T(4,128)S(1)}, u32[]{:S(2)}, u32[]{:S(2)}) collective-permute-start(s32[1,4,128]{2,1,0:T(4,128)S(1)} %copy-done.12), channel_id=1, source_target_pairs={{0,1},{1,0},{2,3},{3,2},{4,5},{5,4},{6,7},{7,6},{8,9},{9,8},{10,11... | collective-permute-start | bytes 6152 | tf_op jit(solution)/shard_map/ppermute | solution.py:332
  34.7 5.0 %collective-permute-start.11 = (bf16[256,256]{1,0:T(8,128)(2,1)S(1)}, bf16[256,256]{1,0:T(8,128)(2,1)S(1)}, u32[]{:S(2)}, u32[]{:S(2)}) collective-permute-start(bf16[256,256]{1,0:T(8,128)(2,1)S(1)} %get-tuple-element.25), channel_id=1, source_target_pairs={{0,2},{2,0},{4,6},{6,4},{8,10},{10,8},{12,14},{14,12},{16,18},{18,... | collective-permute-start | bytes 393224 | tf_op jit(solution)/shard_map/ppermute | solution.py:364
  34.8 8.7 %collective-permute-start.13 = (bf16[256,256]{1,0:T(8,128)(2,1)S(1)}, bf16[256,256]{1,0:T(8,128)(2,1)S(1)}, u32[]{:S(2)}, u32[]{:S(2)}) collective-permute-start(bf16[256,256]{1,0:T(8,128)(2,1)S(1)} %get-tuple-element.26), channel_id=1, source_target_pairs={{0,30},{2,4},{4,2},{6,8},{8,6},{10,12},{12,10},{14,16},{16,14},{18... | collective-permute-start | bytes 393224 | tf_op jit(solution)/shard_map/ppermute | solution.py:364
  39.8 7.3 %collective-permute-start.12 = (bf16[256,256]{1,0:T(8,128)(2,1)S(1)}, bf16[256,256]{1,0:T(8,128)(2,1)S(1)}, u32[]{:S(2)}, u32[]{:S(2)}) collective-permute-start(bf16[256,256]{1,0:T(8,128)(2,1)S(1)} %collective-permute-done.11.refs_0_), channel_id=1, source_target_pairs={{0,1},{1,0},{2,3},{3,2},{4,5},{5,4},{6,7},{7,6},{8,9},{9,8},{10,11... | collective-permute-start | bytes 393224 | tf_op jit(solution)/shard_map/ppermute | solution.py:332
  43.5 5.6 %collective-permute-start.14 = (bf16[256,256]{1,0:T(8,128)(2,1)S(1)}, bf16[256,256]{1,0:T(8,128)(2,1)S(1)}, u32[]{:S(2)}, u32[]{:S(2)}) collective-permute-start(bf16[256,256]{1,0:T(8,128)(2,1)S(1)} %collective-permute-done.13.refs_0_), channel_id=1, source_target_pairs={{0,1},{1,0},{2,3},{3,2},{4,5},{5,4},{6,7},{7,6},{8,9},{9,8},{10,11... | collective-permute-start | bytes 393224 | tf_op jit(solution)/shard_map/ppermute | solution.py:332
  54.6 1.5 %collective-permute-start.15 = (bf16[256,256]{1,0:T(8,128)(2,1)S(1)}, bf16[256,256]{1,0:T(8,128)(2,1)S(1)}, u32[]{:S(2)}, u32[]{:S(2)}) collective-permute-start(bf16[256,256]{1,0:T(8,128)(2,1)S(1)} %get-tuple-element.28), channel_id=1, source_target_pairs={{0,1},{1,0},{2,3},{3,2},{4,5},{5,4},{6,7},{7,6},{8,9},{9,8},{10,11... | collective-permute-start | bytes 393224 | tf_op jit(solution)/shard_map/ppermute | solution.py:332

commit v2 on v1

--- a/solution.py
+++ b/solution.py
@@ -66,18 +66,21 @@
 ROWS = 512
 IN_VMEM = pl.BlockSpec(memory_space=pltpu.VMEM)
 IN_SMEM = pl.BlockSpec(memory_space=pltpu.SMEM)
+IN_HBM = pl.BlockSpec(memory_space=pltpu.HBM)
 
 
 def shaped(shape, dtype):
     return jax.ShapeDtypeStruct(shape, dtype)
 
 
-def call(kernel, outs, args, scratch=(), smem=(), flops=0, limit=24, name=None):
+def call(kernel, outs, args, scratch=(), smem=(), stay=(), flops=0, limit=24, name=None):
     nbytes = sum(a.size * a.dtype.itemsize for a in args)
     return pl.pallas_call(
         kernel,
         out_shape=outs,
-        in_specs=[IN_SMEM if k in smem else IN_VMEM for k in range(len(args))],
+        in_specs=[
+            IN_SMEM if k in smem else IN_HBM if k in stay else IN_VMEM for k in range(len(args))
+        ],
         out_specs=jax.tree.map(lambda _: IN_VMEM, outs),
         scratch_shapes=scratch,
         compiler_params=pltpu.CompilerParams(vmem_limit_bytes=limit << 20),
@@ -111,21 +114,33 @@
     return pl.ds(pl.multiple_of(start, size), size)
 
 
-def pick_kernel(stride, nodes_ref, lists_ref, far_d, far_s, near_d, near_s):
+def face_rows(stride, lists, nodes, far, near):
+    core, par_d, par_s = place(stride)
+    par = jnp.where(core == 0, par_d, par_s)
+    for face, ref in ((2 * core + 1 - par, far), (2 * core + par, near)):
+        for n in range(2):
+            hot = one_hot_rows(lists[n][0, pl.ds(face, 1), :])
+            ref[n * HALF : (n + 1) * HALF, :] = mm(hot, nodes[n]()).astype(BF16)
+
+
+def pick_kernel(stride, own_ref, peer_ref, list_own, list_peer, far, near):
+    nodes = (lambda: own_ref[...]), (lambda: peer_ref[...])
+    face_rows(stride, (list_own, list_peer), nodes, far, near)
+
+
+def index_kernel(stride, edges, loads, live_ref, *refs):
+    hbm, (cols, rows), refs = refs[: loads + 2], refs[loads + 2 : loads + 4], refs[loads + 4 :]
+    vmem, (send_ref, recv_ref, sems) = refs[:loads], refs[loads:]
+    copies = [
+        pltpu.make_async_copy(src, dst, sems.at[k])
+        for k, (src, dst) in enumerate(zip(hbm, (send_ref, recv_ref, *vmem)))
+    ]
+    for copy in copies:
+        copy.start()
     _, par_d, par_s = place(stride)
-    nodes = nodes_ref[...]
-    for face, out in (
-        (1 - par_d, far_d),
-        (3 - par_s, far_s),
-        (par_d, near_d),
-        (2 + par_s, near_s),
-    ):
-        out[...] = mm(one_hot_rows(lists_ref[0, pl.ds(face, 1), :]), nodes).astype(BF16)
-
-
-def index_kernel(stride, edges, send_ref, recv_ref, live_ref, cols, rows):
-    _, par_d, par_s = place(stride)
-    live = live_ref[0, 0]
+    for copy in copies[:2]:
+        copy.wait()
+    live = jnp.broadcast_to(live_ref[...], (1, HALF))
     lane = lax.broadcasted_iota(jnp.int32, (1, HALF), 1)
     for k in range(edges // HALF):
         at = pl.ds(k * HALF, HALF)
@@ -150,6 +165,9 @@
         cols[3, at, :] = column(lo).astype(BF16)
         rows[0:1, at] = jnp.where(lane + k * HALF < live, hi, -1).astype(F32)
         rows[1:2, at] = lo.astype(F32)
+    rows[2:3, :] = jnp.concatenate([live] * (edges // HALF), axis=1).astype(F32)
+    for copy in copies[2:]:
+        copy.wait()
 
 
 def lane_iota(rows):
@@ -198,29 +216,15 @@
     lax.fori_loop(0, edge_ref.shape[0] // ROWS, step, 0)
 
 
-def halo_tables(layer, first, halves, w1_ref, refs, table):
+def halo_tables(layer, own, peer, w1_ref, table):
     core = lax.axis_index("edge")
     w_s = w1_ref[layer, TILE : 2 * TILE, :]
-    if halves:
-        own_d, own_s, peer_d, peer_s = refs
-        for axis, owner, ref in (
-            (0, core, own_d),
-            (1, core, own_s),
-            (0, 1 - core, peer_d),
-            (1, 1 - core, peer_s),
-        ):
-            row = axis * TILE + lax.rem(owner + axis, 2) * HALF
-            table[dyn(row, HALF), :] = mm(ref[...], w_s).astype(BF16)
-    else:
-        own, peer = refs
-        for axis, ref in ((core, own), (1 - core, peer)):
-            table[dyn(axis * TILE, TILE), :] = mm(ref[...], w_s).astype(BF16)
-    return first, first + 1
-
-
-def near_kernel(layer, halves, pre_ref, cols, w1_ref, *refs):
-    refs, (out_ref, table) = refs[:-2], refs[-2:]
-    tiles = halo_tables(layer, 2, halves, w1_ref, refs, table)
+    for axis, ref in ((core, own), (1 - core, peer)):
+        table[dyn(axis * TILE, TILE), :] = mm(ref[...], w_s).astype(BF16)
+
+
+def near_kernel(layer, pre_ref, cols, w1_ref, own, peer, out_ref, table):
+    halo_tables(layer, own, peer, w1_ref, table)
     lanes = lane_iota(ROWS)
 
     def step(k, carry):
@@ -228,9 +232,9 @@
         hi = cols[0, at, :]
         lo = cols[1, at, :]
         acc = pre_ref[at, :]
-        for n, tile in enumerate(tiles):
+        for n in range(2):
             acc = acc + mm(
-                hits(hi, lo, jnp.asarray(tile, BF16), lanes), table[n * TILE : (n + 1) * TILE, :]
+                hits(hi, lo, jnp.asarray(2 + n, BF16), lanes), table[n * TILE : (n + 1) * TILE, :]
             )
         out_ref[at, :] = acc
         return carry
@@ -238,14 +242,16 @@
     lax.fori_loop(0, pre_ref.shape[0] // ROWS, step, 0)
 
 
-def edge_kernel(layer, halves, split, live_ref, pre_ref, cols, rows, edge_ref, w1_ref, w2_ref, gain_ref, *refs):
+def edge_kernel(
+    layer, split, pre_ref, cols, rows, edge_ref, w1_ref, w2_ref, gain_ref, own, peer, out_ref, *refs
+):
     if split:
-        refs, (out_ref, keep_ref, give_ref, table, msgs) = refs[:-5], refs[-5:]
+        keep_ref, give_ref, table, msgs = refs
     else:
-        refs, (out_ref, part_ref, table, msgs) = refs[:-4], refs[-4:]
-    tiles = halo_tables(layer, 4, halves, w1_ref, refs, table)
+        part_ref, table, msgs = refs
+    halo_tables(layer, own, peer, w1_ref, table)
     lanes = lane_iota(ROWS)
-    live = live_ref[0, 0]
+    live = jnp.broadcast_to(rows[2:3, 0:TILE], (ROWS, TILE)).astype(jnp.int32)
     gain = gain_ref[layer : layer + 1, :]
     w2 = w2_ref[layer]
     place_in = lax.broadcasted_iota(jnp.int32, (ROWS, TILE), 0)
@@ -255,9 +261,9 @@
         hi = cols[0, at, :]
         lo = cols[1, at, :]
         acc = pre_ref[at, :]
-        for n, tile in enumerate(tiles):
+        for n in range(2):
             acc = acc + mm(
-                hits(hi, lo, jnp.asarray(tile, BF16), lanes), table[n * TILE : (n + 1) * TILE, :]
+                hits(hi, lo, jnp.asarray(4 + n, BF16), lanes), table[n * TILE : (n + 1) * TILE, :]
             )
         hidden = jnp.maximum(acc, 0.0).astype(BF16)
         message = layer_norm(mm(hidden, w2), gain)
@@ -303,15 +309,15 @@
 def node_kernel(
     stride, layer, own_ref, peer_ref, first, second, list_own, list_peer, w1, b1, w2, gain, out, far, near
 ):
-    core, par_d, par_s = place(stride)
+    core = lax.axis_index("edge")
     for owner, ref in ((core, own_ref), (1 - core, peer_ref)):
         at = dyn(owner * TILE, TILE)
         out[at, :] = updated(layer, ref[...], first[at, :], second[at, :], w1, b1, w2, gain)
-    par = jnp.where(core == 0, par_d, par_s)
-    for face, ref in ((2 * core + 1 - par, far), (2 * core + par, near)):
-        for n, (owner, lists) in enumerate(((core, list_own), (1 - core, list_peer))):
-            hot = one_hot_rows(lists[0, pl.ds(face, 1), :])
-            ref[n * HALF : (n + 1) * HALF, :] = mm(hot, out[dyn(owner * TILE, TILE), :]).astype(BF16)
+    nodes = [
+        functools.partial(out.__getitem__, (dyn(owner * TILE, TILE), slice(None)))
+        for owner in (core, 1 - core)
+    ]
+    face_rows(stride, (list_own, list_peer), nodes, far, near)
 
 
 def last_kernel(layer, nodes_ref, first, second, w1, b1, w2, gain, out):
@@ -355,49 +361,41 @@
     near_d, far_d = met(domains, 1, 0), met(domains, 1, 1)
     near_s, far_s = met(domains, stride, 0), met(domains, stride, 1)
 
-    def sent(value, partner):
-        return lax.ppermute(value, "dom", list(enumerate(partner)))
-
     def sent_by_core(value, partner_d, partner_s):
         pairs = [(2 * d, 2 * p) for d, p in enumerate(partner_d)]
         pairs += [(2 * d + 1, 2 * p + 1) for d, p in enumerate(partner_s)]
         return lax.ppermute(value, ("dom", "edge"), pairs)
 
-    face = shaped((HALF, width), BF16)
     table = pltpu.VMEM((2 * TILE, width), BF16)
     messages = pltpu.VMEM((edges, width), BF16)
     pre_shape = shaped((edges, width), F32)
+    rows_out = shaped((TILE, width), BF16)
     pass_flops = 2 * edges * TILE * width
 
-    picked = call(
-        functools.partial(pick_kernel, stride), [face] * 4, (node_lat, send_rows), name="pick"
-    )
-    halo = [
-        sent(value, partner) for value, partner in zip(picked, (far_d, far_s, near_d, near_s))
-    ]
     peer_nodes = swapped(node_lat)
     peer_lists = swapped(send_rows)
-    cols, rows = call(
-        functools.partial(index_kernel, stride, edges),
-        [shaped((4, edges, HALF), BF16), shaped((2, edges), F32)],
-        (senders[None], receivers[None], live_edges),
-        smem=(2,),
+    loads = (edge_lat, edge_w1, edge_w2, node_w1, node_w2, edge_b1, edge_gain, node_b1, node_gain)
+    hbm = [pltpu.with_memory_space_constraint(a, pltpu.HBM) for a in (senders[None], receivers[None], *loads)]
+    cols, rows, edge_rows, edge_w1, edge_w2, node_w1, node_w2, edge_b1, edge_gain, node_b1, node_gain = call(
+        functools.partial(index_kernel, stride, edges, len(loads)),
+        [shaped((4, edges, HALF), BF16), shaped((3, edges), F32)]
+        + [shaped(a.shape, a.dtype) for a in loads],
+        (live_edges, *hbm),
+        scratch=[pltpu.VMEM((1, edges), jnp.int32)] * 2 + [pltpu.SemaphoreType.DMA((len(hbm),))],
+        stay=range(1, len(hbm) + 1),
         name="index",
     )
-    own_nodes = node_lat
-    edge_rows = edge_lat
+    far_rows, near_rows = call(
+        functools.partial(pick_kernel, stride),
+        [rows_out, rows_out],
+        (node_lat, peer_nodes, send_rows, peer_lists),
+        name="pick",
+    )
     for layer in range(LAYERS):
         last = layer == LAYERS - 1
-        if layer == 0:
-            node_args = (node_lat, peer_nodes)
-            far = (halo[0], halo[1], swapped(halo[0]), swapped(halo[1]))
-            near = (halo[2], halo[3], swapped(halo[2]), swapped(halo[3]))
-        else:
-            node_args = (all_nodes,)
-            far = sent_by_core(far_rows, far_d, far_s)
-            near = sent_by_core(near_rows, near_d, near_s)
-            far = (far, swapped(far))
-            near = (near, swapped(near))
+        node_args = (all_nodes,) if layer else (node_lat, peer_nodes)
+        far = sent_by_core(far_rows, far_d, far_s)
+        near = sent_by_core(near_rows, near_d, near_s)
         pre = call(
             functools.partial(local_kernel, layer, layer > 0),
             pre_shape,
@@ -406,8 +404,11 @@
             flops=5 * pass_flops,
             name="local",
         )
+        pre, near, far = lax.optimization_barrier((pre, near, far))
+        near = (near, swapped(near))
+        far = (far, swapped(far))
         pre = call(
-            functools.partial(near_kernel, layer, layer == 0),
+            functools.partial(near_kernel, layer),
             pre_shape,
             (pre, cols, edge_w1, *near),
             scratch=[table],
@@ -419,11 +420,10 @@
         else:
             outs = [shaped((2 * nodes, width), BF16)]
         edge_rows, *partial = call(
-            functools.partial(edge_kernel, layer, layer == 0, last),
+            functools.partial(edge_kernel, layer, last),
             [shaped((edges, width), BF16)] + outs,
-            (live_edges, pre, cols, rows, edge_rows, edge_w1, edge_w2, edge_gain, *far),
+            (pre, cols, rows, edge_rows, edge_w1, edge_w2, edge_gain, *far),
             scratch=[table, messages],
-            smem=(0,),
             flops=5 * pass_flops,
             name="far",
         )
@@ -437,7 +437,6 @@
                 name="last",
             )
         else:
-            rows_out = shaped((TILE, width), BF16)
             all_nodes, far_rows, near_rows = call(
                 functools.partial(node_kernel, stride, layer),
                 [shaped((2 * nodes, width), BF16), rows_out, rows_out],

time: 57.8 us -> 49 us (0.85)
  local copies, waits for them, and re-layouts: 7.17 us -> 0.01 us
  waiting for transfers between devices: 8.87 us -> 7.34 us
  Pallas kernels: 25.4 us -> 26.7 us
  starting transfers between devices: 14.4 us -> 13.3 us
    ppermute x4 -> x0, starting transfers between devices: 9.11 us -> none  [sent(): return lax.ppermute(value, 'dom', list(enumerate(partner)))]
    ppermute x2 -> x4, starting transfers between devices: 2.75 us -> 11.3 us  [sent_by_core(): return lax.ppermute(value, ('dom', 'edge'), pairs)]
    unnamed x34 -> x4, local copies, waits for them, and re-layouts: 7.17 us -> 0.01 us
    ppermute x2 -> x4, waiting for transfers between devices: 5.93 us -> 3.06 us  [sent_by_core(): return lax.ppermute(value, ('dom', 'edge'), pairs)]
    ppermute x10 -> x8, waiting for transfers between devices: 2.08 us -> 4.27 us  [swapped(): return lax.ppermute(value, 'edge', [(0, 1), (1, 0)])]
    pallas_call x10, Pallas kernels: 25.4 us -> 26.7 us  [call(): pl.pallas_call(kernel, out_shape=outs, in_specs=[IN_SMEM if k in smem els...]
    ppermute x4 -> x0, waiting for transfers between devices: 0.85 us -> none  [sent(): return lax.ppermute(value, 'dom', list(enumerate(partner)))]
    ppermute x10 -> x8, starting transfers between devices: 2.5 us -> 2.02 us  [swapped(): return lax.ppermute(value, 'edge', [(0, 1), (1, 0)])]
  transfers between devices with their start and end apart: 16 -> 12, of which waited for: 5 -> 6; matrix products, arithmetic and copies ran while one was open for 0% -> 0% of each run, Pallas kernels for 22% -> 27%
where the time goes in v2:
time: 49 us; the launch traced here: 48.8 us
  Pallas kernels  26.7 us (54%)
  starting transfers between devices  13.3 us (27%)
  waiting for transfers between devices  7.34 us (15%)
  between operations  1.44 us (3%)
    pallas_call x10, Pallas kernels, call(): pl.pallas_call(kernel, out_shape=outs, in_specs=[IN_SMEM if k in smem els...  26.7 us
    ppermute x4, starting transfers between devices, sent_by_core(): return lax.ppermute(value, ('dom', 'edge'), pairs)  11.3 us
    ppermute x8, waiting for transfers between devices, swapped(): return lax.ppermute(value, 'edge', [(0, 1), (1, 0)])  4.27 us
    ppermute x4, waiting for transfers between devices, sent_by_core(): return lax.ppermute(value, ('dom', 'edge'), pairs)  3.06 us
    ppermute x8, starting transfers between devices, swapped(): return lax.ppermute(value, 'edge', [(0, 1), (1, 0)])  2.02 us
  transfers between devices with their start and end apart: 12, of which 6 were waited for; matrix products, arithmetic and copies ran while one was open for 0% of the time, Pallas kernels for 27%

profile of v2, /device:TPU:0, one launch (start us, length us, event | category | flops | bytes accessed | tf_op | source)
XLA Modules:
  0.0 48.8 jit_solution(16083772764839456787)
XLA Ops:
  0.6 0.0 copy-start
  0.6 0.0 copy-start.1
  0.7 0.6 %collective-permute-start = (bf16[256,256]{1,0:T(8,128)(2,1)}, bf16[256,256]{1,0:T(8,128)(2,1)S(1)}, u32[]{:S(2)}, u32[]{:S(2)}) collective-permute-start(bf16[256,256]{1,0:T(8,128)(2,1)} %own_ref.3), channel_id=1, source_target_pairs={{0,1},{1,0},{2,3},{3,2},{4,5},{5,4},{6,7},{7,6},{8,9},{9,8},{10,11... | collective-permute-start | bytes 393224 | tf_op jit(solution)/shard_map/ppermute | solution.py:338
  1.2 0.1 collective-permute-start.1
  1.9 2.0 %index.1 = (bf16[4,3072,128]{2,1,0:T(8,128)(2,1)S(1)}, f32[3,3072]{1,0:T(4,128)S(1)}, bf16[3072,256]{1,0:T(8,128)(2,1)S(1)}, bf16[2,768,256]{2,1,0:T(8,128)(2,1)...) custom-call(s32[1,1]{1,0:T(1,128)S(6)} %copy.16.live_ref, ...), custom_call_target="tpu_custom_call" | custom-call | bytes 3440644 | tf_op jit(solution)/shard_map/index/pallas_call | solution.py:78
  4.0 0.0 collective-permute-done.1.list_peer
  4.0 0.0 collective-permute-done.refs_1_.peer_ref
  4.0 0.0 copy-done
  4.0 0.0 copy-done.1
  4.0 0.3 pick.1
  4.3 3.0 %collective-permute-start.2 = (bf16[256,256]{1,0:T(8,128)(2,1)S(1)}, bf16[256,256]{1,0:T(8,128)(2,1)S(1)}, u32[]{:S(2)}, u32[]{:S(2)}) collective-permute-start(bf16[256,256]{1,0:T(8,128)(2,1)S(1)} %get-tuple-element.33), channel_id=1, source_target_pairs={{0,2},{2,0},{4,6},{6,4},{8,10},{10,8},{12,14},{14,12},{16,18},{18,... | collective-permute-start | bytes 393224 | tf_op jit(solution)/shard_map/ppermute | solution.py:367
  7.3 4.5 %collective-permute-start.3 = (bf16[256,256]{1,0:T(8,128)(2,1)S(1)}, bf16[256,256]{1,0:T(8,128)(2,1)S(1)}, u32[]{:S(2)}, u32[]{:S(2)}) collective-permute-start(bf16[256,256]{1,0:T(8,128)(2,1)S(1)} %get-tuple-element.34), channel_id=1, source_target_pairs={{0,30},{2,4},{4,2},{6,8},{8,6},{10,12},{12,10},{14,16},{16,14},{18... | collective-permute-start | bytes 393224 | tf_op jit(solution)/shard_map/ppermute | solution.py:367
  11.8 3.5 %local.2.pre_ref = f32[3072,256]{1,0:T(8,128)S(1)} custom-call(bf16[3072,256]{1,0:T(8,128)(2,1)S(1)} %get-tuple-element.29.edge_ref, bf16[4,3072,128]{2,1,0:T(8,128)(2,1)S(1)} %get-tuple-element.30.cols, bf16[256,256]{1,0:T(8,128)(2,1)S(1)} %copy-done, bf16[256,256]{1,0:T(8,128)(2,1)S(1)} %collective-permute-done.refs_1_.peer_ref, ...), custom_call_target="tpu_custom_call" | custom-call | flops 2013265920 | bytes 5769216 | tf_op jit(solution)/shard_map/local/pallas_call | solution.py:78
  15.4 0.0 collective-permute-done.2.own
  15.4 1.3 %collective-permute-done.3.own = bf16[256,256]{1,0:T(8,128)(2,1)S(1)} collective-permute-done((bf16[256,256]{1,0:T(8,128)(2,1)S(1)}, bf16[256,256]{1,0:T(8,128)(2,1)S(1)}, u32[]{:S(2)}, u32[]{:S(2)}) %collective-permute-start.3) | collective-permute-done | bytes 131104 | tf_op jit(solution)/shard_map/ppermute | solution.py:367
  16.7 0.0 collective-permute-start.4
  16.7 0.5 %collective-permute-start.5 = (bf16[256,256]{1,0:T(8,128)(2,1)S(1)}, bf16[256,256]{1,0:T(8,128)(2,1)S(1)}, u32[]{:S(2)}, u32[]{:S(2)}) collective-permute-start(bf16[256,256]{1,0:T(8,128)(2,1)S(1)} %collective-permute-done.3.own), channel_id=1, source_target_pairs={{0,1},{1,0},{2,3},{3,2},{4,5},{5,4},{6,7},{7,6},{8,9},{9,8},{10,11... | collective-permute-start | bytes 393224 | tf_op jit(solution)/shard_map/ppermute | solution.py:338
  17.2 0.8 %collective-permute-done.4.peer = bf16[256,256]{1,0:T(8,128)(2,1)S(1)} collective-permute-done((bf16[256,256]{1,0:T(8,128)(2,1)S(1)}, bf16[256,256]{1,0:T(8,128)(2,1)S(1)}, u32[]{:S(2)}, u32[]{:S(2)}) %collective-permute-start.4) | collective-permute-done | bytes 131104 | tf_op jit(solution)/shard_map/ppermute | solution.py:338
  18.1 2.1 %near.2.pre_ref = f32[3072,256]{1,0:T(8,128)S(1)} custom-call(f32[3072,256]{1,0:T(8,128)S(1)} %local.2.pre_ref, bf16[4,3072,128]{2,1,0:T(8,128)(2,1)S(1)} %get-tuple-element.30.cols, bf16[2,768,256]{2,1,0:T(8,128)(2,1)S(1)} %get-tuple-element.31.refs_2_.w1_ref.refs_1_, bf16[256,256]{1,0:T(8,128)(2,1)S(1)} %collective-permute-done.2.own, ...), custom_call_target="tpu_custom_call" | custom-call | flops 805306368 | bytes 7340032 | tf_op jit(solution)/shard_map/near/pallas_call | solution.py:78
  20.2 0.0 collective-permute-done.5.peer
  20.2 5.3 %far.2 = (bf16[3072,256]{1,0:T(8,128)(2,1)S(1)}, bf16[512,256]{1,0:T(8,128)(2,1)S(1)}) custom-call(f32[3072,256]{1,0:T(8,128)S(1)} %near.2.pre_ref, bf16[4,3072,128]{2,1,0:T(8,128)(2,1)S(1)} %get-tuple-element.30.cols, f32[3,3072]{1,0:T(4,128)S(1)} %get-tuple-element.37.rows, bf16[3072,256]{1,0:T(8,128)(2,1)S(1)} %get-tuple-element.29.edge_ref, ...), custom_call_target="tpu_custom_call" | custom-call | flops 2013265920 | bytes 9213952 | tf_op jit(solution)/shard_map/far/pallas_call | solution.py:78
  25.5 0.2 collective-permute-start.6
  25.8 1.4 %collective-permute-done.6.second = bf16[512,256]{1,0:T(8,128)(2,1)S(1)} collective-permute-done((bf16[512,256]{1,0:T(8,128)(2,1)S(1)}, bf16[512,256]{1,0:T(8,128)(2,1)S(1)}, u32[]{:S(2)}, u32[]{:S(2)}) %collective-permute-start.6) | collective-permute-done | bytes 262176 | tf_op jit(solution)/shard_map/ppermute | solution.py:338
  27.1 1.1 %nodes.1 = (bf16[512,256]{1,0:T(8,128)(2,1)S(1)}, bf16[256,256]{1,0:T(8,128)(2,1)S(1)}, bf16[256,256]{1,0:T(8,128)(2,1)S(1)}) custom-call(bf16[256,256]{1,0:T(8,128)(2,1)S(1)} %copy-done, bf16[256,256]{1,0:T(8,128)(2,1)S(1)} %collective-permute-done.refs_1_.peer_ref, bf16[512,256]{1,0:T(8,128)(2,1)S(1)} %get-tuple-element.41.first, ...), custom_call_target="tpu_custom_call" | custom-call | bytes 1581056 | tf_op jit(solution)/shard_map/nodes/pallas_call | solution.py:78
  28.2 0.1 collective-permute-start.7
  28.3 3.8 %collective-permute-start.8 = (bf16[256,256]{1,0:T(8,128)(2,1)S(1)}, bf16[256,256]{1,0:T(8,128)(2,1)S(1)}, u32[]{:S(2)}, u32[]{:S(2)}) collective-permute-start(bf16[256,256]{1,0:T(8,128)(2,1)S(1)} %get-tuple-element.49), channel_id=1, source_target_pairs={{0,30},{2,4},{4,2},{6,8},{8,6},{10,12},{12,10},{14,16},{16,14},{18... | collective-permute-start | bytes 393224 | tf_op jit(solution)/shard_map/ppermute | solution.py:367
  32.0 3.5 %local.3.pre_ref = f32[3072,256]{1,0:T(8,128)S(1)} custom-call(bf16[3072,256]{1,0:T(8,128)(2,1)S(1)} %get-tuple-element.47.edge_ref, bf16[4,3072,128]{2,1,0:T(8,128)(2,1)S(1)} %get-tuple-element.30.cols, bf16[512,256]{1,0:T(8,128)(2,1)S(1)} %get-tuple-element.46.refs_0_.nodes_ref, bf16[2,768,256]{2,1,0:T(8,128)(2,1)S(1)} %get-tuple-element.31.refs_2_.w1_ref.refs_1_, ...), custom_call_target="tpu_custom_call" | custom-call | flops 2013265920 | bytes 5769216 | tf_op jit(solution)/shard_map/local/pallas_call | solution.py:78
  35.5 0.0 collective-permute-done.7.own
  35.6 1.7 %collective-permute-done.8.own = bf16[256,256]{1,0:T(8,128)(2,1)S(1)} collective-permute-done((bf16[256,256]{1,0:T(8,128)(2,1)S(1)}, bf16[256,256]{1,0:T(8,128)(2,1)S(1)}, u32[]{:S(2)}, u32[]{:S(2)}) %collective-permute-start.8) | collective-permute-done | bytes 131104 | tf_op jit(solution)/shard_map/ppermute | solution.py:367
  37.3 0.0 collective-permute-start.9
  37.3 0.5 %collective-permute-start.10 = (bf16[256,256]{1,0:T(8,128)(2,1)S(1)}, bf16[256,256]{1,0:T(8,128)(2,1)S(1)}, u32[]{:S(2)}, u32[]{:S(2)}) collective-permute-start(bf16[256,256]{1,0:T(8,128)(2,1)S(1)} %collective-permute-done.8.own), channel_id=1, source_target_pairs={{0,1},{1,0},{2,3},{3,2},{4,5},{5,4},{6,7},{7,6},{8,9},{9,8},{10,11... | collective-permute-start | bytes 393224 | tf_op jit(solution)/shard_map/ppermute | solution.py:338
  37.8 0.8 %collective-permute-done.9.peer = bf16[256,256]{1,0:T(8,128)(2,1)S(1)} collective-permute-done((bf16[256,256]{1,0:T(8,128)(2,1)S(1)}, bf16[256,256]{1,0:T(8,128)(2,1)S(1)}, u32[]{:S(2)}, u32[]{:S(2)}) %collective-permute-start.9) | collective-permute-done | bytes 131104 | tf_op jit(solution)/shard_map/ppermute | solution.py:338
  38.6 2.1 %near.3.pre_ref = f32[3072,256]{1,0:T(8,128)S(1)} custom-call(f32[3072,256]{1,0:T(8,128)S(1)} %local.3.pre_ref, bf16[4,3072,128]{2,1,0:T(8,128)(2,1)S(1)} %get-tuple-element.30.cols, bf16[2,768,256]{2,1,0:T(8,128)(2,1)S(1)} %get-tuple-element.31.refs_2_.w1_ref.refs_1_, bf16[256,256]{1,0:T(8,128)(2,1)S(1)} %collective-permute-done.7.own, ...), custom_call_target="tpu_custom_call" | custom-call | flops 805306368 | bytes 7340032 | tf_op jit(solution)/shard_map/near/pallas_call | solution.py:78
  40.7 0.0 collective-permute-done.10.peer
  40.7 5.5 %far.3 = (bf16[3072,256]{1,0:T(8,128)(2,1)}, bf16[256,256]{1,0:T(8,128)(2,1)S(1)}, bf16[256,256]{1,0:T(8,128)(2,1)S(1)}) custom-call(f32[3072,256]{1,0:T(8,128)S(1)} %near.3.pre_ref, bf16[4,3072,128]{2,1,0:T(8,128)(2,1)S(1)} %get-tuple-element.30.cols, f32[3,3072]{1,0:T(4,128)S(1)} %get-tuple-element.37.rows, ...), custom_call_target="tpu_custom_call" | custom-call | flops 2013265920 | bytes 9213952 | tf_op jit(solution)/shard_map/far/pallas_call | solution.py:78
  46.3 0.1 collective-permute-start.11
  46.4 1.2 %collective-permute-done.11.second = bf16[256,256]{1,0:T(8,128)(2,1)S(1)} collective-permute-done((bf16[256,256]{1,0:T(8,128)(2,1)S(1)}, bf16[256,256]{1,0:T(8,128)(2,1)S(1)}, u32[]{:S(2)}, u32[]{:S(2)}) %collective-permute-start.11) | collective-permute-done | bytes 131104 | tf_op jit(solution)/shard_map/ppermute | solution.py:338
  47.6 1.2 %last.1 = bf16[256,256]{1,0:T(8,128)(2,1)} custom-call(bf16[512,256]{1,0:T(8,128)(2,1)S(1)} %get-tuple-element.46.refs_0_.nodes_ref, bf16[256,256]{1,0:T(8,128)(2,1)S(1)} %get-tuple-element.53.first, bf16[256,256]{1,0:T(8,128)(2,1)S(1)} %collective-permute-done.11.second, bf16[2,512,256]{2,1,0:T(8,128)(2,1)S(1)} %get-tuple-element.42.w1, ...), custom_call_target="tpu_custom_call" | custom-call | bytes 1314816 | tf_op jit(solution)/shard_map/last/pallas_call | solution.py:78
Async XLA Ops:
  0.6 3.4 %copy-start = (bf16[256,256]{1,0:T(8,128)(2,1)S(1)}, bf16[256,256]{1,0:T(8,128)(2,1)}, u32[]{:S(2)}) copy-start(bf16[256,256]{1,0:T(8,128)(2,1)} %own_ref.3) | copy-start | bytes 393220
  0.6 3.4 %copy-start.1 = (s32[1,4,128]{2,1,0:T(4,128)S(1)}, s32[1,4,128]{2,1,0:T(4,128)}, u32[]{:S(2)}) copy-start(s32[1,4,128]{2,1,0:T(4,128)} %list_own.3) | copy-start | bytes 6148
  0.7 3.4 %collective-permute-start = (bf16[256,256]{1,0:T(8,128)(2,1)}, bf16[256,256]{1,0:T(8,128)(2,1)S(1)}, u32[]{:S(2)}, u32[]{:S(2)}) collective-permute-start(bf16[256,256]{1,0:T(8,128)(2,1)} %own_ref.3), channel_id=1, source_target_pairs={{0,1},{1,0},{2,3},{3,2},{4,5},{5,4},{6,7},{7,6},{8,9},{9,8},{10,11... | collective-permute-start | bytes 393224 | tf_op jit(solution)/shard_map/ppermute | solution.py:338
  1.2 2.8 %collective-permute-start.1 = (s32[1,4,128]{2,1,0:T(4,128)}, s32[1,4,128]{2,1,0:T(4,128)S(1)}, u32[]{:S(2)}, u32[]{:S(2)}) collective-permute-start(s32[1,4,128]{2,1,0:T(4,128)} %list_own.3), channel_id=1, source_target_pairs={{0,1},{1,0},{2,3},{3,2},{4,5},{5,4},{6,7},{7,6},{8,9},{9,8},{10,11... | collective-permute-start | bytes 6152 | tf_op jit(solution)/shard_map/ppermute | solution.py:338
  4.3 11.0 %collective-permute-start.2 = (bf16[256,256]{1,0:T(8,128)(2,1)S(1)}, bf16[256,256]{1,0:T(8,128)(2,1)S(1)}, u32[]{:S(2)}, u32[]{:S(2)}) collective-permute-start(bf16[256,256]{1,0:T(8,128)(2,1)S(1)} %get-tuple-element.33), channel_id=1, source_target_pairs={{0,2},{2,0},{4,6},{6,4},{8,10},{10,8},{12,14},{14,12},{16,18},{18,... | collective-permute-start | bytes 393224 | tf_op jit(solution)/shard_map/ppermute | solution.py:367
  7.3 9.4 %collective-permute-start.3 = (bf16[256,256]{1,0:T(8,128)(2,1)S(1)}, bf16[256,256]{1,0:T(8,128)(2,1)S(1)}, u32[]{:S(2)}, u32[]{:S(2)}) collective-permute-start(bf16[256,256]{1,0:T(8,128)(2,1)S(1)} %get-tuple-element.34), channel_id=1, source_target_pairs={{0,30},{2,4},{4,2},{6,8},{8,6},{10,12},{12,10},{14,16},{16,14},{18... | collective-permute-start | bytes 393224 | tf_op jit(solution)/shard_map/ppermute | solution.py:367
  16.7 1.3 %collective-permute-start.4 = (bf16[256,256]{1,0:T(8,128)(2,1)S(1)}, bf16[256,256]{1,0:T(8,128)(2,1)S(1)}, u32[]{:S(2)}, u32[]{:S(2)}) collective-permute-start(bf16[256,256]{1,0:T(8,128)(2,1)S(1)} %collective-permute-done.2.own), channel_id=1, source_target_pairs={{0,1},{1,0},{2,3},{3,2},{4,5},{5,4},{6,7},{7,6},{8,9},{9,8},{10,11... | collective-permute-start | bytes 393224 | tf_op jit(solution)/shard_map/ppermute | solution.py:338
  16.7 3.5 %collective-permute-start.5 = (bf16[256,256]{1,0:T(8,128)(2,1)S(1)}, bf16[256,256]{1,0:T(8,128)(2,1)S(1)}, u32[]{:S(2)}, u32[]{:S(2)}) collective-permute-start(bf16[256,256]{1,0:T(8,128)(2,1)S(1)} %collective-permute-done.3.own), channel_id=1, source_target_pairs={{0,1},{1,0},{2,3},{3,2},{4,5},{5,4},{6,7},{7,6},{8,9},{9,8},{10,11... | collective-permute-start | bytes 393224 | tf_op jit(solution)/shard_map/ppermute | solution.py:338
  25.5 1.6 %collective-permute-start.6 = (bf16[512,256]{1,0:T(8,128)(2,1)S(1)}, bf16[512,256]{1,0:T(8,128)(2,1)S(1)}, u32[]{:S(2)}, u32[]{:S(2)}) collective-permute-start(bf16[512,256]{1,0:T(8,128)(2,1)S(1)} %get-tuple-element.41.first), channel_id=1, source_target_pairs={{0,1},{1,0},{2,3},{3,2},{4,5},{5,4},{6,7},{7,6},{8,9},{9,8},{10,11... | collective-permute-start | bytes 786440 | tf_op jit(solution)/shard_map/ppermute | solution.py:338
  28.2 7.3 %collective-permute-start.7 = (bf16[256,256]{1,0:T(8,128)(2,1)S(1)}, bf16[256,256]{1,0:T(8,128)(2,1)S(1)}, u32[]{:S(2)}, u32[]{:S(2)}) collective-permute-start(bf16[256,256]{1,0:T(8,128)(2,1)S(1)} %get-tuple-element.48), channel_id=1, source_target_pairs={{0,2},{2,0},{4,6},{6,4},{8,10},{10,8},{12,14},{14,12},{16,18},{18,... | collective-permute-start | bytes 393224 | tf_op jit(solution)/shard_map/ppermute | solution.py:367
  28.3 9.0 %collective-permute-start.8 = (bf16[256,256]{1,0:T(8,128)(2,1)S(1)}, bf16[256,256]{1,0:T(8,128)(2,1)S(1)}, u32[]{:S(2)}, u32[]{:S(2)}) collective-permute-start(bf16[256,256]{1,0:T(8,128)(2,1)S(1)} %get-tuple-element.49), channel_id=1, source_target_pairs={{0,30},{2,4},{4,2},{6,8},{8,6},{10,12},{12,10},{14,16},{16,14},{18... | collective-permute-start | bytes 393224 | tf_op jit(solution)/shard_map/ppermute | solution.py:367
  37.3 1.3 %collective-permute-start.9 = (bf16[256,256]{1,0:T(8,128)(2,1)S(1)}, bf16[256,256]{1,0:T(8,128)(2,1)S(1)}, u32[]{:S(2)}, u32[]{:S(2)}) collective-permute-start(bf16[256,256]{1,0:T(8,128)(2,1)S(1)} %collective-permute-done.7.own), channel_id=1, source_target_pairs={{0,1},{1,0},{2,3},{3,2},{4,5},{5,4},{6,7},{7,6},{8,9},{9,8},{10,11... | collective-permute-start | bytes 393224 | tf_op jit(solution)/shard_map/ppermute | solution.py:338
  37.3 3.5 %collective-permute-start.10 = (bf16[256,256]{1,0:T(8,128)(2,1)S(1)}, bf16[256,256]{1,0:T(8,128)(2,1)S(1)}, u32[]{:S(2)}, u32[]{:S(2)}) collective-permute-start(bf16[256,256]{1,0:T(8,128)(2,1)S(1)} %collective-permute-done.8.own), channel_id=1, source_target_pairs={{0,1},{1,0},{2,3},{3,2},{4,5},{5,4},{6,7},{7,6},{8,9},{9,8},{10,11... | collective-permute-start | bytes 393224 | tf_op jit(solution)/shard_map/ppermute | solution.py:338
  46.3 1.3 %collective-permute-start.11 = (bf16[256,256]{1,0:T(8,128)(2,1)S(1)}, bf16[256,256]{1,0:T(8,128)(2,1)S(1)}, u32[]{:S(2)}, u32[]{:S(2)}) collective-permute-start(bf16[256,256]{1,0:T(8,128)(2,1)S(1)} %get-tuple-element.54), channel_id=1, source_target_pairs={{0,1},{1,0},{2,3},{3,2},{4,5},{5,4},{6,7},{7,6},{8,9},{9,8},{10,11... | collective-permute-start | bytes 393224 | tf_op jit(solution)/shard_map/ppermute | solution.py:338

commit v3 on v2

--- a/solution.py
+++ b/solution.py
@@ -64,6 +64,8 @@
 TILE = 256
 HALF = 128
 ROWS = 512
+LOCAL_ROWS = 1024
+I16 = jnp.int16
 IN_VMEM = pl.BlockSpec(memory_space=pltpu.VMEM)
 IN_SMEM = pl.BlockSpec(memory_space=pltpu.SMEM)
 IN_HBM = pl.BlockSpec(memory_space=pltpu.HBM)
@@ -100,18 +102,18 @@
 
 
 def column(row):
-    return jnp.transpose(jnp.broadcast_to(row.astype(F32), (HALF, HALF)))
+    return jnp.transpose(jnp.broadcast_to(row, (HALF, HALF)))
 
 
 def one_hot_rows(row):
     col = column(row)
-    lane = lax.broadcasted_iota(jnp.int32, (HALF, HALF), 1).astype(F32)
-    parts = [jnp.where(col == lane + float(k), 1.0, 0.0) for k in (0, HALF)]
+    lane = lax.broadcasted_iota(jnp.int32, (HALF, HALF), 1)
+    parts = [jnp.where(col == lane + k, 1.0, 0.0) for k in (0, HALF)]
     return jnp.concatenate(parts, axis=1).astype(BF16)
 
 
-def dyn(start, size):
-    return pl.ds(pl.multiple_of(start, size), size)
+def dyn(start, size, unit=None):
+    return pl.ds(pl.multiple_of(start, unit or size), size)
 
 
 def face_rows(stride, lists, nodes, far, near):
@@ -128,9 +130,9 @@
     face_rows(stride, (list_own, list_peer), nodes, far, near)
 
 
-def index_kernel(stride, edges, loads, live_ref, *refs):
-    hbm, (cols, rows), refs = refs[: loads + 2], refs[loads + 2 : loads + 4], refs[loads + 4 :]
-    vmem, (send_ref, recv_ref, sems) = refs[:loads], refs[loads:]
+def index_kernel(stride, edges, loads, *refs):
+    hbm, cols, refs = refs[: loads + 2], refs[loads + 2], refs[loads + 3 :]
+    recv_ref, vmem, (send_ref, sems) = refs[0], refs[1 : loads + 1], refs[loads + 1 :]
     copies = [
         pltpu.make_async_copy(src, dst, sems.at[k])
         for k, (src, dst) in enumerate(zip(hbm, (send_ref, recv_ref, *vmem)))
@@ -140,8 +142,6 @@
     _, par_d, par_s = place(stride)
     for copy in copies[:2]:
         copy.wait()
-    live = jnp.broadcast_to(live_ref[...], (1, HALF))
-    lane = lax.broadcasted_iota(jnp.int32, (1, HALF), 1)
     for k in range(edges // HALF):
         at = pl.ds(k * HALF, HALF)
         v = send_ref[:, at]
@@ -153,67 +153,48 @@
         near = (face & 1) != par
         tile = jnp.where(near, 2, 4) + core
         at_tile = ((owner ^ core) & 1) * HALF + (j & (HALF - 1))
-        local = v < 2 * TILE
-        hi = jnp.where(local, lax.shift_right_arithmetic(v, 8), tile)
-        lo = jnp.where(local, v & (TILE - 1), at_tile)
-        cols[0, at, :] = column(hi).astype(BF16)
-        cols[1, at, :] = column(lo).astype(BF16)
-        v = recv_ref[:, at]
-        hi = lax.shift_right_arithmetic(v, 8)
-        lo = v & (TILE - 1)
-        cols[2, at, :] = column(hi).astype(BF16)
-        cols[3, at, :] = column(lo).astype(BF16)
-        rows[0:1, at] = jnp.where(lane + k * HALF < live, hi, -1).astype(F32)
-        rows[1:2, at] = lo.astype(F32)
-    rows[2:3, :] = jnp.concatenate([live] * (edges // HALF), axis=1).astype(F32)
+        spot = jnp.where(v < 2 * TILE, v, tile * TILE + at_tile)
+        cols[0, at, :] = column(spot).astype(I16)
+        cols[1, at, :] = column(recv_ref[:, at]).astype(I16)
     for copy in copies[2:]:
         copy.wait()
 
 
-def lane_iota(rows):
-    lane = lax.broadcasted_iota(jnp.int32, (rows, HALF), 1).astype(F32)
-    return lane.astype(BF16), (lane + float(HALF)).astype(BF16)
-
-
-def hits(hi, lo, tile, lanes):
-    at = jnp.where(hi == tile, lo, jnp.asarray(-1, BF16))
-    one = jnp.ones(at.shape, BF16)
-    zero = jnp.zeros(at.shape, BF16)
-    return jnp.concatenate([jnp.where(at == lane, one, zero) for lane in lanes], axis=1)
-
-
-def local_kernel(layer, stacked, edge_ref, cols, *refs):
-    if stacked:
-        dom_ref, w1_ref, b1_ref, pre_ref, t_s, t_r = refs
-        dom = dom_ref[...]
-        t_s[...] = mm(dom, w1_ref[layer, TILE : 2 * TILE, :]).astype(BF16)
-        t_r[...] = mm(dom, w1_ref[layer, 2 * TILE :, :]).astype(BF16)
+def hits(spots, first, tiles):
+    one = jnp.ones(spots.shape, BF16)
+    zero = jnp.zeros(spots.shape, BF16)
+    lane = lax.broadcasted_iota(jnp.int32, spots.shape, 1)
+    parts = [
+        jnp.where(spots == (lane + (first * TILE + k * HALF)).astype(I16), one, zero)
+        for k in range(2 * tiles)
+    ]
+    return jnp.concatenate(parts, axis=1)
+
+
+def local_kernel(layer, edge_ref, cols, *refs):
+    if layer:
+        dom_ref, w1_ref, b1_ref, pre_ref, table = refs
+        parts = ((0, 2 * TILE, dom_ref),)
     else:
-        own_ref, peer_ref, w1_ref, b1_ref, pre_ref, t_s, t_r = refs
+        own_ref, peer_ref, w1_ref, b1_ref, pre_ref, table = refs
         core = lax.axis_index("edge")
-        for owner, ref in ((core, own_ref), (1 - core, peer_ref)):
-            at = dyn(owner * TILE, TILE)
-            t_s[at, :] = mm(ref[...], w1_ref[layer, TILE : 2 * TILE, :]).astype(BF16)
-            t_r[at, :] = mm(ref[...], w1_ref[layer, 2 * TILE :, :]).astype(BF16)
-    lanes = lane_iota(ROWS)
+        parts = ((core * TILE, TILE, own_ref), ((1 - core) * TILE, TILE, peer_ref))
+    for k in (1, 2):
+        for start, size, ref in parts:
+            table[dyn((2 * k - 2) * TILE + start, size, TILE), :] = mm(
+                ref[...], w1_ref[layer, k * TILE : (k + 1) * TILE, :]
+            ).astype(BF16)
     bias = b1_ref[layer : layer + 1, :]
-    w_e = w1_ref[layer, 0:TILE, :]
 
     def step(k, carry):
-        at = dyn(k * ROWS, ROWS)
-        acc = mm(edge_ref[at, :], w_e)
-        for base, table in ((0, t_s), (2, t_r)):
-            hi = cols[base, at, :]
-            lo = cols[base + 1, at, :]
-            for tile in range(2):
-                acc = acc + mm(
-                    hits(hi, lo, jnp.asarray(tile, BF16), lanes),
-                    table[tile * TILE : (tile + 1) * TILE, :],
-                )
+        at = dyn(k * LOCAL_ROWS, LOCAL_ROWS)
+        acc = mm(edge_ref[at, :], w1_ref[layer, 0:TILE, :])
+        acc = acc + mm(hits(cols[0, at, :], 0, 2), table[0 : 2 * TILE, :])
+        acc = acc + mm(hits(cols[1, at, :], 0, 2), table[2 * TILE :, :])
         pre_ref[at, :] = acc + bias
         return carry
 
-    lax.fori_loop(0, edge_ref.shape[0] // ROWS, step, 0)
+    lax.fori_loop(0, edge_ref.shape[0] // LOCAL_ROWS, step, 0)
 
 
 def halo_tables(layer, own, peer, w1_ref, table):
@@ -225,77 +206,64 @@
 
 def near_kernel(layer, pre_ref, cols, w1_ref, own, peer, out_ref, table):
     halo_tables(layer, own, peer, w1_ref, table)
-    lanes = lane_iota(ROWS)
 
     def step(k, carry):
-        at = dyn(k * ROWS, ROWS)
-        hi = cols[0, at, :]
-        lo = cols[1, at, :]
-        acc = pre_ref[at, :]
-        for n in range(2):
-            acc = acc + mm(
-                hits(hi, lo, jnp.asarray(2 + n, BF16), lanes), table[n * TILE : (n + 1) * TILE, :]
-            )
-        out_ref[at, :] = acc
+        at = dyn(k * LOCAL_ROWS, LOCAL_ROWS)
+        out_ref[at, :] = pre_ref[at, :] + mm(hits(cols[0, at, :], 2, 2), table[...])
         return carry
 
-    lax.fori_loop(0, pre_ref.shape[0] // ROWS, step, 0)
+    lax.fori_loop(0, pre_ref.shape[0] // LOCAL_ROWS, step, 0)
 
 
 def edge_kernel(
-    layer, split, pre_ref, cols, rows, edge_ref, w1_ref, w2_ref, gain_ref, own, peer, out_ref, *refs
+    layer, split, live_ref, pre_ref, cols, recv_ref, edge_ref, w1_ref, w2_ref, gain_ref, own, peer, out_ref, *refs
 ):
     if split:
-        keep_ref, give_ref, table, msgs = refs
+        keep_ref, give_ref, table, raw, msgs, sums = refs
     else:
-        part_ref, table, msgs = refs
+        part_ref, table, raw, msgs, sums = refs
     halo_tables(layer, own, peer, w1_ref, table)
-    lanes = lane_iota(ROWS)
-    live = jnp.broadcast_to(rows[2:3, 0:TILE], (ROWS, TILE)).astype(jnp.int32)
     gain = gain_ref[layer : layer + 1, :]
-    w2 = w2_ref[layer]
-    place_in = lax.broadcasted_iota(jnp.int32, (ROWS, TILE), 0)
-
-    def step(k, carry):
-        at = dyn(k * ROWS, ROWS)
-        hi = cols[0, at, :]
-        lo = cols[1, at, :]
-        acc = pre_ref[at, :]
-        for n in range(2):
-            acc = acc + mm(
-                hits(hi, lo, jnp.asarray(4 + n, BF16), lanes), table[n * TILE : (n + 1) * TILE, :]
-            )
-        hidden = jnp.maximum(acc, 0.0).astype(BF16)
-        message = layer_norm(mm(hidden, w2), gain)
-        msgs[at, :] = message.astype(BF16)
-        message = jnp.where(place_in + k * ROWS < live, message, 0.0)
-        out_ref[at, :] = (edge_ref[at, :].astype(F32) + message).astype(BF16)
-        return carry
-
+    live = live_ref[0, 0]
     count = edge_ref.shape[0] // ROWS
-    lax.fori_loop(0, count, step, 0)
-    spot = lax.broadcasted_iota(jnp.int32, (TILE, ROWS), 0).astype(F32).astype(BF16)
-    one = jnp.ones((TILE, ROWS), BF16)
-    zero = jnp.zeros((TILE, ROWS), BF16)
-    sums = [None, None]
-    for k in range(count):
-        at = pl.ds(k * ROWS, ROWS)
-        hi = rows[0:1, at]
-        lo = rows[1:2, at]
-        msg = msgs[at, :]
-        for n in range(2):
-            here = jnp.where(hi == float(n), lo, -1.0).astype(BF16)
-            hot = jnp.where(jnp.broadcast_to(here, (TILE, ROWS)) == spot, one, zero)
-            part = mm(hot, msg)
-            sums[n] = part if sums[n] is None else sums[n] + part
+
+    def gather(at):
+        acc = pre_ref[at, :] + mm(hits(cols[0, at, :], 4, 2), table[...])
+        hidden = jnp.maximum(acc.astype(BF16), jnp.asarray(0, BF16))
+        raw[at, :] = mm(hidden, w2_ref[layer])
+
+    def norm(at, first):
+        values = raw[at, :]
+        center = values - jnp.mean(values, axis=-1, keepdims=True)
+        spread = jnp.mean(center * center, axis=-1, keepdims=True)
+        scale = lax.rsqrt(spread + eps_norm)
+        row = lax.broadcasted_iota(jnp.int32, scale.shape, 0) + first
+        scale = jnp.where(row < live, scale, 0.0)
+        message = (center * scale * gain).astype(BF16)
+        msgs[at, :] = message
+        out_ref[at, :] = edge_ref[at, :] + message
+
+    def segment(at, first):
+        shape = (2 * TILE, ROWS)
+        spot = lax.broadcasted_iota(jnp.int32, shape, 0).astype(I16)
+        here = jnp.broadcast_to(recv_ref[:, at].astype(I16), shape)
+        hot = jnp.where(here == spot, jnp.ones(shape, BF16), jnp.zeros(shape, BF16))
+        part = mm(hot, msgs[at, :])
+        sums[...] = part if first else sums[...] + part
+
+    for k in range(count + 2):
+        if k >= 2:
+            segment(pl.ds((k - 2) * ROWS, ROWS), k == 2)
+        if 1 <= k <= count:
+            norm(pl.ds((k - 1) * ROWS, ROWS), (k - 1) * ROWS)
+        if k < count:
+            gather(pl.ds(k * ROWS, ROWS))
     if split:
         core = lax.axis_index("edge")
-        mine = core == 0
-        keep_ref[...] = jnp.where(mine, sums[0], sums[1]).astype(BF16)
-        give_ref[...] = jnp.where(mine, sums[1], sums[0]).astype(BF16)
+        keep_ref[...] = sums[dyn(core * TILE, TILE), :].astype(BF16)
+        give_ref[...] = sums[dyn((1 - core) * TILE, TILE), :].astype(BF16)
     else:
-        for n in range(2):
-            part_ref[n * TILE : (n + 1) * TILE, :] = sums[n].astype(BF16)
+        part_ref[...] = sums[...].astype(BF16)
 
 
 def updated(layer, nodes, first, second, w1_ref, b1_ref, w2_ref, gain_ref):
@@ -376,13 +344,13 @@
     peer_lists = swapped(send_rows)
     loads = (edge_lat, edge_w1, edge_w2, node_w1, node_w2, edge_b1, edge_gain, node_b1, node_gain)
     hbm = [pltpu.with_memory_space_constraint(a, pltpu.HBM) for a in (senders[None], receivers[None], *loads)]
-    cols, rows, edge_rows, edge_w1, edge_w2, node_w1, node_w2, edge_b1, edge_gain, node_b1, node_gain = call(
+    cols, recv_row, edge_rows, edge_w1, edge_w2, node_w1, node_w2, edge_b1, edge_gain, node_b1, node_gain = call(
         functools.partial(index_kernel, stride, edges, len(loads)),
-        [shaped((4, edges, HALF), BF16), shaped((3, edges), F32)]
+        [shaped((2, edges, HALF), I16), shaped((1, edges), jnp.int32)]
         + [shaped(a.shape, a.dtype) for a in loads],
-        (live_edges, *hbm),
-        scratch=[pltpu.VMEM((1, edges), jnp.int32)] * 2 + [pltpu.SemaphoreType.DMA((len(hbm),))],
-        stay=range(1, len(hbm) + 1),
+        hbm,
+        scratch=[pltpu.VMEM((1, edges), jnp.int32), pltpu.SemaphoreType.DMA((len(hbm),))],
+        stay=range(len(hbm)),
         name="index",
     )
     far_rows, near_rows = call(
@@ -394,17 +362,17 @@
     for layer in range(LAYERS):
         last = layer == LAYERS - 1
         node_args = (all_nodes,) if layer else (node_lat, peer_nodes)
+        near = sent_by_core(near_rows, near_d, near_s)
         far = sent_by_core(far_rows, far_d, far_s)
-        near = sent_by_core(near_rows, near_d, near_s)
         pre = call(
-            functools.partial(local_kernel, layer, layer > 0),
+            functools.partial(local_kernel, layer),
             pre_shape,
             (edge_rows, cols, *node_args, edge_w1, edge_b1),
-            scratch=[table, table],
+            scratch=[pltpu.VMEM((4 * TILE, width), BF16)],
             flops=5 * pass_flops,
             name="local",
         )
-        pre, near, far = lax.optimization_barrier((pre, near, far))
+        pre, near, far, live_edges = lax.optimization_barrier((pre, near, far, live_edges))
         near = (near, swapped(near))
         far = (far, swapped(far))
         pre = call(
@@ -422,8 +390,9 @@
         edge_rows, *partial = call(
             functools.partial(edge_kernel, layer, last),
             [shaped((edges, width), BF16)] + outs,
-            (pre, cols, rows, edge_rows, edge_w1, edge_w2, edge_gain, *far),
-            scratch=[table, messages],
+            (live_edges, pre, cols, recv_row, edge_rows, edge_w1, edge_w2, edge_gain, *far),
+            scratch=[table, pltpu.VMEM((edges, width), F32), messages, pltpu.VMEM((2 * nodes, width), F32)],
+            smem=(0,),
             flops=5 * pass_flops,
             name="far",
         )

time: 49 us -> 43.7 us (0.89)
  Pallas kernels: 26.7 us -> 20.7 us
  waiting for transfers between devices: 7.34 us -> 8 us
    pallas_call x10, Pallas kernels: 26.7 us -> 20.7 us  [call(): pl.pallas_call(kernel, out_shape=outs, in_specs=[IN_SMEM if k in smem els...]
    ppermute x4, waiting for transfers between devices: 3.06 us -> 4.4 us  [sent_by_core(): return lax.ppermute(value, ('dom', 'edge'), pairs)]
    ppermute x8, waiting for transfers between devices: 4.27 us -> 3.6 us  [swapped(): return lax.ppermute(value, 'edge', [(0, 1), (1, 0)])]
  transfers between devices with their start and end apart: 12 -> 12, of which waited for: 6 -> 6; matrix products, arithmetic and copies ran while one was open for 0% -> 0% of each run, Pallas kernels for 27% -> 25%
where the time goes in v3:
time: 43.7 us; the launch traced here: 43.5 us
  Pallas kernels  20.7 us (47%)
  starting transfers between devices  13.4 us (31%)
  waiting for transfers between devices  8 us (18%)
  between operations  1.42 us (3%)
    pallas_call x10, Pallas kernels, call(): pl.pallas_call(kernel, out_shape=outs, in_specs=[IN_SMEM if k in smem els...  20.7 us
    ppermute x4, starting transfers between devices, sent_by_core(): return lax.ppermute(value, ('dom', 'edge'), pairs)  11.3 us
    ppermute x4, waiting for transfers between devices, sent_by_core(): return lax.ppermute(value, ('dom', 'edge'), pairs)  4.4 us
    ppermute x8, waiting for transfers between devices, swapped(): return lax.ppermute(value, 'edge', [(0, 1), (1, 0)])  3.6 us
    ppermute x8, starting transfers between devices, swapped(): return lax.ppermute(value, 'edge', [(0, 1), (1, 0)])  2.04 us
  transfers between devices with their start and end apart: 12, of which 6 were waited for; matrix products, arithmetic and copies ran while one was open for 0% of the time, Pallas kernels for 25%

profile of v3, /device:TPU:0, one launch (start us, length us, event | category | flops | bytes accessed | tf_op | source)
XLA Modules:
  0.0 43.5 jit_solution(12735306898158145298)
XLA Ops:
  0.6 0.6 %collective-permute-start = (bf16[256,256]{1,0:T(8,128)(2,1)}, bf16[256,256]{1,0:T(8,128)(2,1)S(1)}, u32[]{:S(2)}, u32[]{:S(2)}) collective-permute-start(bf16[256,256]{1,0:T(8,128)(2,1)} %own_ref.3), channel_id=1, source_target_pairs={{0,1},{1,0},{2,3},{3,2},{4,5},{5,4},{6,7},{7,6},{8,9},{9,8},{10,11... | collective-permute-start | bytes 393224 | tf_op jit(solution)/shard_map/ppermute | solution.py:306
  1.2 0.1 collective-permute-start.1
  1.3 0.0 copy-start
  1.3 0.0 copy-start.1
  1.3 2.1 %index.1 = (s16[2,3072,128]{2,1,0:T(8,128)(2,1)S(1)}, s32[1,3072]{1,0:T(1,128)S(1)}, bf16[3072,256]{1,0:T(8,128)(2,1)S(1)}, bf16[2,768,256]{2,1,0:T(8,128)(2,1)S...) custom-call(s32[1,3072]{1,0:T(1,128)} %bitcast.2, ...), custom_call_target="tpu_custom_call" | custom-call | bytes 3440640 | tf_op jit(solution)/shard_map/index/pallas_call | solution.py:80
  3.3 0.0 collective-permute-done.1.list_peer
  3.4 0.0 collective-permute-done.refs_1_.peer_ref
  3.4 0.0 copy-done
  3.4 0.0 copy-done.1
  3.4 0.3 pick.1
  3.7 3.0 %collective-permute-start.2 = (bf16[256,256]{1,0:T(8,128)(2,1)S(1)}, bf16[256,256]{1,0:T(8,128)(2,1)S(1)}, u32[]{:S(2)}, u32[]{:S(2)}) collective-permute-start(bf16[256,256]{1,0:T(8,128)(2,1)S(1)} %get-tuple-element.35), channel_id=1, source_target_pairs={{0,2},{2,0},{4,6},{6,4},{8,10},{10,8},{12,14},{14,12},{16,18},{18,... | collective-permute-start | bytes 393224 | tf_op jit(solution)/shard_map/ppermute | solution.py:335
  6.7 4.5 %collective-permute-start.3 = (bf16[256,256]{1,0:T(8,128)(2,1)S(1)}, bf16[256,256]{1,0:T(8,128)(2,1)S(1)}, u32[]{:S(2)}, u32[]{:S(2)}) collective-permute-start(bf16[256,256]{1,0:T(8,128)(2,1)S(1)} %get-tuple-element.36), channel_id=1, source_target_pairs={{0,30},{2,4},{4,2},{6,8},{8,6},{10,12},{12,10},{14,16},{16,14},{18... | collective-permute-start | bytes 393224 | tf_op jit(solution)/shard_map/ppermute | solution.py:335
  11.2 2.9 %local.2.pre_ref = f32[3072,256]{1,0:T(8,128)S(1)} custom-call(bf16[3072,256]{1,0:T(8,128)(2,1)S(1)} %get-tuple-element.31.edge_ref, s16[2,3072,128]{2,1,0:T(8,128)(2,1)S(1)} %get-tuple-element.32.cols, bf16[256,256]{1,0:T(8,128)(2,1)S(1)} %copy-done, bf16[256,256]{1,0:T(8,128)(2,1)S(1)} %collective-permute-done.refs_1_.peer_ref, ...), custom_call_target="tpu_custom_call" | custom-call | flops 2013265920 | bytes 4196352 | tf_op jit(solution)/shard_map/local/pallas_call | solution.py:80
  14.1 0.0 collective-permute-done.2.own
  14.1 2.0 %collective-permute-done.3.own = bf16[256,256]{1,0:T(8,128)(2,1)S(1)} collective-permute-done((bf16[256,256]{1,0:T(8,128)(2,1)S(1)}, bf16[256,256]{1,0:T(8,128)(2,1)S(1)}, u32[]{:S(2)}, u32[]{:S(2)}) %collective-permute-start.3) | collective-permute-done | bytes 131104 | tf_op jit(solution)/shard_map/ppermute | solution.py:335
  16.1 0.0 collective-permute-start.4
  16.1 0.5 %collective-permute-start.5 = (bf16[256,256]{1,0:T(8,128)(2,1)S(1)}, bf16[256,256]{1,0:T(8,128)(2,1)S(1)}, u32[]{:S(2)}, u32[]{:S(2)}) collective-permute-start(bf16[256,256]{1,0:T(8,128)(2,1)S(1)} %collective-permute-done.3.own), channel_id=1, source_target_pairs={{0,1},{1,0},{2,3},{3,2},{4,5},{5,4},{6,7},{7,6},{8,9},{9,8},{10,11... | collective-permute-start | bytes 393224 | tf_op jit(solution)/shard_map/ppermute | solution.py:306
  17.2 0.2 collective-permute-done.4.peer
  17.4 1.6 %near.2.pre_ref = f32[3072,256]{1,0:T(8,128)S(1)} custom-call(f32[3072,256]{1,0:T(8,128)S(1)} %local.2.pre_ref, s16[2,3072,128]{2,1,0:T(8,128)(2,1)S(1)} %get-tuple-element.32.cols, bf16[2,768,256]{2,1,0:T(8,128)(2,1)S(1)} %get-tuple-element.33.refs_2_.w1_ref.refs_1_, bf16[256,256]{1,0:T(8,128)(2,1)S(1)} %collective-permute-done.2.own, ...), custom_call_target="tpu_custom_call" | custom-call | flops 805306368 | bytes 5767168 | tf_op jit(solution)/shard_map/near/pallas_call | solution.py:80
  19.0 0.0 collective-permute-done.5.peer
  19.0 3.3 %far.2 = (bf16[3072,256]{1,0:T(8,128)(2,1)S(1)}, bf16[512,256]{1,0:T(8,128)(2,1)S(1)}) custom-call(s32[1,1]{1,0:T(1,128)S(6)} %copy.16.live_ref, f32[3072,256]{1,0:T(8,128)S(1)} %near.2.pre_ref, s16[2,3072,128]{2,1,0:T(8,128)(2,1)S(1)} %get-tuple-element.32.cols, s32[1,3072]{1,0:T(1,128)S(1)} %get-tuple-element.40.recv_ref, ...), custom_call_target="tpu_custom_call" | custom-call | flops 2013265920 | bytes 7616516 | tf_op jit(solution)/shard_map/far/pallas_call | solution.py:80
  22.3 0.2 collective-permute-start.6
  22.5 1.4 %collective-permute-done.6.second = bf16[512,256]{1,0:T(8,128)(2,1)S(1)} collective-permute-done((bf16[512,256]{1,0:T(8,128)(2,1)S(1)}, bf16[512,256]{1,0:T(8,128)(2,1)S(1)}, u32[]{:S(2)}, u32[]{:S(2)}) %collective-permute-start.6) | collective-permute-done | bytes 262176 | tf_op jit(solution)/shard_map/ppermute | solution.py:306
  23.9 1.1 %nodes.1 = (bf16[512,256]{1,0:T(8,128)(2,1)S(1)}, bf16[256,256]{1,0:T(8,128)(2,1)S(1)}, bf16[256,256]{1,0:T(8,128)(2,1)S(1)}) custom-call(bf16[256,256]{1,0:T(8,128)(2,1)S(1)} %copy-done, bf16[256,256]{1,0:T(8,128)(2,1)S(1)} %collective-permute-done.refs_1_.peer_ref, bf16[512,256]{1,0:T(8,128)(2,1)S(1)} %get-tuple-element.44.first, ...), custom_call_target="tpu_custom_call" | custom-call | bytes 1581056 | tf_op jit(solution)/shard_map/nodes/pallas_call | solution.py:80
  24.9 0.1 collective-permute-start.7
  25.0 3.8 %collective-permute-start.8 = (bf16[256,256]{1,0:T(8,128)(2,1)S(1)}, bf16[256,256]{1,0:T(8,128)(2,1)S(1)}, u32[]{:S(2)}, u32[]{:S(2)}) collective-permute-start(bf16[256,256]{1,0:T(8,128)(2,1)S(1)} %get-tuple-element.52), channel_id=1, source_target_pairs={{0,30},{2,4},{4,2},{6,8},{8,6},{10,12},{12,10},{14,16},{16,14},{18... | collective-permute-start | bytes 393224 | tf_op jit(solution)/shard_map/ppermute | solution.py:335
  28.8 2.8 %local.3.pre_ref = f32[3072,256]{1,0:T(8,128)S(1)} custom-call(bf16[3072,256]{1,0:T(8,128)(2,1)S(1)} %get-tuple-element.50.edge_ref, s16[2,3072,128]{2,1,0:T(8,128)(2,1)S(1)} %get-tuple-element.32.cols, bf16[512,256]{1,0:T(8,128)(2,1)S(1)} %get-tuple-element.49.refs_0_.nodes_ref, bf16[2,768,256]{2,1,0:T(8,128)(2,1)S(1)} %get-tuple-element.33.refs_2_.w1_ref.refs_1_, ...), custom_call_target="tpu_custom_call" | custom-call | flops 2013265920 | bytes 4196352 | tf_op jit(solution)/shard_map/local/pallas_call | solution.py:80
  31.6 0.0 collective-permute-done.7.own
  31.6 2.4 %collective-permute-done.8.own = bf16[256,256]{1,0:T(8,128)(2,1)S(1)} collective-permute-done((bf16[256,256]{1,0:T(8,128)(2,1)S(1)}, bf16[256,256]{1,0:T(8,128)(2,1)S(1)}, u32[]{:S(2)}, u32[]{:S(2)}) %collective-permute-start.8) | collective-permute-done | bytes 131104 | tf_op jit(solution)/shard_map/ppermute | solution.py:335
  34.0 0.0 collective-permute-start.9
  34.0 0.5 %collective-permute-start.10 = (bf16[256,256]{1,0:T(8,128)(2,1)S(1)}, bf16[256,256]{1,0:T(8,128)(2,1)S(1)}, u32[]{:S(2)}, u32[]{:S(2)}) collective-permute-start(bf16[256,256]{1,0:T(8,128)(2,1)S(1)} %collective-permute-done.8.own), channel_id=1, source_target_pairs={{0,1},{1,0},{2,3},{3,2},{4,5},{5,4},{6,7},{7,6},{8,9},{9,8},{10,11... | collective-permute-start | bytes 393224 | tf_op jit(solution)/shard_map/ppermute | solution.py:306
  34.5 0.8 %collective-permute-done.9.peer = bf16[256,256]{1,0:T(8,128)(2,1)S(1)} collective-permute-done((bf16[256,256]{1,0:T(8,128)(2,1)S(1)}, bf16[256,256]{1,0:T(8,128)(2,1)S(1)}, u32[]{:S(2)}, u32[]{:S(2)}) %collective-permute-start.9) | collective-permute-done | bytes 131104 | tf_op jit(solution)/shard_map/ppermute | solution.py:306
  35.4 1.6 %near.3.pre_ref = f32[3072,256]{1,0:T(8,128)S(1)} custom-call(f32[3072,256]{1,0:T(8,128)S(1)} %local.3.pre_ref, s16[2,3072,128]{2,1,0:T(8,128)(2,1)S(1)} %get-tuple-element.32.cols, bf16[2,768,256]{2,1,0:T(8,128)(2,1)S(1)} %get-tuple-element.33.refs_2_.w1_ref.refs_1_, bf16[256,256]{1,0:T(8,128)(2,1)S(1)} %collective-permute-done.7.own, ...), custom_call_target="tpu_custom_call" | custom-call | flops 805306368 | bytes 5767168 | tf_op jit(solution)/shard_map/near/pallas_call | solution.py:80
  36.9 0.0 collective-permute-done.10.peer
  36.9 4.1 %far.3 = (bf16[3072,256]{1,0:T(8,128)(2,1)}, bf16[256,256]{1,0:T(8,128)(2,1)S(1)}, bf16[256,256]{1,0:T(8,128)(2,1)S(1)}) custom-call(s32[1,1]{1,0:T(1,128)S(6)} %copy.16.live_ref, f32[3072,256]{1,0:T(8,128)S(1)} %near.3.pre_ref, s16[2,3072,128]{2,1,0:T(8,128)(2,1)S(1)} %get-tuple-element.32.cols, s32[1,3072]{1,0:T(1,128)S(1)} %get-tuple-element.40.recv_ref, ...), custom_call_target="tpu_custom_call" | custom-call | flops 2013265920 | bytes 7616516 | tf_op jit(solution)/shard_map/far/pallas_call | solution.py:80
  41.0 0.2 collective-permute-start.11
  41.1 1.2 %collective-permute-done.11.second = bf16[256,256]{1,0:T(8,128)(2,1)S(1)} collective-permute-done((bf16[256,256]{1,0:T(8,128)(2,1)S(1)}, bf16[256,256]{1,0:T(8,128)(2,1)S(1)}, u32[]{:S(2)}, u32[]{:S(2)}) %collective-permute-start.11) | collective-permute-done | bytes 131104 | tf_op jit(solution)/shard_map/ppermute | solution.py:306
  42.3 1.2 %last.1 = bf16[256,256]{1,0:T(8,128)(2,1)} custom-call(bf16[512,256]{1,0:T(8,128)(2,1)S(1)} %get-tuple-element.49.refs_0_.nodes_ref, bf16[256,256]{1,0:T(8,128)(2,1)S(1)} %get-tuple-element.57.first, bf16[256,256]{1,0:T(8,128)(2,1)S(1)} %collective-permute-done.11.second, bf16[2,512,256]{2,1,0:T(8,128)(2,1)S(1)} %get-tuple-element.45.w1, ...), custom_call_target="tpu_custom_call" | custom-call | bytes 1314816 | tf_op jit(solution)/shard_map/last/pallas_call | solution.py:80
Async XLA Ops:
  0.6 2.7 %collective-permute-start = (bf16[256,256]{1,0:T(8,128)(2,1)}, bf16[256,256]{1,0:T(8,128)(2,1)S(1)}, u32[]{:S(2)}, u32[]{:S(2)}) collective-permute-start(bf16[256,256]{1,0:T(8,128)(2,1)} %own_ref.3), channel_id=1, source_target_pairs={{0,1},{1,0},{2,3},{3,2},{4,5},{5,4},{6,7},{7,6},{8,9},{9,8},{10,11... | collective-permute-start | bytes 393224 | tf_op jit(solution)/shard_map/ppermute | solution.py:306
  1.2 2.2 %collective-permute-start.1 = (s32[1,4,128]{2,1,0:T(4,128)}, s32[1,4,128]{2,1,0:T(4,128)S(1)}, u32[]{:S(2)}, u32[]{:S(2)}) collective-permute-start(s32[1,4,128]{2,1,0:T(4,128)} %list_own.3), channel_id=1, source_target_pairs={{0,1},{1,0},{2,3},{3,2},{4,5},{5,4},{6,7},{7,6},{8,9},{9,8},{10,11... | collective-permute-start | bytes 6152 | tf_op jit(solution)/shard_map/ppermute | solution.py:306
  1.3 2.1 %copy-start = (bf16[256,256]{1,0:T(8,128)(2,1)S(1)}, bf16[256,256]{1,0:T(8,128)(2,1)}, u32[]{:S(2)}) copy-start(bf16[256,256]{1,0:T(8,128)(2,1)} %own_ref.3) | copy-start | bytes 393220
  1.3 2.1 %copy-start.1 = (s32[1,4,128]{2,1,0:T(4,128)S(1)}, s32[1,4,128]{2,1,0:T(4,128)}, u32[]{:S(2)}) copy-start(s32[1,4,128]{2,1,0:T(4,128)} %list_own.3) | copy-start | bytes 6148
  3.7 10.4 %collective-permute-start.2 = (bf16[256,256]{1,0:T(8,128)(2,1)S(1)}, bf16[256,256]{1,0:T(8,128)(2,1)S(1)}, u32[]{:S(2)}, u32[]{:S(2)}) collective-permute-start(bf16[256,256]{1,0:T(8,128)(2,1)S(1)} %get-tuple-element.35), channel_id=1, source_target_pairs={{0,2},{2,0},{4,6},{6,4},{8,10},{10,8},{12,14},{14,12},{16,18},{18,... | collective-permute-start | bytes 393224 | tf_op jit(solution)/shard_map/ppermute | solution.py:335
  6.7 9.4 %collective-permute-start.3 = (bf16[256,256]{1,0:T(8,128)(2,1)S(1)}, bf16[256,256]{1,0:T(8,128)(2,1)S(1)}, u32[]{:S(2)}, u32[]{:S(2)}) collective-permute-start(bf16[256,256]{1,0:T(8,128)(2,1)S(1)} %get-tuple-element.36), channel_id=1, source_target_pairs={{0,30},{2,4},{4,2},{6,8},{8,6},{10,12},{12,10},{14,16},{16,14},{18... | collective-permute-start | bytes 393224 | tf_op jit(solution)/shard_map/ppermute | solution.py:335
  16.1 1.3 %collective-permute-start.4 = (bf16[256,256]{1,0:T(8,128)(2,1)S(1)}, bf16[256,256]{1,0:T(8,128)(2,1)S(1)}, u32[]{:S(2)}, u32[]{:S(2)}) collective-permute-start(bf16[256,256]{1,0:T(8,128)(2,1)S(1)} %collective-permute-done.2.own), channel_id=1, source_target_pairs={{0,1},{1,0},{2,3},{3,2},{4,5},{5,4},{6,7},{7,6},{8,9},{9,8},{10,11... | collective-permute-start | bytes 393224 | tf_op jit(solution)/shard_map/ppermute | solution.py:306
  16.1 2.9 %collective-permute-start.5 = (bf16[256,256]{1,0:T(8,128)(2,1)S(1)}, bf16[256,256]{1,0:T(8,128)(2,1)S(1)}, u32[]{:S(2)}, u32[]{:S(2)}) collective-permute-start(bf16[256,256]{1,0:T(8,128)(2,1)S(1)} %collective-permute-done.3.own), channel_id=1, source_target_pairs={{0,1},{1,0},{2,3},{3,2},{4,5},{5,4},{6,7},{7,6},{8,9},{9,8},{10,11... | collective-permute-start | bytes 393224 | tf_op jit(solution)/shard_map/ppermute | solution.py:306
  22.3 1.6 %collective-permute-start.6 = (bf16[512,256]{1,0:T(8,128)(2,1)S(1)}, bf16[512,256]{1,0:T(8,128)(2,1)S(1)}, u32[]{:S(2)}, u32[]{:S(2)}) collective-permute-start(bf16[512,256]{1,0:T(8,128)(2,1)S(1)} %get-tuple-element.44.first), channel_id=1, source_target_pairs={{0,1},{1,0},{2,3},{3,2},{4,5},{5,4},{6,7},{7,6},{8,9},{9,8},{10,11... | collective-permute-start | bytes 786440 | tf_op jit(solution)/shard_map/ppermute | solution.py:306
  24.9 6.7 %collective-permute-start.7 = (bf16[256,256]{1,0:T(8,128)(2,1)S(1)}, bf16[256,256]{1,0:T(8,128)(2,1)S(1)}, u32[]{:S(2)}, u32[]{:S(2)}) collective-permute-start(bf16[256,256]{1,0:T(8,128)(2,1)S(1)} %get-tuple-element.51), channel_id=1, source_target_pairs={{0,2},{2,0},{4,6},{6,4},{8,10},{10,8},{12,14},{14,12},{16,18},{18,... | collective-permute-start | bytes 393224 | tf_op jit(solution)/shard_map/ppermute | solution.py:335
  25.0 9.0 %collective-permute-start.8 = (bf16[256,256]{1,0:T(8,128)(2,1)S(1)}, bf16[256,256]{1,0:T(8,128)(2,1)S(1)}, u32[]{:S(2)}, u32[]{:S(2)}) collective-permute-start(bf16[256,256]{1,0:T(8,128)(2,1)S(1)} %get-tuple-element.52), channel_id=1, source_target_pairs={{0,30},{2,4},{4,2},{6,8},{8,6},{10,12},{12,10},{14,16},{16,14},{18... | collective-permute-start | bytes 393224 | tf_op jit(solution)/shard_map/ppermute | solution.py:335
  34.0 1.3 %collective-permute-start.9 = (bf16[256,256]{1,0:T(8,128)(2,1)S(1)}, bf16[256,256]{1,0:T(8,128)(2,1)S(1)}, u32[]{:S(2)}, u32[]{:S(2)}) collective-permute-start(bf16[256,256]{1,0:T(8,128)(2,1)S(1)} %collective-permute-done.7.own), channel_id=1, source_target_pairs={{0,1},{1,0},{2,3},{3,2},{4,5},{5,4},{6,7},{7,6},{8,9},{9,8},{10,11... | collective-permute-start | bytes 393224 | tf_op jit(solution)/shard_map/ppermute | solution.py:306
  34.0 2.9 %collective-permute-start.10 = (bf16[256,256]{1,0:T(8,128)(2,1)S(1)}, bf16[256,256]{1,0:T(8,128)(2,1)S(1)}, u32[]{:S(2)}, u32[]{:S(2)}) collective-permute-start(bf16[256,256]{1,0:T(8,128)(2,1)S(1)} %collective-permute-done.8.own), channel_id=1, source_target_pairs={{0,1},{1,0},{2,3},{3,2},{4,5},{5,4},{6,7},{7,6},{8,9},{9,8},{10,11... | collective-permute-start | bytes 393224 | tf_op jit(solution)/shard_map/ppermute | solution.py:306
  41.0 1.3 %collective-permute-start.11 = (bf16[256,256]{1,0:T(8,128)(2,1)S(1)}, bf16[256,256]{1,0:T(8,128)(2,1)S(1)}, u32[]{:S(2)}, u32[]{:S(2)}) collective-permute-start(bf16[256,256]{1,0:T(8,128)(2,1)S(1)} %get-tuple-element.58), channel_id=1, source_target_pairs={{0,1},{1,0},{2,3},{3,2},{4,5},{5,4},{6,7},{7,6},{8,9},{9,8},{10,11... | collective-permute-start | bytes 393224 | tf_op jit(solution)/shard_map/ppermute | solution.py:306

commit v4 on v3

--- a/solution.py
+++ b/solution.py
@@ -75,7 +75,7 @@
     return jax.ShapeDtypeStruct(shape, dtype)
 
 
-def call(kernel, outs, args, scratch=(), smem=(), stay=(), flops=0, limit=24, name=None):
+def call(kernel, outs, args, scratch=(), smem=(), stay=(), leave=(), flops=0, limit=24, name=None):
     nbytes = sum(a.size * a.dtype.itemsize for a in args)
     return pl.pallas_call(
         kernel,
@@ -83,7 +83,9 @@
         in_specs=[
             IN_SMEM if k in smem else IN_HBM if k in stay else IN_VMEM for k in range(len(args))
         ],
-        out_specs=jax.tree.map(lambda _: IN_VMEM, outs),
+        out_specs=[IN_HBM if k in leave else IN_VMEM for k in range(len(outs))]
+        if isinstance(outs, list)
+        else IN_VMEM,
         scratch_shapes=scratch,
         compiler_params=pltpu.CompilerParams(vmem_limit_bytes=limit << 20),
         cost_estimate=pl.CostEstimate(flops=flops, transcendentals=0, bytes_accessed=nbytes),
@@ -122,12 +124,26 @@
     for face, ref in ((2 * core + 1 - par, far), (2 * core + par, near)):
         for n in range(2):
             hot = one_hot_rows(lists[n][0, pl.ds(face, 1), :])
-            ref[n * HALF : (n + 1) * HALF, :] = mm(hot, nodes[n]()).astype(BF16)
+            ref[n * HALF : (n + 1) * HALF, :] = mm(hot, nodes[n]).astype(BF16)
 
 
 def pick_kernel(stride, own_ref, peer_ref, list_own, list_peer, far, near):
-    nodes = (lambda: own_ref[...]), (lambda: peer_ref[...])
-    face_rows(stride, (list_own, list_peer), nodes, far, near)
+    face_rows(stride, (list_own, list_peer), (own_ref[...], peer_ref[...]), far, near)
+
+
+def load_kernel(count, *refs):
+    hbm, vmem, sems = refs[:count], refs[count:-1], refs[-1]
+    copies = [
+        pltpu.make_async_copy(src, dst, sems.at[k]) for k, (src, dst) in enumerate(zip(hbm, vmem))
+    ]
+    for copy in copies:
+        copy.start()
+    for copy in copies:
+        copy.wait()
+
+
+def in_hbm(arrays):
+    return [pltpu.with_memory_space_constraint(a, pltpu.HBM) for a in arrays]
 
 
 def index_kernel(stride, edges, loads, *refs):
@@ -204,12 +220,14 @@
         table[dyn(axis * TILE, TILE), :] = mm(ref[...], w_s).astype(BF16)
 
 
-def near_kernel(layer, pre_ref, cols, w1_ref, own, peer, out_ref, table):
-    halo_tables(layer, own, peer, w1_ref, table)
+def near_kernel(layer, peer, pre_ref, cols, w1_ref, rows_ref, out_ref):
+    core = lax.axis_index("edge")
+    tile = 3 - core if peer else 2 + core
+    table = mm(rows_ref[...], w1_ref[layer, TILE : 2 * TILE, :]).astype(BF16)
 
     def step(k, carry):
         at = dyn(k * LOCAL_ROWS, LOCAL_ROWS)
-        out_ref[at, :] = pre_ref[at, :] + mm(hits(cols[0, at, :], 2, 2), table[...])
+        out_ref[at, :] = pre_ref[at, :] + mm(hits(cols[0, at, :], tile, 1), table)
         return carry
 
     lax.fori_loop(0, pre_ref.shape[0] // LOCAL_ROWS, step, 0)
@@ -219,9 +237,10 @@
     layer, split, live_ref, pre_ref, cols, recv_ref, edge_ref, w1_ref, w2_ref, gain_ref, own, peer, out_ref, *refs
 ):
     if split:
-        keep_ref, give_ref, table, raw, msgs, sums = refs
+        keep_ref, give_ref, table, raw, msgs, sums, block_ref, sems = refs
     else:
         part_ref, table, raw, msgs, sums = refs
+        block_ref = out_ref
     halo_tables(layer, own, peer, w1_ref, table)
     gain = gain_ref[layer : layer + 1, :]
     live = live_ref[0, 0]
@@ -241,7 +260,7 @@
         scale = jnp.where(row < live, scale, 0.0)
         message = (center * scale * gain).astype(BF16)
         msgs[at, :] = message
-        out_ref[at, :] = edge_ref[at, :] + message
+        block_ref[at, :] = edge_ref[at, :] + message
 
     def segment(at, first):
         shape = (2 * TILE, ROWS)
@@ -251,17 +270,26 @@
         part = mm(hot, msgs[at, :])
         sums[...] = part if first else sums[...] + part
 
+    copies = []
     for k in range(count + 2):
         if k >= 2:
             segment(pl.ds((k - 2) * ROWS, ROWS), k == 2)
         if 1 <= k <= count:
-            norm(pl.ds((k - 1) * ROWS, ROWS), (k - 1) * ROWS)
+            at = pl.ds((k - 1) * ROWS, ROWS)
+            norm(at, (k - 1) * ROWS)
+            if split:
+                copies.append(
+                    pltpu.make_async_copy(block_ref.at[at, :], out_ref.at[at, :], sems.at[k - 1])
+                )
+                copies[-1].start()
         if k < count:
             gather(pl.ds(k * ROWS, ROWS))
     if split:
         core = lax.axis_index("edge")
         keep_ref[...] = sums[dyn(core * TILE, TILE), :].astype(BF16)
         give_ref[...] = sums[dyn((1 - core) * TILE, TILE), :].astype(BF16)
+        for copy in copies:
+            copy.wait()
     else:
         part_ref[...] = sums[...].astype(BF16)
 
@@ -278,13 +306,11 @@
     stride, layer, own_ref, peer_ref, first, second, list_own, list_peer, w1, b1, w2, gain, out, far, near
 ):
     core = lax.axis_index("edge")
+    nodes = []
     for owner, ref in ((core, own_ref), (1 - core, peer_ref)):
         at = dyn(owner * TILE, TILE)
-        out[at, :] = updated(layer, ref[...], first[at, :], second[at, :], w1, b1, w2, gain)
-    nodes = [
-        functools.partial(out.__getitem__, (dyn(owner * TILE, TILE), slice(None)))
-        for owner in (core, 1 - core)
-    ]
+        nodes.append(updated(layer, ref[...], first[at, :], second[at, :], w1, b1, w2, gain))
+        out[at, :] = nodes[-1]
     face_rows(stride, (list_own, list_peer), nodes, far, near)
 
 
@@ -342,8 +368,25 @@
 
     peer_nodes = swapped(node_lat)
     peer_lists = swapped(send_rows)
+    node_lat, send_rows = call(
+        functools.partial(load_kernel, 2),
+        [shaped(a.shape, a.dtype) for a in (node_lat, send_rows)],
+        in_hbm((node_lat, send_rows)),
+        scratch=[pltpu.SemaphoreType.DMA((2,))],
+        stay=(0, 1),
+        name="load",
+    )
+    far_rows, near_rows = call(
+        functools.partial(pick_kernel, stride),
+        [rows_out, rows_out],
+        (node_lat, peer_nodes, send_rows, peer_lists),
+        name="pick",
+    )
     loads = (edge_lat, edge_w1, edge_w2, node_w1, node_w2, edge_b1, edge_gain, node_b1, node_gain)
-    hbm = [pltpu.with_memory_space_constraint(a, pltpu.HBM) for a in (senders[None], receivers[None], *loads)]
+    far_rows, near_rows, *hbm = lax.optimization_barrier(
+        (far_rows, near_rows, senders[None], receivers[None], *loads)
+    )
+    hbm = in_hbm(hbm)
     cols, recv_row, edge_rows, edge_w1, edge_w2, node_w1, node_w2, edge_b1, edge_gain, node_b1, node_gain = call(
         functools.partial(index_kernel, stride, edges, len(loads)),
         [shaped((2, edges, HALF), I16), shaped((1, edges), jnp.int32)]
@@ -352,12 +395,6 @@
         scratch=[pltpu.VMEM((1, edges), jnp.int32), pltpu.SemaphoreType.DMA((len(hbm),))],
         stay=range(len(hbm)),
         name="index",
-    )
-    far_rows, near_rows = call(
-        functools.partial(pick_kernel, stride),
-        [rows_out, rows_out],
-        (node_lat, peer_nodes, send_rows, peer_lists),
-        name="pick",
     )
     for layer in range(LAYERS):
         last = layer == LAYERS - 1
@@ -372,17 +409,15 @@
             flops=5 * pass_flops,
             name="local",
         )
-        pre, near, far, live_edges = lax.optimization_barrier((pre, near, far, live_edges))
-        near = (near, swapped(near))
-        far = (far, swapped(far))
-        pre = call(
-            functools.partial(near_kernel, layer),
-            pre_shape,
-            (pre, cols, edge_w1, *near),
-            scratch=[table],
-            flops=2 * pass_flops,
-            name="near",
+        pre, near, live_edges = lax.optimization_barrier((pre, near, live_edges))
+        near_other = swapped(near)
+        add = functools.partial(
+            call, outs=pre_shape, flops=pass_flops, name="near"
         )
+        pre = add(functools.partial(near_kernel, layer, False), args=(pre, cols, edge_w1, near))
+        pre, far = lax.optimization_barrier((pre, far))
+        far_other = swapped(far)
+        pre = add(functools.partial(near_kernel, layer, True), args=(pre, cols, edge_w1, near_other))
         if last:
             outs = [shaped((nodes, width), BF16)] * 2
         else:
@@ -390,9 +425,16 @@
         edge_rows, *partial = call(
             functools.partial(edge_kernel, layer, last),
             [shaped((edges, width), BF16)] + outs,
-            (live_edges, pre, cols, recv_row, edge_rows, edge_w1, edge_w2, edge_gain, *far),
-            scratch=[table, pltpu.VMEM((edges, width), F32), messages, pltpu.VMEM((2 * nodes, width), F32)],
+            (live_edges, pre, cols, recv_row, edge_rows, edge_w1, edge_w2, edge_gain, far, far_other),
+            scratch=[
+                table,
+                pltpu.VMEM((edges, width), F32),
+                messages,
+                pltpu.VMEM((2 * nodes, width), F32),
+            ]
+            + last * [messages, pltpu.SemaphoreType.DMA((edges // ROWS,))],
             smem=(0,),
+            leave=last * (0,),
             flops=5 * pass_flops,
             name="far",
         )

time: 43.7 us -> 41.1 us (0.941)
  waiting for transfers between devices: 8 us -> 5.61 us
  starting transfers between devices: 13.4 us -> 11.3 us
  Pallas kernels: 20.7 us -> 22.6 us
    ppermute x4, starting transfers between devices: 11.3 us -> 9.4 us  [sent_by_core(): return lax.ppermute(value, ('dom', 'edge'), pairs)]
    ppermute x4, waiting for transfers between devices: 4.4 us -> 2.48 us  [sent_by_core(): return lax.ppermute(value, ('dom', 'edge'), pairs)]
    pallas_call x10 -> x13, Pallas kernels: 20.7 us -> 22.6 us  [call(): pl.pallas_call(kernel, out_shape=outs, in_specs=[IN_SMEM if k in smem els...]
    ppermute x8, waiting for transfers between devices: 3.6 us -> 3.13 us  [swapped(): return lax.ppermute(value, 'edge', [(0, 1), (1, 0)])]
  transfers between devices with their start and end apart: 12 -> 12, of which waited for: 6 -> 5; matrix products, arithmetic and copies ran while one was open for 0% -> 0% of each run, Pallas kernels for 25% -> 32%
where the time goes in v4:
time: 41.1 us; the launch traced here: 40.9 us
  Pallas kernels  22.6 us (55%)
  starting transfers between devices  11.3 us (27%)
  waiting for transfers between devices  5.61 us (14%)
  between operations  1.43 us (3%)
    pallas_call x13, Pallas kernels, call(): pl.pallas_call(kernel, out_shape=outs, in_specs=[IN_SMEM if k in smem els...  22.6 us
    ppermute x4, starting transfers between devices, sent_by_core(): return lax.ppermute(value, ('dom', 'edge'), pairs)  9.4 us
    ppermute x8, waiting for transfers between devices, swapped(): return lax.ppermute(value, 'edge', [(0, 1), (1, 0)])  3.13 us
    ppermute x4, waiting for transfers between devices, sent_by_core(): return lax.ppermute(value, ('dom', 'edge'), pairs)  2.48 us
    ppermute x8, starting transfers between devices, swapped(): return lax.ppermute(value, 'edge', [(0, 1), (1, 0)])  1.86 us
  transfers between devices with their start and end apart: 12, of which 5 were waited for; matrix products, arithmetic and copies ran while one was open for 0% of the time, Pallas kernels for 32%

profile of v4, /device:TPU:0, one launch (start us, length us, event | category | flops | bytes accessed | tf_op | source)
XLA Modules:
  0.0 40.9 jit_solution(12828724449859695248)
XLA Ops:
  0.6 0.6 %collective-permute-start = (bf16[256,256]{1,0:T(8,128)(2,1)}, bf16[256,256]{1,0:T(8,128)(2,1)S(1)}, u32[]{:S(2)}, u32[]{:S(2)}) collective-permute-start(bf16[256,256]{1,0:T(8,128)(2,1)} %refs_0_.1), channel_id=1, source_target_pairs={{0,1},{1,0},{2,3},{3,2},{4,5},{5,4},{6,7},{7,6},{8,9},{9,8},{10,11... | collective-permute-start | bytes 393224 | tf_op jit(solution)/shard_map/ppermute | solution.py:332
  1.2 0.1 collective-permute-start.1
  1.3 0.9 %load.1 = (bf16[256,256]{1,0:T(8,128)(2,1)S(1)}, s32[1,4,128]{2,1,0:T(4,128)S(1)}) custom-call(bf16[256,256]{1,0:T(8,128)(2,1)} %refs_0_.1, s32[1,4,128]{2,1,0:T(4,128)} %refs_1_.1), custom_call_target="tpu_custom_call" | custom-call | bytes 133120 | tf_op jit(solution)/shard_map/load/pallas_call | solution.py:80
  2.2 0.4 collective-permute-done.1.list_peer
  2.6 0.0 collective-permute-done.peer_ref.refs_1_
  2.6 0.3 pick.1
  2.9 2.7 %collective-permute-start.2 = (bf16[256,256]{1,0:T(8,128)(2,1)S(1)}, bf16[256,256]{1,0:T(8,128)(2,1)S(1)}, u32[]{:S(2)}, u32[]{:S(2)}) collective-permute-start(bf16[256,256]{1,0:T(8,128)(2,1)S(1)} %get-tuple-element.67), channel_id=1, source_target_pairs={{0,2},{2,0},{4,6},{6,4},{8,10},{10,8},{12,14},{14,12},{16,18},{18,... | collective-permute-start | bytes 393224 | tf_op jit(solution)/shard_map/ppermute | solution.py:361
  5.6 4.5 %collective-permute-start.3 = (bf16[256,256]{1,0:T(8,128)(2,1)S(1)}, bf16[256,256]{1,0:T(8,128)(2,1)S(1)}, u32[]{:S(2)}, u32[]{:S(2)}) collective-permute-start(bf16[256,256]{1,0:T(8,128)(2,1)S(1)} %get-tuple-element.71), channel_id=1, source_target_pairs={{0,30},{2,4},{4,2},{6,8},{8,6},{10,12},{12,10},{14,16},{16,14},{18... | collective-permute-start | bytes 393224 | tf_op jit(solution)/shard_map/ppermute | solution.py:361
  10.1 2.0 %index.1 = (s16[2,3072,128]{2,1,0:T(8,128)(2,1)S(1)}, s32[1,3072]{1,0:T(1,128)S(1)}, bf16[3072,256]{1,0:T(8,128)(2,1)S(1)}, bf16[2,768,256]{2,1,0:T(8,128)(2,1)S...) custom-call(s32[1,3072]{1,0:T(1,128)} %bitcast.2, ...), custom_call_target="tpu_custom_call" | custom-call | bytes 3440640 | tf_op jit(solution)/shard_map/index/pallas_call | solution.py:80
  12.2 2.9 %local.2.pre_ref = f32[3072,256]{1,0:T(8,128)S(1)} custom-call(bf16[3072,256]{1,0:T(8,128)(2,1)S(1)} %get-tuple-element.63.edge_ref, s16[2,3072,128]{2,1,0:T(8,128)(2,1)S(1)} %get-tuple-element.64.cols, bf16[256,256]{1,0:T(8,128)(2,1)S(1)} %get-tuple-element.48.own_ref.refs_0_, bf16[256,256]{1,0:T(8,128)(2,1)S(1)} %collective-permute-done.peer_ref.refs_1_, ...), custom_call_target="tpu_custom_call" | custom-call | flops 2013265920 | bytes 4196352 | tf_op jit(solution)/shard_map/local/pallas_call | solution.py:80
  15.0 0.0 collective-permute-done.2.rows_ref
  15.0 0.1 collective-permute-start.4
  15.1 1.1 %near.4.pre_ref = f32[3072,256]{1,0:T(8,128)S(1)} custom-call(f32[3072,256]{1,0:T(8,128)S(1)} %local.2.pre_ref, s16[2,3072,128]{2,1,0:T(8,128)(2,1)S(1)} %get-tuple-element.64.cols, bf16[2,768,256]{2,1,0:T(8,128)(2,1)S(1)} %get-tuple-element.65.refs_2_.w1_ref.refs_1_, bf16[256,256]{1,0:T(8,128)(2,1)S(1)} %collective-permute-done.2.rows_ref), custom_call_target="tpu_custom_call" | custom-call | flops 402653184 | bytes 5636096 | tf_op jit(solution)/shard_map/near/pallas_call | solution.py:80
  16.2 0.0 collective-permute-done.3.own
  16.3 0.6 %collective-permute-start.5 = (bf16[256,256]{1,0:T(8,128)(2,1)S(1)}, bf16[256,256]{1,0:T(8,128)(2,1)S(1)}, u32[]{:S(2)}, u32[]{:S(2)}) collective-permute-start(bf16[256,256]{1,0:T(8,128)(2,1)S(1)} %collective-permute-done.3.own), channel_id=1, source_target_pairs={{0,1},{1,0},{2,3},{3,2},{4,5},{5,4},{6,7},{7,6},{8,9},{9,8},{10,11... | collective-permute-start | bytes 393224 | tf_op jit(solution)/shard_map/ppermute | solution.py:332
  17.5 0.0 collective-permute-done.4.rows_ref
  17.5 1.1 %near.5.pre_ref = f32[3072,256]{1,0:T(8,128)S(1)} custom-call(f32[3072,256]{1,0:T(8,128)S(1)} %near.4.pre_ref, s16[2,3072,128]{2,1,0:T(8,128)(2,1)S(1)} %get-tuple-element.64.cols, bf16[2,768,256]{2,1,0:T(8,128)(2,1)S(1)} %get-tuple-element.65.refs_2_.w1_ref.refs_1_, bf16[256,256]{1,0:T(8,128)(2,1)S(1)} %collective-permute-done.4.rows_ref), custom_call_target="tpu_custom_call" | custom-call | flops 402653184 | bytes 5636096 | tf_op jit(solution)/shard_map/near/pallas_call | solution.py:80
  18.6 0.0 collective-permute-done.5.peer
  18.6 3.3 %far.2 = (bf16[3072,256]{1,0:T(8,128)(2,1)S(1)}, bf16[512,256]{1,0:T(8,128)(2,1)S(1)}) custom-call(s32[1,1]{1,0:T(1,128)S(6)} %copy.16.live_ref, f32[3072,256]{1,0:T(8,128)S(1)} %near.5.pre_ref, s16[2,3072,128]{2,1,0:T(8,128)(2,1)S(1)} %get-tuple-element.64.cols, s32[1,3072]{1,0:T(1,128)S(1)} %get-tuple-element.73.recv_ref, ...), custom_call_target="tpu_custom_call" | custom-call | flops 2013265920 | bytes 7616516 | tf_op jit(solution)/shard_map/far/pallas_call | solution.py:80
  21.9 0.1 collective-permute-start.6
  22.0 1.5 %collective-permute-done.6.second = bf16[512,256]{1,0:T(8,128)(2,1)S(1)} collective-permute-done((bf16[512,256]{1,0:T(8,128)(2,1)S(1)}, bf16[512,256]{1,0:T(8,128)(2,1)S(1)}, u32[]{:S(2)}, u32[]{:S(2)}) %collective-permute-start.6) | collective-permute-done | bytes 262176 | tf_op jit(solution)/shard_map/ppermute | solution.py:332
  23.5 1.0 %nodes.1 = (bf16[512,256]{1,0:T(8,128)(2,1)S(1)}, bf16[256,256]{1,0:T(8,128)(2,1)S(1)}, bf16[256,256]{1,0:T(8,128)(2,1)S(1)}) custom-call(bf16[256,256]{1,0:T(8,128)(2,1)S(1)} %get-tuple-element.48.own_ref.refs_0_, bf16[256,256]{1,0:T(8,128)(2,1)S(1)} %collective-permute-done.peer_ref.refs_1_, bf16[512,256]{1,0:T(8,128)(2,1)S(1)} %get-tuple-element.77.first, ...), custom_call_target="tpu_custom_call" | custom-call | bytes 1581056 | tf_op jit(solution)/shard_map/nodes/pallas_call | solution.py:80
  24.5 0.1 collective-permute-start.7
  24.6 2.1 %collective-permute-start.8 = (bf16[256,256]{1,0:T(8,128)(2,1)S(1)}, bf16[256,256]{1,0:T(8,128)(2,1)S(1)}, u32[]{:S(2)}, u32[]{:S(2)}) collective-permute-start(bf16[256,256]{1,0:T(8,128)(2,1)S(1)} %get-tuple-element.88), channel_id=1, source_target_pairs={{0,30},{2,4},{4,2},{6,8},{8,6},{10,12},{12,10},{14,16},{16,14},{18... | collective-permute-start | bytes 393224 | tf_op jit(solution)/shard_map/ppermute | solution.py:361
  26.7 2.8 %local.3.pre_ref = f32[3072,256]{1,0:T(8,128)S(1)} custom-call(bf16[3072,256]{1,0:T(8,128)(2,1)S(1)} %get-tuple-element.83.edge_ref, s16[2,3072,128]{2,1,0:T(8,128)(2,1)S(1)} %get-tuple-element.64.cols, bf16[512,256]{1,0:T(8,128)(2,1)S(1)} %get-tuple-element.82.refs_0_.nodes_ref, bf16[2,768,256]{2,1,0:T(8,128)(2,1)S(1)} %get-tuple-element.65.refs_2_.w1_ref.refs_1_, ...), custom_call_target="tpu_custom_call" | custom-call | flops 2013265920 | bytes 4196352 | tf_op jit(solution)/shard_map/local/pallas_call | solution.py:80
  29.5 0.0 collective-permute-done.7.rows_ref
  29.6 0.1 collective-permute-start.9
  29.7 1.1 %near.6.pre_ref = f32[3072,256]{1,0:T(8,128)S(1)} custom-call(f32[3072,256]{1,0:T(8,128)S(1)} %local.3.pre_ref, s16[2,3072,128]{2,1,0:T(8,128)(2,1)S(1)} %get-tuple-element.64.cols, bf16[2,768,256]{2,1,0:T(8,128)(2,1)S(1)} %get-tuple-element.65.refs_2_.w1_ref.refs_1_, bf16[256,256]{1,0:T(8,128)(2,1)S(1)} %collective-permute-done.7.rows_ref), custom_call_target="tpu_custom_call" | custom-call | flops 402653184 | bytes 5636096 | tf_op jit(solution)/shard_map/near/pallas_call | solution.py:80
  30.8 2.4 %collective-permute-done.8.own = bf16[256,256]{1,0:T(8,128)(2,1)S(1)} collective-permute-done((bf16[256,256]{1,0:T(8,128)(2,1)S(1)}, bf16[256,256]{1,0:T(8,128)(2,1)S(1)}, u32[]{:S(2)}, u32[]{:S(2)}) %collective-permute-start.8) | collective-permute-done | bytes 131104 | tf_op jit(solution)/shard_map/ppermute | solution.py:361
  33.3 0.0 collective-permute-start.10
  33.3 0.0 collective-permute-done.9.rows_ref
  33.3 1.1 %near.7.pre_ref = f32[3072,256]{1,0:T(8,128)S(1)} custom-call(f32[3072,256]{1,0:T(8,128)S(1)} %near.6.pre_ref, s16[2,3072,128]{2,1,0:T(8,128)(2,1)S(1)} %get-tuple-element.64.cols, bf16[2,768,256]{2,1,0:T(8,128)(2,1)S(1)} %get-tuple-element.65.refs_2_.w1_ref.refs_1_, bf16[256,256]{1,0:T(8,128)(2,1)S(1)} %collective-permute-done.9.rows_ref), custom_call_target="tpu_custom_call" | custom-call | flops 402653184 | bytes 5636096 | tf_op jit(solution)/shard_map/near/pallas_call | solution.py:80
  34.4 0.2 collective-permute-done.10.peer
  34.6 3.7 %far.3 = (bf16[3072,256]{1,0:T(8,128)(2,1)}, bf16[256,256]{1,0:T(8,128)(2,1)S(1)}, bf16[256,256]{1,0:T(8,128)(2,1)S(1)}) custom-call(s32[1,1]{1,0:T(1,128)S(6)} %copy.16.live_ref, f32[3072,256]{1,0:T(8,128)S(1)} %near.7.pre_ref, s16[2,3072,128]{2,1,0:T(8,128)(2,1)S(1)} %get-tuple-element.64.cols, s32[1,3072]{1,0:T(1,128)S(1)} %get-tuple-element.73.recv_ref, ...), custom_call_target="tpu_custom_call" | custom-call | flops 2013265920 | bytes 7616516 | tf_op jit(solution)/shard_map/far/pallas_call | solution.py:80
  38.3 0.4 collective-permute-start.11
  38.7 1.0 %collective-permute-done.11.second = bf16[256,256]{1,0:T(8,128)(2,1)S(1)} collective-permute-done((bf16[256,256]{1,0:T(8,128)(2,1)S(1)}, bf16[256,256]{1,0:T(8,128)(2,1)S(1)}, u32[]{:S(2)}, u32[]{:S(2)}) %collective-permute-start.11) | collective-permute-done | bytes 131104 | tf_op jit(solution)/shard_map/ppermute | solution.py:332
  39.7 1.2 %last.1 = bf16[256,256]{1,0:T(8,128)(2,1)} custom-call(bf16[512,256]{1,0:T(8,128)(2,1)S(1)} %get-tuple-element.82.refs_0_.nodes_ref, bf16[256,256]{1,0:T(8,128)(2,1)S(1)} %get-tuple-element.91.first, bf16[256,256]{1,0:T(8,128)(2,1)S(1)} %collective-permute-done.11.second, bf16[2,512,256]{2,1,0:T(8,128)(2,1)S(1)} %get-tuple-element.78.w1, ...), custom_call_target="tpu_custom_call" | custom-call | bytes 1314816 | tf_op jit(solution)/shard_map/last/pallas_call | solution.py:80
Async XLA Ops:
  0.6 1.9 %collective-permute-start = (bf16[256,256]{1,0:T(8,128)(2,1)}, bf16[256,256]{1,0:T(8,128)(2,1)S(1)}, u32[]{:S(2)}, u32[]{:S(2)}) collective-permute-start(bf16[256,256]{1,0:T(8,128)(2,1)} %refs_0_.1), channel_id=1, source_target_pairs={{0,1},{1,0},{2,3},{3,2},{4,5},{5,4},{6,7},{7,6},{8,9},{9,8},{10,11... | collective-permute-start | bytes 393224 | tf_op jit(solution)/shard_map/ppermute | solution.py:332
  1.2 1.4 %collective-permute-start.1 = (s32[1,4,128]{2,1,0:T(4,128)}, s32[1,4,128]{2,1,0:T(4,128)S(1)}, u32[]{:S(2)}, u32[]{:S(2)}) collective-permute-start(s32[1,4,128]{2,1,0:T(4,128)} %refs_1_.1), channel_id=1, source_target_pairs={{0,1},{1,0},{2,3},{3,2},{4,5},{5,4},{6,7},{7,6},{8,9},{9,8},{10,11... | collective-permute-start | bytes 6152 | tf_op jit(solution)/shard_map/ppermute | solution.py:332
  2.9 12.2 %collective-permute-start.2 = (bf16[256,256]{1,0:T(8,128)(2,1)S(1)}, bf16[256,256]{1,0:T(8,128)(2,1)S(1)}, u32[]{:S(2)}, u32[]{:S(2)}) collective-permute-start(bf16[256,256]{1,0:T(8,128)(2,1)S(1)} %get-tuple-element.67), channel_id=1, source_target_pairs={{0,2},{2,0},{4,6},{6,4},{8,10},{10,8},{12,14},{14,12},{16,18},{18,... | collective-permute-start | bytes 393224 | tf_op jit(solution)/shard_map/ppermute | solution.py:361
  5.6 10.7 %collective-permute-start.3 = (bf16[256,256]{1,0:T(8,128)(2,1)S(1)}, bf16[256,256]{1,0:T(8,128)(2,1)S(1)}, u32[]{:S(2)}, u32[]{:S(2)}) collective-permute-start(bf16[256,256]{1,0:T(8,128)(2,1)S(1)} %get-tuple-element.71), channel_id=1, source_target_pairs={{0,30},{2,4},{4,2},{6,8},{8,6},{10,12},{12,10},{14,16},{16,14},{18... | collective-permute-start | bytes 393224 | tf_op jit(solution)/shard_map/ppermute | solution.py:361
  15.0 2.4 %collective-permute-start.4 = (bf16[256,256]{1,0:T(8,128)(2,1)S(1)}, bf16[256,256]{1,0:T(8,128)(2,1)S(1)}, u32[]{:S(2)}, u32[]{:S(2)}) collective-permute-start(bf16[256,256]{1,0:T(8,128)(2,1)S(1)} %collective-permute-done.2.rows_ref), channel_id=1, source_target_pairs={{0,1},{1,0},{2,3},{3,2},{4,5},{5,4},{6,7},{7,6},{8,9},{9,8},{10,11... | collective-permute-start | bytes 393224 | tf_op jit(solution)/shard_map/ppermute | solution.py:332
  16.3 2.3 %collective-permute-start.5 = (bf16[256,256]{1,0:T(8,128)(2,1)S(1)}, bf16[256,256]{1,0:T(8,128)(2,1)S(1)}, u32[]{:S(2)}, u32[]{:S(2)}) collective-permute-start(bf16[256,256]{1,0:T(8,128)(2,1)S(1)} %collective-permute-done.3.own), channel_id=1, source_target_pairs={{0,1},{1,0},{2,3},{3,2},{4,5},{5,4},{6,7},{7,6},{8,9},{9,8},{10,11... | collective-permute-start | bytes 393224 | tf_op jit(solution)/shard_map/ppermute | solution.py:332
  21.9 1.6 %collective-permute-start.6 = (bf16[512,256]{1,0:T(8,128)(2,1)S(1)}, bf16[512,256]{1,0:T(8,128)(2,1)S(1)}, u32[]{:S(2)}, u32[]{:S(2)}) collective-permute-start(bf16[512,256]{1,0:T(8,128)(2,1)S(1)} %get-tuple-element.77.first), channel_id=1, source_target_pairs={{0,1},{1,0},{2,3},{3,2},{4,5},{5,4},{6,7},{7,6},{8,9},{9,8},{10,11... | collective-permute-start | bytes 786440 | tf_op jit(solution)/shard_map/ppermute | solution.py:332
  24.5 5.0 %collective-permute-start.7 = (bf16[256,256]{1,0:T(8,128)(2,1)S(1)}, bf16[256,256]{1,0:T(8,128)(2,1)S(1)}, u32[]{:S(2)}, u32[]{:S(2)}) collective-permute-start(bf16[256,256]{1,0:T(8,128)(2,1)S(1)} %get-tuple-element.84), channel_id=1, source_target_pairs={{0,2},{2,0},{4,6},{6,4},{8,10},{10,8},{12,14},{14,12},{16,18},{18,... | collective-permute-start | bytes 393224 | tf_op jit(solution)/shard_map/ppermute | solution.py:361
  24.6 8.6 %collective-permute-start.8 = (bf16[256,256]{1,0:T(8,128)(2,1)S(1)}, bf16[256,256]{1,0:T(8,128)(2,1)S(1)}, u32[]{:S(2)}, u32[]{:S(2)}) collective-permute-start(bf16[256,256]{1,0:T(8,128)(2,1)S(1)} %get-tuple-element.88), channel_id=1, source_target_pairs={{0,30},{2,4},{4,2},{6,8},{8,6},{10,12},{12,10},{14,16},{16,14},{18... | collective-permute-start | bytes 393224 | tf_op jit(solution)/shard_map/ppermute | solution.py:361
  29.6 3.7 %collective-permute-start.9 = (bf16[256,256]{1,0:T(8,128)(2,1)S(1)}, bf16[256,256]{1,0:T(8,128)(2,1)S(1)}, u32[]{:S(2)}, u32[]{:S(2)}) collective-permute-start(bf16[256,256]{1,0:T(8,128)(2,1)S(1)} %collective-permute-done.7.rows_ref), channel_id=1, source_target_pairs={{0,1},{1,0},{2,3},{3,2},{4,5},{5,4},{6,7},{7,6},{8,9},{9,8},{10,11... | collective-permute-start | bytes 393224 | tf_op jit(solution)/shard_map/ppermute | solution.py:332
  33.3 1.3 %collective-permute-start.10 = (bf16[256,256]{1,0:T(8,128)(2,1)S(1)}, bf16[256,256]{1,0:T(8,128)(2,1)S(1)}, u32[]{:S(2)}, u32[]{:S(2)}) collective-permute-start(bf16[256,256]{1,0:T(8,128)(2,1)S(1)} %collective-permute-done.8.own), channel_id=1, source_target_pairs={{0,1},{1,0},{2,3},{3,2},{4,5},{5,4},{6,7},{7,6},{8,9},{9,8},{10,11... | collective-permute-start | bytes 393224 | tf_op jit(solution)/shard_map/ppermute | solution.py:332
  38.3 1.4 %collective-permute-start.11 = (bf16[256,256]{1,0:T(8,128)(2,1)S(1)}, bf16[256,256]{1,0:T(8,128)(2,1)S(1)}, u32[]{:S(2)}, u32[]{:S(2)}) collective-permute-start(bf16[256,256]{1,0:T(8,128)(2,1)S(1)} %get-tuple-element.92), channel_id=1, source_target_pairs={{0,1},{1,0},{2,3},{3,2},{4,5},{5,4},{6,7},{7,6},{8,9},{9,8},{10,11... | collective-permute-start | bytes 393224 | tf_op jit(solution)/shard_map/ppermute | solution.py:332

commit v5 on v4

--- a/solution.py
+++ b/solution.py
@@ -107,10 +107,10 @@
     return jnp.transpose(jnp.broadcast_to(row, (HALF, HALF)))
 
 
-def one_hot_rows(row):
+def one_hot_rows(row, width):
     col = column(row)
     lane = lax.broadcasted_iota(jnp.int32, (HALF, HALF), 1)
-    parts = [jnp.where(col == lane + k, 1.0, 0.0) for k in (0, HALF)]
+    parts = [jnp.where(col == lane + k, 1.0, 0.0) for k in range(0, width, HALF)]
     return jnp.concatenate(parts, axis=1).astype(BF16)
 
 
@@ -118,17 +118,17 @@
     return pl.ds(pl.multiple_of(start, unit or size), size)
 
 
-def face_rows(stride, lists, nodes, far, near):
+def faces(stride):
     core, par_d, par_s = place(stride)
     par = jnp.where(core == 0, par_d, par_s)
-    for face, ref in ((2 * core + 1 - par, far), (2 * core + par, near)):
-        for n in range(2):
-            hot = one_hot_rows(lists[n][0, pl.ds(face, 1), :])
-            ref[n * HALF : (n + 1) * HALF, :] = mm(hot, nodes[n]).astype(BF16)
+    return 2 * core + 1 - par, 2 * core + par
 
 
 def pick_kernel(stride, own_ref, peer_ref, list_own, list_peer, far, near):
-    face_rows(stride, (list_own, list_peer), (own_ref[...], peer_ref[...]), far, near)
+    for face, ref in zip(faces(stride), (far, near)):
+        for n, (lists, nodes) in enumerate(((list_own, own_ref), (list_peer, peer_ref))):
+            hot = one_hot_rows(lists[0, pl.ds(face, 1), :], TILE)
+            ref[n * HALF : (n + 1) * HALF, :] = mm(hot, nodes[...]).astype(BF16)
 
 
 def load_kernel(count, *refs):
@@ -146,18 +146,14 @@
     return [pltpu.with_memory_space_constraint(a, pltpu.HBM) for a in arrays]
 
 
-def index_kernel(stride, edges, loads, *refs):
-    hbm, cols, refs = refs[: loads + 2], refs[loads + 2], refs[loads + 3 :]
-    recv_ref, vmem, (send_ref, sems) = refs[0], refs[1 : loads + 1], refs[loads + 1 :]
+def index_kernel(stride, edges, loads, send_ref, recv_ref, *refs):
+    hbm, cols, vmem, sems = refs[:loads], refs[loads], refs[loads + 1 : -1], refs[-1]
     copies = [
-        pltpu.make_async_copy(src, dst, sems.at[k])
-        for k, (src, dst) in enumerate(zip(hbm, (send_ref, recv_ref, *vmem)))
+        pltpu.make_async_copy(src, dst, sems.at[k]) for k, (src, dst) in enumerate(zip(hbm, vmem))
     ]
     for copy in copies:
         copy.start()
     _, par_d, par_s = place(stride)
-    for copy in copies[:2]:
-        copy.wait()
     for k in range(edges // HALF):
         at = pl.ds(k * HALF, HALF)
         v = send_ref[:, at]
@@ -172,7 +168,7 @@
         spot = jnp.where(v < 2 * TILE, v, tile * TILE + at_tile)
         cols[0, at, :] = column(spot).astype(I16)
         cols[1, at, :] = column(recv_ref[:, at]).astype(I16)
-    for copy in copies[2:]:
+    for copy in copies:
         copy.wait()
 
 
@@ -237,10 +233,9 @@
     layer, split, live_ref, pre_ref, cols, recv_ref, edge_ref, w1_ref, w2_ref, gain_ref, own, peer, out_ref, *refs
 ):
     if split:
-        keep_ref, give_ref, table, raw, msgs, sums, block_ref, sems = refs
+        keep_ref, give_ref, table, raw, msgs, sums = refs
     else:
         part_ref, table, raw, msgs, sums = refs
-        block_ref = out_ref
     halo_tables(layer, own, peer, w1_ref, table)
     gain = gain_ref[layer : layer + 1, :]
     live = live_ref[0, 0]
@@ -260,7 +255,7 @@
         scale = jnp.where(row < live, scale, 0.0)
         message = (center * scale * gain).astype(BF16)
         msgs[at, :] = message
-        block_ref[at, :] = edge_ref[at, :] + message
+        out_ref[at, :] = edge_ref[at, :] + message
 
     def segment(at, first):
         shape = (2 * TILE, ROWS)
@@ -270,26 +265,17 @@
         part = mm(hot, msgs[at, :])
         sums[...] = part if first else sums[...] + part
 
-    copies = []
     for k in range(count + 2):
         if k >= 2:
             segment(pl.ds((k - 2) * ROWS, ROWS), k == 2)
         if 1 <= k <= count:
-            at = pl.ds((k - 1) * ROWS, ROWS)
-            norm(at, (k - 1) * ROWS)
-            if split:
-                copies.append(
-                    pltpu.make_async_copy(block_ref.at[at, :], out_ref.at[at, :], sems.at[k - 1])
-                )
-                copies[-1].start()
+            norm(pl.ds((k - 1) * ROWS, ROWS), (k - 1) * ROWS)
         if k < count:
             gather(pl.ds(k * ROWS, ROWS))
     if split:
         core = lax.axis_index("edge")
         keep_ref[...] = sums[dyn(core * TILE, TILE), :].astype(BF16)
         give_ref[...] = sums[dyn((1 - core) * TILE, TILE), :].astype(BF16)
-        for copy in copies:
-            copy.wait()
     else:
         part_ref[...] = sums[...].astype(BF16)
 
@@ -303,15 +289,17 @@
 
 
 def node_kernel(
-    stride, layer, own_ref, peer_ref, first, second, list_own, list_peer, w1, b1, w2, gain, out, far, near
+    stride, layer, own_ref, peer_ref, first, second, list_own, list_peer, w1, b1, w2, gain, out, far, near, old
 ):
     core = lax.axis_index("edge")
-    nodes = []
-    for owner, ref in ((core, own_ref), (1 - core, peer_ref)):
-        at = dyn(owner * TILE, TILE)
-        nodes.append(updated(layer, ref[...], first[at, :], second[at, :], w1, b1, w2, gain))
-        out[at, :] = nodes[-1]
-    face_rows(stride, (list_own, list_peer), nodes, far, near)
+    old[dyn(core * TILE, TILE), :] = own_ref[...]
+    old[dyn((1 - core) * TILE, TILE), :] = peer_ref[...]
+    nodes = updated(layer, old[...], first[...], second[...], w1, b1, w2, gain)
+    out[...] = nodes
+    for face, ref in zip(faces(stride), (far, near)):
+        for n, (owner, lists) in enumerate(((core, list_own), (1 - core, list_peer))):
+            hot = one_hot_rows(lists[0, pl.ds(face, 1), :] + owner * TILE, 2 * TILE)
+            ref[n * HALF : (n + 1) * HALF, :] = mm(hot, nodes).astype(BF16)
 
 
 def last_kernel(layer, nodes_ref, first, second, w1, b1, w2, gain, out):
@@ -368,12 +356,14 @@
 
     peer_nodes = swapped(node_lat)
     peer_lists = swapped(send_rows)
-    node_lat, send_rows = call(
-        functools.partial(load_kernel, 2),
-        [shaped(a.shape, a.dtype) for a in (node_lat, send_rows)],
-        in_hbm((node_lat, send_rows)),
-        scratch=[pltpu.SemaphoreType.DMA((2,))],
-        stay=(0, 1),
+    send_at, recv_at = senders[None], receivers[None]
+    first = (node_lat, send_rows, send_at, recv_at)
+    node_lat, send_rows, send_at, recv_at = call(
+        functools.partial(load_kernel, len(first)),
+        [shaped(a.shape, a.dtype) for a in first],
+        in_hbm(first),
+        scratch=[pltpu.SemaphoreType.DMA((len(first),))],
+        stay=range(len(first)),
         name="load",
     )
     far_rows, near_rows = call(
@@ -383,17 +373,16 @@
         name="pick",
     )
     loads = (edge_lat, edge_w1, edge_w2, node_w1, node_w2, edge_b1, edge_gain, node_b1, node_gain)
-    far_rows, near_rows, *hbm = lax.optimization_barrier(
-        (far_rows, near_rows, senders[None], receivers[None], *loads)
+    far_rows, near_rows, send_at, recv_at, *hbm = lax.optimization_barrier(
+        (far_rows, near_rows, send_at, recv_at, *loads)
     )
     hbm = in_hbm(hbm)
-    cols, recv_row, edge_rows, edge_w1, edge_w2, node_w1, node_w2, edge_b1, edge_gain, node_b1, node_gain = call(
+    cols, edge_rows, edge_w1, edge_w2, node_w1, node_w2, edge_b1, edge_gain, node_b1, node_gain = call(
         functools.partial(index_kernel, stride, edges, len(loads)),
-        [shaped((2, edges, HALF), I16), shaped((1, edges), jnp.int32)]
-        + [shaped(a.shape, a.dtype) for a in loads],
-        hbm,
-        scratch=[pltpu.VMEM((1, edges), jnp.int32), pltpu.SemaphoreType.DMA((len(hbm),))],
-        stay=range(len(hbm)),
+        [shaped((2, edges, HALF), I16)] + [shaped(a.shape, a.dtype) for a in loads],
+        (send_at, recv_at, *hbm),
+        scratch=[pltpu.SemaphoreType.DMA((len(hbm),))],
+        stay=range(2, len(hbm) + 2),
         name="index",
     )
     for layer in range(LAYERS):
@@ -425,22 +414,28 @@
         edge_rows, *partial = call(
             functools.partial(edge_kernel, layer, last),
             [shaped((edges, width), BF16)] + outs,
-            (live_edges, pre, cols, recv_row, edge_rows, edge_w1, edge_w2, edge_gain, far, far_other),
+            (live_edges, pre, cols, recv_at, edge_rows, edge_w1, edge_w2, edge_gain, far, far_other),
             scratch=[
                 table,
                 pltpu.VMEM((edges, width), F32),
                 messages,
                 pltpu.VMEM((2 * nodes, width), F32),
-            ]
-            + last * [messages, pltpu.SemaphoreType.DMA((edges // ROWS,))],
+            ],
             smem=(0,),
-            leave=last * (0,),
             flops=5 * pass_flops,
             name="far",
         )
         other = swapped(partial[-1])
         weights = (node_w1, node_b1, node_w2, node_gain)
         if last:
+            (edge_out,) = call(
+                functools.partial(load_kernel, 1),
+                [shaped((edges, width), BF16)],
+                (edge_rows,),
+                scratch=[pltpu.SemaphoreType.DMA((1,))],
+                leave=(0,),
+                name="store",
+            )
             out = call(
                 functools.partial(last_kernel, layer),
                 shaped((nodes, width), BF16),
@@ -452,9 +447,10 @@
                 functools.partial(node_kernel, stride, layer),
                 [shaped((2 * nodes, width), BF16), rows_out, rows_out],
                 (*node_args, partial[0], other, send_rows, peer_lists, *weights),
+                scratch=[table],
                 name="nodes",
             )
-    return out, edge_rows
+    return out, edge_out
 
 
 def shards(*args):

time: 41.1 us -> 41.7 us (1.015)
  Pallas kernels: 22.6 us -> 24.2 us
  waiting for transfers between devices: 5.61 us -> 4.69 us
    pallas_call x13 -> x14, Pallas kernels: 22.6 us -> 24.2 us  [call(): pl.pallas_call(kernel, out_shape=outs, in_specs=[IN_SMEM if k in smem els...]
    ppermute x8, waiting for transfers between devices: 3.13 us -> 2.09 us  [swapped(): return lax.ppermute(value, 'edge', [(0, 1), (1, 0)])]
  transfers between devices with their start and end apart: 12 -> 12, of which waited for: 5 -> 5; matrix products, arithmetic and copies ran while one was open for 0% -> 0% of each run, Pallas kernels for 32% -> 36%
where the time goes in v5:
time: 41.7 us; the launch traced here: 41.5 us
  Pallas kernels  24.2 us (58%)
  starting transfers between devices  11.1 us (27%)
  waiting for transfers between devices  4.69 us (11%)
  between operations  1.44 us (3%)
    pallas_call x14, Pallas kernels, call(): pl.pallas_call(kernel, out_shape=outs, in_specs=[IN_SMEM if k in smem els...  24.2 us
    ppermute x4, starting transfers between devices, sent_by_core(): return lax.ppermute(value, ('dom', 'edge'), pairs)  9.28 us
    ppermute x4, waiting for transfers between devices, sent_by_core(): return lax.ppermute(value, ('dom', 'edge'), pairs)  2.59 us
    ppermute x8, waiting for transfers between devices, swapped(): return lax.ppermute(value, 'edge', [(0, 1), (1, 0)])  2.09 us
    ppermute x8, starting transfers between devices, swapped(): return lax.ppermute(value, 'edge', [(0, 1), (1, 0)])  1.85 us
  transfers between devices with their start and end apart: 12, of which 5 were waited for; matrix products, arithmetic and copies ran while one was open for 0% of the time, Pallas kernels for 36%

profile of v5, /device:TPU:0, one launch (start us, length us, event | category | flops | bytes accessed | tf_op | source)
XLA Modules:
  0.0 41.5 jit_solution(12406296356350284526)
XLA Ops:
  0.6 0.6 %collective-permute-start = (bf16[256,256]{1,0:T(8,128)(2,1)}, bf16[256,256]{1,0:T(8,128)(2,1)S(1)}, u32[]{:S(2)}, u32[]{:S(2)}) collective-permute-start(bf16[256,256]{1,0:T(8,128)(2,1)} %refs_0_.1), channel_id=1, source_target_pairs={{0,1},{1,0},{2,3},{3,2},{4,5},{5,4},{6,7},{7,6},{8,9},{9,8},{10,11... | collective-permute-start | bytes 393224 | tf_op jit(solution)/shard_map/ppermute | solution.py:320
  1.2 0.1 collective-permute-start.1
  1.3 0.9 %load.1 = (bf16[256,256]{1,0:T(8,128)(2,1)S(1)}, s32[1,4,128]{2,1,0:T(4,128)S(1)}, s32[1,3072]{1,0:T(1,128)S(1)}, s32[1,3072]{1,0:T(1,128)S(1)}) custom-call(bf16[256,256]{1,0:T(8,128)(2,1)} %refs_0_.1, s32[1,4,128]{2,1,0:T(4,128)} %refs_1_.1, s32[1,3072]{1,0:T(1,128)} %bitcast.2, s32[1,3072]{1,0:T(1,128)} %bitcast.3), custom_call_target="tpu_custom_call" | custom-call | bytes 157696 | tf_op jit(solution)/shard_map/load/pallas_call | solution.py:80
  2.2 0.3 collective-permute-done.1.list_peer
  2.6 0.0 collective-permute-done.peer_ref.refs_1_
  2.6 0.3 pick.1
  2.9 2.7 %collective-permute-start.2 = (bf16[256,256]{1,0:T(8,128)(2,1)S(1)}, bf16[256,256]{1,0:T(8,128)(2,1)S(1)}, u32[]{:S(2)}, u32[]{:S(2)}) collective-permute-start(bf16[256,256]{1,0:T(8,128)(2,1)S(1)} %get-tuple-element.70), channel_id=1, source_target_pairs={{0,2},{2,0},{4,6},{6,4},{8,10},{10,8},{12,14},{14,12},{16,18},{18,... | collective-permute-start | bytes 393224 | tf_op jit(solution)/shard_map/ppermute | solution.py:349
  5.6 4.5 %collective-permute-start.3 = (bf16[256,256]{1,0:T(8,128)(2,1)S(1)}, bf16[256,256]{1,0:T(8,128)(2,1)S(1)}, u32[]{:S(2)}, u32[]{:S(2)}) collective-permute-start(bf16[256,256]{1,0:T(8,128)(2,1)S(1)} %get-tuple-element.74), channel_id=1, source_target_pairs={{0,30},{2,4},{4,2},{6,8},{8,6},{10,12},{12,10},{14,16},{16,14},{18... | collective-permute-start | bytes 393224 | tf_op jit(solution)/shard_map/ppermute | solution.py:349
  10.1 2.7 %index.1 = (s16[2,3072,128]{2,1,0:T(8,128)(2,1)S(1)}, bf16[3072,256]{1,0:T(8,128)(2,1)S(1)}, bf16[2,768,256]{2,1,0:T(8,128)(2,1)S(1)}, bf16[2,256,256]{2,1,0:T(8...) custom-call(s32[1,3072]{1,0:T(1,128)S(1)} %get-tuple-element.55.send, ...), custom_call_target="tpu_custom_call" | custom-call | bytes 3440640 | tf_op jit(solution)/shard_map/index/pallas_call | solution.py:80
  12.9 2.9 %local.2.pre_ref = f32[3072,256]{1,0:T(8,128)S(1)} custom-call(bf16[3072,256]{1,0:T(8,128)(2,1)S(1)} %get-tuple-element.66.edge_ref, s16[2,3072,128]{2,1,0:T(8,128)(2,1)S(1)} %get-tuple-element.67.cols, bf16[256,256]{1,0:T(8,128)(2,1)S(1)} %get-tuple-element.49.own_ref.refs_0_, bf16[256,256]{1,0:T(8,128)(2,1)S(1)} %collective-permute-done.peer_ref.refs_1_, ...), custom_call_target="tpu_custom_call" | custom-call | flops 2013265920 | bytes 4196352 | tf_op jit(solution)/shard_map/local/pallas_call | solution.py:80
  15.7 0.0 collective-permute-done.2.rows_ref
  15.7 0.1 collective-permute-start.4
  15.8 1.1 %near.4.pre_ref = f32[3072,256]{1,0:T(8,128)S(1)} custom-call(f32[3072,256]{1,0:T(8,128)S(1)} %local.2.pre_ref, s16[2,3072,128]{2,1,0:T(8,128)(2,1)S(1)} %get-tuple-element.67.cols, bf16[2,768,256]{2,1,0:T(8,128)(2,1)S(1)} %get-tuple-element.68.refs_2_.w1_ref.refs_1_, bf16[256,256]{1,0:T(8,128)(2,1)S(1)} %collective-permute-done.2.rows_ref), custom_call_target="tpu_custom_call" | custom-call | flops 402653184 | bytes 5636096 | tf_op jit(solution)/shard_map/near/pallas_call | solution.py:80
  16.9 0.0 collective-permute-done.3.own
  17.0 0.6 %collective-permute-start.5 = (bf16[256,256]{1,0:T(8,128)(2,1)S(1)}, bf16[256,256]{1,0:T(8,128)(2,1)S(1)}, u32[]{:S(2)}, u32[]{:S(2)}) collective-permute-start(bf16[256,256]{1,0:T(8,128)(2,1)S(1)} %collective-permute-done.3.own), channel_id=1, source_target_pairs={{0,1},{1,0},{2,3},{3,2},{4,5},{5,4},{6,7},{7,6},{8,9},{9,8},{10,11... | collective-permute-start | bytes 393224 | tf_op jit(solution)/shard_map/ppermute | solution.py:320
  18.2 0.0 collective-permute-done.4.rows_ref
  18.2 1.1 %near.5.pre_ref = f32[3072,256]{1,0:T(8,128)S(1)} custom-call(f32[3072,256]{1,0:T(8,128)S(1)} %near.4.pre_ref, s16[2,3072,128]{2,1,0:T(8,128)(2,1)S(1)} %get-tuple-element.67.cols, bf16[2,768,256]{2,1,0:T(8,128)(2,1)S(1)} %get-tuple-element.68.refs_2_.w1_ref.refs_1_, bf16[256,256]{1,0:T(8,128)(2,1)S(1)} %collective-permute-done.4.rows_ref), custom_call_target="tpu_custom_call" | custom-call | flops 402653184 | bytes 5636096 | tf_op jit(solution)/shard_map/near/pallas_call | solution.py:80
  19.3 0.0 collective-permute-done.5.peer
  19.3 3.3 %far.2 = (bf16[3072,256]{1,0:T(8,128)(2,1)S(1)}, bf16[512,256]{1,0:T(8,128)(2,1)S(1)}) custom-call(s32[1,1]{1,0:T(1,128)S(6)} %copy.16.live_ref, f32[3072,256]{1,0:T(8,128)S(1)} %near.5.pre_ref, s16[2,3072,128]{2,1,0:T(8,128)(2,1)S(1)} %get-tuple-element.67.cols, s32[1,3072]{1,0:T(1,128)S(1)} %get-tuple-element.56.recv_ref, ...), custom_call_target="tpu_custom_call" | custom-call | flops 2013265920 | bytes 7616516 | tf_op jit(solution)/shard_map/far/pallas_call | solution.py:80
  22.6 0.1 collective-permute-start.6
  22.7 1.5 %collective-permute-done.6.second = bf16[512,256]{1,0:T(8,128)(2,1)S(1)} collective-permute-done((bf16[512,256]{1,0:T(8,128)(2,1)S(1)}, bf16[512,256]{1,0:T(8,128)(2,1)S(1)}, u32[]{:S(2)}, u32[]{:S(2)}) %collective-permute-start.6) | collective-permute-done | bytes 262176 | tf_op jit(solution)/shard_map/ppermute | solution.py:320
  24.2 1.1 %nodes.1 = (bf16[512,256]{1,0:T(8,128)(2,1)S(1)}, bf16[256,256]{1,0:T(8,128)(2,1)S(1)}, bf16[256,256]{1,0:T(8,128)(2,1)S(1)}) custom-call(bf16[256,256]{1,0:T(8,128)(2,1)S(1)} %get-tuple-element.49.own_ref.refs_0_, bf16[256,256]{1,0:T(8,128)(2,1)S(1)} %collective-permute-done.peer_ref.refs_1_, bf16[512,256]{1,0:T(8,128)(2,1)S(1)} %get-tuple-element.79.first, ...), custom_call_target="tpu_custom_call" | custom-call | bytes 1581056 | tf_op jit(solution)/shard_map/nodes/pallas_call | solution.py:80
  25.3 0.1 collective-permute-start.7
  25.4 2.0 %collective-permute-start.8 = (bf16[256,256]{1,0:T(8,128)(2,1)S(1)}, bf16[256,256]{1,0:T(8,128)(2,1)S(1)}, u32[]{:S(2)}, u32[]{:S(2)}) collective-permute-start(bf16[256,256]{1,0:T(8,128)(2,1)S(1)} %get-tuple-element.90), channel_id=1, source_target_pairs={{0,30},{2,4},{4,2},{6,8},{8,6},{10,12},{12,10},{14,16},{16,14},{18... | collective-permute-start | bytes 393224 | tf_op jit(solution)/shard_map/ppermute | solution.py:349
  27.3 2.8 %local.3.pre_ref = f32[3072,256]{1,0:T(8,128)S(1)} custom-call(bf16[3072,256]{1,0:T(8,128)(2,1)S(1)} %get-tuple-element.85.edge_ref, s16[2,3072,128]{2,1,0:T(8,128)(2,1)S(1)} %get-tuple-element.67.cols, bf16[512,256]{1,0:T(8,128)(2,1)S(1)} %get-tuple-element.84.refs_0_.nodes_ref, bf16[2,768,256]{2,1,0:T(8,128)(2,1)S(1)} %get-tuple-element.68.refs_2_.w1_ref.refs_1_, ...), custom_call_target="tpu_custom_call" | custom-call | flops 2013265920 | bytes 4196352 | tf_op jit(solution)/shard_map/local/pallas_call | solution.py:80
  30.2 0.1 collective-permute-done.7.rows_ref
  30.3 0.1 collective-permute-start.9
  30.4 1.1 %near.6.pre_ref = f32[3072,256]{1,0:T(8,128)S(1)} custom-call(f32[3072,256]{1,0:T(8,128)S(1)} %local.3.pre_ref, s16[2,3072,128]{2,1,0:T(8,128)(2,1)S(1)} %get-tuple-element.67.cols, bf16[2,768,256]{2,1,0:T(8,128)(2,1)S(1)} %get-tuple-element.68.refs_2_.w1_ref.refs_1_, bf16[256,256]{1,0:T(8,128)(2,1)S(1)} %collective-permute-done.7.rows_ref), custom_call_target="tpu_custom_call" | custom-call | flops 402653184 | bytes 5636096 | tf_op jit(solution)/shard_map/near/pallas_call | solution.py:80
  31.6 2.4 %collective-permute-done.8.own = bf16[256,256]{1,0:T(8,128)(2,1)S(1)} collective-permute-done((bf16[256,256]{1,0:T(8,128)(2,1)S(1)}, bf16[256,256]{1,0:T(8,128)(2,1)S(1)}, u32[]{:S(2)}, u32[]{:S(2)}) %collective-permute-start.8) | collective-permute-done | bytes 131104 | tf_op jit(solution)/shard_map/ppermute | solution.py:349
  34.0 0.0 collective-permute-start.10
  34.0 0.0 collective-permute-done.9.rows_ref
  34.0 1.1 %near.7.pre_ref = f32[3072,256]{1,0:T(8,128)S(1)} custom-call(f32[3072,256]{1,0:T(8,128)S(1)} %near.6.pre_ref, s16[2,3072,128]{2,1,0:T(8,128)(2,1)S(1)} %get-tuple-element.67.cols, bf16[2,768,256]{2,1,0:T(8,128)(2,1)S(1)} %get-tuple-element.68.refs_2_.w1_ref.refs_1_, bf16[256,256]{1,0:T(8,128)(2,1)S(1)} %collective-permute-done.9.rows_ref), custom_call_target="tpu_custom_call" | custom-call | flops 402653184 | bytes 5636096 | tf_op jit(solution)/shard_map/near/pallas_call | solution.py:80
  35.1 0.2 collective-permute-done.10.peer
  35.3 3.4 %far.3 = (bf16[3072,256]{1,0:T(8,128)(2,1)S(1)}, bf16[256,256]{1,0:T(8,128)(2,1)S(1)}, bf16[256,256]{1,0:T(8,128)(2,1)S(1)}) custom-call(s32[1,1]{1,0:T(1,128)S(6)} %copy.16.live_ref, f32[3072,256]{1,0:T(8,128)S(1)} %near.7.pre_ref, s16[2,3072,128]{2,1,0:T(8,128)(2,1)S(1)} %get-tuple-element.67.cols, s32[1,3072]{1,0:T(1,128)S(1)} %get-tuple-element.56.recv_ref, ...), custom_call_target="tpu_custom_call" | custom-call | flops 2013265920 | bytes 7616516 | tf_op jit(solution)/shard_map/far/pallas_call | solution.py:80
  38.7 0.4 collective-permute-start.11
  39.1 1.1 %store.1 = bf16[3072,256]{1,0:T(8,128)(2,1)} custom-call(bf16[3072,256]{1,0:T(8,128)(2,1)S(1)} %get-tuple-element.95.refs_0_), custom_call_target="tpu_custom_call" | custom-call | bytes 1572864 | tf_op jit(solution)/shard_map/store/pallas_call | solution.py:80
  40.3 0.0 collective-permute-done.11.second
  40.3 1.2 %last.1 = bf16[256,256]{1,0:T(8,128)(2,1)} custom-call(bf16[512,256]{1,0:T(8,128)(2,1)S(1)} %get-tuple-element.84.refs_0_.nodes_ref, bf16[256,256]{1,0:T(8,128)(2,1)S(1)} %get-tuple-element.93.first, bf16[256,256]{1,0:T(8,128)(2,1)S(1)} %collective-permute-done.11.second, bf16[2,512,256]{2,1,0:T(8,128)(2,1)S(1)} %get-tuple-element.80.w1, ...), custom_call_target="tpu_custom_call" | custom-call | bytes 1314816 | tf_op jit(solution)/shard_map/last/pallas_call | solution.py:80
Async XLA Ops:
  0.6 1.9 %collective-permute-start = (bf16[256,256]{1,0:T(8,128)(2,1)}, bf16[256,256]{1,0:T(8,128)(2,1)S(1)}, u32[]{:S(2)}, u32[]{:S(2)}) collective-permute-start(bf16[256,256]{1,0:T(8,128)(2,1)} %refs_0_.1), channel_id=1, source_target_pairs={{0,1},{1,0},{2,3},{3,2},{4,5},{5,4},{6,7},{7,6},{8,9},{9,8},{10,11... | collective-permute-start | bytes 393224 | tf_op jit(solution)/shard_map/ppermute | solution.py:320
  1.2 1.4 %collective-permute-start.1 = (s32[1,4,128]{2,1,0:T(4,128)}, s32[1,4,128]{2,1,0:T(4,128)S(1)}, u32[]{:S(2)}, u32[]{:S(2)}) collective-permute-start(s32[1,4,128]{2,1,0:T(4,128)} %refs_1_.1), channel_id=1, source_target_pairs={{0,1},{1,0},{2,3},{3,2},{4,5},{5,4},{6,7},{7,6},{8,9},{9,8},{10,11... | collective-permute-start | bytes 6152 | tf_op jit(solution)/shard_map/ppermute | solution.py:320
  2.9 12.9 %collective-permute-start.2 = (bf16[256,256]{1,0:T(8,128)(2,1)S(1)}, bf16[256,256]{1,0:T(8,128)(2,1)S(1)}, u32[]{:S(2)}, u32[]{:S(2)}) collective-permute-start(bf16[256,256]{1,0:T(8,128)(2,1)S(1)} %get-tuple-element.70), channel_id=1, source_target_pairs={{0,2},{2,0},{4,6},{6,4},{8,10},{10,8},{12,14},{14,12},{16,18},{18,... | collective-permute-start | bytes 393224 | tf_op jit(solution)/shard_map/ppermute | solution.py:349
  5.6 11.4 %collective-permute-start.3 = (bf16[256,256]{1,0:T(8,128)(2,1)S(1)}, bf16[256,256]{1,0:T(8,128)(2,1)S(1)}, u32[]{:S(2)}, u32[]{:S(2)}) collective-permute-start(bf16[256,256]{1,0:T(8,128)(2,1)S(1)} %get-tuple-element.74), channel_id=1, source_target_pairs={{0,30},{2,4},{4,2},{6,8},{8,6},{10,12},{12,10},{14,16},{16,14},{18... | collective-permute-start | bytes 393224 | tf_op jit(solution)/shard_map/ppermute | solution.py:349
  15.7 2.4 %collective-permute-start.4 = (bf16[256,256]{1,0:T(8,128)(2,1)S(1)}, bf16[256,256]{1,0:T(8,128)(2,1)S(1)}, u32[]{:S(2)}, u32[]{:S(2)}) collective-permute-start(bf16[256,256]{1,0:T(8,128)(2,1)S(1)} %collective-permute-done.2.rows_ref), channel_id=1, source_target_pairs={{0,1},{1,0},{2,3},{3,2},{4,5},{5,4},{6,7},{7,6},{8,9},{9,8},{10,11... | collective-permute-start | bytes 393224 | tf_op jit(solution)/shard_map/ppermute | solution.py:320
  17.0 2.3 %collective-permute-start.5 = (bf16[256,256]{1,0:T(8,128)(2,1)S(1)}, bf16[256,256]{1,0:T(8,128)(2,1)S(1)}, u32[]{:S(2)}, u32[]{:S(2)}) collective-permute-start(bf16[256,256]{1,0:T(8,128)(2,1)S(1)} %collective-permute-done.3.own), channel_id=1, source_target_pairs={{0,1},{1,0},{2,3},{3,2},{4,5},{5,4},{6,7},{7,6},{8,9},{9,8},{10,11... | collective-permute-start | bytes 393224 | tf_op jit(solution)/shard_map/ppermute | solution.py:320
  22.6 1.6 %collective-permute-start.6 = (bf16[512,256]{1,0:T(8,128)(2,1)S(1)}, bf16[512,256]{1,0:T(8,128)(2,1)S(1)}, u32[]{:S(2)}, u32[]{:S(2)}) collective-permute-start(bf16[512,256]{1,0:T(8,128)(2,1)S(1)} %get-tuple-element.79.first), channel_id=1, source_target_pairs={{0,1},{1,0},{2,3},{3,2},{4,5},{5,4},{6,7},{7,6},{8,9},{9,8},{10,11... | collective-permute-start | bytes 786440 | tf_op jit(solution)/shard_map/ppermute | solution.py:320
  25.3 5.0 %collective-permute-start.7 = (bf16[256,256]{1,0:T(8,128)(2,1)S(1)}, bf16[256,256]{1,0:T(8,128)(2,1)S(1)}, u32[]{:S(2)}, u32[]{:S(2)}) collective-permute-start(bf16[256,256]{1,0:T(8,128)(2,1)S(1)} %get-tuple-element.86), channel_id=1, source_target_pairs={{0,2},{2,0},{4,6},{6,4},{8,10},{10,8},{12,14},{14,12},{16,18},{18,... | collective-permute-start | bytes 393224 | tf_op jit(solution)/shard_map/ppermute | solution.py:349
  25.4 8.6 %collective-permute-start.8 = (bf16[256,256]{1,0:T(8,128)(2,1)S(1)}, bf16[256,256]{1,0:T(8,128)(2,1)S(1)}, u32[]{:S(2)}, u32[]{:S(2)}) collective-permute-start(bf16[256,256]{1,0:T(8,128)(2,1)S(1)} %get-tuple-element.90), channel_id=1, source_target_pairs={{0,30},{2,4},{4,2},{6,8},{8,6},{10,12},{12,10},{14,16},{16,14},{18... | collective-permute-start | bytes 393224 | tf_op jit(solution)/shard_map/ppermute | solution.py:349
  30.3 3.7 %collective-permute-start.9 = (bf16[256,256]{1,0:T(8,128)(2,1)S(1)}, bf16[256,256]{1,0:T(8,128)(2,1)S(1)}, u32[]{:S(2)}, u32[]{:S(2)}) collective-permute-start(bf16[256,256]{1,0:T(8,128)(2,1)S(1)} %collective-permute-done.7.rows_ref), channel_id=1, source_target_pairs={{0,1},{1,0},{2,3},{3,2},{4,5},{5,4},{6,7},{7,6},{8,9},{9,8},{10,11... | collective-permute-start | bytes 393224 | tf_op jit(solution)/shard_map/ppermute | solution.py:320
  34.0 1.3 %collective-permute-start.10 = (bf16[256,256]{1,0:T(8,128)(2,1)S(1)}, bf16[256,256]{1,0:T(8,128)(2,1)S(1)}, u32[]{:S(2)}, u32[]{:S(2)}) collective-permute-start(bf16[256,256]{1,0:T(8,128)(2,1)S(1)} %collective-permute-done.8.own), channel_id=1, source_target_pairs={{0,1},{1,0},{2,3},{3,2},{4,5},{5,4},{6,7},{7,6},{8,9},{9,8},{10,11... | collective-permute-start | bytes 393224 | tf_op jit(solution)/shard_map/ppermute | solution.py:320
  38.7 1.5 %collective-permute-start.11 = (bf16[256,256]{1,0:T(8,128)(2,1)S(1)}, bf16[256,256]{1,0:T(8,128)(2,1)S(1)}, u32[]{:S(2)}, u32[]{:S(2)}) collective-permute-start(bf16[256,256]{1,0:T(8,128)(2,1)S(1)} %get-tuple-element.94), channel_id=1, source_target_pairs={{0,1},{1,0},{2,3},{3,2},{4,5},{5,4},{6,7},{7,6},{8,9},{9,8},{10,11... | collective-permute-start | bytes 393224 | tf_op jit(solution)/shard_map/ppermute | solution.py:320

commit v6 on v5

--- a/solution.py
+++ b/solution.py
@@ -146,30 +146,20 @@
     return [pltpu.with_memory_space_constraint(a, pltpu.HBM) for a in arrays]
 
 
-def index_kernel(stride, edges, loads, send_ref, recv_ref, *refs):
-    hbm, cols, vmem, sems = refs[:loads], refs[loads], refs[loads + 1 : -1], refs[-1]
-    copies = [
-        pltpu.make_async_copy(src, dst, sems.at[k]) for k, (src, dst) in enumerate(zip(hbm, vmem))
-    ]
-    for copy in copies:
-        copy.start()
+def columns(stride, send_ref, recv_ref, cols, at):
     _, par_d, par_s = place(stride)
-    for k in range(edges // HALF):
-        at = pl.ds(k * HALF, HALF)
-        v = send_ref[:, at]
-        j = v - 2 * TILE
-        owner = lax.shift_right_arithmetic(j, 9)
-        face = lax.shift_right_arithmetic(j, 7) & 3
-        core = lax.shift_right_arithmetic(face, 1)
-        par = jnp.where(core == 0, par_d, par_s)
-        near = (face & 1) != par
-        tile = jnp.where(near, 2, 4) + core
-        at_tile = ((owner ^ core) & 1) * HALF + (j & (HALF - 1))
-        spot = jnp.where(v < 2 * TILE, v, tile * TILE + at_tile)
-        cols[0, at, :] = column(spot).astype(I16)
-        cols[1, at, :] = column(recv_ref[:, at]).astype(I16)
-    for copy in copies:
-        copy.wait()
+    v = send_ref[:, at]
+    j = v - 2 * TILE
+    owner = lax.shift_right_arithmetic(j, 9)
+    face = lax.shift_right_arithmetic(j, 7) & 3
+    core = lax.shift_right_arithmetic(face, 1)
+    par = jnp.where(core == 0, par_d, par_s)
+    near = (face & 1) != par
+    tile = jnp.where(near, 2, 4) + core
+    at_tile = ((owner ^ core) & 1) * HALF + (j & (HALF - 1))
+    spot = jnp.where(v < 2 * TILE, v, tile * TILE + at_tile)
+    cols[0, at, :] = column(spot).astype(I16)
+    cols[1, at, :] = column(recv_ref[:, at]).astype(I16)
 
 
 def hits(spots, first, tiles):
@@ -183,27 +173,56 @@
     return jnp.concatenate(parts, axis=1)
 
 
-def local_kernel(layer, edge_ref, cols, *refs):
-    if layer:
-        dom_ref, w1_ref, b1_ref, pre_ref, table = refs
-        parts = ((0, 2 * TILE, dom_ref),)
-    else:
-        own_ref, peer_ref, w1_ref, b1_ref, pre_ref, table = refs
-        core = lax.axis_index("edge")
-        parts = ((core * TILE, TILE, own_ref), ((1 - core) * TILE, TILE, peer_ref))
+def project(layer, parts, w1_ref, table):
     for k in (1, 2):
         for start, size, ref in parts:
             table[dyn((2 * k - 2) * TILE + start, size, TILE), :] = mm(
                 ref[...], w1_ref[layer, k * TILE : (k + 1) * TILE, :]
             ).astype(BF16)
-    bias = b1_ref[layer : layer + 1, :]
+
+
+def local_block(layer, at, edge_ref, cols, w1_ref, b1_ref, table, pre_ref):
+    acc = mm(edge_ref[at, :], w1_ref[layer, 0:TILE, :])
+    acc = acc + mm(hits(cols[0, at, :], 0, 2), table[0 : 2 * TILE, :])
+    acc = acc + mm(hits(cols[1, at, :], 0, 2), table[2 * TILE :, :])
+    pre_ref[at, :] = acc + b1_ref[layer : layer + 1, :]
+
+
+def first_kernel(stride, loads, send_ref, recv_ref, own_ref, peer_ref, w1_ref, b1_ref, *refs):
+    hbm, (pre_ref, cols), refs = refs[:loads], refs[loads : loads + 2], refs[loads + 2 :]
+    vmem, (table, sems) = refs[:loads], refs[loads:]
+    edge_hbm, edge_ref = hbm[0], vmem[0]
+    edges = edge_ref.shape[0]
+    blocks = [pl.ds(start, LOCAL_ROWS) for start in range(0, edges, LOCAL_ROWS)]
+    copies = [(edge_hbm.at[at, :], edge_ref.at[at, :]) for at in blocks]
+    copies += zip(hbm[1:], vmem[1:])
+    copies = [pltpu.make_async_copy(*ends, sems.at[k]) for k, ends in enumerate(copies)]
+    for copy in copies:
+        copy.start()
+    core = lax.axis_index("edge")
+    parts = ((core * TILE, TILE, own_ref), ((1 - core) * TILE, TILE, peer_ref))
+
+    def make(k):
+        for start in range(k * LOCAL_ROWS, (k + 1) * LOCAL_ROWS, HALF):
+            columns(stride, send_ref, recv_ref, cols, pl.ds(start, HALF))
+
+    make(0)
+    project(0, parts, w1_ref, table)
+    for k, at in enumerate(blocks):
+        copies[k].wait()
+        if k + 1 < len(blocks):
+            make(k + 1)
+        local_block(0, at, edge_ref, cols, w1_ref, b1_ref, table, pre_ref)
+    for copy in copies[len(blocks) :]:
+        copy.wait()
+
+
+def local_kernel(layer, edge_ref, cols, dom_ref, w1_ref, b1_ref, pre_ref, table):
+    project(layer, ((0, 2 * TILE, dom_ref),), w1_ref, table)
 
     def step(k, carry):
         at = dyn(k * LOCAL_ROWS, LOCAL_ROWS)
-        acc = mm(edge_ref[at, :], w1_ref[layer, 0:TILE, :])
-        acc = acc + mm(hits(cols[0, at, :], 0, 2), table[0 : 2 * TILE, :])
-        acc = acc + mm(hits(cols[1, at, :], 0, 2), table[2 * TILE :, :])
-        pre_ref[at, :] = acc + bias
+        local_block(layer, at, edge_ref, cols, w1_ref, b1_ref, table, pre_ref)
         return carry
 
     lax.fori_loop(0, edge_ref.shape[0] // LOCAL_ROWS, step, 0)
@@ -221,12 +240,14 @@
     tile = 3 - core if peer else 2 + core
     table = mm(rows_ref[...], w1_ref[layer, TILE : 2 * TILE, :]).astype(BF16)
 
+    half = pre_ref.shape[0] // 2
+
     def step(k, carry):
-        at = dyn(k * LOCAL_ROWS, LOCAL_ROWS)
+        at = dyn(k * half, half)
         out_ref[at, :] = pre_ref[at, :] + mm(hits(cols[0, at, :], tile, 1), table)
         return carry
 
-    lax.fori_loop(0, pre_ref.shape[0] // LOCAL_ROWS, step, 0)
+    lax.fori_loop(0, 2, step, 0)
 
 
 def edge_kernel(
@@ -357,8 +378,8 @@
     peer_nodes = swapped(node_lat)
     peer_lists = swapped(send_rows)
     send_at, recv_at = senders[None], receivers[None]
-    first = (node_lat, send_rows, send_at, recv_at)
-    node_lat, send_rows, send_at, recv_at = call(
+    first = (node_lat, send_rows, send_at, recv_at, edge_w1, edge_b1)
+    node_lat, send_rows, send_at, recv_at, edge_w1, edge_b1 = call(
         functools.partial(load_kernel, len(first)),
         [shaped(a.shape, a.dtype) for a in first],
         in_hbm(first),
@@ -372,32 +393,34 @@
         (node_lat, peer_nodes, send_rows, peer_lists),
         name="pick",
     )
-    loads = (edge_lat, edge_w1, edge_w2, node_w1, node_w2, edge_b1, edge_gain, node_b1, node_gain)
-    far_rows, near_rows, send_at, recv_at, *hbm = lax.optimization_barrier(
-        (far_rows, near_rows, send_at, recv_at, *loads)
-    )
-    hbm = in_hbm(hbm)
-    cols, edge_rows, edge_w1, edge_w2, node_w1, node_w2, edge_b1, edge_gain, node_b1, node_gain = call(
-        functools.partial(index_kernel, stride, edges, len(loads)),
-        [shaped((2, edges, HALF), I16)] + [shaped(a.shape, a.dtype) for a in loads],
-        (send_at, recv_at, *hbm),
-        scratch=[pltpu.SemaphoreType.DMA((len(hbm),))],
-        stay=range(2, len(hbm) + 2),
-        name="index",
-    )
     for layer in range(LAYERS):
         last = layer == LAYERS - 1
-        node_args = (all_nodes,) if layer else (node_lat, peer_nodes)
         near = sent_by_core(near_rows, near_d, near_s)
         far = sent_by_core(far_rows, far_d, far_s)
-        pre = call(
-            functools.partial(local_kernel, layer),
-            pre_shape,
-            (edge_rows, cols, *node_args, edge_w1, edge_b1),
-            scratch=[pltpu.VMEM((4 * TILE, width), BF16)],
-            flops=5 * pass_flops,
-            name="local",
-        )
+        if layer == 0:
+            loads = (edge_lat, edge_w2, node_w1, node_w2, edge_gain, node_b1, node_gain)
+            pre, cols, edge_rows, edge_w2, node_w1, node_w2, edge_gain, node_b1, node_gain = call(
+                functools.partial(first_kernel, stride, len(loads)),
+                [pre_shape, shaped((2, edges, HALF), I16)]
+                + [shaped(a.shape, a.dtype) for a in loads],
+                (send_at, recv_at, node_lat, peer_nodes, edge_w1, edge_b1, *in_hbm(loads)),
+                scratch=[
+                    pltpu.VMEM((4 * TILE, width), BF16),
+                    pltpu.SemaphoreType.DMA((edges // LOCAL_ROWS + len(loads) - 1,)),
+                ],
+                stay=range(6, 6 + len(loads)),
+                flops=5 * pass_flops,
+                name="first",
+            )
+        else:
+            pre = call(
+                functools.partial(local_kernel, layer),
+                pre_shape,
+                (edge_rows, cols, all_nodes, edge_w1, edge_b1),
+                scratch=[pltpu.VMEM((4 * TILE, width), BF16)],
+                flops=5 * pass_flops,
+                name="local",
+            )
         pre, near, live_edges = lax.optimization_barrier((pre, near, live_edges))
         near_other = swapped(near)
         add = functools.partial(
@@ -446,7 +469,7 @@
             all_nodes, far_rows, near_rows = call(
                 functools.partial(node_kernel, stride, layer),
                 [shaped((2 * nodes, width), BF16), rows_out, rows_out],
-                (*node_args, partial[0], other, send_rows, peer_lists, *weights),
+                (node_lat, peer_nodes, partial[0], other, send_rows, peer_lists, *weights),
                 scratch=[table],
                 name="nodes",
             )
@@ -460,7 +483,7 @@
         lax.axis_size("edge") == 2
         and domains % 8 == 0
         and node_lat.shape == (TILE, TILE)
-        and edge_lat.shape[0] % ROWS == 0
+        and edge_lat.shape[0] % LOCAL_ROWS == 0
         and send_rows.shape[1:] == (4, HALF)
         and args[6].shape == (LAYERS, 3 * TILE, TILE)
     )

time: 41.7 us -> 41 us (0.983)
  Pallas kernels: 24.2 us -> 23.5 us
    pallas_call x14 -> x13, Pallas kernels: 24.2 us -> 23.5 us  [call(): pl.pallas_call(kernel, out_shape=outs, in_specs=[IN_SMEM if k in smem els...]
  transfers between devices with their start and end apart: 12 -> 12, of which waited for: 5 -> 4; matrix products, arithmetic and copies ran while one was open for 0% -> 0% of each run, Pallas kernels for 36% -> 35%
where the time goes in v6:
time: 41 us; the launch traced here: 40.9 us
  Pallas kernels  23.5 us (57%)
  starting transfers between devices  11.5 us (28%)
  waiting for transfers between devices  4.39 us (11%)
  between operations  1.44 us (4%)
    pallas_call x13, Pallas kernels, call(): pl.pallas_call(kernel, out_shape=outs, in_specs=[IN_SMEM if k in smem els...  23.5 us
    ppermute x4, starting transfers between devices, sent_by_core(): return lax.ppermute(value, ('dom', 'edge'), pairs)  9.54 us
    ppermute x4, waiting for transfers between devices, sent_by_core(): return lax.ppermute(value, ('dom', 'edge'), pairs)  2.46 us
    ppermute x8, starting transfers between devices, swapped(): return lax.ppermute(value, 'edge', [(0, 1), (1, 0)])  2 us
    ppermute x8, waiting for transfers between devices, swapped(): return lax.ppermute(value, 'edge', [(0, 1), (1, 0)])  1.93 us
  transfers between devices with their start and end apart: 12, of which 4 were waited for; matrix products, arithmetic and copies ran while one was open for 0% of the time, Pallas kernels for 35%

profile of v6, /device:TPU:0, one launch (start us, length us, event | category | flops | bytes accessed | tf_op | source)
XLA Modules:
  0.0 40.9 jit_solution(7246657250141899849)
XLA Ops:
  0.6 0.6 %collective-permute-start = (bf16[256,256]{1,0:T(8,128)(2,1)}, bf16[256,256]{1,0:T(8,128)(2,1)S(1)}, u32[]{:S(2)}, u32[]{:S(2)}) collective-permute-start(bf16[256,256]{1,0:T(8,128)(2,1)} %refs_0_.2), channel_id=1, source_target_pairs={{0,1},{1,0},{2,3},{3,2},{4,5},{5,4},{6,7},{7,6},{8,9},{9,8},{10,11... | collective-permute-start | bytes 393224 | tf_op jit(solution)/shard_map/ppermute | solution.py:341
  1.2 0.1 collective-permute-start.1
  1.3 1.3 %load.1 = (bf16[256,256]{1,0:T(8,128)(2,1)S(1)}, s32[1,4,128]{2,1,0:T(4,128)S(1)}, s32[1,3072]{1,0:T(1,128)S(1)}, s32[1,3072]{1,0:T(1,128)S(1)}, bf16[2,768,256]{2,1,0:T(8,128)(2,1)S(1)}, /*index=5*/f32[2,256]{1,0:T(2,128)S(1)}) custom-call(bf16[256,256]{1,0:T(8,128)(2,1)} %refs_0_.2, s32[1,4,128]{2,1,0:T(4,128)} %refs_1_.2, s32[1,3072]{1,0:T(1,128)} %bitcast.2, ...), custom_call_target="tpu_custom_call" | custom-call | bytes 946176 | tf_op jit(solution)/shard_map/load/pallas_call | solution.py:80
  2.6 0.0 collective-permute-done.1.list_peer
  2.6 0.0 collective-permute-done.peer_ref
  2.6 0.3 pick.1
  2.9 3.0 %collective-permute-start.2 = (bf16[256,256]{1,0:T(8,128)(2,1)S(1)}, bf16[256,256]{1,0:T(8,128)(2,1)S(1)}, u32[]{:S(2)}, u32[]{:S(2)}) collective-permute-start(bf16[256,256]{1,0:T(8,128)(2,1)S(1)} %get-tuple-element.44), channel_id=1, source_target_pairs={{0,2},{2,0},{4,6},{6,4},{8,10},{10,8},{12,14},{14,12},{16,18},{18,... | collective-permute-start | bytes 393224 | tf_op jit(solution)/shard_map/ppermute | solution.py:370
  5.9 4.5 %collective-permute-start.3 = (bf16[256,256]{1,0:T(8,128)(2,1)S(1)}, bf16[256,256]{1,0:T(8,128)(2,1)S(1)}, u32[]{:S(2)}, u32[]{:S(2)}) collective-permute-start(bf16[256,256]{1,0:T(8,128)(2,1)S(1)} %get-tuple-element.49), channel_id=1, source_target_pairs={{0,30},{2,4},{4,2},{6,8},{8,6},{10,12},{12,10},{14,16},{16,14},{18... | collective-permute-start | bytes 393224 | tf_op jit(solution)/shard_map/ppermute | solution.py:370
  10.4 5.0 %first.1 = (f32[3072,256]{1,0:T(8,128)S(1)}, s16[2,3072,128]{2,1,0:T(8,128)(2,1)S(1)}, bf16[3072,256]{1,0:T(8,128)(2,1)S(1)}, bf16[2,256,256]{2,1,0:T(8,128)(2,1...) custom-call(s32[1,3072]{1,0:T(1,128)S(1)} %get-tuple-element.38.send, ...), custom_call_target="tpu_custom_call" | custom-call | flops 2013265920 | bytes 3702784 | tf_op jit(solution)/shard_map/first/pallas_call | solution.py:80
  15.4 0.0 collective-permute-done.2.rows_ref
  15.4 0.1 collective-permute-start.4
  15.5 1.1 %near.4.pre_ref = f32[3072,256]{1,0:T(8,128)S(1)} custom-call(f32[3072,256]{1,0:T(8,128)S(1)} %get-tuple-element.46.pre_ref, s16[2,3072,128]{2,1,0:T(8,128)(2,1)S(1)} %get-tuple-element.47.cols, bf16[2,768,256]{2,1,0:T(8,128)(2,1)S(1)} %get-tuple-element.40.w1_ref, bf16[256,256]{1,0:T(8,128)(2,1)S(1)} %collective-permute-done.2.rows_ref), custom_call_target="tpu_custom_call" | custom-call | flops 402653184 | bytes 5636096 | tf_op jit(solution)/shard_map/near/pallas_call | solution.py:80
  16.7 0.0 collective-permute-done.3.own
  16.7 0.6 %collective-permute-start.5 = (bf16[256,256]{1,0:T(8,128)(2,1)S(1)}, bf16[256,256]{1,0:T(8,128)(2,1)S(1)}, u32[]{:S(2)}, u32[]{:S(2)}) collective-permute-start(bf16[256,256]{1,0:T(8,128)(2,1)S(1)} %collective-permute-done.3.own), channel_id=1, source_target_pairs={{0,1},{1,0},{2,3},{3,2},{4,5},{5,4},{6,7},{7,6},{8,9},{9,8},{10,11... | collective-permute-start | bytes 393224 | tf_op jit(solution)/shard_map/ppermute | solution.py:341
  17.9 0.0 collective-permute-done.4.rows_ref
  17.9 0.9 %near.5.pre_ref = f32[3072,256]{1,0:T(8,128)S(1)} custom-call(f32[3072,256]{1,0:T(8,128)S(1)} %near.4.pre_ref, s16[2,3072,128]{2,1,0:T(8,128)(2,1)S(1)} %get-tuple-element.47.cols, bf16[2,768,256]{2,1,0:T(8,128)(2,1)S(1)} %get-tuple-element.40.w1_ref, bf16[256,256]{1,0:T(8,128)(2,1)S(1)} %collective-permute-done.4.rows_ref), custom_call_target="tpu_custom_call" | custom-call | flops 402653184 | bytes 5636096 | tf_op jit(solution)/shard_map/near/pallas_call | solution.py:80
  18.8 0.0 collective-permute-done.5.peer
  18.8 3.3 %far.2 = (bf16[3072,256]{1,0:T(8,128)(2,1)S(1)}, bf16[512,256]{1,0:T(8,128)(2,1)S(1)}) custom-call(s32[1,1]{1,0:T(1,128)S(6)} %copy.16.live_ref, f32[3072,256]{1,0:T(8,128)S(1)} %near.5.pre_ref, s16[2,3072,128]{2,1,0:T(8,128)(2,1)S(1)} %get-tuple-element.47.cols, s32[1,3072]{1,0:T(1,128)S(1)} %get-tuple-element.39.recv_ref, ...), custom_call_target="tpu_custom_call" | custom-call | flops 2013265920 | bytes 7616516 | tf_op jit(solution)/shard_map/far/pallas_call | solution.py:80
  22.1 0.1 collective-permute-start.6
  22.2 1.5 %collective-permute-done.6.second = bf16[512,256]{1,0:T(8,128)(2,1)S(1)} collective-permute-done((bf16[512,256]{1,0:T(8,128)(2,1)S(1)}, bf16[512,256]{1,0:T(8,128)(2,1)S(1)}, u32[]{:S(2)}, u32[]{:S(2)}) %collective-permute-start.6) | collective-permute-done | bytes 262176 | tf_op jit(solution)/shard_map/ppermute | solution.py:341
  23.7 1.1 %nodes.1 = (bf16[512,256]{1,0:T(8,128)(2,1)S(1)}, bf16[256,256]{1,0:T(8,128)(2,1)S(1)}, bf16[256,256]{1,0:T(8,128)(2,1)S(1)}) custom-call(bf16[256,256]{1,0:T(8,128)(2,1)S(1)} %get-tuple-element.37.own_ref, bf16[256,256]{1,0:T(8,128)(2,1)S(1)} %collective-permute-done.peer_ref, bf16[512,256]{1,0:T(8,128)(2,1)S(1)} %get-tuple-element.55.first, ...), custom_call_target="tpu_custom_call" | custom-call | bytes 1581056 | tf_op jit(solution)/shard_map/nodes/pallas_call | solution.py:80
  24.8 0.1 collective-permute-start.7
  24.9 2.0 %collective-permute-start.8 = (bf16[256,256]{1,0:T(8,128)(2,1)S(1)}, bf16[256,256]{1,0:T(8,128)(2,1)S(1)}, u32[]{:S(2)}, u32[]{:S(2)}) collective-permute-start(bf16[256,256]{1,0:T(8,128)(2,1)S(1)} %get-tuple-element.66), channel_id=1, source_target_pairs={{0,30},{2,4},{4,2},{6,8},{8,6},{10,12},{12,10},{14,16},{16,14},{18... | collective-permute-start | bytes 393224 | tf_op jit(solution)/shard_map/ppermute | solution.py:370
  26.9 2.8 %local.1.pre_ref = f32[3072,256]{1,0:T(8,128)S(1)} custom-call(bf16[3072,256]{1,0:T(8,128)(2,1)S(1)} %get-tuple-element.61.edge_ref, s16[2,3072,128]{2,1,0:T(8,128)(2,1)S(1)} %get-tuple-element.47.cols, bf16[512,256]{1,0:T(8,128)(2,1)S(1)} %get-tuple-element.60.dom_ref.nodes_ref, bf16[2,768,256]{2,1,0:T(8,128)(2,1)S(1)} %get-tuple-element.40.w1_ref, ...), custom_call_target="tpu_custom_call" | custom-call | flops 2013265920 | bytes 4196352 | tf_op jit(solution)/shard_map/local/pallas_call | solution.py:80
  29.7 0.1 collective-permute-done.7.rows_ref
  29.8 0.4 collective-permute-start.9
  30.2 0.9 %near.6.pre_ref = f32[3072,256]{1,0:T(8,128)S(1)} custom-call(f32[3072,256]{1,0:T(8,128)S(1)} %local.1.pre_ref, s16[2,3072,128]{2,1,0:T(8,128)(2,1)S(1)} %get-tuple-element.47.cols, bf16[2,768,256]{2,1,0:T(8,128)(2,1)S(1)} %get-tuple-element.40.w1_ref, bf16[256,256]{1,0:T(8,128)(2,1)S(1)} %collective-permute-done.7.rows_ref), custom_call_target="tpu_custom_call" | custom-call | flops 402653184 | bytes 5636096 | tf_op jit(solution)/shard_map/near/pallas_call | solution.py:80
  31.2 2.3 %collective-permute-done.8.own = bf16[256,256]{1,0:T(8,128)(2,1)S(1)} collective-permute-done((bf16[256,256]{1,0:T(8,128)(2,1)S(1)}, bf16[256,256]{1,0:T(8,128)(2,1)S(1)}, u32[]{:S(2)}, u32[]{:S(2)}) %collective-permute-start.8) | collective-permute-done | bytes 131104 | tf_op jit(solution)/shard_map/ppermute | solution.py:370
  33.5 0.0 collective-permute-start.10
  33.5 0.0 collective-permute-done.9.rows_ref
  33.5 0.9 %near.7.pre_ref = f32[3072,256]{1,0:T(8,128)S(1)} custom-call(f32[3072,256]{1,0:T(8,128)S(1)} %near.6.pre_ref, s16[2,3072,128]{2,1,0:T(8,128)(2,1)S(1)} %get-tuple-element.47.cols, bf16[2,768,256]{2,1,0:T(8,128)(2,1)S(1)} %get-tuple-element.40.w1_ref, bf16[256,256]{1,0:T(8,128)(2,1)S(1)} %collective-permute-done.9.rows_ref), custom_call_target="tpu_custom_call" | custom-call | flops 402653184 | bytes 5636096 | tf_op jit(solution)/shard_map/near/pallas_call | solution.py:80
  34.5 0.4 collective-permute-done.10.peer
  34.9 3.4 %far.3 = (bf16[3072,256]{1,0:T(8,128)(2,1)S(1)}, bf16[256,256]{1,0:T(8,128)(2,1)S(1)}, bf16[256,256]{1,0:T(8,128)(2,1)S(1)}) custom-call(s32[1,1]{1,0:T(1,128)S(6)} %copy.16.live_ref, f32[3072,256]{1,0:T(8,128)S(1)} %near.7.pre_ref, s16[2,3072,128]{2,1,0:T(8,128)(2,1)S(1)} %get-tuple-element.47.cols, s32[1,3072]{1,0:T(1,128)S(1)} %get-tuple-element.39.recv_ref, ...), custom_call_target="tpu_custom_call" | custom-call | flops 2013265920 | bytes 7616516 | tf_op jit(solution)/shard_map/far/pallas_call | solution.py:80
  38.2 0.2 collective-permute-start.11
  38.5 1.1 %store.1 = bf16[3072,256]{1,0:T(8,128)(2,1)} custom-call(bf16[3072,256]{1,0:T(8,128)(2,1)S(1)} %get-tuple-element.71.refs_0_), custom_call_target="tpu_custom_call" | custom-call | bytes 1572864 | tf_op jit(solution)/shard_map/store/pallas_call | solution.py:80
  39.6 0.0 collective-permute-done.11.second
  39.6 1.2 %last.1 = bf16[256,256]{1,0:T(8,128)(2,1)} custom-call(bf16[512,256]{1,0:T(8,128)(2,1)S(1)} %get-tuple-element.60.dom_ref.nodes_ref, bf16[256,256]{1,0:T(8,128)(2,1)S(1)} %get-tuple-element.69.first, bf16[256,256]{1,0:T(8,128)(2,1)S(1)} %collective-permute-done.11.second, bf16[2,512,256]{2,1,0:T(8,128)(2,1)S(1)} %get-tuple-element.56.w1, ...), custom_call_target="tpu_custom_call" | custom-call | bytes 1314816 | tf_op jit(solution)/shard_map/last/pallas_call | solution.py:80
Async XLA Ops:
  0.6 2.0 %collective-permute-start = (bf16[256,256]{1,0:T(8,128)(2,1)}, bf16[256,256]{1,0:T(8,128)(2,1)S(1)}, u32[]{:S(2)}, u32[]{:S(2)}) collective-permute-start(bf16[256,256]{1,0:T(8,128)(2,1)} %refs_0_.2), channel_id=1, source_target_pairs={{0,1},{1,0},{2,3},{3,2},{4,5},{5,4},{6,7},{7,6},{8,9},{9,8},{10,11... | collective-permute-start | bytes 393224 | tf_op jit(solution)/shard_map/ppermute | solution.py:341
  1.2 1.4 %collective-permute-start.1 = (s32[1,4,128]{2,1,0:T(4,128)}, s32[1,4,128]{2,1,0:T(4,128)S(1)}, u32[]{:S(2)}, u32[]{:S(2)}) collective-permute-start(s32[1,4,128]{2,1,0:T(4,128)} %refs_1_.2), channel_id=1, source_target_pairs={{0,1},{1,0},{2,3},{3,2},{4,5},{5,4},{6,7},{7,6},{8,9},{9,8},{10,11... | collective-permute-start | bytes 6152 | tf_op jit(solution)/shard_map/ppermute | solution.py:341
  2.9 12.5 %collective-permute-start.2 = (bf16[256,256]{1,0:T(8,128)(2,1)S(1)}, bf16[256,256]{1,0:T(8,128)(2,1)S(1)}, u32[]{:S(2)}, u32[]{:S(2)}) collective-permute-start(bf16[256,256]{1,0:T(8,128)(2,1)S(1)} %get-tuple-element.44), channel_id=1, source_target_pairs={{0,2},{2,0},{4,6},{6,4},{8,10},{10,8},{12,14},{14,12},{16,18},{18,... | collective-permute-start | bytes 393224 | tf_op jit(solution)/shard_map/ppermute | solution.py:370
  5.9 10.8 %collective-permute-start.3 = (bf16[256,256]{1,0:T(8,128)(2,1)S(1)}, bf16[256,256]{1,0:T(8,128)(2,1)S(1)}, u32[]{:S(2)}, u32[]{:S(2)}) collective-permute-start(bf16[256,256]{1,0:T(8,128)(2,1)S(1)} %get-tuple-element.49), channel_id=1, source_target_pairs={{0,30},{2,4},{4,2},{6,8},{8,6},{10,12},{12,10},{14,16},{16,14},{18... | collective-permute-start | bytes 393224 | tf_op jit(solution)/shard_map/ppermute | solution.py:370
  15.4 2.4 %collective-permute-start.4 = (bf16[256,256]{1,0:T(8,128)(2,1)S(1)}, bf16[256,256]{1,0:T(8,128)(2,1)S(1)}, u32[]{:S(2)}, u32[]{:S(2)}) collective-permute-start(bf16[256,256]{1,0:T(8,128)(2,1)S(1)} %collective-permute-done.2.rows_ref), channel_id=1, source_target_pairs={{0,1},{1,0},{2,3},{3,2},{4,5},{5,4},{6,7},{7,6},{8,9},{9,8},{10,11... | collective-permute-start | bytes 393224 | tf_op jit(solution)/shard_map/ppermute | solution.py:341
  16.7 2.2 %collective-permute-start.5 = (bf16[256,256]{1,0:T(8,128)(2,1)S(1)}, bf16[256,256]{1,0:T(8,128)(2,1)S(1)}, u32[]{:S(2)}, u32[]{:S(2)}) collective-permute-start(bf16[256,256]{1,0:T(8,128)(2,1)S(1)} %collective-permute-done.3.own), channel_id=1, source_target_pairs={{0,1},{1,0},{2,3},{3,2},{4,5},{5,4},{6,7},{7,6},{8,9},{9,8},{10,11... | collective-permute-start | bytes 393224 | tf_op jit(solution)/shard_map/ppermute | solution.py:341
  22.1 1.6 %collective-permute-start.6 = (bf16[512,256]{1,0:T(8,128)(2,1)S(1)}, bf16[512,256]{1,0:T(8,128)(2,1)S(1)}, u32[]{:S(2)}, u32[]{:S(2)}) collective-permute-start(bf16[512,256]{1,0:T(8,128)(2,1)S(1)} %get-tuple-element.55.first), channel_id=1, source_target_pairs={{0,1},{1,0},{2,3},{3,2},{4,5},{5,4},{6,7},{7,6},{8,9},{9,8},{10,11... | collective-permute-start | bytes 786440 | tf_op jit(solution)/shard_map/ppermute | solution.py:341
  24.8 5.0 %collective-permute-start.7 = (bf16[256,256]{1,0:T(8,128)(2,1)S(1)}, bf16[256,256]{1,0:T(8,128)(2,1)S(1)}, u32[]{:S(2)}, u32[]{:S(2)}) collective-permute-start(bf16[256,256]{1,0:T(8,128)(2,1)S(1)} %get-tuple-element.62), channel_id=1, source_target_pairs={{0,2},{2,0},{4,6},{6,4},{8,10},{10,8},{12,14},{14,12},{16,18},{18,... | collective-permute-start | bytes 393224 | tf_op jit(solution)/shard_map/ppermute | solution.py:370
  24.9 8.6 %collective-permute-start.8 = (bf16[256,256]{1,0:T(8,128)(2,1)S(1)}, bf16[256,256]{1,0:T(8,128)(2,1)S(1)}, u32[]{:S(2)}, u32[]{:S(2)}) collective-permute-start(bf16[256,256]{1,0:T(8,128)(2,1)S(1)} %get-tuple-element.66), channel_id=1, source_target_pairs={{0,30},{2,4},{4,2},{6,8},{8,6},{10,12},{12,10},{14,16},{16,14},{18... | collective-permute-start | bytes 393224 | tf_op jit(solution)/shard_map/ppermute | solution.py:370
  29.8 3.7 %collective-permute-start.9 = (bf16[256,256]{1,0:T(8,128)(2,1)S(1)}, bf16[256,256]{1,0:T(8,128)(2,1)S(1)}, u32[]{:S(2)}, u32[]{:S(2)}) collective-permute-start(bf16[256,256]{1,0:T(8,128)(2,1)S(1)} %collective-permute-done.7.rows_ref), channel_id=1, source_target_pairs={{0,1},{1,0},{2,3},{3,2},{4,5},{5,4},{6,7},{7,6},{8,9},{9,8},{10,11... | collective-permute-start | bytes 393224 | tf_op jit(solution)/shard_map/ppermute | solution.py:341
  33.5 1.3 %collective-permute-start.10 = (bf16[256,256]{1,0:T(8,128)(2,1)S(1)}, bf16[256,256]{1,0:T(8,128)(2,1)S(1)}, u32[]{:S(2)}, u32[]{:S(2)}) collective-permute-start(bf16[256,256]{1,0:T(8,128)(2,1)S(1)} %collective-permute-done.8.own), channel_id=1, source_target_pairs={{0,1},{1,0},{2,3},{3,2},{4,5},{5,4},{6,7},{7,6},{8,9},{9,8},{10,11... | collective-permute-start | bytes 393224 | tf_op jit(solution)/shard_map/ppermute | solution.py:341
  38.2 1.4 %collective-permute-start.11 = (bf16[256,256]{1,0:T(8,128)(2,1)S(1)}, bf16[256,256]{1,0:T(8,128)(2,1)S(1)}, u32[]{:S(2)}, u32[]{:S(2)}) collective-permute-start(bf16[256,256]{1,0:T(8,128)(2,1)S(1)} %get-tuple-element.70), channel_id=1, source_target_pairs={{0,1},{1,0},{2,3},{3,2},{4,5},{5,4},{6,7},{7,6},{8,9},{9,8},{10,11... | collective-permute-start | bytes 393224 | tf_op jit(solution)/shard_map/ppermute | solution.py:341

commit v7 on v6

--- a/solution.py
+++ b/solution.py
@@ -75,7 +75,7 @@
     return jax.ShapeDtypeStruct(shape, dtype)
 
 
-def call(kernel, outs, args, scratch=(), smem=(), stay=(), leave=(), flops=0, limit=24, name=None):
+def call(kernel, outs, args, scratch=(), smem=(), stay=(), leave=(), flops=0, limit=24):
     nbytes = sum(a.size * a.dtype.itemsize for a in args)
     return pl.pallas_call(
         kernel,
@@ -89,7 +89,6 @@
         scratch_shapes=scratch,
         compiler_params=pltpu.CompilerParams(vmem_limit_bytes=limit << 20),
         cost_estimate=pl.CostEstimate(flops=flops, transcendentals=0, bytes_accessed=nbytes),
-        name=name,
     )(*args)
 
 
@@ -124,17 +123,23 @@
     return 2 * core + 1 - par, 2 * core + par
 
 
+def face_hits(stride, lists):
+    rows = [one_hot_rows(lists[0, pl.ds(face, 1), :], TILE) for face in faces(stride)]
+    return jnp.concatenate(rows, axis=0)
+
+
 def pick_kernel(stride, own_ref, peer_ref, list_own, list_peer, far, near):
-    for face, ref in zip(faces(stride), (far, near)):
-        for n, (lists, nodes) in enumerate(((list_own, own_ref), (list_peer, peer_ref))):
-            hot = one_hot_rows(lists[0, pl.ds(face, 1), :], TILE)
-            ref[n * HALF : (n + 1) * HALF, :] = mm(hot, nodes[...]).astype(BF16)
+    for n, (lists, nodes) in enumerate(((list_own, own_ref), (list_peer, peer_ref))):
+        picked = mm(face_hits(stride, lists), nodes[...]).astype(BF16)
+        far[n * HALF : (n + 1) * HALF, :] = picked[:HALF]
+        near[n * HALF : (n + 1) * HALF, :] = picked[HALF:]
 
 
 def load_kernel(count, *refs):
     hbm, vmem, sems = refs[:count], refs[count:-1], refs[-1]
     copies = [
-        pltpu.make_async_copy(src, dst, sems.at[k]) for k, (src, dst) in enumerate(zip(hbm, vmem))
+        pltpu.make_async_copy(src if len(src.shape) == len(dst.shape) else src.at[0], dst, sems.at[k])
+        for k, (src, dst) in enumerate(zip(hbm, vmem))
     ]
     for copy in copies:
         copy.start()
@@ -173,16 +178,16 @@
     return jnp.concatenate(parts, axis=1)
 
 
-def project(layer, parts, w1_ref, table):
+def project(parts, w1_ref, table):
     for k in (1, 2):
         for start, size, ref in parts:
             table[dyn((2 * k - 2) * TILE + start, size, TILE), :] = mm(
-                ref[...], w1_ref[layer, k * TILE : (k + 1) * TILE, :]
+                ref[...], w1_ref[k * TILE : (k + 1) * TILE, :]
             ).astype(BF16)
 
 
 def local_block(layer, at, edge_ref, cols, w1_ref, b1_ref, table, pre_ref):
-    acc = mm(edge_ref[at, :], w1_ref[layer, 0:TILE, :])
+    acc = mm(edge_ref[at, :], w1_ref[0:TILE, :])
     acc = acc + mm(hits(cols[0, at, :], 0, 2), table[0 : 2 * TILE, :])
     acc = acc + mm(hits(cols[1, at, :], 0, 2), table[2 * TILE :, :])
     pre_ref[at, :] = acc + b1_ref[layer : layer + 1, :]
@@ -192,13 +197,11 @@
     hbm, (pre_ref, cols), refs = refs[:loads], refs[loads : loads + 2], refs[loads + 2 :]
     vmem, (table, sems) = refs[:loads], refs[loads:]
     edge_hbm, edge_ref = hbm[0], vmem[0]
-    edges = edge_ref.shape[0]
-    blocks = [pl.ds(start, LOCAL_ROWS) for start in range(0, edges, LOCAL_ROWS)]
+    blocks = [pl.ds(start, LOCAL_ROWS) for start in range(0, edge_ref.shape[0], LOCAL_ROWS)]
     copies = [(edge_hbm.at[at, :], edge_ref.at[at, :]) for at in blocks]
-    copies += zip(hbm[1:], vmem[1:])
+    copies += [(hbm[1].at[1], vmem[1])] + list(zip(hbm[2:], vmem[2:]))
     copies = [pltpu.make_async_copy(*ends, sems.at[k]) for k, ends in enumerate(copies)]
-    for copy in copies:
-        copy.start()
+    copies[0].start()
     core = lax.axis_index("edge")
     parts = ((core * TILE, TILE, own_ref), ((1 - core) * TILE, TILE, peer_ref))
 
@@ -207,18 +210,22 @@
             columns(stride, send_ref, recv_ref, cols, pl.ds(start, HALF))
 
     make(0)
-    project(0, parts, w1_ref, table)
+    project(parts, w1_ref, table)
     for k, at in enumerate(blocks):
         copies[k].wait()
         if k + 1 < len(blocks):
+            copies[k + 1].start()
             make(k + 1)
+        else:
+            for copy in copies[len(blocks) :]:
+                copy.start()
         local_block(0, at, edge_ref, cols, w1_ref, b1_ref, table, pre_ref)
     for copy in copies[len(blocks) :]:
         copy.wait()
 
 
 def local_kernel(layer, edge_ref, cols, dom_ref, w1_ref, b1_ref, pre_ref, table):
-    project(layer, ((0, 2 * TILE, dom_ref),), w1_ref, table)
+    project(((0, 2 * TILE, dom_ref),), w1_ref, table)
 
     def step(k, carry):
         at = dyn(k * LOCAL_ROWS, LOCAL_ROWS)
@@ -228,18 +235,17 @@
     lax.fori_loop(0, edge_ref.shape[0] // LOCAL_ROWS, step, 0)
 
 
-def halo_tables(layer, own, peer, w1_ref, table):
+def halo_tables(own, peer, w1_ref, table):
     core = lax.axis_index("edge")
-    w_s = w1_ref[layer, TILE : 2 * TILE, :]
+    w_s = w1_ref[TILE : 2 * TILE, :]
     for axis, ref in ((core, own), (1 - core, peer)):
         table[dyn(axis * TILE, TILE), :] = mm(ref[...], w_s).astype(BF16)
 
 
-def near_kernel(layer, peer, pre_ref, cols, w1_ref, rows_ref, out_ref):
+def tile_kernel(first, peer, pre_ref, cols, w1_ref, rows_ref, out_ref):
     core = lax.axis_index("edge")
-    tile = 3 - core if peer else 2 + core
-    table = mm(rows_ref[...], w1_ref[layer, TILE : 2 * TILE, :]).astype(BF16)
-
+    tile = first + (1 - core if peer else core)
+    table = mm(rows_ref[...], w1_ref[TILE : 2 * TILE, :]).astype(BF16)
     half = pre_ref.shape[0] // 2
 
     def step(k, carry):
@@ -251,40 +257,47 @@
 
 
 def edge_kernel(
-    layer, split, live_ref, pre_ref, cols, recv_ref, edge_ref, w1_ref, w2_ref, gain_ref, own, peer, out_ref, *refs
+    layer, split, live_ref, pre_ref, cols, recv_ref, edge_ref, w1_ref, w2_ref, gain_ref, *refs
 ):
+    own, peer, refs = (None, *refs[:1], refs[1:]) if split else (*refs[:2], refs[2:])
+    out_ref, refs = refs[0], refs[1:]
     if split:
         keep_ref, give_ref, table, raw, msgs, sums = refs
     else:
         part_ref, table, raw, msgs, sums = refs
-    halo_tables(layer, own, peer, w1_ref, table)
+    if split:
+        first, tiles = 5 - lax.axis_index("edge"), 1
+        table[0:TILE, :] = mm(peer[...], w1_ref[TILE : 2 * TILE, :]).astype(BF16)
+    else:
+        first, tiles = 4, 2
+        halo_tables(own, peer, w1_ref, table)
     gain = gain_ref[layer : layer + 1, :]
     live = live_ref[0, 0]
     count = edge_ref.shape[0] // ROWS
 
     def gather(at):
-        acc = pre_ref[at, :] + mm(hits(cols[0, at, :], 4, 2), table[...])
+        acc = pre_ref[at, :] + mm(hits(cols[0, at, :], first, tiles), table[0 : tiles * TILE, :])
         hidden = jnp.maximum(acc.astype(BF16), jnp.asarray(0, BF16))
         raw[at, :] = mm(hidden, w2_ref[layer])
 
-    def norm(at, first):
+    def norm(at, start):
         values = raw[at, :]
         center = values - jnp.mean(values, axis=-1, keepdims=True)
         spread = jnp.mean(center * center, axis=-1, keepdims=True)
         scale = lax.rsqrt(spread + eps_norm)
-        row = lax.broadcasted_iota(jnp.int32, scale.shape, 0) + first
+        row = lax.broadcasted_iota(jnp.int32, scale.shape, 0) + start
         scale = jnp.where(row < live, scale, 0.0)
         message = (center * scale * gain).astype(BF16)
         msgs[at, :] = message
         out_ref[at, :] = edge_ref[at, :] + message
 
-    def segment(at, first):
+    def segment(at, new):
         shape = (2 * TILE, ROWS)
         spot = lax.broadcasted_iota(jnp.int32, shape, 0).astype(I16)
         here = jnp.broadcast_to(recv_ref[:, at].astype(I16), shape)
         hot = jnp.where(here == spot, jnp.ones(shape, BF16), jnp.zeros(shape, BF16))
         part = mm(hot, msgs[at, :])
-        sums[...] = part if first else sums[...] + part
+        sums[...] = part if new else sums[...] + part
 
     for k in range(count + 2):
         if k >= 2:
@@ -310,17 +323,17 @@
 
 
 def node_kernel(
-    stride, layer, own_ref, peer_ref, first, second, list_own, list_peer, w1, b1, w2, gain, out, far, near, old
+    stride, layer, own_ref, peer_ref, first, second, list_own, list_peer, w1, b1, w2, gain, out, far, near
 ):
     core = lax.axis_index("edge")
-    old[dyn(core * TILE, TILE), :] = own_ref[...]
-    old[dyn((1 - core) * TILE, TILE), :] = peer_ref[...]
-    nodes = updated(layer, old[...], first[...], second[...], w1, b1, w2, gain)
-    out[...] = nodes
-    for face, ref in zip(faces(stride), (far, near)):
-        for n, (owner, lists) in enumerate(((core, list_own), (1 - core, list_peer))):
-            hot = one_hot_rows(lists[0, pl.ds(face, 1), :] + owner * TILE, 2 * TILE)
-            ref[n * HALF : (n + 1) * HALF, :] = mm(hot, nodes).astype(BF16)
+    hot = [face_hits(stride, lists) for lists in (list_own, list_peer)]
+    for n, (owner, ref) in enumerate(((core, own_ref), (1 - core, peer_ref))):
+        at = dyn(owner * TILE, TILE)
+        nodes = updated(layer, ref[...], first[at, :], second[at, :], w1, b1, w2, gain)
+        out[at, :] = nodes
+        picked = mm(hot[n], nodes).astype(BF16)
+        far[n * HALF : (n + 1) * HALF, :] = picked[:HALF]
+        near[n * HALF : (n + 1) * HALF, :] = picked[HALF:]
 
 
 def last_kernel(layer, nodes_ref, first, second, w1, b1, w2, gain, out):
@@ -378,58 +391,68 @@
     peer_nodes = swapped(node_lat)
     peer_lists = swapped(send_rows)
     send_at, recv_at = senders[None], receivers[None]
-    first = (node_lat, send_rows, send_at, recv_at, edge_w1, edge_b1)
-    node_lat, send_rows, send_at, recv_at, edge_w1, edge_b1 = call(
+    first = (node_lat, send_rows, send_at, recv_at, edge_b1, edge_w1)
+    node_lat, send_rows, send_at, recv_at, edge_b1, first_w1 = call(
         functools.partial(load_kernel, len(first)),
-        [shaped(a.shape, a.dtype) for a in first],
+        [shaped(a.shape, a.dtype) for a in first[:-1]] + [shaped(edge_w1.shape[1:], BF16)],
         in_hbm(first),
         scratch=[pltpu.SemaphoreType.DMA((len(first),))],
         stay=range(len(first)),
-        name="load",
     )
     far_rows, near_rows = call(
         functools.partial(pick_kernel, stride),
         [rows_out, rows_out],
         (node_lat, peer_nodes, send_rows, peer_lists),
-        name="pick",
     )
     for layer in range(LAYERS):
         last = layer == LAYERS - 1
         near = sent_by_core(near_rows, near_d, near_s)
         far = sent_by_core(far_rows, far_d, far_s)
         if layer == 0:
-            loads = (edge_lat, edge_w2, node_w1, node_w2, edge_gain, node_b1, node_gain)
-            pre, cols, edge_rows, edge_w2, node_w1, node_w2, edge_gain, node_b1, node_gain = call(
+            loads = (edge_lat, edge_w1, edge_w2, node_w1, node_w2, edge_gain, node_b1, node_gain)
+            pre, cols, edge_rows, next_w1, edge_w2, node_w1, node_w2, edge_gain, node_b1, node_gain = call(
                 functools.partial(first_kernel, stride, len(loads)),
                 [pre_shape, shaped((2, edges, HALF), I16)]
-                + [shaped(a.shape, a.dtype) for a in loads],
-                (send_at, recv_at, node_lat, peer_nodes, edge_w1, edge_b1, *in_hbm(loads)),
+                + [shaped(a.shape[1:] if a is edge_w1 else a.shape, a.dtype) for a in loads],
+                (send_at, recv_at, node_lat, peer_nodes, first_w1, edge_b1, *in_hbm(loads)),
                 scratch=[
                     pltpu.VMEM((4 * TILE, width), BF16),
                     pltpu.SemaphoreType.DMA((edges // LOCAL_ROWS + len(loads) - 1,)),
                 ],
                 stay=range(6, 6 + len(loads)),
                 flops=5 * pass_flops,
-                name="first",
             )
         else:
             pre = call(
                 functools.partial(local_kernel, layer),
                 pre_shape,
-                (edge_rows, cols, all_nodes, edge_w1, edge_b1),
+                (edge_rows, cols, all_nodes, next_w1, edge_b1),
                 scratch=[pltpu.VMEM((4 * TILE, width), BF16)],
                 flops=5 * pass_flops,
-                name="local",
             )
+        w1 = next_w1 if layer else first_w1
+
+        def add(first, peer, pre, rows):
+            return call(
+                functools.partial(tile_kernel, first, peer),
+                pre_shape,
+                (pre, cols, w1, rows),
+                flops=pass_flops,
+            )
+
         pre, near, live_edges = lax.optimization_barrier((pre, near, live_edges))
         near_other = swapped(near)
-        add = functools.partial(
-            call, outs=pre_shape, flops=pass_flops, name="near"
-        )
-        pre = add(functools.partial(near_kernel, layer, False), args=(pre, cols, edge_w1, near))
-        pre, far = lax.optimization_barrier((pre, far))
-        far_other = swapped(far)
-        pre = add(functools.partial(near_kernel, layer, True), args=(pre, cols, edge_w1, near_other))
+        if last:
+            pre = add(2, False, pre, near)
+            pre = add(2, True, pre, near_other)
+            pre, far = lax.optimization_barrier((pre, far))
+            far_other = (swapped(far),)
+            pre = add(4, False, pre, far)
+        else:
+            pre = add(2, False, pre, near)
+            pre, far = lax.optimization_barrier((pre, far))
+            far_other = (far, swapped(far))
+            pre = add(2, True, pre, near_other)
         if last:
             outs = [shaped((nodes, width), BF16)] * 2
         else:
@@ -437,7 +460,7 @@
         edge_rows, *partial = call(
             functools.partial(edge_kernel, layer, last),
             [shaped((edges, width), BF16)] + outs,
-            (live_edges, pre, cols, recv_at, edge_rows, edge_w1, edge_w2, edge_gain, far, far_other),
+            (live_edges, pre, cols, recv_at, edge_rows, w1, edge_w2, edge_gain, *far_other),
             scratch=[
                 table,
                 pltpu.VMEM((edges, width), F32),
@@ -446,7 +469,6 @@
             ],
             smem=(0,),
             flops=5 * pass_flops,
-            name="far",
         )
         other = swapped(partial[-1])
         weights = (node_w1, node_b1, node_w2, node_gain)
@@ -457,21 +479,17 @@
                 (edge_rows,),
                 scratch=[pltpu.SemaphoreType.DMA((1,))],
                 leave=(0,),
-                name="store",
             )
             out = call(
                 functools.partial(last_kernel, layer),
                 shaped((nodes, width), BF16),
                 (all_nodes, partial[0], other, *weights),
-                name="last",
             )
         else:
             all_nodes, far_rows, near_rows = call(
                 functools.partial(node_kernel, stride, layer),
                 [shaped((2 * nodes, width), BF16), rows_out, rows_out],
                 (node_lat, peer_nodes, partial[0], other, send_rows, peer_lists, *weights),
-                scratch=[table],
-                name="nodes",
             )
     return out, edge_out
 

time: 41 us -> 45.7 us (1.11)
  waiting for transfers between devices: 4.39 us -> 9.22 us
  starting transfers between devices: 11.5 us -> 10.7 us
  Pallas kernels: 23.5 us -> 24.1 us
    ppermute x4, waiting for transfers between devices: 2.46 us -> 7.16 us  [sent_by_core(): return lax.ppermute(value, ('dom', 'edge'), pairs)]
    pallas_call x13 -> x14, Pallas kernels: 23.5 us -> 24.1 us  [call(): pl.pallas_call(kernel, out_shape=outs, in_specs=[IN_SMEM if k in smem els...]
    ppermute x4, starting transfers between devices: 9.54 us -> 9.08 us  [sent_by_core(): return lax.ppermute(value, ('dom', 'edge'), pairs)]
  transfers between devices with their start and end apart: 12 -> 12, of which waited for: 4 -> 5; matrix products, arithmetic and copies ran while one was open for 0% -> 0% of each run, Pallas kernels for 35% -> 34%
where the time goes in v7:
time: 45.7 us; the launch traced here: 45.4 us
  Pallas kernels  24.1 us (53%)
  starting transfers between devices  10.7 us (23%)
  waiting for transfers between devices  9.22 us (20%)
  between operations  1.44 us (3%)
    pallas_call x14, Pallas kernels, call(): pl.pallas_call(kernel, out_shape=outs, in_specs=[IN_SMEM if k in smem els...  24.1 us
    ppermute x4, starting transfers between devices, sent_by_core(): return lax.ppermute(value, ('dom', 'edge'), pairs)  9.08 us
    ppermute x4, waiting for transfers between devices, sent_by_core(): return lax.ppermute(value, ('dom', 'edge'), pairs)  7.16 us
    ppermute x8, waiting for transfers between devices, swapped(): return lax.ppermute(value, 'edge', [(0, 1), (1, 0)])  2.06 us
    ppermute x8, starting transfers between devices, swapped(): return lax.ppermute(value, 'edge', [(0, 1), (1, 0)])  1.57 us
  transfers between devices with their start and end apart: 12, of which 5 were waited for; matrix products, arithmetic and copies ran while one was open for 0% of the time, Pallas kernels for 34%

profile of v7, /device:TPU:0, one launch (start us, length us, event | category | flops | bytes accessed | tf_op | source)
XLA Modules:
  0.0 45.4 jit_solution(5006953592897858661)
XLA Ops:
  0.6 0.6 %collective-permute-start = (bf16[256,256]{1,0:T(8,128)(2,1)}, bf16[256,256]{1,0:T(8,128)(2,1)S(1)}, u32[]{:S(2)}, u32[]{:S(2)}) collective-permute-start(bf16[256,256]{1,0:T(8,128)(2,1)} %refs_0_.2), channel_id=1, source_target_pairs={{0,1},{1,0},{2,3},{3,2},{4,5},{5,4},{6,7},{7,6},{8,9},{9,8},{10,11... | collective-permute-start | bytes 393224 | tf_op jit(solution)/shard_map/ppermute | solution.py:354
  1.2 0.1 collective-permute-start.1
  1.3 1.2 %shard_map.149 = (bf16[256,256]{1,0:T(8,128)(2,1)S(1)}, s32[1,4,128]{2,1,0:T(4,128)S(1)}, s32[1,3072]{1,0:T(1,128)S(1)}, s32[1,3072]{1,0:T(1,128)S(1)}, f32[2,25...) custom-call(bf16[256,256]{1,0:T(8,128)(2,1)} %refs_0_.2, s32[1,4,128]{2,1,0:T(4,128)} %refs_1_.2, s32[1,3072]{1,0:T(1,128)} %bitcast.2, ...), custom_call_target="tpu_custom_call" | custom-call | bytes 946176 | tf_op jit(solution)/shard_map/pallas_call | solution.py:80
  2.5 0.1 collective-permute-done.1.list_peer
  2.6 0.0 collective-permute-done.peer_ref
  2.6 0.3 shard_map.151
  2.9 2.9 %collective-permute-start.2 = (bf16[256,256]{1,0:T(8,128)(2,1)S(1)}, bf16[256,256]{1,0:T(8,128)(2,1)S(1)}, u32[]{:S(2)}, u32[]{:S(2)}) collective-permute-start(bf16[256,256]{1,0:T(8,128)(2,1)S(1)} %get-tuple-element.45), channel_id=1, source_target_pairs={{0,2},{2,0},{4,6},{6,4},{8,10},{10,8},{12,14},{14,12},{16,18},{18,... | collective-permute-start | bytes 393224 | tf_op jit(solution)/shard_map/ppermute | solution.py:383
  5.8 4.5 %collective-permute-start.3 = (bf16[256,256]{1,0:T(8,128)(2,1)S(1)}, bf16[256,256]{1,0:T(8,128)(2,1)S(1)}, u32[]{:S(2)}, u32[]{:S(2)}) collective-permute-start(bf16[256,256]{1,0:T(8,128)(2,1)S(1)} %get-tuple-element.50), channel_id=1, source_target_pairs={{0,30},{2,4},{4,2},{6,8},{8,6},{10,12},{12,10},{14,16},{16,14},{18... | collective-permute-start | bytes 393224 | tf_op jit(solution)/shard_map/ppermute | solution.py:383
  10.3 5.3 %shard_map.150 = (f32[3072,256]{1,0:T(8,128)S(1)}, s16[2,3072,128]{2,1,0:T(8,128)(2,1)S(1)}, bf16[3072,256]{1,0:T(8,128)(2,1)S(1)}, bf16[768,256]{1,0:T(8,128)(2...) custom-call(s32[1,3072]{1,0:T(1,128)S(1)} %get-tuple-element.39.send, ...), custom_call_target="tpu_custom_call" | custom-call | flops 2013265920 | bytes 4096000 | tf_op jit(solution)/shard_map/pallas_call | solution.py:80
  15.6 0.0 collective-permute-done.2.rows_ref
  15.6 0.1 collective-permute-start.4
  15.7 1.1 %shard_map.152.pre_ref = f32[3072,256]{1,0:T(8,128)S(1)} custom-call(f32[3072,256]{1,0:T(8,128)S(1)} %get-tuple-element.47.pre_ref, s16[2,3072,128]{2,1,0:T(8,128)(2,1)S(1)} %get-tuple-element.48.cols, bf16[768,256]{1,0:T(8,128)(2,1)S(1)} %get-tuple-element.41.w1_ref, bf16[256,256]{1,0:T(8,128)(2,1)S(1)} %collective-permute-done.2.rows_ref), custom_call_target="tpu_custom_call" | custom-call | flops 402653184 | bytes 5242880 | tf_op jit(solution)/shard_map/pallas_call | solution.py:80
  16.8 0.0 collective-permute-done.3.refs_0_
  16.8 0.6 %collective-permute-start.5 = (bf16[256,256]{1,0:T(8,128)(2,1)S(1)}, bf16[256,256]{1,0:T(8,128)(2,1)S(1)}, u32[]{:S(2)}, u32[]{:S(2)}) collective-permute-start(bf16[256,256]{1,0:T(8,128)(2,1)S(1)} %collective-permute-done.3.refs_0_), channel_id=1, source_target_pairs={{0,1},{1,0},{2,3},{3,2},{4,5},{5,4},{6,7},{7,6},{8,9},{9,8},{10,11... | collective-permute-start | bytes 393224 | tf_op jit(solution)/shard_map/ppermute | solution.py:354
  18.0 0.0 collective-permute-done.4.rows_ref
  18.0 0.9 %shard_map.153.pre_ref = f32[3072,256]{1,0:T(8,128)S(1)} custom-call(f32[3072,256]{1,0:T(8,128)S(1)} %shard_map.152.pre_ref, s16[2,3072,128]{2,1,0:T(8,128)(2,1)S(1)} %get-tuple-element.48.cols, bf16[768,256]{1,0:T(8,128)(2,1)S(1)} %get-tuple-element.41.w1_ref, bf16[256,256]{1,0:T(8,128)(2,1)S(1)} %collective-permute-done.4.rows_ref), custom_call_target="tpu_custom_call" | custom-call | flops 402653184 | bytes 5242880 | tf_op jit(solution)/shard_map/pallas_call | solution.py:80
  19.0 0.0 collective-permute-done.5.refs_1_
  19.0 3.3 %shard_map.154 = (bf16[3072,256]{1,0:T(8,128)(2,1)S(1)}, bf16[512,256]{1,0:T(8,128)(2,1)S(1)}) custom-call(s32[1,1]{1,0:T(1,128)S(6)} %copy.16.live_ref, f32[3072,256]{1,0:T(8,128)S(1)} %shard_map.153.pre_ref, s16[2,3072,128]{2,1,0:T(8,128)(2,1)S(1)} %get-tuple-element.48.cols, s32[1,3072]{1,0:T(1,128)S(1)} %get-tuple-element.40.recv_ref, ...), custom_call_target="tpu_custom_call" | custom-call | flops 2013265920 | bytes 7223300 | tf_op jit(solution)/shard_map/pallas_call | solution.py:80
  22.3 0.1 collective-permute-start.6
  22.4 1.5 %collective-permute-done.6.second = bf16[512,256]{1,0:T(8,128)(2,1)S(1)} collective-permute-done((bf16[512,256]{1,0:T(8,128)(2,1)S(1)}, bf16[512,256]{1,0:T(8,128)(2,1)S(1)}, u32[]{:S(2)}, u32[]{:S(2)}) %collective-permute-start.6) | collective-permute-done | bytes 262176 | tf_op jit(solution)/shard_map/ppermute | solution.py:354
  24.0 1.2 %shard_map.155 = (bf16[512,256]{1,0:T(8,128)(2,1)S(1)}, bf16[256,256]{1,0:T(8,128)(2,1)S(1)}, bf16[256,256]{1,0:T(8,128)(2,1)S(1)}) custom-call(bf16[256,256]{1,0:T(8,128)(2,1)S(1)} %get-tuple-element.38.own_ref, bf16[256,256]{1,0:T(8,128)(2,1)S(1)} %collective-permute-done.peer_ref, bf16[512,256]{1,0:T(8,128)(2,1)S(1)} %get-tuple-element.56.first, ...), custom_call_target="tpu_custom_call" | custom-call | bytes 1581056 | tf_op jit(solution)/shard_map/pallas_call | solution.py:80
  25.1 0.1 collective-permute-start.7
  25.2 2.8 %shard_map.156.pre_ref = f32[3072,256]{1,0:T(8,128)S(1)} custom-call(bf16[3072,256]{1,0:T(8,128)(2,1)S(1)} %get-tuple-element.62.edge_ref, s16[2,3072,128]{2,1,0:T(8,128)(2,1)S(1)} %get-tuple-element.48.cols, bf16[512,256]{1,0:T(8,128)(2,1)S(1)} %get-tuple-element.61.dom_ref.nodes_ref, bf16[768,256]{1,0:T(8,128)(2,1)S(1)} %get-tuple-element.63.w1_ref, ...), custom_call_target="tpu_custom_call" | custom-call | flops 2013265920 | bytes 3803136 | tf_op jit(solution)/shard_map/pallas_call | solution.py:80
  28.1 2.1 %collective-permute-done.7.rows_ref = bf16[256,256]{1,0:T(8,128)(2,1)S(1)} collective-permute-done((bf16[256,256]{1,0:T(8,128)(2,1)S(1)}, bf16[256,256]{1,0:T(8,128)(2,1)S(1)}, u32[]{:S(2)}, u32[]{:S(2)}) %collective-permute-start.7) | collective-permute-done | bytes 131104 | tf_op jit(solution)/shard_map/ppermute | solution.py:383
  30.2 0.0 collective-permute-start.8
  30.2 1.6 %collective-permute-start.9 = (bf16[256,256]{1,0:T(8,128)(2,1)S(1)}, bf16[256,256]{1,0:T(8,128)(2,1)S(1)}, u32[]{:S(2)}, u32[]{:S(2)}) collective-permute-start(bf16[256,256]{1,0:T(8,128)(2,1)S(1)} %get-tuple-element.68), channel_id=1, source_target_pairs={{0,30},{2,4},{4,2},{6,8},{8,6},{10,12},{12,10},{14,16},{16,14},{18... | collective-permute-start | bytes 393224 | tf_op jit(solution)/shard_map/ppermute | solution.py:383
  31.8 0.9 %shard_map.157.pre_ref = f32[3072,256]{1,0:T(8,128)S(1)} custom-call(f32[3072,256]{1,0:T(8,128)S(1)} %shard_map.156.pre_ref, s16[2,3072,128]{2,1,0:T(8,128)(2,1)S(1)} %get-tuple-element.48.cols, bf16[768,256]{1,0:T(8,128)(2,1)S(1)} %get-tuple-element.63.w1_ref, bf16[256,256]{1,0:T(8,128)(2,1)S(1)} %collective-permute-done.7.rows_ref), custom_call_target="tpu_custom_call" | custom-call | flops 402653184 | bytes 5242880 | tf_op jit(solution)/shard_map/pallas_call | solution.py:80
  32.7 0.0 collective-permute-done.8.rows_ref
  32.7 0.9 %shard_map.158.pre_ref = f32[3072,256]{1,0:T(8,128)S(1)} custom-call(f32[3072,256]{1,0:T(8,128)S(1)} %shard_map.157.pre_ref, s16[2,3072,128]{2,1,0:T(8,128)(2,1)S(1)} %get-tuple-element.48.cols, bf16[768,256]{1,0:T(8,128)(2,1)S(1)} %get-tuple-element.63.w1_ref, bf16[256,256]{1,0:T(8,128)(2,1)S(1)} %collective-permute-done.8.rows_ref), custom_call_target="tpu_custom_call" | custom-call | flops 402653184 | bytes 5242880 | tf_op jit(solution)/shard_map/pallas_call | solution.py:80
  33.7 5.1 %collective-permute-done.9.rows_ref = bf16[256,256]{1,0:T(8,128)(2,1)S(1)} collective-permute-done((bf16[256,256]{1,0:T(8,128)(2,1)S(1)}, bf16[256,256]{1,0:T(8,128)(2,1)S(1)}, u32[]{:S(2)}, u32[]{:S(2)}) %collective-permute-start.9) | collective-permute-done | bytes 131104 | tf_op jit(solution)/shard_map/ppermute | solution.py:383
  38.7 0.0 collective-permute-start.10
  38.8 0.9 %shard_map.159.pre_ref = f32[3072,256]{1,0:T(8,128)S(1)} custom-call(f32[3072,256]{1,0:T(8,128)S(1)} %shard_map.158.pre_ref, s16[2,3072,128]{2,1,0:T(8,128)(2,1)S(1)} %get-tuple-element.48.cols, bf16[768,256]{1,0:T(8,128)(2,1)S(1)} %get-tuple-element.63.w1_ref, bf16[256,256]{1,0:T(8,128)(2,1)S(1)} %collective-permute-done.9.rows_ref), custom_call_target="tpu_custom_call" | custom-call | flops 402653184 | bytes 5242880 | tf_op jit(solution)/shard_map/pallas_call | solution.py:80
  39.7 0.4 collective-permute-done.10.refs_0_
  40.1 2.7 %shard_map.160 = (bf16[3072,256]{1,0:T(8,128)(2,1)S(1)}, bf16[256,256]{1,0:T(8,128)(2,1)S(1)}, bf16[256,256]{1,0:T(8,128)(2,1)S(1)}) custom-call(s32[1,1]{1,0:T(1,128)S(6)} %copy.16.live_ref, f32[3072,256]{1,0:T(8,128)S(1)} %shard_map.159.pre_ref, s16[2,3072,128]{2,1,0:T(8,128)(2,1)S(1)} %get-tuple-element.48.cols, ...), custom_call_target="tpu_custom_call" | custom-call | flops 2013265920 | bytes 7092228 | tf_op jit(solution)/shard_map/pallas_call | solution.py:80
  42.8 0.2 collective-permute-start.11
  43.0 1.1 %shard_map.162 = bf16[3072,256]{1,0:T(8,128)(2,1)} custom-call(bf16[3072,256]{1,0:T(8,128)(2,1)S(1)} %get-tuple-element.73.refs_0_), custom_call_target="tpu_custom_call" | custom-call | bytes 1572864 | tf_op jit(solution)/shard_map/pallas_call | solution.py:80
  44.2 0.0 collective-permute-done.11.second
  44.2 1.2 %shard_map.161 = bf16[256,256]{1,0:T(8,128)(2,1)} custom-call(bf16[512,256]{1,0:T(8,128)(2,1)S(1)} %get-tuple-element.61.dom_ref.nodes_ref, bf16[256,256]{1,0:T(8,128)(2,1)S(1)} %get-tuple-element.71.first, bf16[256,256]{1,0:T(8,128)(2,1)S(1)} %collective-permute-done.11.second, bf16[2,512,256]{2,1,0:T(8,128)(2,1)S(1)} %get-tuple-element.57.w1, ...), custom_call_target="tpu_custom_call" | custom-call | bytes 1314816 | tf_op jit(solution)/shard_map/pallas_call | solution.py:80
Async XLA Ops:
  0.6 1.9 %collective-permute-start = (bf16[256,256]{1,0:T(8,128)(2,1)}, bf16[256,256]{1,0:T(8,128)(2,1)S(1)}, u32[]{:S(2)}, u32[]{:S(2)}) collective-permute-start(bf16[256,256]{1,0:T(8,128)(2,1)} %refs_0_.2), channel_id=1, source_target_pairs={{0,1},{1,0},{2,3},{3,2},{4,5},{5,4},{6,7},{7,6},{8,9},{9,8},{10,11... | collective-permute-start | bytes 393224 | tf_op jit(solution)/shard_map/ppermute | solution.py:354
  1.2 1.4 %collective-permute-start.1 = (s32[1,4,128]{2,1,0:T(4,128)}, s32[1,4,128]{2,1,0:T(4,128)S(1)}, u32[]{:S(2)}, u32[]{:S(2)}) collective-permute-start(s32[1,4,128]{2,1,0:T(4,128)} %refs_1_.2), channel_id=1, source_target_pairs={{0,1},{1,0},{2,3},{3,2},{4,5},{5,4},{6,7},{7,6},{8,9},{9,8},{10,11... | collective-permute-start | bytes 6152 | tf_op jit(solution)/shard_map/ppermute | solution.py:354
  2.9 12.7 %collective-permute-start.2 = (bf16[256,256]{1,0:T(8,128)(2,1)S(1)}, bf16[256,256]{1,0:T(8,128)(2,1)S(1)}, u32[]{:S(2)}, u32[]{:S(2)}) collective-permute-start(bf16[256,256]{1,0:T(8,128)(2,1)S(1)} %get-tuple-element.45), channel_id=1, source_target_pairs={{0,2},{2,0},{4,6},{6,4},{8,10},{10,8},{12,14},{14,12},{16,18},{18,... | collective-permute-start | bytes 393224 | tf_op jit(solution)/shard_map/ppermute | solution.py:383
  5.8 11.1 %collective-permute-start.3 = (bf16[256,256]{1,0:T(8,128)(2,1)S(1)}, bf16[256,256]{1,0:T(8,128)(2,1)S(1)}, u32[]{:S(2)}, u32[]{:S(2)}) collective-permute-start(bf16[256,256]{1,0:T(8,128)(2,1)S(1)} %get-tuple-element.50), channel_id=1, source_target_pairs={{0,30},{2,4},{4,2},{6,8},{8,6},{10,12},{12,10},{14,16},{16,14},{18... | collective-permute-start | bytes 393224 | tf_op jit(solution)/shard_map/ppermute | solution.py:383
  15.6 2.4 %collective-permute-start.4 = (bf16[256,256]{1,0:T(8,128)(2,1)S(1)}, bf16[256,256]{1,0:T(8,128)(2,1)S(1)}, u32[]{:S(2)}, u32[]{:S(2)}) collective-permute-start(bf16[256,256]{1,0:T(8,128)(2,1)S(1)} %collective-permute-done.2.rows_ref), channel_id=1, source_target_pairs={{0,1},{1,0},{2,3},{3,2},{4,5},{5,4},{6,7},{7,6},{8,9},{9,8},{10,11... | collective-permute-start | bytes 393224 | tf_op jit(solution)/shard_map/ppermute | solution.py:354
  16.8 2.2 %collective-permute-start.5 = (bf16[256,256]{1,0:T(8,128)(2,1)S(1)}, bf16[256,256]{1,0:T(8,128)(2,1)S(1)}, u32[]{:S(2)}, u32[]{:S(2)}) collective-permute-start(bf16[256,256]{1,0:T(8,128)(2,1)S(1)} %collective-permute-done.3.refs_0_), channel_id=1, source_target_pairs={{0,1},{1,0},{2,3},{3,2},{4,5},{5,4},{6,7},{7,6},{8,9},{9,8},{10,11... | collective-permute-start | bytes 393224 | tf_op jit(solution)/shard_map/ppermute | solution.py:354
  22.3 1.6 %collective-permute-start.6 = (bf16[512,256]{1,0:T(8,128)(2,1)S(1)}, bf16[512,256]{1,0:T(8,128)(2,1)S(1)}, u32[]{:S(2)}, u32[]{:S(2)}) collective-permute-start(bf16[512,256]{1,0:T(8,128)(2,1)S(1)} %get-tuple-element.56.first), channel_id=1, source_target_pairs={{0,1},{1,0},{2,3},{3,2},{4,5},{5,4},{6,7},{7,6},{8,9},{9,8},{10,11... | collective-permute-start | bytes 786440 | tf_op jit(solution)/shard_map/ppermute | solution.py:354
  25.1 5.0 %collective-permute-start.7 = (bf16[256,256]{1,0:T(8,128)(2,1)S(1)}, bf16[256,256]{1,0:T(8,128)(2,1)S(1)}, u32[]{:S(2)}, u32[]{:S(2)}) collective-permute-start(bf16[256,256]{1,0:T(8,128)(2,1)S(1)} %get-tuple-element.64), channel_id=1, source_target_pairs={{0,2},{2,0},{4,6},{6,4},{8,10},{10,8},{12,14},{14,12},{16,18},{18,... | collective-permute-start | bytes 393224 | tf_op jit(solution)/shard_map/ppermute | solution.py:383
  30.2 2.6 %collective-permute-start.8 = (bf16[256,256]{1,0:T(8,128)(2,1)S(1)}, bf16[256,256]{1,0:T(8,128)(2,1)S(1)}, u32[]{:S(2)}, u32[]{:S(2)}) collective-permute-start(bf16[256,256]{1,0:T(8,128)(2,1)S(1)} %collective-permute-done.7.rows_ref), channel_id=1, source_target_pairs={{0,1},{1,0},{2,3},{3,2},{4,5},{5,4},{6,7},{7,6},{8,9},{9,8},{10,11... | collective-permute-start | bytes 393224 | tf_op jit(solution)/shard_map/ppermute | solution.py:354
  30.2 8.6 %collective-permute-start.9 = (bf16[256,256]{1,0:T(8,128)(2,1)S(1)}, bf16[256,256]{1,0:T(8,128)(2,1)S(1)}, u32[]{:S(2)}, u32[]{:S(2)}) collective-permute-start(bf16[256,256]{1,0:T(8,128)(2,1)S(1)} %get-tuple-element.68), channel_id=1, source_target_pairs={{0,30},{2,4},{4,2},{6,8},{8,6},{10,12},{12,10},{14,16},{16,14},{18... | collective-permute-start | bytes 393224 | tf_op jit(solution)/shard_map/ppermute | solution.py:383
  38.7 1.3 %collective-permute-start.10 = (bf16[256,256]{1,0:T(8,128)(2,1)S(1)}, bf16[256,256]{1,0:T(8,128)(2,1)S(1)}, u32[]{:S(2)}, u32[]{:S(2)}) collective-permute-start(bf16[256,256]{1,0:T(8,128)(2,1)S(1)} %collective-permute-done.9.rows_ref), channel_id=1, source_target_pairs={{0,1},{1,0},{2,3},{3,2},{4,5},{5,4},{6,7},{7,6},{8,9},{9,8},{10,11... | collective-permute-start | bytes 393224 | tf_op jit(solution)/shard_map/ppermute | solution.py:354
  42.8 1.4 %collective-permute-start.11 = (bf16[256,256]{1,0:T(8,128)(2,1)S(1)}, bf16[256,256]{1,0:T(8,128)(2,1)S(1)}, u32[]{:S(2)}, u32[]{:S(2)}) collective-permute-start(bf16[256,256]{1,0:T(8,128)(2,1)S(1)} %get-tuple-element.72), channel_id=1, source_target_pairs={{0,1},{1,0},{2,3},{3,2},{4,5},{5,4},{6,7},{7,6},{8,9},{9,8},{10,11... | collective-permute-start | bytes 393224 | tf_op jit(solution)/shard_map/ppermute | solution.py:354

commit v8 on v7

--- a/solution.py
+++ b/solution.py
@@ -124,15 +124,13 @@
 
 
 def face_hits(stride, lists):
-    rows = [one_hot_rows(lists[0, pl.ds(face, 1), :], TILE) for face in faces(stride)]
-    return jnp.concatenate(rows, axis=0)
+    return [one_hot_rows(lists[0, pl.ds(face, 1), :], TILE) for face in faces(stride)]
 
 
 def pick_kernel(stride, own_ref, peer_ref, list_own, list_peer, far, near):
     for n, (lists, nodes) in enumerate(((list_own, own_ref), (list_peer, peer_ref))):
-        picked = mm(face_hits(stride, lists), nodes[...]).astype(BF16)
-        far[n * HALF : (n + 1) * HALF, :] = picked[:HALF]
-        near[n * HALF : (n + 1) * HALF, :] = picked[HALF:]
+        for rows, out_rows in zip(face_hits(stride, lists), (far, near)):
+            out_rows[n * HALF : (n + 1) * HALF, :] = mm(rows, nodes[...]).astype(BF16)
 
 
 def load_kernel(count, *refs):
@@ -186,8 +184,8 @@
             ).astype(BF16)
 
 
-def local_block(layer, at, edge_ref, cols, w1_ref, b1_ref, table, pre_ref):
-    acc = mm(edge_ref[at, :], w1_ref[0:TILE, :])
+def local_block(layer, at, cols, b1_ref, table, pre_ref, edges=None):
+    acc = 0.0 if edges is None else mm(*edges)
     acc = acc + mm(hits(cols[0, at, :], 0, 2), table[0 : 2 * TILE, :])
     acc = acc + mm(hits(cols[1, at, :], 0, 2), table[2 * TILE :, :])
     pre_ref[at, :] = acc + b1_ref[layer : layer + 1, :]
@@ -196,12 +194,11 @@
 def first_kernel(stride, loads, send_ref, recv_ref, own_ref, peer_ref, w1_ref, b1_ref, *refs):
     hbm, (pre_ref, cols), refs = refs[:loads], refs[loads : loads + 2], refs[loads + 2 :]
     vmem, (table, sems) = refs[:loads], refs[loads:]
-    edge_hbm, edge_ref = hbm[0], vmem[0]
-    blocks = [pl.ds(start, LOCAL_ROWS) for start in range(0, edge_ref.shape[0], LOCAL_ROWS)]
-    copies = [(edge_hbm.at[at, :], edge_ref.at[at, :]) for at in blocks]
-    copies += [(hbm[1].at[1], vmem[1])] + list(zip(hbm[2:], vmem[2:]))
-    copies = [pltpu.make_async_copy(*ends, sems.at[k]) for k, ends in enumerate(copies)]
-    copies[0].start()
+    ends = [(hbm[0].at[1], vmem[0])] + list(zip(hbm[1:], vmem[1:]))
+    copies = [pltpu.make_async_copy(*pair, sems.at[k]) for k, pair in enumerate(ends)]
+    for copy in copies:
+        copy.start()
+    blocks = [pl.ds(start, LOCAL_ROWS) for start in range(0, pre_ref.shape[0], LOCAL_ROWS)]
     core = lax.axis_index("edge")
     parts = ((core * TILE, TILE, own_ref), ((1 - core) * TILE, TILE, peer_ref))
 
@@ -212,15 +209,10 @@
     make(0)
     project(parts, w1_ref, table)
     for k, at in enumerate(blocks):
-        copies[k].wait()
         if k + 1 < len(blocks):
-            copies[k + 1].start()
             make(k + 1)
-        else:
-            for copy in copies[len(blocks) :]:
-                copy.start()
-        local_block(0, at, edge_ref, cols, w1_ref, b1_ref, table, pre_ref)
-    for copy in copies[len(blocks) :]:
+        local_block(0, at, cols, b1_ref, table, pre_ref)
+    for copy in copies:
         copy.wait()
 
 
@@ -229,7 +221,8 @@
 
     def step(k, carry):
         at = dyn(k * LOCAL_ROWS, LOCAL_ROWS)
-        local_block(layer, at, edge_ref, cols, w1_ref, b1_ref, table, pre_ref)
+        edges = (edge_ref[at, :], w1_ref[0:TILE, :])
+        local_block(layer, at, cols, b1_ref, table, pre_ref, edges)
         return carry
 
     lax.fori_loop(0, edge_ref.shape[0] // LOCAL_ROWS, step, 0)
@@ -242,7 +235,8 @@
         table[dyn(axis * TILE, TILE), :] = mm(ref[...], w_s).astype(BF16)
 
 
-def tile_kernel(first, peer, pre_ref, cols, w1_ref, rows_ref, out_ref):
+def tile_kernel(first, peer, pre_ref, cols, w1_ref, rows_ref, *refs):
+    out_ref = refs[-1]
     core = lax.axis_index("edge")
     tile = first + (1 - core if peer else core)
     table = mm(rows_ref[...], w1_ref[TILE : 2 * TILE, :]).astype(BF16)
@@ -250,7 +244,10 @@
 
     def step(k, carry):
         at = dyn(k * half, half)
-        out_ref[at, :] = pre_ref[at, :] + mm(hits(cols[0, at, :], tile, 1), table)
+        acc = pre_ref[at, :] + mm(hits(cols[0, at, :], tile, 1), table)
+        if len(refs) == 2:
+            acc = acc + mm(refs[0][at, :], w1_ref[0:TILE, :])
+        out_ref[at, :] = acc
         return carry
 
     lax.fori_loop(0, 2, step, 0)
@@ -326,14 +323,15 @@
     stride, layer, own_ref, peer_ref, first, second, list_own, list_peer, w1, b1, w2, gain, out, far, near
 ):
     core = lax.axis_index("edge")
-    hot = [face_hits(stride, lists) for lists in (list_own, list_peer)]
-    for n, (owner, ref) in enumerate(((core, own_ref), (1 - core, peer_ref))):
+    nodes = []
+    for owner, ref in ((core, own_ref), (1 - core, peer_ref)):
         at = dyn(owner * TILE, TILE)
-        nodes = updated(layer, ref[...], first[at, :], second[at, :], w1, b1, w2, gain)
-        out[at, :] = nodes
-        picked = mm(hot[n], nodes).astype(BF16)
-        far[n * HALF : (n + 1) * HALF, :] = picked[:HALF]
-        near[n * HALF : (n + 1) * HALF, :] = picked[HALF:]
+        nodes.append(updated(layer, ref[...], first[at, :], second[at, :], w1, b1, w2, gain))
+        out[at, :] = nodes[-1]
+    for face, ref in zip(faces(stride), (far, near)):
+        for n, lists in enumerate((list_own, list_peer)):
+            rows = one_hot_rows(lists[0, pl.ds(face, 1), :], TILE)
+            ref[n * HALF : (n + 1) * HALF, :] = mm(rows, nodes[n]).astype(BF16)
 
 
 def last_kernel(layer, nodes_ref, first, second, w1, b1, w2, gain, out):
@@ -409,15 +407,15 @@
         near = sent_by_core(near_rows, near_d, near_s)
         far = sent_by_core(far_rows, far_d, far_s)
         if layer == 0:
-            loads = (edge_lat, edge_w1, edge_w2, node_w1, node_w2, edge_gain, node_b1, node_gain)
-            pre, cols, edge_rows, next_w1, edge_w2, node_w1, node_w2, edge_gain, node_b1, node_gain = call(
+            loads = (edge_w1, edge_lat, edge_w2, node_w1, node_w2, edge_gain, node_b1, node_gain)
+            pre, cols, next_w1, edge_rows, edge_w2, node_w1, node_w2, edge_gain, node_b1, node_gain = call(
                 functools.partial(first_kernel, stride, len(loads)),
                 [pre_shape, shaped((2, edges, HALF), I16)]
                 + [shaped(a.shape[1:] if a is edge_w1 else a.shape, a.dtype) for a in loads],
                 (send_at, recv_at, node_lat, peer_nodes, first_w1, edge_b1, *in_hbm(loads)),
                 scratch=[
                     pltpu.VMEM((4 * TILE, width), BF16),
-                    pltpu.SemaphoreType.DMA((edges // LOCAL_ROWS + len(loads) - 1,)),
+                    pltpu.SemaphoreType.DMA((len(loads),)),
                 ],
                 stay=range(6, 6 + len(loads)),
                 flops=5 * pass_flops,
@@ -432,11 +430,11 @@
             )
         w1 = next_w1 if layer else first_w1
 
-        def add(first, peer, pre, rows):
+        def add(first, peer, pre, rows, *edges):
             return call(
                 functools.partial(tile_kernel, first, peer),
                 pre_shape,
-                (pre, cols, w1, rows),
+                (pre, cols, w1, rows, *edges),
                 flops=pass_flops,
             )
 
@@ -449,7 +447,7 @@
             far_other = (swapped(far),)
             pre = add(4, False, pre, far)
         else:
-            pre = add(2, False, pre, near)
+            pre = add(2, False, pre, near, edge_rows)
             pre, far = lax.optimization_barrier((pre, far))
             far_other = (far, swapped(far))
             pre = add(2, True, pre, near_other)

time: 45.7 us -> 43.5 us (0.952)
  Pallas kernels: 24.1 us -> 21.6 us
  starting transfers between devices: 10.7 us -> 12.6 us
  waiting for transfers between devices: 9.22 us -> 7.57 us
    pallas_call x14, Pallas kernels: 24.1 us -> 21.6 us  [call(): pl.pallas_call(kernel, out_shape=outs, in_specs=[IN_SMEM if k in smem els...]
    ppermute x4, starting transfers between devices: 9.08 us -> 11.1 us  [sent_by_core(): return lax.ppermute(value, ('dom', 'edge'), pairs)]
    ppermute x4, waiting for transfers between devices: 7.16 us -> 5.87 us  [sent_by_core(): return lax.ppermute(value, ('dom', 'edge'), pairs)]
  transfers between devices with their start and end apart: 12 -> 12, of which waited for: 5 -> 6; matrix products, arithmetic and copies ran while one was open for 0% -> 0% of each run, Pallas kernels for 34% -> 30%
where the time goes in v8:
time: 43.5 us; the launch traced here: 43.3 us
  Pallas kernels  21.6 us (50%)
  starting transfers between devices  12.6 us (29%)
  waiting for transfers between devices  7.57 us (17%)
  between operations  1.43 us (3%)
    pallas_call x14, Pallas kernels, call(): pl.pallas_call(kernel, out_shape=outs, in_specs=[IN_SMEM if k in smem els...  21.6 us
    ppermute x4, starting transfers between devices, sent_by_core(): return lax.ppermute(value, ('dom', 'edge'), pairs)  11.1 us
    ppermute x4, waiting for transfers between devices, sent_by_core(): return lax.ppermute(value, ('dom', 'edge'), pairs)  5.87 us
    ppermute x8, waiting for transfers between devices, swapped(): return lax.ppermute(value, 'edge', [(0, 1), (1, 0)])  1.71 us
    ppermute x8, starting transfers between devices, swapped(): return lax.ppermute(value, 'edge', [(0, 1), (1, 0)])  1.52 us
  transfers between devices with their start and end apart: 12, of which 6 were waited for; matrix products, arithmetic and copies ran while one was open for 0% of the time, Pallas kernels for 30%

profile of v8, /device:TPU:0, one launch (start us, length us, event | category | flops | bytes accessed | tf_op | source)
XLA Modules:
  0.0 43.3 jit_solution(16135074556935245614)
XLA Ops:
  0.6 0.6 %collective-permute-start = (bf16[256,256]{1,0:T(8,128)(2,1)}, bf16[256,256]{1,0:T(8,128)(2,1)S(1)}, u32[]{:S(2)}, u32[]{:S(2)}) collective-permute-start(bf16[256,256]{1,0:T(8,128)(2,1)} %refs_0_.2), channel_id=1, source_target_pairs={{0,1},{1,0},{2,3},{3,2},{4,5},{5,4},{6,7},{7,6},{8,9},{9,8},{10,11... | collective-permute-start | bytes 393224 | tf_op jit(solution)/shard_map/ppermute | solution.py:352
  1.2 0.1 collective-permute-start.1
  1.3 1.2 %shard_map.149 = (bf16[256,256]{1,0:T(8,128)(2,1)S(1)}, s32[1,4,128]{2,1,0:T(4,128)S(1)}, s32[1,3072]{1,0:T(1,128)S(1)}, s32[1,3072]{1,0:T(1,128)S(1)}, f32[2,25...) custom-call(bf16[256,256]{1,0:T(8,128)(2,1)} %refs_0_.2, s32[1,4,128]{2,1,0:T(4,128)} %refs_1_.2, s32[1,3072]{1,0:T(1,128)} %bitcast.2, ...), custom_call_target="tpu_custom_call" | custom-call | bytes 946176 | tf_op jit(solution)/shard_map/pallas_call | solution.py:80
  2.5 0.1 collective-permute-done.1.list_peer
  2.6 0.0 collective-permute-done.peer_ref
  2.6 0.3 shard_map.151
  2.9 2.9 %collective-permute-start.2 = (bf16[256,256]{1,0:T(8,128)(2,1)S(1)}, bf16[256,256]{1,0:T(8,128)(2,1)S(1)}, u32[]{:S(2)}, u32[]{:S(2)}) collective-permute-start(bf16[256,256]{1,0:T(8,128)(2,1)S(1)} %get-tuple-element.45), channel_id=1, source_target_pairs={{0,2},{2,0},{4,6},{6,4},{8,10},{10,8},{12,14},{14,12},{16,18},{18,... | collective-permute-start | bytes 393224 | tf_op jit(solution)/shard_map/ppermute | solution.py:381
  5.8 4.5 %collective-permute-start.3 = (bf16[256,256]{1,0:T(8,128)(2,1)S(1)}, bf16[256,256]{1,0:T(8,128)(2,1)S(1)}, u32[]{:S(2)}, u32[]{:S(2)}) collective-permute-start(bf16[256,256]{1,0:T(8,128)(2,1)S(1)} %get-tuple-element.51), channel_id=1, source_target_pairs={{0,30},{2,4},{4,2},{6,8},{8,6},{10,12},{12,10},{14,16},{16,14},{18... | collective-permute-start | bytes 393224 | tf_op jit(solution)/shard_map/ppermute | solution.py:381
  10.3 2.6 %shard_map.150 = (f32[3072,256]{1,0:T(8,128)S(1)}, s16[2,3072,128]{2,1,0:T(8,128)(2,1)S(1)}, bf16[768,256]{1,0:T(8,128)(2,1)S(1)}, bf16[3072,256]{1,0:T(8,128)(2...) custom-call(s32[1,3072]{1,0:T(1,128)S(1)} %get-tuple-element.39.send, ...), custom_call_target="tpu_custom_call" | custom-call | flops 2013265920 | bytes 4096000 | tf_op jit(solution)/shard_map/pallas_call | solution.py:80
  12.9 0.0 collective-permute-done.2.rows_ref
  12.9 0.1 collective-permute-start.4
  13.0 1.5 %shard_map.152.pre_ref = f32[3072,256]{1,0:T(8,128)S(1)} custom-call(f32[3072,256]{1,0:T(8,128)S(1)} %get-tuple-element.47.pre_ref, s16[2,3072,128]{2,1,0:T(8,128)(2,1)S(1)} %get-tuple-element.48.cols, bf16[768,256]{1,0:T(8,128)(2,1)S(1)} %get-tuple-element.41.w1_ref, bf16[256,256]{1,0:T(8,128)(2,1)S(1)} %collective-permute-done.2.rows_ref, ...), custom_call_target="tpu_custom_call" | custom-call | flops 402653184 | bytes 6815744 | tf_op jit(solution)/shard_map/pallas_call | solution.py:80
  14.5 0.7 %collective-permute-done.3.refs_0_ = bf16[256,256]{1,0:T(8,128)(2,1)S(1)} collective-permute-done((bf16[256,256]{1,0:T(8,128)(2,1)S(1)}, bf16[256,256]{1,0:T(8,128)(2,1)S(1)}, u32[]{:S(2)}, u32[]{:S(2)}) %collective-permute-start.3) | collective-permute-done | bytes 131104 | tf_op jit(solution)/shard_map/ppermute | solution.py:381
  15.2 0.0 collective-permute-start.5
  15.9 0.0 collective-permute-done.4.rows_ref
  15.9 0.9 %shard_map.153.pre_ref = f32[3072,256]{1,0:T(8,128)S(1)} custom-call(f32[3072,256]{1,0:T(8,128)S(1)} %shard_map.152.pre_ref, s16[2,3072,128]{2,1,0:T(8,128)(2,1)S(1)} %get-tuple-element.48.cols, bf16[768,256]{1,0:T(8,128)(2,1)S(1)} %get-tuple-element.41.w1_ref, bf16[256,256]{1,0:T(8,128)(2,1)S(1)} %collective-permute-done.4.rows_ref), custom_call_target="tpu_custom_call" | custom-call | flops 402653184 | bytes 5242880 | tf_op jit(solution)/shard_map/pallas_call | solution.py:80
  16.9 0.0 collective-permute-done.5.refs_1_
  16.9 3.3 %shard_map.154 = (bf16[3072,256]{1,0:T(8,128)(2,1)S(1)}, bf16[512,256]{1,0:T(8,128)(2,1)S(1)}) custom-call(s32[1,1]{1,0:T(1,128)S(6)} %copy.16.live_ref, f32[3072,256]{1,0:T(8,128)S(1)} %shard_map.153.pre_ref, s16[2,3072,128]{2,1,0:T(8,128)(2,1)S(1)} %get-tuple-element.48.cols, s32[1,3072]{1,0:T(1,128)S(1)} %get-tuple-element.40.recv_ref, ...), custom_call_target="tpu_custom_call" | custom-call | flops 2013265920 | bytes 7223300 | tf_op jit(solution)/shard_map/pallas_call | solution.py:80
  20.2 0.6 %collective-permute-start.6 = (bf16[512,256]{1,0:T(8,128)(2,1)S(1)}, bf16[512,256]{1,0:T(8,128)(2,1)S(1)}, u32[]{:S(2)}, u32[]{:S(2)}) collective-permute-start(bf16[512,256]{1,0:T(8,128)(2,1)S(1)} %get-tuple-element.56.first), channel_id=1, source_target_pairs={{0,1},{1,0},{2,3},{3,2},{4,5},{5,4},{6,7},{7,6},{8,9},{9,8},{10,11... | collective-permute-start | bytes 786440 | tf_op jit(solution)/shard_map/ppermute | solution.py:352
  20.7 1.2 %collective-permute-done.6.second = bf16[512,256]{1,0:T(8,128)(2,1)S(1)} collective-permute-done((bf16[512,256]{1,0:T(8,128)(2,1)S(1)}, bf16[512,256]{1,0:T(8,128)(2,1)S(1)}, u32[]{:S(2)}, u32[]{:S(2)}) %collective-permute-start.6) | collective-permute-done | bytes 262176 | tf_op jit(solution)/shard_map/ppermute | solution.py:352
  21.9 1.1 %shard_map.155 = (bf16[512,256]{1,0:T(8,128)(2,1)S(1)}, bf16[256,256]{1,0:T(8,128)(2,1)S(1)}, bf16[256,256]{1,0:T(8,128)(2,1)S(1)}) custom-call(bf16[256,256]{1,0:T(8,128)(2,1)S(1)} %get-tuple-element.38.own_ref, bf16[256,256]{1,0:T(8,128)(2,1)S(1)} %collective-permute-done.peer_ref, bf16[512,256]{1,0:T(8,128)(2,1)S(1)} %get-tuple-element.56.first, ...), custom_call_target="tpu_custom_call" | custom-call | bytes 1581056 | tf_op jit(solution)/shard_map/pallas_call | solution.py:80
  23.0 0.1 collective-permute-start.7
  23.0 2.9 %shard_map.156.pre_ref = f32[3072,256]{1,0:T(8,128)S(1)} custom-call(bf16[3072,256]{1,0:T(8,128)(2,1)S(1)} %get-tuple-element.62.edge_ref, s16[2,3072,128]{2,1,0:T(8,128)(2,1)S(1)} %get-tuple-element.48.cols, bf16[512,256]{1,0:T(8,128)(2,1)S(1)} %get-tuple-element.61.dom_ref.nodes_ref, bf16[768,256]{1,0:T(8,128)(2,1)S(1)} %get-tuple-element.63.w1_ref, ...), custom_call_target="tpu_custom_call" | custom-call | flops 2013265920 | bytes 3803136 | tf_op jit(solution)/shard_map/pallas_call | solution.py:80
  25.9 2.1 %collective-permute-done.7.rows_ref = bf16[256,256]{1,0:T(8,128)(2,1)S(1)} collective-permute-done((bf16[256,256]{1,0:T(8,128)(2,1)S(1)}, bf16[256,256]{1,0:T(8,128)(2,1)S(1)}, u32[]{:S(2)}, u32[]{:S(2)}) %collective-permute-start.7) | collective-permute-done | bytes 131104 | tf_op jit(solution)/shard_map/ppermute | solution.py:381
  28.0 0.0 collective-permute-start.8
  28.0 3.6 %collective-permute-start.9 = (bf16[256,256]{1,0:T(8,128)(2,1)S(1)}, bf16[256,256]{1,0:T(8,128)(2,1)S(1)}, u32[]{:S(2)}, u32[]{:S(2)}) collective-permute-start(bf16[256,256]{1,0:T(8,128)(2,1)S(1)} %get-tuple-element.68), channel_id=1, source_target_pairs={{0,30},{2,4},{4,2},{6,8},{8,6},{10,12},{12,10},{14,16},{16,14},{18... | collective-permute-start | bytes 393224 | tf_op jit(solution)/shard_map/ppermute | solution.py:381
  31.6 0.9 %shard_map.157.pre_ref = f32[3072,256]{1,0:T(8,128)S(1)} custom-call(f32[3072,256]{1,0:T(8,128)S(1)} %shard_map.156.pre_ref, s16[2,3072,128]{2,1,0:T(8,128)(2,1)S(1)} %get-tuple-element.48.cols, bf16[768,256]{1,0:T(8,128)(2,1)S(1)} %get-tuple-element.63.w1_ref, bf16[256,256]{1,0:T(8,128)(2,1)S(1)} %collective-permute-done.7.rows_ref), custom_call_target="tpu_custom_call" | custom-call | flops 402653184 | bytes 5242880 | tf_op jit(solution)/shard_map/pallas_call | solution.py:80
  32.6 0.0 collective-permute-done.8.rows_ref
  32.6 0.9 %shard_map.158.pre_ref = f32[3072,256]{1,0:T(8,128)S(1)} custom-call(f32[3072,256]{1,0:T(8,128)S(1)} %shard_map.157.pre_ref, s16[2,3072,128]{2,1,0:T(8,128)(2,1)S(1)} %get-tuple-element.48.cols, bf16[768,256]{1,0:T(8,128)(2,1)S(1)} %get-tuple-element.63.w1_ref, bf16[256,256]{1,0:T(8,128)(2,1)S(1)} %collective-permute-done.8.rows_ref), custom_call_target="tpu_custom_call" | custom-call | flops 402653184 | bytes 5242880 | tf_op jit(solution)/shard_map/pallas_call | solution.py:80
  33.5 3.0 %collective-permute-done.9.rows_ref = bf16[256,256]{1,0:T(8,128)(2,1)S(1)} collective-permute-done((bf16[256,256]{1,0:T(8,128)(2,1)S(1)}, bf16[256,256]{1,0:T(8,128)(2,1)S(1)}, u32[]{:S(2)}, u32[]{:S(2)}) %collective-permute-start.9) | collective-permute-done | bytes 131104 | tf_op jit(solution)/shard_map/ppermute | solution.py:381
  36.6 0.0 collective-permute-start.10
  36.6 0.9 %shard_map.159.pre_ref = f32[3072,256]{1,0:T(8,128)S(1)} custom-call(f32[3072,256]{1,0:T(8,128)S(1)} %shard_map.158.pre_ref, s16[2,3072,128]{2,1,0:T(8,128)(2,1)S(1)} %get-tuple-element.48.cols, bf16[768,256]{1,0:T(8,128)(2,1)S(1)} %get-tuple-element.63.w1_ref, bf16[256,256]{1,0:T(8,128)(2,1)S(1)} %collective-permute-done.9.rows_ref), custom_call_target="tpu_custom_call" | custom-call | flops 402653184 | bytes 5242880 | tf_op jit(solution)/shard_map/pallas_call | solution.py:80
  37.5 0.4 collective-permute-done.10.refs_0_
  37.9 2.7 %shard_map.160 = (bf16[3072,256]{1,0:T(8,128)(2,1)S(1)}, bf16[256,256]{1,0:T(8,128)(2,1)S(1)}, bf16[256,256]{1,0:T(8,128)(2,1)S(1)}) custom-call(s32[1,1]{1,0:T(1,128)S(6)} %copy.16.live_ref, f32[3072,256]{1,0:T(8,128)S(1)} %shard_map.159.pre_ref, s16[2,3072,128]{2,1,0:T(8,128)(2,1)S(1)} %get-tuple-element.48.cols, ...), custom_call_target="tpu_custom_call" | custom-call | flops 2013265920 | bytes 7092228 | tf_op jit(solution)/shard_map/pallas_call | solution.py:80
  40.6 0.2 collective-permute-start.11
  40.9 1.1 %shard_map.162 = bf16[3072,256]{1,0:T(8,128)(2,1)} custom-call(bf16[3072,256]{1,0:T(8,128)(2,1)S(1)} %get-tuple-element.73.refs_0_), custom_call_target="tpu_custom_call" | custom-call | bytes 1572864 | tf_op jit(solution)/shard_map/pallas_call | solution.py:80
  42.0 0.0 collective-permute-done.11.second
  42.1 1.2 %shard_map.161 = bf16[256,256]{1,0:T(8,128)(2,1)} custom-call(bf16[512,256]{1,0:T(8,128)(2,1)S(1)} %get-tuple-element.61.dom_ref.nodes_ref, bf16[256,256]{1,0:T(8,128)(2,1)S(1)} %get-tuple-element.71.first, bf16[256,256]{1,0:T(8,128)(2,1)S(1)} %collective-permute-done.11.second, bf16[2,512,256]{2,1,0:T(8,128)(2,1)S(1)} %get-tuple-element.57.w1, ...), custom_call_target="tpu_custom_call" | custom-call | bytes 1314816 | tf_op jit(solution)/shard_map/pallas_call | solution.py:80
Async XLA Ops:
  0.6 1.9 %collective-permute-start = (bf16[256,256]{1,0:T(8,128)(2,1)}, bf16[256,256]{1,0:T(8,128)(2,1)S(1)}, u32[]{:S(2)}, u32[]{:S(2)}) collective-permute-start(bf16[256,256]{1,0:T(8,128)(2,1)} %refs_0_.2), channel_id=1, source_target_pairs={{0,1},{1,0},{2,3},{3,2},{4,5},{5,4},{6,7},{7,6},{8,9},{9,8},{10,11... | collective-permute-start | bytes 393224 | tf_op jit(solution)/shard_map/ppermute | solution.py:352
  1.2 1.4 %collective-permute-start.1 = (s32[1,4,128]{2,1,0:T(4,128)}, s32[1,4,128]{2,1,0:T(4,128)S(1)}, u32[]{:S(2)}, u32[]{:S(2)}) collective-permute-start(s32[1,4,128]{2,1,0:T(4,128)} %refs_1_.2), channel_id=1, source_target_pairs={{0,1},{1,0},{2,3},{3,2},{4,5},{5,4},{6,7},{7,6},{8,9},{9,8},{10,11... | collective-permute-start | bytes 6152 | tf_op jit(solution)/shard_map/ppermute | solution.py:352
  2.9 10.1 %collective-permute-start.2 = (bf16[256,256]{1,0:T(8,128)(2,1)S(1)}, bf16[256,256]{1,0:T(8,128)(2,1)S(1)}, u32[]{:S(2)}, u32[]{:S(2)}) collective-permute-start(bf16[256,256]{1,0:T(8,128)(2,1)S(1)} %get-tuple-element.45), channel_id=1, source_target_pairs={{0,2},{2,0},{4,6},{6,4},{8,10},{10,8},{12,14},{14,12},{16,18},{18,... | collective-permute-start | bytes 393224 | tf_op jit(solution)/shard_map/ppermute | solution.py:381
  5.8 9.5 %collective-permute-start.3 = (bf16[256,256]{1,0:T(8,128)(2,1)S(1)}, bf16[256,256]{1,0:T(8,128)(2,1)S(1)}, u32[]{:S(2)}, u32[]{:S(2)}) collective-permute-start(bf16[256,256]{1,0:T(8,128)(2,1)S(1)} %get-tuple-element.51), channel_id=1, source_target_pairs={{0,30},{2,4},{4,2},{6,8},{8,6},{10,12},{12,10},{14,16},{16,14},{18... | collective-permute-start | bytes 393224 | tf_op jit(solution)/shard_map/ppermute | solution.py:381
  12.9 3.0 %collective-permute-start.4 = (bf16[256,256]{1,0:T(8,128)(2,1)S(1)}, bf16[256,256]{1,0:T(8,128)(2,1)S(1)}, u32[]{:S(2)}, u32[]{:S(2)}) collective-permute-start(bf16[256,256]{1,0:T(8,128)(2,1)S(1)} %collective-permute-done.2.rows_ref), channel_id=1, source_target_pairs={{0,1},{1,0},{2,3},{3,2},{4,5},{5,4},{6,7},{7,6},{8,9},{9,8},{10,11... | collective-permute-start | bytes 393224 | tf_op jit(solution)/shard_map/ppermute | solution.py:352
  15.2 1.6 %collective-permute-start.5 = (bf16[256,256]{1,0:T(8,128)(2,1)S(1)}, bf16[256,256]{1,0:T(8,128)(2,1)S(1)}, u32[]{:S(2)}, u32[]{:S(2)}) collective-permute-start(bf16[256,256]{1,0:T(8,128)(2,1)S(1)} %collective-permute-done.3.refs_0_), channel_id=1, source_target_pairs={{0,1},{1,0},{2,3},{3,2},{4,5},{5,4},{6,7},{7,6},{8,9},{9,8},{10,11... | collective-permute-start | bytes 393224 | tf_op jit(solution)/shard_map/ppermute | solution.py:352
  20.2 1.7 %collective-permute-start.6 = (bf16[512,256]{1,0:T(8,128)(2,1)S(1)}, bf16[512,256]{1,0:T(8,128)(2,1)S(1)}, u32[]{:S(2)}, u32[]{:S(2)}) collective-permute-start(bf16[512,256]{1,0:T(8,128)(2,1)S(1)} %get-tuple-element.56.first), channel_id=1, source_target_pairs={{0,1},{1,0},{2,3},{3,2},{4,5},{5,4},{6,7},{7,6},{8,9},{9,8},{10,11... | collective-permute-start | bytes 786440 | tf_op jit(solution)/shard_map/ppermute | solution.py:352
  23.0 5.0 %collective-permute-start.7 = (bf16[256,256]{1,0:T(8,128)(2,1)S(1)}, bf16[256,256]{1,0:T(8,128)(2,1)S(1)}, u32[]{:S(2)}, u32[]{:S(2)}) collective-permute-start(bf16[256,256]{1,0:T(8,128)(2,1)S(1)} %get-tuple-element.64), channel_id=1, source_target_pairs={{0,2},{2,0},{4,6},{6,4},{8,10},{10,8},{12,14},{14,12},{16,18},{18,... | collective-permute-start | bytes 393224 | tf_op jit(solution)/shard_map/ppermute | solution.py:381
  28.0 4.6 %collective-permute-start.8 = (bf16[256,256]{1,0:T(8,128)(2,1)S(1)}, bf16[256,256]{1,0:T(8,128)(2,1)S(1)}, u32[]{:S(2)}, u32[]{:S(2)}) collective-permute-start(bf16[256,256]{1,0:T(8,128)(2,1)S(1)} %collective-permute-done.7.rows_ref), channel_id=1, source_target_pairs={{0,1},{1,0},{2,3},{3,2},{4,5},{5,4},{6,7},{7,6},{8,9},{9,8},{10,11... | collective-permute-start | bytes 393224 | tf_op jit(solution)/shard_map/ppermute | solution.py:352
  28.0 8.6 %collective-permute-start.9 = (bf16[256,256]{1,0:T(8,128)(2,1)S(1)}, bf16[256,256]{1,0:T(8,128)(2,1)S(1)}, u32[]{:S(2)}, u32[]{:S(2)}) collective-permute-start(bf16[256,256]{1,0:T(8,128)(2,1)S(1)} %get-tuple-element.68), channel_id=1, source_target_pairs={{0,30},{2,4},{4,2},{6,8},{8,6},{10,12},{12,10},{14,16},{16,14},{18... | collective-permute-start | bytes 393224 | tf_op jit(solution)/shard_map/ppermute | solution.py:381
  36.6 1.3 %collective-permute-start.10 = (bf16[256,256]{1,0:T(8,128)(2,1)S(1)}, bf16[256,256]{1,0:T(8,128)(2,1)S(1)}, u32[]{:S(2)}, u32[]{:S(2)}) collective-permute-start(bf16[256,256]{1,0:T(8,128)(2,1)S(1)} %collective-permute-done.9.rows_ref), channel_id=1, source_target_pairs={{0,1},{1,0},{2,3},{3,2},{4,5},{5,4},{6,7},{7,6},{8,9},{9,8},{10,11... | collective-permute-start | bytes 393224 | tf_op jit(solution)/shard_map/ppermute | solution.py:352
  40.6 1.4 %collective-permute-start.11 = (bf16[256,256]{1,0:T(8,128)(2,1)S(1)}, bf16[256,256]{1,0:T(8,128)(2,1)S(1)}, u32[]{:S(2)}, u32[]{:S(2)}) collective-permute-start(bf16[256,256]{1,0:T(8,128)(2,1)S(1)} %get-tuple-element.72), channel_id=1, source_target_pairs={{0,1},{1,0},{2,3},{3,2},{4,5},{5,4},{6,7},{7,6},{8,9},{9,8},{10,11... | collective-permute-start | bytes 393224 | tf_op jit(solution)/shard_map/ppermute | solution.py:352

commit v9 on v8

--- a/solution.py
+++ b/solution.py
@@ -228,13 +228,6 @@
     lax.fori_loop(0, edge_ref.shape[0] // LOCAL_ROWS, step, 0)
 
 
-def halo_tables(own, peer, w1_ref, table):
-    core = lax.axis_index("edge")
-    w_s = w1_ref[TILE : 2 * TILE, :]
-    for axis, ref in ((core, own), (1 - core, peer)):
-        table[dyn(axis * TILE, TILE), :] = mm(ref[...], w_s).astype(BF16)
-
-
 def tile_kernel(first, peer, pre_ref, cols, w1_ref, rows_ref, *refs):
     out_ref = refs[-1]
     core = lax.axis_index("edge")
@@ -254,26 +247,20 @@
 
 
 def edge_kernel(
-    layer, split, live_ref, pre_ref, cols, recv_ref, edge_ref, w1_ref, w2_ref, gain_ref, *refs
+    layer, split, live_ref, pre_ref, cols, recv_ref, edge_ref, w1_ref, w2_ref, gain_ref, peer, out_ref, *refs
 ):
-    own, peer, refs = (None, *refs[:1], refs[1:]) if split else (*refs[:2], refs[2:])
-    out_ref, refs = refs[0], refs[1:]
     if split:
         keep_ref, give_ref, table, raw, msgs, sums = refs
     else:
         part_ref, table, raw, msgs, sums = refs
-    if split:
-        first, tiles = 5 - lax.axis_index("edge"), 1
-        table[0:TILE, :] = mm(peer[...], w1_ref[TILE : 2 * TILE, :]).astype(BF16)
-    else:
-        first, tiles = 4, 2
-        halo_tables(own, peer, w1_ref, table)
+    tile = 5 - lax.axis_index("edge")
+    table[...] = mm(peer[...], w1_ref[TILE : 2 * TILE, :]).astype(BF16)
     gain = gain_ref[layer : layer + 1, :]
     live = live_ref[0, 0]
     count = edge_ref.shape[0] // ROWS
 
     def gather(at):
-        acc = pre_ref[at, :] + mm(hits(cols[0, at, :], first, tiles), table[0 : tiles * TILE, :])
+        acc = pre_ref[at, :] + mm(hits(cols[0, at, :], tile, 1), table[...])
         hidden = jnp.maximum(acc.astype(BF16), jnp.asarray(0, BF16))
         raw[at, :] = mm(hidden, w2_ref[layer])
 
@@ -380,7 +367,7 @@
         pairs += [(2 * d + 1, 2 * p + 1) for d, p in enumerate(partner_s)]
         return lax.ppermute(value, ("dom", "edge"), pairs)
 
-    table = pltpu.VMEM((2 * TILE, width), BF16)
+    table = pltpu.VMEM((TILE, width), BF16)
     messages = pltpu.VMEM((edges, width), BF16)
     pre_shape = shaped((edges, width), F32)
     rows_out = shaped((TILE, width), BF16)
@@ -440,17 +427,11 @@
 
         pre, near, live_edges = lax.optimization_barrier((pre, near, live_edges))
         near_other = swapped(near)
-        if last:
-            pre = add(2, False, pre, near)
-            pre = add(2, True, pre, near_other)
-            pre, far = lax.optimization_barrier((pre, far))
-            far_other = (swapped(far),)
-            pre = add(4, False, pre, far)
-        else:
-            pre = add(2, False, pre, near, edge_rows)
-            pre, far = lax.optimization_barrier((pre, far))
-            far_other = (far, swapped(far))
-            pre = add(2, True, pre, near_other)
+        pre = add(2, False, pre, near, *(() if layer else (edge_rows,)))
+        pre = add(2, True, pre, near_other)
+        pre, far = lax.optimization_barrier((pre, far))
+        far_other = swapped(far)
+        pre = add(4, False, pre, far)
         if last:
             outs = [shaped((nodes, width), BF16)] * 2
         else:
@@ -458,7 +439,7 @@
         edge_rows, *partial = call(
             functools.partial(edge_kernel, layer, last),
             [shaped((edges, width), BF16)] + outs,
-            (live_edges, pre, cols, recv_at, edge_rows, w1, edge_w2, edge_gain, *far_other),
+            (live_edges, pre, cols, recv_at, edge_rows, w1, edge_w2, edge_gain, far_other),
             scratch=[
                 table,
                 pltpu.VMEM((edges, width), F32),

time: 43.5 us -> 46.5 us (1.069)
  starting transfers between devices: 12.6 us -> 14.7 us
  waiting for transfers between devices: 7.57 us -> 8.27 us
    ppermute x4, starting transfers between devices: 11.1 us -> 13.3 us  [sent_by_core(): return lax.ppermute(value, ('dom', 'edge'), pairs)]
    ppermute x4, waiting for transfers between devices: 5.87 us -> 6.57 us  [sent_by_core(): return lax.ppermute(value, ('dom', 'edge'), pairs)]
    pallas_call x14 -> x15, Pallas kernels: 21.6 us -> 21.9 us  [call(): pl.pallas_call(kernel, out_shape=outs, in_specs=[IN_SMEM if k in smem els...]
  transfers between devices with their start and end apart: 12 -> 12, of which waited for: 6 -> 7; matrix products, arithmetic and copies ran while one was open for 0% -> 0% of each run, Pallas kernels for 30% -> 30%
where the time goes in v9:
time: 46.5 us; the launch traced here: 46.4 us
  Pallas kernels  21.9 us (47%)
  starting transfers between devices  14.7 us (32%)
  waiting for transfers between devices  8.27 us (18%)
  between operations  1.43 us (3%)
    pallas_call x15, Pallas kernels, call(): pl.pallas_call(kernel, out_shape=outs, in_specs=[IN_SMEM if k in smem els...  21.9 us
    ppermute x4, starting transfers between devices, sent_by_core(): return lax.ppermute(value, ('dom', 'edge'), pairs)  13.3 us
    ppermute x4, waiting for transfers between devices, sent_by_core(): return lax.ppermute(value, ('dom', 'edge'), pairs)  6.57 us
    ppermute x8, waiting for transfers between devices, swapped(): return lax.ppermute(value, 'edge', [(0, 1), (1, 0)])  1.7 us
    ppermute x8, starting transfers between devices, swapped(): return lax.ppermute(value, 'edge', [(0, 1), (1, 0)])  1.44 us
  transfers between devices with their start and end apart: 12, of which 7 were waited for; matrix products, arithmetic and copies ran while one was open for 0% of the time, Pallas kernels for 30%

profile of v9, /device:TPU:0, one launch (start us, length us, event | category | flops | bytes accessed | tf_op | source)
XLA Modules:
  0.0 46.4 jit_solution(17542910807370967410)
XLA Ops:
  0.6 0.6 %collective-permute-start = (bf16[256,256]{1,0:T(8,128)(2,1)}, bf16[256,256]{1,0:T(8,128)(2,1)S(1)}, u32[]{:S(2)}, u32[]{:S(2)}) collective-permute-start(bf16[256,256]{1,0:T(8,128)(2,1)} %refs_0_.2), channel_id=1, source_target_pairs={{0,1},{1,0},{2,3},{3,2},{4,5},{5,4},{6,7},{7,6},{8,9},{9,8},{10,11... | collective-permute-start | bytes 393224 | tf_op jit(solution)/shard_map/ppermute | solution.py:339
  1.2 0.1 collective-permute-start.1
  1.3 1.2 %shard_map.149 = (bf16[256,256]{1,0:T(8,128)(2,1)S(1)}, s32[1,4,128]{2,1,0:T(4,128)S(1)}, s32[1,3072]{1,0:T(1,128)S(1)}, s32[1,3072]{1,0:T(1,128)S(1)}, f32[2,25...) custom-call(bf16[256,256]{1,0:T(8,128)(2,1)} %refs_0_.2, s32[1,4,128]{2,1,0:T(4,128)} %refs_1_.2, s32[1,3072]{1,0:T(1,128)} %bitcast.2, ...), custom_call_target="tpu_custom_call" | custom-call | bytes 946176 | tf_op jit(solution)/shard_map/pallas_call | solution.py:80
  2.5 0.1 collective-permute-done.1.list_peer
  2.6 0.0 collective-permute-done.peer_ref
  2.6 0.3 shard_map.151
  2.9 2.9 %collective-permute-start.2 = (bf16[256,256]{1,0:T(8,128)(2,1)S(1)}, bf16[256,256]{1,0:T(8,128)(2,1)S(1)}, u32[]{:S(2)}, u32[]{:S(2)}) collective-permute-start(bf16[256,256]{1,0:T(8,128)(2,1)S(1)} %get-tuple-element.45), channel_id=1, source_target_pairs={{0,2},{2,0},{4,6},{6,4},{8,10},{10,8},{12,14},{14,12},{16,18},{18,... | collective-permute-start | bytes 393224 | tf_op jit(solution)/shard_map/ppermute | solution.py:368
  5.8 2.6 %shard_map.150 = (f32[3072,256]{1,0:T(8,128)S(1)}, s16[2,3072,128]{2,1,0:T(8,128)(2,1)S(1)}, bf16[768,256]{1,0:T(8,128)(2,1)S(1)}, bf16[3072,256]{1,0:T(8,128)(2...) custom-call(s32[1,3072]{1,0:T(1,128)S(1)} %get-tuple-element.39.send, ...), custom_call_target="tpu_custom_call" | custom-call | flops 2013265920 | bytes 4096000 | tf_op jit(solution)/shard_map/pallas_call | solution.py:80
  8.4 0.3 collective-permute-done.2.rows_ref
  8.7 0.0 collective-permute-start.3
  8.7 6.0 %collective-permute-start.4 = (bf16[256,256]{1,0:T(8,128)(2,1)S(1)}, bf16[256,256]{1,0:T(8,128)(2,1)S(1)}, u32[]{:S(2)}, u32[]{:S(2)}) collective-permute-start(bf16[256,256]{1,0:T(8,128)(2,1)S(1)} %get-tuple-element.51), channel_id=1, source_target_pairs={{0,30},{2,4},{4,2},{6,8},{8,6},{10,12},{12,10},{14,16},{16,14},{18... | collective-permute-start | bytes 393224 | tf_op jit(solution)/shard_map/ppermute | solution.py:368
  14.7 1.5 %shard_map.152.pre_ref = f32[3072,256]{1,0:T(8,128)S(1)} custom-call(f32[3072,256]{1,0:T(8,128)S(1)} %get-tuple-element.47.pre_ref, s16[2,3072,128]{2,1,0:T(8,128)(2,1)S(1)} %get-tuple-element.48.cols, bf16[768,256]{1,0:T(8,128)(2,1)S(1)} %get-tuple-element.41.w1_ref, bf16[256,256]{1,0:T(8,128)(2,1)S(1)} %collective-permute-done.2.rows_ref, ...), custom_call_target="tpu_custom_call" | custom-call | flops 402653184 | bytes 6815744 | tf_op jit(solution)/shard_map/pallas_call | solution.py:80
  16.2 0.0 collective-permute-done.3.rows_ref
  16.2 0.9 %shard_map.153.pre_ref = f32[3072,256]{1,0:T(8,128)S(1)} custom-call(f32[3072,256]{1,0:T(8,128)S(1)} %shard_map.152.pre_ref, s16[2,3072,128]{2,1,0:T(8,128)(2,1)S(1)} %get-tuple-element.48.cols, bf16[768,256]{1,0:T(8,128)(2,1)S(1)} %get-tuple-element.41.w1_ref, bf16[256,256]{1,0:T(8,128)(2,1)S(1)} %collective-permute-done.3.rows_ref), custom_call_target="tpu_custom_call" | custom-call | flops 402653184 | bytes 5242880 | tf_op jit(solution)/shard_map/pallas_call | solution.py:80
  17.2 1.8 %collective-permute-done.4.rows_ref = bf16[256,256]{1,0:T(8,128)(2,1)S(1)} collective-permute-done((bf16[256,256]{1,0:T(8,128)(2,1)S(1)}, bf16[256,256]{1,0:T(8,128)(2,1)S(1)}, u32[]{:S(2)}, u32[]{:S(2)}) %collective-permute-start.4) | collective-permute-done | bytes 131104 | tf_op jit(solution)/shard_map/ppermute | solution.py:368
  19.0 0.0 collective-permute-start.5
  19.6 0.9 %shard_map.154.pre_ref = f32[3072,256]{1,0:T(8,128)S(1)} custom-call(f32[3072,256]{1,0:T(8,128)S(1)} %shard_map.153.pre_ref, s16[2,3072,128]{2,1,0:T(8,128)(2,1)S(1)} %get-tuple-element.48.cols, bf16[768,256]{1,0:T(8,128)(2,1)S(1)} %get-tuple-element.41.w1_ref, bf16[256,256]{1,0:T(8,128)(2,1)S(1)} %collective-permute-done.4.rows_ref), custom_call_target="tpu_custom_call" | custom-call | flops 402653184 | bytes 5242880 | tf_op jit(solution)/shard_map/pallas_call | solution.py:80
  20.6 0.0 collective-permute-done.5.peer
  20.6 2.6 %shard_map.155 = (bf16[3072,256]{1,0:T(8,128)(2,1)S(1)}, bf16[512,256]{1,0:T(8,128)(2,1)S(1)}) custom-call(s32[1,1]{1,0:T(1,128)S(6)} %copy.16.live_ref, f32[3072,256]{1,0:T(8,128)S(1)} %shard_map.154.pre_ref, s16[2,3072,128]{2,1,0:T(8,128)(2,1)S(1)} %get-tuple-element.48.cols, s32[1,3072]{1,0:T(1,128)S(1)} %get-tuple-element.40.recv_ref, ...), custom_call_target="tpu_custom_call" | custom-call | flops 2013265920 | bytes 7092228 | tf_op jit(solution)/shard_map/pallas_call | solution.py:80
  23.3 0.6 %collective-permute-start.6 = (bf16[512,256]{1,0:T(8,128)(2,1)S(1)}, bf16[512,256]{1,0:T(8,128)(2,1)S(1)}, u32[]{:S(2)}, u32[]{:S(2)}) collective-permute-start(bf16[512,256]{1,0:T(8,128)(2,1)S(1)} %get-tuple-element.56.first), channel_id=1, source_target_pairs={{0,1},{1,0},{2,3},{3,2},{4,5},{5,4},{6,7},{7,6},{8,9},{9,8},{10,11... | collective-permute-start | bytes 786440 | tf_op jit(solution)/shard_map/ppermute | solution.py:339
  23.8 1.2 %collective-permute-done.6.second = bf16[512,256]{1,0:T(8,128)(2,1)S(1)} collective-permute-done((bf16[512,256]{1,0:T(8,128)(2,1)S(1)}, bf16[512,256]{1,0:T(8,128)(2,1)S(1)}, u32[]{:S(2)}, u32[]{:S(2)}) %collective-permute-start.6) | collective-permute-done | bytes 262176 | tf_op jit(solution)/shard_map/ppermute | solution.py:339
  25.0 1.1 %shard_map.156 = (bf16[512,256]{1,0:T(8,128)(2,1)S(1)}, bf16[256,256]{1,0:T(8,128)(2,1)S(1)}, bf16[256,256]{1,0:T(8,128)(2,1)S(1)}) custom-call(bf16[256,256]{1,0:T(8,128)(2,1)S(1)} %get-tuple-element.38.own_ref, bf16[256,256]{1,0:T(8,128)(2,1)S(1)} %collective-permute-done.peer_ref, bf16[512,256]{1,0:T(8,128)(2,1)S(1)} %get-tuple-element.56.first, ...), custom_call_target="tpu_custom_call" | custom-call | bytes 1581056 | tf_op jit(solution)/shard_map/pallas_call | solution.py:80
  26.0 0.1 collective-permute-start.7
  26.1 2.8 %shard_map.157.pre_ref = f32[3072,256]{1,0:T(8,128)S(1)} custom-call(bf16[3072,256]{1,0:T(8,128)(2,1)S(1)} %get-tuple-element.62.edge_ref, s16[2,3072,128]{2,1,0:T(8,128)(2,1)S(1)} %get-tuple-element.48.cols, bf16[512,256]{1,0:T(8,128)(2,1)S(1)} %get-tuple-element.61.dom_ref.nodes_ref, bf16[768,256]{1,0:T(8,128)(2,1)S(1)} %get-tuple-element.63.w1_ref, ...), custom_call_target="tpu_custom_call" | custom-call | flops 2013265920 | bytes 3803136 | tf_op jit(solution)/shard_map/pallas_call | solution.py:80
  29.0 2.1 %collective-permute-done.7.rows_ref = bf16[256,256]{1,0:T(8,128)(2,1)S(1)} collective-permute-done((bf16[256,256]{1,0:T(8,128)(2,1)S(1)}, bf16[256,256]{1,0:T(8,128)(2,1)S(1)}, u32[]{:S(2)}, u32[]{:S(2)}) %collective-permute-start.7) | collective-permute-done | bytes 131104 | tf_op jit(solution)/shard_map/ppermute | solution.py:368
  31.1 0.0 collective-permute-start.8
  31.1 4.3 %collective-permute-start.9 = (bf16[256,256]{1,0:T(8,128)(2,1)S(1)}, bf16[256,256]{1,0:T(8,128)(2,1)S(1)}, u32[]{:S(2)}, u32[]{:S(2)}) collective-permute-start(bf16[256,256]{1,0:T(8,128)(2,1)S(1)} %get-tuple-element.68), channel_id=1, source_target_pairs={{0,30},{2,4},{4,2},{6,8},{8,6},{10,12},{12,10},{14,16},{16,14},{18... | collective-permute-start | bytes 393224 | tf_op jit(solution)/shard_map/ppermute | solution.py:368
  35.4 0.9 %shard_map.158.pre_ref = f32[3072,256]{1,0:T(8,128)S(1)} custom-call(f32[3072,256]{1,0:T(8,128)S(1)} %shard_map.157.pre_ref, s16[2,3072,128]{2,1,0:T(8,128)(2,1)S(1)} %get-tuple-element.48.cols, bf16[768,256]{1,0:T(8,128)(2,1)S(1)} %get-tuple-element.63.w1_ref, bf16[256,256]{1,0:T(8,128)(2,1)S(1)} %collective-permute-done.7.rows_ref), custom_call_target="tpu_custom_call" | custom-call | flops 402653184 | bytes 5242880 | tf_op jit(solution)/shard_map/pallas_call | solution.py:80
  36.3 0.0 collective-permute-done.8.rows_ref
  36.3 0.9 %shard_map.159.pre_ref = f32[3072,256]{1,0:T(8,128)S(1)} custom-call(f32[3072,256]{1,0:T(8,128)S(1)} %shard_map.158.pre_ref, s16[2,3072,128]{2,1,0:T(8,128)(2,1)S(1)} %get-tuple-element.48.cols, bf16[768,256]{1,0:T(8,128)(2,1)S(1)} %get-tuple-element.63.w1_ref, bf16[256,256]{1,0:T(8,128)(2,1)S(1)} %collective-permute-done.8.rows_ref), custom_call_target="tpu_custom_call" | custom-call | flops 402653184 | bytes 5242880 | tf_op jit(solution)/shard_map/pallas_call | solution.py:80
  37.3 2.4 %collective-permute-done.9.rows_ref = bf16[256,256]{1,0:T(8,128)(2,1)S(1)} collective-permute-done((bf16[256,256]{1,0:T(8,128)(2,1)S(1)}, bf16[256,256]{1,0:T(8,128)(2,1)S(1)}, u32[]{:S(2)}, u32[]{:S(2)}) %collective-permute-start.9) | collective-permute-done | bytes 131104 | tf_op jit(solution)/shard_map/ppermute | solution.py:368
  39.6 0.0 collective-permute-start.10
  39.7 0.9 %shard_map.160.pre_ref = f32[3072,256]{1,0:T(8,128)S(1)} custom-call(f32[3072,256]{1,0:T(8,128)S(1)} %shard_map.159.pre_ref, s16[2,3072,128]{2,1,0:T(8,128)(2,1)S(1)} %get-tuple-element.48.cols, bf16[768,256]{1,0:T(8,128)(2,1)S(1)} %get-tuple-element.63.w1_ref, bf16[256,256]{1,0:T(8,128)(2,1)S(1)} %collective-permute-done.9.rows_ref), custom_call_target="tpu_custom_call" | custom-call | flops 402653184 | bytes 5242880 | tf_op jit(solution)/shard_map/pallas_call | solution.py:80
  40.6 0.4 collective-permute-done.10.peer
  41.0 2.7 %shard_map.161 = (bf16[3072,256]{1,0:T(8,128)(2,1)S(1)}, bf16[256,256]{1,0:T(8,128)(2,1)S(1)}, bf16[256,256]{1,0:T(8,128)(2,1)S(1)}) custom-call(s32[1,1]{1,0:T(1,128)S(6)} %copy.16.live_ref, f32[3072,256]{1,0:T(8,128)S(1)} %shard_map.160.pre_ref, s16[2,3072,128]{2,1,0:T(8,128)(2,1)S(1)} %get-tuple-element.48.cols, ...), custom_call_target="tpu_custom_call" | custom-call | flops 2013265920 | bytes 7092228 | tf_op jit(solution)/shard_map/pallas_call | solution.py:80
  43.7 0.2 collective-permute-start.11
  44.0 1.1 %shard_map.163 = bf16[3072,256]{1,0:T(8,128)(2,1)} custom-call(bf16[3072,256]{1,0:T(8,128)(2,1)S(1)} %get-tuple-element.73.refs_0_), custom_call_target="tpu_custom_call" | custom-call | bytes 1572864 | tf_op jit(solution)/shard_map/pallas_call | solution.py:80
  45.1 0.0 collective-permute-done.11.second
  45.1 1.2 %shard_map.162 = bf16[256,256]{1,0:T(8,128)(2,1)} custom-call(bf16[512,256]{1,0:T(8,128)(2,1)S(1)} %get-tuple-element.61.dom_ref.nodes_ref, bf16[256,256]{1,0:T(8,128)(2,1)S(1)} %get-tuple-element.71.first, bf16[256,256]{1,0:T(8,128)(2,1)S(1)} %collective-permute-done.11.second, bf16[2,512,256]{2,1,0:T(8,128)(2,1)S(1)} %get-tuple-element.57.w1, ...), custom_call_target="tpu_custom_call" | custom-call | bytes 1314816 | tf_op jit(solution)/shard_map/pallas_call | solution.py:80
Async XLA Ops:
  0.6 1.9 %collective-permute-start = (bf16[256,256]{1,0:T(8,128)(2,1)}, bf16[256,256]{1,0:T(8,128)(2,1)S(1)}, u32[]{:S(2)}, u32[]{:S(2)}) collective-permute-start(bf16[256,256]{1,0:T(8,128)(2,1)} %refs_0_.2), channel_id=1, source_target_pairs={{0,1},{1,0},{2,3},{3,2},{4,5},{5,4},{6,7},{7,6},{8,9},{9,8},{10,11... | collective-permute-start | bytes 393224 | tf_op jit(solution)/shard_map/ppermute | solution.py:339
  1.2 1.4 %collective-permute-start.1 = (s32[1,4,128]{2,1,0:T(4,128)}, s32[1,4,128]{2,1,0:T(4,128)S(1)}, u32[]{:S(2)}, u32[]{:S(2)}) collective-permute-start(s32[1,4,128]{2,1,0:T(4,128)} %refs_1_.2), channel_id=1, source_target_pairs={{0,1},{1,0},{2,3},{3,2},{4,5},{5,4},{6,7},{7,6},{8,9},{9,8},{10,11... | collective-permute-start | bytes 6152 | tf_op jit(solution)/shard_map/ppermute | solution.py:339
  2.9 5.8 %collective-permute-start.2 = (bf16[256,256]{1,0:T(8,128)(2,1)S(1)}, bf16[256,256]{1,0:T(8,128)(2,1)S(1)}, u32[]{:S(2)}, u32[]{:S(2)}) collective-permute-start(bf16[256,256]{1,0:T(8,128)(2,1)S(1)} %get-tuple-element.45), channel_id=1, source_target_pairs={{0,2},{2,0},{4,6},{6,4},{8,10},{10,8},{12,14},{14,12},{16,18},{18,... | collective-permute-start | bytes 393224 | tf_op jit(solution)/shard_map/ppermute | solution.py:368
  8.7 7.5 %collective-permute-start.3 = (bf16[256,256]{1,0:T(8,128)(2,1)S(1)}, bf16[256,256]{1,0:T(8,128)(2,1)S(1)}, u32[]{:S(2)}, u32[]{:S(2)}) collective-permute-start(bf16[256,256]{1,0:T(8,128)(2,1)S(1)} %collective-permute-done.2.rows_ref), channel_id=1, source_target_pairs={{0,1},{1,0},{2,3},{3,2},{4,5},{5,4},{6,7},{7,6},{8,9},{9,8},{10,11... | collective-permute-start | bytes 393224 | tf_op jit(solution)/shard_map/ppermute | solution.py:339
  8.7 10.3 %collective-permute-start.4 = (bf16[256,256]{1,0:T(8,128)(2,1)S(1)}, bf16[256,256]{1,0:T(8,128)(2,1)S(1)}, u32[]{:S(2)}, u32[]{:S(2)}) collective-permute-start(bf16[256,256]{1,0:T(8,128)(2,1)S(1)} %get-tuple-element.51), channel_id=1, source_target_pairs={{0,30},{2,4},{4,2},{6,8},{8,6},{10,12},{12,10},{14,16},{16,14},{18... | collective-permute-start | bytes 393224 | tf_op jit(solution)/shard_map/ppermute | solution.py:368
  19.0 1.6 %collective-permute-start.5 = (bf16[256,256]{1,0:T(8,128)(2,1)S(1)}, bf16[256,256]{1,0:T(8,128)(2,1)S(1)}, u32[]{:S(2)}, u32[]{:S(2)}) collective-permute-start(bf16[256,256]{1,0:T(8,128)(2,1)S(1)} %collective-permute-done.4.rows_ref), channel_id=1, source_target_pairs={{0,1},{1,0},{2,3},{3,2},{4,5},{5,4},{6,7},{7,6},{8,9},{9,8},{10,11... | collective-permute-start | bytes 393224 | tf_op jit(solution)/shard_map/ppermute | solution.py:339
  23.3 1.7 %collective-permute-start.6 = (bf16[512,256]{1,0:T(8,128)(2,1)S(1)}, bf16[512,256]{1,0:T(8,128)(2,1)S(1)}, u32[]{:S(2)}, u32[]{:S(2)}) collective-permute-start(bf16[512,256]{1,0:T(8,128)(2,1)S(1)} %get-tuple-element.56.first), channel_id=1, source_target_pairs={{0,1},{1,0},{2,3},{3,2},{4,5},{5,4},{6,7},{7,6},{8,9},{9,8},{10,11... | collective-permute-start | bytes 786440 | tf_op jit(solution)/shard_map/ppermute | solution.py:339
  26.0 5.0 %collective-permute-start.7 = (bf16[256,256]{1,0:T(8,128)(2,1)S(1)}, bf16[256,256]{1,0:T(8,128)(2,1)S(1)}, u32[]{:S(2)}, u32[]{:S(2)}) collective-permute-start(bf16[256,256]{1,0:T(8,128)(2,1)S(1)} %get-tuple-element.64), channel_id=1, source_target_pairs={{0,2},{2,0},{4,6},{6,4},{8,10},{10,8},{12,14},{14,12},{16,18},{18,... | collective-permute-start | bytes 393224 | tf_op jit(solution)/shard_map/ppermute | solution.py:368
  31.1 5.2 %collective-permute-start.8 = (bf16[256,256]{1,0:T(8,128)(2,1)S(1)}, bf16[256,256]{1,0:T(8,128)(2,1)S(1)}, u32[]{:S(2)}, u32[]{:S(2)}) collective-permute-start(bf16[256,256]{1,0:T(8,128)(2,1)S(1)} %collective-permute-done.7.rows_ref), channel_id=1, source_target_pairs={{0,1},{1,0},{2,3},{3,2},{4,5},{5,4},{6,7},{7,6},{8,9},{9,8},{10,11... | collective-permute-start | bytes 393224 | tf_op jit(solution)/shard_map/ppermute | solution.py:339
  31.1 8.6 %collective-permute-start.9 = (bf16[256,256]{1,0:T(8,128)(2,1)S(1)}, bf16[256,256]{1,0:T(8,128)(2,1)S(1)}, u32[]{:S(2)}, u32[]{:S(2)}) collective-permute-start(bf16[256,256]{1,0:T(8,128)(2,1)S(1)} %get-tuple-element.68), channel_id=1, source_target_pairs={{0,30},{2,4},{4,2},{6,8},{8,6},{10,12},{12,10},{14,16},{16,14},{18... | collective-permute-start | bytes 393224 | tf_op jit(solution)/shard_map/ppermute | solution.py:368
  39.6 1.3 %collective-permute-start.10 = (bf16[256,256]{1,0:T(8,128)(2,1)S(1)}, bf16[256,256]{1,0:T(8,128)(2,1)S(1)}, u32[]{:S(2)}, u32[]{:S(2)}) collective-permute-start(bf16[256,256]{1,0:T(8,128)(2,1)S(1)} %collective-permute-done.9.rows_ref), channel_id=1, source_target_pairs={{0,1},{1,0},{2,3},{3,2},{4,5},{5,4},{6,7},{7,6},{8,9},{9,8},{10,11... | collective-permute-start | bytes 393224 | tf_op jit(solution)/shard_map/ppermute | solution.py:339
  43.7 1.4 %collective-permute-start.11 = (bf16[256,256]{1,0:T(8,128)(2,1)S(1)}, bf16[256,256]{1,0:T(8,128)(2,1)S(1)}, u32[]{:S(2)}, u32[]{:S(2)}) collective-permute-start(bf16[256,256]{1,0:T(8,128)(2,1)S(1)} %get-tuple-element.72), channel_id=1, source_target_pairs={{0,1},{1,0},{2,3},{3,2},{4,5},{5,4},{6,7},{7,6},{8,9},{9,8},{10,11... | collective-permute-start | bytes 393224 | tf_op jit(solution)/shard_map/ppermute | solution.py:339

commit v10 on v9

--- a/solution.py
+++ b/solution.py
@@ -127,9 +127,10 @@
     return [one_hot_rows(lists[0, pl.ds(face, 1), :], TILE) for face in faces(stride)]
 
 
-def pick_kernel(stride, own_ref, peer_ref, list_own, list_peer, far, near):
+def pick_kernel(stride, own_ref, peer_ref, list_own, list_peer, far, near, hot):
     for n, (lists, nodes) in enumerate(((list_own, own_ref), (list_peer, peer_ref))):
-        for rows, out_rows in zip(face_hits(stride, lists), (far, near)):
+        for k, (rows, out_rows) in enumerate(zip(face_hits(stride, lists), (far, near))):
+            hot[2 * n + k] = rows
             out_rows[n * HALF : (n + 1) * HALF, :] = mm(rows, nodes[...]).astype(BF16)
 
 
@@ -138,6 +139,18 @@
     copies = [
         pltpu.make_async_copy(src if len(src.shape) == len(dst.shape) else src.at[0], dst, sems.at[k])
         for k, (src, dst) in enumerate(zip(hbm, vmem))
+    ]
+    for copy in copies:
+        copy.start()
+    for copy in copies:
+        copy.wait()
+
+
+def store_kernel(rows, vmem, hbm, sems):
+    blocks = [pl.ds(start, rows) for start in range(0, hbm.shape[0], rows)]
+    copies = [
+        pltpu.make_async_copy(vmem.at[at, :], hbm.at[at, :], sems.at[k])
+        for k, at in enumerate(blocks)
     ]
     for copy in copies:
         copy.start()
@@ -306,19 +319,16 @@
     return (nodes.astype(F32) + step).astype(BF16)
 
 
-def node_kernel(
-    stride, layer, own_ref, peer_ref, first, second, list_own, list_peer, w1, b1, w2, gain, out, far, near
-):
+def node_kernel(layer, own_ref, peer_ref, first, second, hot, w1, b1, w2, gain, out, far, near):
     core = lax.axis_index("edge")
     nodes = []
     for owner, ref in ((core, own_ref), (1 - core, peer_ref)):
         at = dyn(owner * TILE, TILE)
         nodes.append(updated(layer, ref[...], first[at, :], second[at, :], w1, b1, w2, gain))
         out[at, :] = nodes[-1]
-    for face, ref in zip(faces(stride), (far, near)):
-        for n, lists in enumerate((list_own, list_peer)):
-            rows = one_hot_rows(lists[0, pl.ds(face, 1), :], TILE)
-            ref[n * HALF : (n + 1) * HALF, :] = mm(rows, nodes[n]).astype(BF16)
+    for n in range(2):
+        for k, ref in enumerate((far, near)):
+            ref[n * HALF : (n + 1) * HALF, :] = mm(hot[2 * n + k], nodes[n]).astype(BF16)
 
 
 def last_kernel(layer, nodes_ref, first, second, w1, b1, w2, gain, out):
@@ -384,9 +394,9 @@
         scratch=[pltpu.SemaphoreType.DMA((len(first),))],
         stay=range(len(first)),
     )
-    far_rows, near_rows = call(
+    far_rows, near_rows, hot = call(
         functools.partial(pick_kernel, stride),
-        [rows_out, rows_out],
+        [rows_out, rows_out, shaped((4, HALF, TILE), BF16)],
         (node_lat, peer_nodes, send_rows, peer_lists),
     )
     for layer in range(LAYERS):
@@ -453,10 +463,10 @@
         weights = (node_w1, node_b1, node_w2, node_gain)
         if last:
             (edge_out,) = call(
-                functools.partial(load_kernel, 1),
+                functools.partial(store_kernel, ROWS),
                 [shaped((edges, width), BF16)],
                 (edge_rows,),
-                scratch=[pltpu.SemaphoreType.DMA((1,))],
+                scratch=[pltpu.SemaphoreType.DMA((edges // ROWS,))],
                 leave=(0,),
             )
             out = call(
@@ -466,9 +476,9 @@
             )
         else:
             all_nodes, far_rows, near_rows = call(
-                functools.partial(node_kernel, stride, layer),
+                functools.partial(node_kernel, layer),
                 [shaped((2 * nodes, width), BF16), rows_out, rows_out],
-                (node_lat, peer_nodes, partial[0], other, send_rows, peer_lists, *weights),
+                (node_lat, peer_nodes, partial[0], other, hot, *weights),
             )
     return out, edge_out
 

time: 46.5 us -> 46.5 us (level)
  no operation moved by 1% of the time
where the time goes in v10:
time: 46.5 us; the launch traced here: 46.3 us
  Pallas kernels  21.9 us (47%)
  starting transfers between devices  14.7 us (32%)
  waiting for transfers between devices  8.23 us (18%)
  between operations  1.44 us (3%)
    pallas_call x15, Pallas kernels, call(): pl.pallas_call(kernel, out_shape=outs, in_specs=[IN_SMEM if k in smem els...  21.9 us
    ppermute x4, starting transfers between devices, sent_by_core(): return lax.ppermute(value, ('dom', 'edge'), pairs)  13.3 us
    ppermute x4, waiting for transfers between devices, sent_by_core(): return lax.ppermute(value, ('dom', 'edge'), pairs)  6.56 us
    ppermute x8, waiting for transfers between devices, swapped(): return lax.ppermute(value, 'edge', [(0, 1), (1, 0)])  1.67 us
    ppermute x8, starting transfers between devices, swapped(): return lax.ppermute(value, 'edge', [(0, 1), (1, 0)])  1.43 us
  transfers between devices with their start and end apart: 12, of which 7 were waited for; matrix products, arithmetic and copies ran while one was open for 0% of the time, Pallas kernels for 30%

profile of v10, /device:TPU:0, one launch (start us, length us, event | category | flops | bytes accessed | tf_op | source)
XLA Modules:
  0.0 46.3 jit_solution(7161389824916535118)
XLA Ops:
  0.6 0.6 %collective-permute-start = (bf16[256,256]{1,0:T(8,128)(2,1)}, bf16[256,256]{1,0:T(8,128)(2,1)S(1)}, u32[]{:S(2)}, u32[]{:S(2)}) collective-permute-start(bf16[256,256]{1,0:T(8,128)(2,1)} %refs_0_.2), channel_id=1, source_target_pairs={{0,1},{1,0},{2,3},{3,2},{4,5},{5,4},{6,7},{7,6},{8,9},{9,8},{10,11... | collective-permute-start | bytes 393224 | tf_op jit(solution)/shard_map/ppermute | solution.py:349
  1.2 0.1 collective-permute-start.1
  1.3 1.2 %shard_map.149 = (bf16[256,256]{1,0:T(8,128)(2,1)S(1)}, s32[1,4,128]{2,1,0:T(4,128)S(1)}, s32[1,3072]{1,0:T(1,128)S(1)}, s32[1,3072]{1,0:T(1,128)S(1)}, f32[2,25...) custom-call(bf16[256,256]{1,0:T(8,128)(2,1)} %refs_0_.2, s32[1,4,128]{2,1,0:T(4,128)} %refs_1_.2, s32[1,3072]{1,0:T(1,128)} %bitcast.2, ...), custom_call_target="tpu_custom_call" | custom-call | bytes 946176 | tf_op jit(solution)/shard_map/pallas_call | solution.py:80
  2.5 0.1 collective-permute-done.1.list_peer
  2.6 0.0 collective-permute-done.peer_ref
  2.6 0.3 shard_map.151
  2.9 2.9 %collective-permute-start.2 = (bf16[256,256]{1,0:T(8,128)(2,1)S(1)}, bf16[256,256]{1,0:T(8,128)(2,1)S(1)}, u32[]{:S(2)}, u32[]{:S(2)}) collective-permute-start(bf16[256,256]{1,0:T(8,128)(2,1)S(1)} %get-tuple-element.46), channel_id=1, source_target_pairs={{0,2},{2,0},{4,6},{6,4},{8,10},{10,8},{12,14},{14,12},{16,18},{18,... | collective-permute-start | bytes 393224 | tf_op jit(solution)/shard_map/ppermute | solution.py:378
  5.8 2.6 %shard_map.150 = (f32[3072,256]{1,0:T(8,128)S(1)}, s16[2,3072,128]{2,1,0:T(8,128)(2,1)S(1)}, bf16[768,256]{1,0:T(8,128)(2,1)S(1)}, bf16[3072,256]{1,0:T(8,128)(2...) custom-call(s32[1,3072]{1,0:T(1,128)S(1)} %get-tuple-element.40.send, ...), custom_call_target="tpu_custom_call" | custom-call | flops 2013265920 | bytes 4096000 | tf_op jit(solution)/shard_map/pallas_call | solution.py:80
  8.4 0.3 collective-permute-done.2.rows_ref
  8.7 0.0 collective-permute-start.3
  8.7 6.0 %collective-permute-start.4 = (bf16[256,256]{1,0:T(8,128)(2,1)S(1)}, bf16[256,256]{1,0:T(8,128)(2,1)S(1)}, u32[]{:S(2)}, u32[]{:S(2)}) collective-permute-start(bf16[256,256]{1,0:T(8,128)(2,1)S(1)} %get-tuple-element.52), channel_id=1, source_target_pairs={{0,30},{2,4},{4,2},{6,8},{8,6},{10,12},{12,10},{14,16},{16,14},{18... | collective-permute-start | bytes 393224 | tf_op jit(solution)/shard_map/ppermute | solution.py:378
  14.7 1.5 %shard_map.152.pre_ref = f32[3072,256]{1,0:T(8,128)S(1)} custom-call(f32[3072,256]{1,0:T(8,128)S(1)} %get-tuple-element.48.pre_ref, s16[2,3072,128]{2,1,0:T(8,128)(2,1)S(1)} %get-tuple-element.49.cols, bf16[768,256]{1,0:T(8,128)(2,1)S(1)} %get-tuple-element.42.w1_ref, bf16[256,256]{1,0:T(8,128)(2,1)S(1)} %collective-permute-done.2.rows_ref, ...), custom_call_target="tpu_custom_call" | custom-call | flops 402653184 | bytes 6815744 | tf_op jit(solution)/shard_map/pallas_call | solution.py:80
  16.2 0.0 collective-permute-done.3.rows_ref
  16.2 0.9 %shard_map.153.pre_ref = f32[3072,256]{1,0:T(8,128)S(1)} custom-call(f32[3072,256]{1,0:T(8,128)S(1)} %shard_map.152.pre_ref, s16[2,3072,128]{2,1,0:T(8,128)(2,1)S(1)} %get-tuple-element.49.cols, bf16[768,256]{1,0:T(8,128)(2,1)S(1)} %get-tuple-element.42.w1_ref, bf16[256,256]{1,0:T(8,128)(2,1)S(1)} %collective-permute-done.3.rows_ref), custom_call_target="tpu_custom_call" | custom-call | flops 402653184 | bytes 5242880 | tf_op jit(solution)/shard_map/pallas_call | solution.py:80
  17.2 1.8 %collective-permute-done.4.rows_ref = bf16[256,256]{1,0:T(8,128)(2,1)S(1)} collective-permute-done((bf16[256,256]{1,0:T(8,128)(2,1)S(1)}, bf16[256,256]{1,0:T(8,128)(2,1)S(1)}, u32[]{:S(2)}, u32[]{:S(2)}) %collective-permute-start.4) | collective-permute-done | bytes 131104 | tf_op jit(solution)/shard_map/ppermute | solution.py:378
  19.0 0.0 collective-permute-start.5
  19.6 0.9 %shard_map.154.pre_ref = f32[3072,256]{1,0:T(8,128)S(1)} custom-call(f32[3072,256]{1,0:T(8,128)S(1)} %shard_map.153.pre_ref, s16[2,3072,128]{2,1,0:T(8,128)(2,1)S(1)} %get-tuple-element.49.cols, bf16[768,256]{1,0:T(8,128)(2,1)S(1)} %get-tuple-element.42.w1_ref, bf16[256,256]{1,0:T(8,128)(2,1)S(1)} %collective-permute-done.4.rows_ref), custom_call_target="tpu_custom_call" | custom-call | flops 402653184 | bytes 5242880 | tf_op jit(solution)/shard_map/pallas_call | solution.py:80
  20.6 0.0 collective-permute-done.5.peer
  20.6 2.6 %shard_map.155 = (bf16[3072,256]{1,0:T(8,128)(2,1)S(1)}, bf16[512,256]{1,0:T(8,128)(2,1)S(1)}) custom-call(s32[1,1]{1,0:T(1,128)S(6)} %copy.16.live_ref, f32[3072,256]{1,0:T(8,128)S(1)} %shard_map.154.pre_ref, s16[2,3072,128]{2,1,0:T(8,128)(2,1)S(1)} %get-tuple-element.49.cols, s32[1,3072]{1,0:T(1,128)S(1)} %get-tuple-element.41.recv_ref, ...), custom_call_target="tpu_custom_call" | custom-call | flops 2013265920 | bytes 7092228 | tf_op jit(solution)/shard_map/pallas_call | solution.py:80
  23.3 0.6 %collective-permute-start.6 = (bf16[512,256]{1,0:T(8,128)(2,1)S(1)}, bf16[512,256]{1,0:T(8,128)(2,1)S(1)}, u32[]{:S(2)}, u32[]{:S(2)}) collective-permute-start(bf16[512,256]{1,0:T(8,128)(2,1)S(1)} %get-tuple-element.57.first), channel_id=1, source_target_pairs={{0,1},{1,0},{2,3},{3,2},{4,5},{5,4},{6,7},{7,6},{8,9},{9,8},{10,11... | collective-permute-start | bytes 786440 | tf_op jit(solution)/shard_map/ppermute | solution.py:349
  23.8 1.2 %collective-permute-done.6.second = bf16[512,256]{1,0:T(8,128)(2,1)S(1)} collective-permute-done((bf16[512,256]{1,0:T(8,128)(2,1)S(1)}, bf16[512,256]{1,0:T(8,128)(2,1)S(1)}, u32[]{:S(2)}, u32[]{:S(2)}) %collective-permute-start.6) | collective-permute-done | bytes 262176 | tf_op jit(solution)/shard_map/ppermute | solution.py:349
  25.0 1.0 %shard_map.156 = (bf16[512,256]{1,0:T(8,128)(2,1)S(1)}, bf16[256,256]{1,0:T(8,128)(2,1)S(1)}, bf16[256,256]{1,0:T(8,128)(2,1)S(1)}) custom-call(bf16[256,256]{1,0:T(8,128)(2,1)S(1)} %get-tuple-element.39.own_ref, bf16[256,256]{1,0:T(8,128)(2,1)S(1)} %collective-permute-done.peer_ref, bf16[512,256]{1,0:T(8,128)(2,1)S(1)} %get-tuple-element.57.first, ...), custom_call_target="tpu_custom_call" | custom-call | bytes 1839104 | tf_op jit(solution)/shard_map/pallas_call | solution.py:80
  26.0 0.1 collective-permute-start.7
  26.1 2.9 %shard_map.157.pre_ref = f32[3072,256]{1,0:T(8,128)S(1)} custom-call(bf16[3072,256]{1,0:T(8,128)(2,1)S(1)} %get-tuple-element.64.edge_ref, s16[2,3072,128]{2,1,0:T(8,128)(2,1)S(1)} %get-tuple-element.49.cols, bf16[512,256]{1,0:T(8,128)(2,1)S(1)} %get-tuple-element.63.dom_ref.nodes_ref, bf16[768,256]{1,0:T(8,128)(2,1)S(1)} %get-tuple-element.65.w1_ref, ...), custom_call_target="tpu_custom_call" | custom-call | flops 2013265920 | bytes 3803136 | tf_op jit(solution)/shard_map/pallas_call | solution.py:80
  28.9 2.1 %collective-permute-done.7.rows_ref = bf16[256,256]{1,0:T(8,128)(2,1)S(1)} collective-permute-done((bf16[256,256]{1,0:T(8,128)(2,1)S(1)}, bf16[256,256]{1,0:T(8,128)(2,1)S(1)}, u32[]{:S(2)}, u32[]{:S(2)}) %collective-permute-start.7) | collective-permute-done | bytes 131104 | tf_op jit(solution)/shard_map/ppermute | solution.py:378
  31.0 0.0 collective-permute-start.8
  31.0 4.3 %collective-permute-start.9 = (bf16[256,256]{1,0:T(8,128)(2,1)S(1)}, bf16[256,256]{1,0:T(8,128)(2,1)S(1)}, u32[]{:S(2)}, u32[]{:S(2)}) collective-permute-start(bf16[256,256]{1,0:T(8,128)(2,1)S(1)} %get-tuple-element.70), channel_id=1, source_target_pairs={{0,30},{2,4},{4,2},{6,8},{8,6},{10,12},{12,10},{14,16},{16,14},{18... | collective-permute-start | bytes 393224 | tf_op jit(solution)/shard_map/ppermute | solution.py:378
  35.3 0.9 %shard_map.158.pre_ref = f32[3072,256]{1,0:T(8,128)S(1)} custom-call(f32[3072,256]{1,0:T(8,128)S(1)} %shard_map.157.pre_ref, s16[2,3072,128]{2,1,0:T(8,128)(2,1)S(1)} %get-tuple-element.49.cols, bf16[768,256]{1,0:T(8,128)(2,1)S(1)} %get-tuple-element.65.w1_ref, bf16[256,256]{1,0:T(8,128)(2,1)S(1)} %collective-permute-done.7.rows_ref), custom_call_target="tpu_custom_call" | custom-call | flops 402653184 | bytes 5242880 | tf_op jit(solution)/shard_map/pallas_call | solution.py:80
  36.3 0.0 collective-permute-done.8.rows_ref
  36.3 0.9 %shard_map.159.pre_ref = f32[3072,256]{1,0:T(8,128)S(1)} custom-call(f32[3072,256]{1,0:T(8,128)S(1)} %shard_map.158.pre_ref, s16[2,3072,128]{2,1,0:T(8,128)(2,1)S(1)} %get-tuple-element.49.cols, bf16[768,256]{1,0:T(8,128)(2,1)S(1)} %get-tuple-element.65.w1_ref, bf16[256,256]{1,0:T(8,128)(2,1)S(1)} %collective-permute-done.8.rows_ref), custom_call_target="tpu_custom_call" | custom-call | flops 402653184 | bytes 5242880 | tf_op jit(solution)/shard_map/pallas_call | solution.py:80
  37.3 2.4 %collective-permute-done.9.rows_ref = bf16[256,256]{1,0:T(8,128)(2,1)S(1)} collective-permute-done((bf16[256,256]{1,0:T(8,128)(2,1)S(1)}, bf16[256,256]{1,0:T(8,128)(2,1)S(1)}, u32[]{:S(2)}, u32[]{:S(2)}) %collective-permute-start.9) | collective-permute-done | bytes 131104 | tf_op jit(solution)/shard_map/ppermute | solution.py:378
  39.6 0.0 collective-permute-start.10
  39.6 0.9 %shard_map.160.pre_ref = f32[3072,256]{1,0:T(8,128)S(1)} custom-call(f32[3072,256]{1,0:T(8,128)S(1)} %shard_map.159.pre_ref, s16[2,3072,128]{2,1,0:T(8,128)(2,1)S(1)} %get-tuple-element.49.cols, bf16[768,256]{1,0:T(8,128)(2,1)S(1)} %get-tuple-element.65.w1_ref, bf16[256,256]{1,0:T(8,128)(2,1)S(1)} %collective-permute-done.9.rows_ref), custom_call_target="tpu_custom_call" | custom-call | flops 402653184 | bytes 5242880 | tf_op jit(solution)/shard_map/pallas_call | solution.py:80
  40.6 0.4 collective-permute-done.10.peer
  41.0 2.7 %shard_map.161 = (bf16[3072,256]{1,0:T(8,128)(2,1)S(1)}, bf16[256,256]{1,0:T(8,128)(2,1)S(1)}, bf16[256,256]{1,0:T(8,128)(2,1)S(1)}) custom-call(s32[1,1]{1,0:T(1,128)S(6)} %copy.16.live_ref, f32[3072,256]{1,0:T(8,128)S(1)} %shard_map.160.pre_ref, s16[2,3072,128]{2,1,0:T(8,128)(2,1)S(1)} %get-tuple-element.49.cols, ...), custom_call_target="tpu_custom_call" | custom-call | flops 2013265920 | bytes 7092228 | tf_op jit(solution)/shard_map/pallas_call | solution.py:80
  43.7 0.2 collective-permute-start.11
  43.9 1.2 %shard_map.163 = bf16[3072,256]{1,0:T(8,128)(2,1)} custom-call(bf16[3072,256]{1,0:T(8,128)(2,1)S(1)} %get-tuple-element.75.vmem), custom_call_target="tpu_custom_call" | custom-call | bytes 1572864 | tf_op jit(solution)/shard_map/pallas_call | solution.py:80
  45.1 0.0 collective-permute-done.11.second
  45.1 1.2 %shard_map.162 = bf16[256,256]{1,0:T(8,128)(2,1)} custom-call(bf16[512,256]{1,0:T(8,128)(2,1)S(1)} %get-tuple-element.63.dom_ref.nodes_ref, bf16[256,256]{1,0:T(8,128)(2,1)S(1)} %get-tuple-element.73.first, bf16[256,256]{1,0:T(8,128)(2,1)S(1)} %collective-permute-done.11.second, bf16[2,512,256]{2,1,0:T(8,128)(2,1)S(1)} %get-tuple-element.59.w1, ...), custom_call_target="tpu_custom_call" | custom-call | bytes 1314816 | tf_op jit(solution)/shard_map/pallas_call | solution.py:80
Async XLA Ops:
  0.6 1.9 %collective-permute-start = (bf16[256,256]{1,0:T(8,128)(2,1)}, bf16[256,256]{1,0:T(8,128)(2,1)S(1)}, u32[]{:S(2)}, u32[]{:S(2)}) collective-permute-start(bf16[256,256]{1,0:T(8,128)(2,1)} %refs_0_.2), channel_id=1, source_target_pairs={{0,1},{1,0},{2,3},{3,2},{4,5},{5,4},{6,7},{7,6},{8,9},{9,8},{10,11... | collective-permute-start | bytes 393224 | tf_op jit(solution)/shard_map/ppermute | solution.py:349
  1.2 1.4 %collective-permute-start.1 = (s32[1,4,128]{2,1,0:T(4,128)}, s32[1,4,128]{2,1,0:T(4,128)S(1)}, u32[]{:S(2)}, u32[]{:S(2)}) collective-permute-start(s32[1,4,128]{2,1,0:T(4,128)} %refs_1_.2), channel_id=1, source_target_pairs={{0,1},{1,0},{2,3},{3,2},{4,5},{5,4},{6,7},{7,6},{8,9},{9,8},{10,11... | collective-permute-start | bytes 6152 | tf_op jit(solution)/shard_map/ppermute | solution.py:349
  2.9 5.8 %collective-permute-start.2 = (bf16[256,256]{1,0:T(8,128)(2,1)S(1)}, bf16[256,256]{1,0:T(8,128)(2,1)S(1)}, u32[]{:S(2)}, u32[]{:S(2)}) collective-permute-start(bf16[256,256]{1,0:T(8,128)(2,1)S(1)} %get-tuple-element.46), channel_id=1, source_target_pairs={{0,2},{2,0},{4,6},{6,4},{8,10},{10,8},{12,14},{14,12},{16,18},{18,... | collective-permute-start | bytes 393224 | tf_op jit(solution)/shard_map/ppermute | solution.py:378
  8.7 7.5 %collective-permute-start.3 = (bf16[256,256]{1,0:T(8,128)(2,1)S(1)}, bf16[256,256]{1,0:T(8,128)(2,1)S(1)}, u32[]{:S(2)}, u32[]{:S(2)}) collective-permute-start(bf16[256,256]{1,0:T(8,128)(2,1)S(1)} %collective-permute-done.2.rows_ref), channel_id=1, source_target_pairs={{0,1},{1,0},{2,3},{3,2},{4,5},{5,4},{6,7},{7,6},{8,9},{9,8},{10,11... | collective-permute-start | bytes 393224 | tf_op jit(solution)/shard_map/ppermute | solution.py:349
  8.7 10.3 %collective-permute-start.4 = (bf16[256,256]{1,0:T(8,128)(2,1)S(1)}, bf16[256,256]{1,0:T(8,128)(2,1)S(1)}, u32[]{:S(2)}, u32[]{:S(2)}) collective-permute-start(bf16[256,256]{1,0:T(8,128)(2,1)S(1)} %get-tuple-element.52), channel_id=1, source_target_pairs={{0,30},{2,4},{4,2},{6,8},{8,6},{10,12},{12,10},{14,16},{16,14},{18... | collective-permute-start | bytes 393224 | tf_op jit(solution)/shard_map/ppermute | solution.py:378
  19.0 1.6 %collective-permute-start.5 = (bf16[256,256]{1,0:T(8,128)(2,1)S(1)}, bf16[256,256]{1,0:T(8,128)(2,1)S(1)}, u32[]{:S(2)}, u32[]{:S(2)}) collective-permute-start(bf16[256,256]{1,0:T(8,128)(2,1)S(1)} %collective-permute-done.4.rows_ref), channel_id=1, source_target_pairs={{0,1},{1,0},{2,3},{3,2},{4,5},{5,4},{6,7},{7,6},{8,9},{9,8},{10,11... | collective-permute-start | bytes 393224 | tf_op jit(solution)/shard_map/ppermute | solution.py:349
  23.3 1.7 %collective-permute-start.6 = (bf16[512,256]{1,0:T(8,128)(2,1)S(1)}, bf16[512,256]{1,0:T(8,128)(2,1)S(1)}, u32[]{:S(2)}, u32[]{:S(2)}) collective-permute-start(bf16[512,256]{1,0:T(8,128)(2,1)S(1)} %get-tuple-element.57.first), channel_id=1, source_target_pairs={{0,1},{1,0},{2,3},{3,2},{4,5},{5,4},{6,7},{7,6},{8,9},{9,8},{10,11... | collective-permute-start | bytes 786440 | tf_op jit(solution)/shard_map/ppermute | solution.py:349
  26.0 5.0 %collective-permute-start.7 = (bf16[256,256]{1,0:T(8,128)(2,1)S(1)}, bf16[256,256]{1,0:T(8,128)(2,1)S(1)}, u32[]{:S(2)}, u32[]{:S(2)}) collective-permute-start(bf16[256,256]{1,0:T(8,128)(2,1)S(1)} %get-tuple-element.66), channel_id=1, source_target_pairs={{0,2},{2,0},{4,6},{6,4},{8,10},{10,8},{12,14},{14,12},{16,18},{18,... | collective-permute-start | bytes 393224 | tf_op jit(solution)/shard_map/ppermute | solution.py:378
  31.0 5.3 %collective-permute-start.8 = (bf16[256,256]{1,0:T(8,128)(2,1)S(1)}, bf16[256,256]{1,0:T(8,128)(2,1)S(1)}, u32[]{:S(2)}, u32[]{:S(2)}) collective-permute-start(bf16[256,256]{1,0:T(8,128)(2,1)S(1)} %collective-permute-done.7.rows_ref), channel_id=1, source_target_pairs={{0,1},{1,0},{2,3},{3,2},{4,5},{5,4},{6,7},{7,6},{8,9},{9,8},{10,11... | collective-permute-start | bytes 393224 | tf_op jit(solution)/shard_map/ppermute | solution.py:349
  31.0 8.6 %collective-permute-start.9 = (bf16[256,256]{1,0:T(8,128)(2,1)S(1)}, bf16[256,256]{1,0:T(8,128)(2,1)S(1)}, u32[]{:S(2)}, u32[]{:S(2)}) collective-permute-start(bf16[256,256]{1,0:T(8,128)(2,1)S(1)} %get-tuple-element.70), channel_id=1, source_target_pairs={{0,30},{2,4},{4,2},{6,8},{8,6},{10,12},{12,10},{14,16},{16,14},{18... | collective-permute-start | bytes 393224 | tf_op jit(solution)/shard_map/ppermute | solution.py:378
  39.6 1.3 %collective-permute-start.10 = (bf16[256,256]{1,0:T(8,128)(2,1)S(1)}, bf16[256,256]{1,0:T(8,128)(2,1)S(1)}, u32[]{:S(2)}, u32[]{:S(2)}) collective-permute-start(bf16[256,256]{1,0:T(8,128)(2,1)S(1)} %collective-permute-done.9.rows_ref), channel_id=1, source_target_pairs={{0,1},{1,0},{2,3},{3,2},{4,5},{5,4},{6,7},{7,6},{8,9},{9,8},{10,11... | collective-permute-start | bytes 393224 | tf_op jit(solution)/shard_map/ppermute | solution.py:349
  43.7 1.4 %collective-permute-start.11 = (bf16[256,256]{1,0:T(8,128)(2,1)S(1)}, bf16[256,256]{1,0:T(8,128)(2,1)S(1)}, u32[]{:S(2)}, u32[]{:S(2)}) collective-permute-start(bf16[256,256]{1,0:T(8,128)(2,1)S(1)} %get-tuple-element.74), channel_id=1, source_target_pairs={{0,1},{1,0},{2,3},{3,2},{4,5},{5,4},{6,7},{7,6},{8,9},{9,8},{10,11... | collective-permute-start | bytes 393224 | tf_op jit(solution)/shard_map/ppermute | solution.py:349

commit v11 on v10

--- a/solution.py
+++ b/solution.py
@@ -75,7 +75,7 @@
     return jax.ShapeDtypeStruct(shape, dtype)
 
 
-def call(kernel, outs, args, scratch=(), smem=(), stay=(), leave=(), flops=0, limit=24):
+def call(kernel, outs, args, scratch=(), smem=(), stay=(), leave=(), aliases=None, flops=0, limit=24):
     nbytes = sum(a.size * a.dtype.itemsize for a in args)
     return pl.pallas_call(
         kernel,
@@ -87,6 +87,7 @@
         if isinstance(outs, list)
         else IN_VMEM,
         scratch_shapes=scratch,
+        input_output_aliases=aliases or {},
         compiler_params=pltpu.CompilerParams(vmem_limit_bytes=limit << 20),
         cost_estimate=pl.CostEstimate(flops=flops, transcendentals=0, bytes_accessed=nbytes),
     )(*args)
@@ -139,18 +140,6 @@
     copies = [
         pltpu.make_async_copy(src if len(src.shape) == len(dst.shape) else src.at[0], dst, sems.at[k])
         for k, (src, dst) in enumerate(zip(hbm, vmem))
-    ]
-    for copy in copies:
-        copy.start()
-    for copy in copies:
-        copy.wait()
-
-
-def store_kernel(rows, vmem, hbm, sems):
-    blocks = [pl.ds(start, rows) for start in range(0, hbm.shape[0], rows)]
-    copies = [
-        pltpu.make_async_copy(vmem.at[at, :], hbm.at[at, :], sems.at[k])
-        for k, at in enumerate(blocks)
     ]
     for copy in copies:
         copy.start()
@@ -259,14 +248,24 @@
     lax.fori_loop(0, 2, step, 0)
 
 
+def receiver_hits(recv_ref, at, node, nodes):
+    shape = (nodes, ROWS)
+    spot = (lax.broadcasted_iota(jnp.int32, shape, 0) + node).astype(I16)
+    here = jnp.broadcast_to(recv_ref[:, at].astype(I16), shape)
+    return jnp.where(here == spot, jnp.ones(shape, BF16), jnp.zeros(shape, BF16))
+
+
 def edge_kernel(
     layer, split, live_ref, pre_ref, cols, recv_ref, edge_ref, w1_ref, w2_ref, gain_ref, peer, out_ref, *refs
 ):
+    core = lax.axis_index("edge")
     if split:
-        keep_ref, give_ref, table, raw, msgs, sums = refs
+        give_ref, msgs, table, raw, sums = refs
+        node, nodes = (1 - core) * TILE, TILE
     else:
+        node, nodes = 0, 2 * TILE
         part_ref, table, raw, msgs, sums = refs
-    tile = 5 - lax.axis_index("edge")
+    tile = 5 - core
     table[...] = mm(peer[...], w1_ref[TILE : 2 * TILE, :]).astype(BF16)
     gain = gain_ref[layer : layer + 1, :]
     live = live_ref[0, 0]
@@ -289,11 +288,7 @@
         out_ref[at, :] = edge_ref[at, :] + message
 
     def segment(at, new):
-        shape = (2 * TILE, ROWS)
-        spot = lax.broadcasted_iota(jnp.int32, shape, 0).astype(I16)
-        here = jnp.broadcast_to(recv_ref[:, at].astype(I16), shape)
-        hot = jnp.where(here == spot, jnp.ones(shape, BF16), jnp.zeros(shape, BF16))
-        part = mm(hot, msgs[at, :])
+        part = mm(receiver_hits(recv_ref, at, node, nodes), msgs[at, :])
         sums[...] = part if new else sums[...] + part
 
     for k in range(count + 2):
@@ -303,12 +298,30 @@
             norm(pl.ds((k - 1) * ROWS, ROWS), (k - 1) * ROWS)
         if k < count:
             gather(pl.ds(k * ROWS, ROWS))
-    if split:
-        core = lax.axis_index("edge")
-        keep_ref[...] = sums[dyn(core * TILE, TILE), :].astype(BF16)
-        give_ref[...] = sums[dyn((1 - core) * TILE, TILE), :].astype(BF16)
-    else:
-        part_ref[...] = sums[...].astype(BF16)
+    (give_ref if split else part_ref)[...] = sums[...].astype(BF16)
+
+
+def output_copies(edge_ref, hbm, sems, half):
+    rows = edge_ref.shape[0] // 2
+    blocks = [pl.ds(half * rows + start, ROWS) for start in range(0, rows, ROWS)]
+    return [
+        pltpu.make_async_copy(edge_ref.at[at, :], hbm.at[at, :], sems.at[k])
+        for k, at in enumerate(blocks)
+    ]
+
+
+def keep_kernel(recv_ref, msgs, edge_ref, keep_ref, hbm, sems):
+    copies = output_copies(edge_ref, hbm, sems, 0)
+    for copy in copies:
+        copy.start()
+    node = lax.axis_index("edge") * TILE
+    total = 0.0
+    for start in range(0, edge_ref.shape[0], ROWS):
+        at = pl.ds(start, ROWS)
+        total = total + mm(receiver_hits(recv_ref, at, node, TILE), msgs[at, :])
+    keep_ref[...] = total.astype(BF16)
+    for copy in copies:
+        copy.wait()
 
 
 def updated(layer, nodes, first, second, w1_ref, b1_ref, w2_ref, gain_ref):
@@ -331,10 +344,15 @@
             ref[n * HALF : (n + 1) * HALF, :] = mm(hot[2 * n + k], nodes[n]).astype(BF16)
 
 
-def last_kernel(layer, nodes_ref, first, second, w1, b1, w2, gain, out):
+def last_kernel(layer, nodes_ref, first, second, edge_ref, _, w1, b1, w2, gain, out, hbm, sems):
+    copies = output_copies(edge_ref, hbm, sems, 1)
+    for copy in copies:
+        copy.start()
     core = lax.axis_index("edge")
     nodes = nodes_ref[dyn(core * TILE, TILE), :]
     out[...] = updated(layer, nodes, first[...], second[...], w1, b1, w2, gain)
+    for copy in copies:
+        copy.wait()
 
 
 def met(count, stride, odd):
@@ -443,36 +461,38 @@
         far_other = swapped(far)
         pre = add(4, False, pre, far)
         if last:
-            outs = [shaped((nodes, width), BF16)] * 2
+            outs = [shaped((nodes, width), BF16), shaped((edges, width), BF16)]
         else:
             outs = [shaped((2 * nodes, width), BF16)]
         edge_rows, *partial = call(
             functools.partial(edge_kernel, layer, last),
             [shaped((edges, width), BF16)] + outs,
             (live_edges, pre, cols, recv_at, edge_rows, w1, edge_w2, edge_gain, far_other),
-            scratch=[
-                table,
-                pltpu.VMEM((edges, width), F32),
-                messages,
-                pltpu.VMEM((2 * nodes, width), F32),
-            ],
+            scratch=[table, pltpu.VMEM((edges, width), F32)]
+            + ([pltpu.VMEM((nodes, width), F32)] if last else [messages, pltpu.VMEM((2 * nodes, width), F32)]),
             smem=(0,),
             flops=5 * pass_flops,
         )
-        other = swapped(partial[-1])
+        other = swapped(partial[0])
         weights = (node_w1, node_b1, node_w2, node_gain)
         if last:
-            (edge_out,) = call(
-                functools.partial(store_kernel, ROWS),
-                [shaped((edges, width), BF16)],
-                (edge_rows,),
-                scratch=[pltpu.SemaphoreType.DMA((edges // ROWS,))],
-                leave=(0,),
+            sems = [pltpu.SemaphoreType.DMA((edges // ROWS // 2,))]
+            edge_out = shaped((edges, width), BF16)
+            keep, half_out = call(
+                keep_kernel,
+                [shaped((nodes, width), BF16), edge_out],
+                (recv_at, partial[1], edge_rows),
+                scratch=sems,
+                leave=(1,),
             )
-            out = call(
+            out, edge_out = call(
                 functools.partial(last_kernel, layer),
-                shaped((nodes, width), BF16),
-                (all_nodes, partial[0], other, *weights),
+                [shaped((nodes, width), BF16), edge_out],
+                (all_nodes, keep, other, edge_rows, *in_hbm([half_out]), *weights),
+                scratch=sems,
+                stay=(4,),
+                leave=(1,),
+                aliases={4: 1},
             )
         else:
             all_nodes, far_rows, near_rows = call(

time: 46.5 us -> 46.9 us (level)
  transfers between devices with their start and end apart: 12 -> 12, of which waited for: 7 -> 8; matrix products, arithmetic and copies ran while one was open for 0% -> 0% of each run, Pallas kernels for 30% -> 30%
where the time goes in v11:
time: 46.9 us; the launch traced here: 46.7 us
  Pallas kernels  21.9 us (47%)
  starting transfers between devices  14.7 us (31%)
  waiting for transfers between devices  8.53 us (18%)
  between operations  1.59 us (3%)
    pallas_call x15, Pallas kernels, call(): pl.pallas_call(kernel, out_shape=outs, in_specs=[IN_SMEM if k in smem els...  21.9 us
    ppermute x4, starting transfers between devices, sent_by_core(): return lax.ppermute(value, ('dom', 'edge'), pairs)  13.3 us
    ppermute x4, waiting for transfers between devices, sent_by_core(): return lax.ppermute(value, ('dom', 'edge'), pairs)  6.57 us
    ppermute x8, waiting for transfers between devices, swapped(): return lax.ppermute(value, 'edge', [(0, 1), (1, 0)])  1.95 us
    ppermute x8, starting transfers between devices, swapped(): return lax.ppermute(value, 'edge', [(0, 1), (1, 0)])  1.44 us
  transfers between devices with their start and end apart: 12, of which 8 were waited for; matrix products, arithmetic and copies ran while one was open for 0% of the time, Pallas kernels for 30%

profile of v11, /device:TPU:0, one launch (start us, length us, event | category | flops | bytes accessed | tf_op | source)
XLA Modules:
  0.0 46.7 jit_solution(6603954843300954675)
XLA Ops:
  0.6 0.6 %collective-permute-start = (bf16[256,256]{1,0:T(8,128)(2,1)}, bf16[256,256]{1,0:T(8,128)(2,1)S(1)}, u32[]{:S(2)}, u32[]{:S(2)}) collective-permute-start(bf16[256,256]{1,0:T(8,128)(2,1)} %refs_0_.2), channel_id=1, source_target_pairs={{0,1},{1,0},{2,3},{3,2},{4,5},{5,4},{6,7},{7,6},{8,9},{9,8},{10,11... | collective-permute-start | bytes 393224 | tf_op jit(solution)/shard_map/ppermute | solution.py:367
  1.2 0.1 collective-permute-start.1
  1.3 1.2 %shard_map.149 = (bf16[256,256]{1,0:T(8,128)(2,1)S(1)}, s32[1,4,128]{2,1,0:T(4,128)S(1)}, s32[1,3072]{1,0:T(1,128)S(1)}, s32[1,3072]{1,0:T(1,128)S(1)}, f32[2,25...) custom-call(bf16[256,256]{1,0:T(8,128)(2,1)} %refs_0_.2, s32[1,4,128]{2,1,0:T(4,128)} %refs_1_.2, s32[1,3072]{1,0:T(1,128)} %bitcast.2, ...), custom_call_target="tpu_custom_call" | custom-call | bytes 946176 | tf_op jit(solution)/shard_map/pallas_call | solution.py:80
  2.5 0.1 collective-permute-done.1.list_peer
  2.6 0.0 collective-permute-done.peer_ref
  2.6 0.3 shard_map.151
  2.9 2.9 %collective-permute-start.2 = (bf16[256,256]{1,0:T(8,128)(2,1)S(1)}, bf16[256,256]{1,0:T(8,128)(2,1)S(1)}, u32[]{:S(2)}, u32[]{:S(2)}) collective-permute-start(bf16[256,256]{1,0:T(8,128)(2,1)S(1)} %get-tuple-element.48), channel_id=1, source_target_pairs={{0,2},{2,0},{4,6},{6,4},{8,10},{10,8},{12,14},{14,12},{16,18},{18,... | collective-permute-start | bytes 393224 | tf_op jit(solution)/shard_map/ppermute | solution.py:396
  5.8 2.6 %shard_map.150 = (f32[3072,256]{1,0:T(8,128)S(1)}, s16[2,3072,128]{2,1,0:T(8,128)(2,1)S(1)}, bf16[768,256]{1,0:T(8,128)(2,1)S(1)}, bf16[3072,256]{1,0:T(8,128)(2...) custom-call(s32[1,3072]{1,0:T(1,128)S(1)} %get-tuple-element.42.send, ...), custom_call_target="tpu_custom_call" | custom-call | flops 2013265920 | bytes 4096000 | tf_op jit(solution)/shard_map/pallas_call | solution.py:80
  8.4 0.3 collective-permute-done.2.rows_ref
  8.7 0.0 collective-permute-start.3
  8.7 6.0 %collective-permute-start.4 = (bf16[256,256]{1,0:T(8,128)(2,1)S(1)}, bf16[256,256]{1,0:T(8,128)(2,1)S(1)}, u32[]{:S(2)}, u32[]{:S(2)}) collective-permute-start(bf16[256,256]{1,0:T(8,128)(2,1)S(1)} %get-tuple-element.54), channel_id=1, source_target_pairs={{0,30},{2,4},{4,2},{6,8},{8,6},{10,12},{12,10},{14,16},{16,14},{18... | collective-permute-start | bytes 393224 | tf_op jit(solution)/shard_map/ppermute | solution.py:396
  14.7 1.5 %shard_map.152.pre_ref = f32[3072,256]{1,0:T(8,128)S(1)} custom-call(f32[3072,256]{1,0:T(8,128)S(1)} %get-tuple-element.50.pre_ref, s16[2,3072,128]{2,1,0:T(8,128)(2,1)S(1)} %get-tuple-element.51.cols, bf16[768,256]{1,0:T(8,128)(2,1)S(1)} %get-tuple-element.44.w1_ref, bf16[256,256]{1,0:T(8,128)(2,1)S(1)} %collective-permute-done.2.rows_ref, ...), custom_call_target="tpu_custom_call" | custom-call | flops 402653184 | bytes 6815744 | tf_op jit(solution)/shard_map/pallas_call | solution.py:80
  16.2 0.0 collective-permute-done.3.rows_ref
  16.2 0.9 %shard_map.153.pre_ref = f32[3072,256]{1,0:T(8,128)S(1)} custom-call(f32[3072,256]{1,0:T(8,128)S(1)} %shard_map.152.pre_ref, s16[2,3072,128]{2,1,0:T(8,128)(2,1)S(1)} %get-tuple-element.51.cols, bf16[768,256]{1,0:T(8,128)(2,1)S(1)} %get-tuple-element.44.w1_ref, bf16[256,256]{1,0:T(8,128)(2,1)S(1)} %collective-permute-done.3.rows_ref), custom_call_target="tpu_custom_call" | custom-call | flops 402653184 | bytes 5242880 | tf_op jit(solution)/shard_map/pallas_call | solution.py:80
  17.2 1.8 %collective-permute-done.4.rows_ref = bf16[256,256]{1,0:T(8,128)(2,1)S(1)} collective-permute-done((bf16[256,256]{1,0:T(8,128)(2,1)S(1)}, bf16[256,256]{1,0:T(8,128)(2,1)S(1)}, u32[]{:S(2)}, u32[]{:S(2)}) %collective-permute-start.4) | collective-permute-done | bytes 131104 | tf_op jit(solution)/shard_map/ppermute | solution.py:396
  19.0 0.0 collective-permute-start.5
  19.6 0.9 %shard_map.154.pre_ref = f32[3072,256]{1,0:T(8,128)S(1)} custom-call(f32[3072,256]{1,0:T(8,128)S(1)} %shard_map.153.pre_ref, s16[2,3072,128]{2,1,0:T(8,128)(2,1)S(1)} %get-tuple-element.51.cols, bf16[768,256]{1,0:T(8,128)(2,1)S(1)} %get-tuple-element.44.w1_ref, bf16[256,256]{1,0:T(8,128)(2,1)S(1)} %collective-permute-done.4.rows_ref), custom_call_target="tpu_custom_call" | custom-call | flops 402653184 | bytes 5242880 | tf_op jit(solution)/shard_map/pallas_call | solution.py:80
  20.6 0.0 collective-permute-done.5.peer
  20.6 2.6 %shard_map.155 = (bf16[3072,256]{1,0:T(8,128)(2,1)S(1)}, bf16[512,256]{1,0:T(8,128)(2,1)S(1)}) custom-call(s32[1,1]{1,0:T(1,128)S(6)} %copy.18.live_ref, f32[3072,256]{1,0:T(8,128)S(1)} %shard_map.154.pre_ref, s16[2,3072,128]{2,1,0:T(8,128)(2,1)S(1)} %get-tuple-element.51.cols, s32[1,3072]{1,0:T(1,128)S(1)} %get-tuple-element.43.recv_ref, ...), custom_call_target="tpu_custom_call" | custom-call | flops 2013265920 | bytes 7092228 | tf_op jit(solution)/shard_map/pallas_call | solution.py:80
  23.2 0.6 %collective-permute-start.6 = (bf16[512,256]{1,0:T(8,128)(2,1)S(1)}, bf16[512,256]{1,0:T(8,128)(2,1)S(1)}, u32[]{:S(2)}, u32[]{:S(2)}) collective-permute-start(bf16[512,256]{1,0:T(8,128)(2,1)S(1)} %get-tuple-element.59.first), channel_id=1, source_target_pairs={{0,1},{1,0},{2,3},{3,2},{4,5},{5,4},{6,7},{7,6},{8,9},{9,8},{10,11... | collective-permute-start | bytes 786440 | tf_op jit(solution)/shard_map/ppermute | solution.py:367
  23.8 1.2 %collective-permute-done.6.second = bf16[512,256]{1,0:T(8,128)(2,1)S(1)} collective-permute-done((bf16[512,256]{1,0:T(8,128)(2,1)S(1)}, bf16[512,256]{1,0:T(8,128)(2,1)S(1)}, u32[]{:S(2)}, u32[]{:S(2)}) %collective-permute-start.6) | collective-permute-done | bytes 262176 | tf_op jit(solution)/shard_map/ppermute | solution.py:367
  25.0 1.0 %shard_map.156 = (bf16[512,256]{1,0:T(8,128)(2,1)S(1)}, bf16[256,256]{1,0:T(8,128)(2,1)S(1)}, bf16[256,256]{1,0:T(8,128)(2,1)S(1)}) custom-call(bf16[256,256]{1,0:T(8,128)(2,1)S(1)} %get-tuple-element.41.own_ref, bf16[256,256]{1,0:T(8,128)(2,1)S(1)} %collective-permute-done.peer_ref, bf16[512,256]{1,0:T(8,128)(2,1)S(1)} %get-tuple-element.59.first, ...), custom_call_target="tpu_custom_call" | custom-call | bytes 1839104 | tf_op jit(solution)/shard_map/pallas_call | solution.py:80
  26.0 0.1 collective-permute-start.7
  26.1 2.9 %shard_map.157.pre_ref = f32[3072,256]{1,0:T(8,128)S(1)} custom-call(bf16[3072,256]{1,0:T(8,128)(2,1)S(1)} %get-tuple-element.66.edge_ref, s16[2,3072,128]{2,1,0:T(8,128)(2,1)S(1)} %get-tuple-element.51.cols, bf16[512,256]{1,0:T(8,128)(2,1)S(1)} %get-tuple-element.65.dom_ref.nodes_ref, bf16[768,256]{1,0:T(8,128)(2,1)S(1)} %get-tuple-element.67.w1_ref, ...), custom_call_target="tpu_custom_call" | custom-call | flops 2013265920 | bytes 3803136 | tf_op jit(solution)/shard_map/pallas_call | solution.py:80
  28.9 2.1 %collective-permute-done.7.rows_ref = bf16[256,256]{1,0:T(8,128)(2,1)S(1)} collective-permute-done((bf16[256,256]{1,0:T(8,128)(2,1)S(1)}, bf16[256,256]{1,0:T(8,128)(2,1)S(1)}, u32[]{:S(2)}, u32[]{:S(2)}) %collective-permute-start.7) | collective-permute-done | bytes 131104 | tf_op jit(solution)/shard_map/ppermute | solution.py:396
  31.0 0.0 collective-permute-start.8
  31.0 4.3 %collective-permute-start.9 = (bf16[256,256]{1,0:T(8,128)(2,1)S(1)}, bf16[256,256]{1,0:T(8,128)(2,1)S(1)}, u32[]{:S(2)}, u32[]{:S(2)}) collective-permute-start(bf16[256,256]{1,0:T(8,128)(2,1)S(1)} %get-tuple-element.72), channel_id=1, source_target_pairs={{0,30},{2,4},{4,2},{6,8},{8,6},{10,12},{12,10},{14,16},{16,14},{18... | collective-permute-start | bytes 393224 | tf_op jit(solution)/shard_map/ppermute | solution.py:396
  35.3 0.9 %shard_map.158.pre_ref = f32[3072,256]{1,0:T(8,128)S(1)} custom-call(f32[3072,256]{1,0:T(8,128)S(1)} %shard_map.157.pre_ref, s16[2,3072,128]{2,1,0:T(8,128)(2,1)S(1)} %get-tuple-element.51.cols, bf16[768,256]{1,0:T(8,128)(2,1)S(1)} %get-tuple-element.67.w1_ref, bf16[256,256]{1,0:T(8,128)(2,1)S(1)} %collective-permute-done.7.rows_ref), custom_call_target="tpu_custom_call" | custom-call | flops 402653184 | bytes 5242880 | tf_op jit(solution)/shard_map/pallas_call | solution.py:80
  36.3 0.0 collective-permute-done.8.rows_ref
  36.3 0.9 %shard_map.159.pre_ref = f32[3072,256]{1,0:T(8,128)S(1)} custom-call(f32[3072,256]{1,0:T(8,128)S(1)} %shard_map.158.pre_ref, s16[2,3072,128]{2,1,0:T(8,128)(2,1)S(1)} %get-tuple-element.51.cols, bf16[768,256]{1,0:T(8,128)(2,1)S(1)} %get-tuple-element.67.w1_ref, bf16[256,256]{1,0:T(8,128)(2,1)S(1)} %collective-permute-done.8.rows_ref), custom_call_target="tpu_custom_call" | custom-call | flops 402653184 | bytes 5242880 | tf_op jit(solution)/shard_map/pallas_call | solution.py:80
  37.2 2.4 %collective-permute-done.9.rows_ref = bf16[256,256]{1,0:T(8,128)(2,1)S(1)} collective-permute-done((bf16[256,256]{1,0:T(8,128)(2,1)S(1)}, bf16[256,256]{1,0:T(8,128)(2,1)S(1)}, u32[]{:S(2)}, u32[]{:S(2)}) %collective-permute-start.9) | collective-permute-done | bytes 131104 | tf_op jit(solution)/shard_map/ppermute | solution.py:396
  39.6 0.0 collective-permute-start.10
  39.6 0.9 %shard_map.160.pre_ref = f32[3072,256]{1,0:T(8,128)S(1)} custom-call(f32[3072,256]{1,0:T(8,128)S(1)} %shard_map.159.pre_ref, s16[2,3072,128]{2,1,0:T(8,128)(2,1)S(1)} %get-tuple-element.51.cols, bf16[768,256]{1,0:T(8,128)(2,1)S(1)} %get-tuple-element.67.w1_ref, bf16[256,256]{1,0:T(8,128)(2,1)S(1)} %collective-permute-done.9.rows_ref), custom_call_target="tpu_custom_call" | custom-call | flops 402653184 | bytes 5242880 | tf_op jit(solution)/shard_map/pallas_call | solution.py:80
  40.5 0.4 collective-permute-done.10.peer
  40.9 2.6 %shard_map.161 = (bf16[3072,256]{1,0:T(8,128)(2,1)S(1)}, bf16[256,256]{1,0:T(8,128)(2,1)S(1)}, bf16[3072,256]{1,0:T(8,128)(2,1)S(1)}) custom-call(s32[1,1]{1,0:T(1,128)S(6)} %copy.18.live_ref, f32[3072,256]{1,0:T(8,128)S(1)} %shard_map.160.pre_ref, s16[2,3072,128]{2,1,0:T(8,128)(2,1)S(1)} %get-tuple-element.51.cols, ...), custom_call_target="tpu_custom_call" | custom-call | flops 2013265920 | bytes 7092228 | tf_op jit(solution)/shard_map/pallas_call | solution.py:80
  43.5 0.2 collective-permute-start.11
  43.8 0.9 %shard_map.162 = (bf16[256,256]{1,0:T(8,128)(2,1)S(1)}, bf16[3072,256]{1,0:T(8,128)(2,1)}) custom-call(s32[1,3072]{1,0:T(1,128)S(1)} %get-tuple-element.43.recv_ref, bf16[3072,256]{1,0:T(8,128)(2,1)S(1)} %get-tuple-element.75.msgs, bf16[3072,256]{1,0:T(8,128)(2,1)S(1)} %get-tuple-element.76.edge_ref), custom_call_target="tpu_custom_call" | custom-call | bytes 3158016 | tf_op jit(solution)/shard_map/pallas_call | solution.py:80
  44.7 0.3 collective-permute-done.11.second
  45.0 1.6 %shard_map.163 = (bf16[256,256]{1,0:T(8,128)(2,1)}, bf16[3072,256]{1,0:T(8,128)(2,1)}) custom-call(bf16[512,256]{1,0:T(8,128)(2,1)S(1)} %get-tuple-element.65.dom_ref.nodes_ref, bf16[256,256]{1,0:T(8,128)(2,1)S(1)} %get-tuple-element.77.first, bf16[256,256]{1,0:T(8,128)(2,1)S(1)} %collective-permute-done.11.second, ...), custom_call_target="tpu_custom_call", output_to_operand_aliasing={{1}: (4, {})} | custom-call | bytes 4460544 | tf_op jit(solution)/shard_map/pallas_call | solution.py:80
Async XLA Ops:
  0.6 1.9 %collective-permute-start = (bf16[256,256]{1,0:T(8,128)(2,1)}, bf16[256,256]{1,0:T(8,128)(2,1)S(1)}, u32[]{:S(2)}, u32[]{:S(2)}) collective-permute-start(bf16[256,256]{1,0:T(8,128)(2,1)} %refs_0_.2), channel_id=1, source_target_pairs={{0,1},{1,0},{2,3},{3,2},{4,5},{5,4},{6,7},{7,6},{8,9},{9,8},{10,11... | collective-permute-start | bytes 393224 | tf_op jit(solution)/shard_map/ppermute | solution.py:367
  1.2 1.4 %collective-permute-start.1 = (s32[1,4,128]{2,1,0:T(4,128)}, s32[1,4,128]{2,1,0:T(4,128)S(1)}, u32[]{:S(2)}, u32[]{:S(2)}) collective-permute-start(s32[1,4,128]{2,1,0:T(4,128)} %refs_1_.2), channel_id=1, source_target_pairs={{0,1},{1,0},{2,3},{3,2},{4,5},{5,4},{6,7},{7,6},{8,9},{9,8},{10,11... | collective-permute-start | bytes 6152 | tf_op jit(solution)/shard_map/ppermute | solution.py:367
  2.9 5.8 %collective-permute-start.2 = (bf16[256,256]{1,0:T(8,128)(2,1)S(1)}, bf16[256,256]{1,0:T(8,128)(2,1)S(1)}, u32[]{:S(2)}, u32[]{:S(2)}) collective-permute-start(bf16[256,256]{1,0:T(8,128)(2,1)S(1)} %get-tuple-element.48), channel_id=1, source_target_pairs={{0,2},{2,0},{4,6},{6,4},{8,10},{10,8},{12,14},{14,12},{16,18},{18,... | collective-permute-start | bytes 393224 | tf_op jit(solution)/shard_map/ppermute | solution.py:396
  8.7 7.5 %collective-permute-start.3 = (bf16[256,256]{1,0:T(8,128)(2,1)S(1)}, bf16[256,256]{1,0:T(8,128)(2,1)S(1)}, u32[]{:S(2)}, u32[]{:S(2)}) collective-permute-start(bf16[256,256]{1,0:T(8,128)(2,1)S(1)} %collective-permute-done.2.rows_ref), channel_id=1, source_target_pairs={{0,1},{1,0},{2,3},{3,2},{4,5},{5,4},{6,7},{7,6},{8,9},{9,8},{10,11... | collective-permute-start | bytes 393224 | tf_op jit(solution)/shard_map/ppermute | solution.py:367
  8.7 10.3 %collective-permute-start.4 = (bf16[256,256]{1,0:T(8,128)(2,1)S(1)}, bf16[256,256]{1,0:T(8,128)(2,1)S(1)}, u32[]{:S(2)}, u32[]{:S(2)}) collective-permute-start(bf16[256,256]{1,0:T(8,128)(2,1)S(1)} %get-tuple-element.54), channel_id=1, source_target_pairs={{0,30},{2,4},{4,2},{6,8},{8,6},{10,12},{12,10},{14,16},{16,14},{18... | collective-permute-start | bytes 393224 | tf_op jit(solution)/shard_map/ppermute | solution.py:396
  19.0 1.6 %collective-permute-start.5 = (bf16[256,256]{1,0:T(8,128)(2,1)S(1)}, bf16[256,256]{1,0:T(8,128)(2,1)S(1)}, u32[]{:S(2)}, u32[]{:S(2)}) collective-permute-start(bf16[256,256]{1,0:T(8,128)(2,1)S(1)} %collective-permute-done.4.rows_ref), channel_id=1, source_target_pairs={{0,1},{1,0},{2,3},{3,2},{4,5},{5,4},{6,7},{7,6},{8,9},{9,8},{10,11... | collective-permute-start | bytes 393224 | tf_op jit(solution)/shard_map/ppermute | solution.py:367
  23.2 1.7 %collective-permute-start.6 = (bf16[512,256]{1,0:T(8,128)(2,1)S(1)}, bf16[512,256]{1,0:T(8,128)(2,1)S(1)}, u32[]{:S(2)}, u32[]{:S(2)}) collective-permute-start(bf16[512,256]{1,0:T(8,128)(2,1)S(1)} %get-tuple-element.59.first), channel_id=1, source_target_pairs={{0,1},{1,0},{2,3},{3,2},{4,5},{5,4},{6,7},{7,6},{8,9},{9,8},{10,11... | collective-permute-start | bytes 786440 | tf_op jit(solution)/shard_map/ppermute | solution.py:367
  26.0 5.0 %collective-permute-start.7 = (bf16[256,256]{1,0:T(8,128)(2,1)S(1)}, bf16[256,256]{1,0:T(8,128)(2,1)S(1)}, u32[]{:S(2)}, u32[]{:S(2)}) collective-permute-start(bf16[256,256]{1,0:T(8,128)(2,1)S(1)} %get-tuple-element.68), channel_id=1, source_target_pairs={{0,2},{2,0},{4,6},{6,4},{8,10},{10,8},{12,14},{14,12},{16,18},{18,... | collective-permute-start | bytes 393224 | tf_op jit(solution)/shard_map/ppermute | solution.py:396
  31.0 5.2 %collective-permute-start.8 = (bf16[256,256]{1,0:T(8,128)(2,1)S(1)}, bf16[256,256]{1,0:T(8,128)(2,1)S(1)}, u32[]{:S(2)}, u32[]{:S(2)}) collective-permute-start(bf16[256,256]{1,0:T(8,128)(2,1)S(1)} %collective-permute-done.7.rows_ref), channel_id=1, source_target_pairs={{0,1},{1,0},{2,3},{3,2},{4,5},{5,4},{6,7},{7,6},{8,9},{9,8},{10,11... | collective-permute-start | bytes 393224 | tf_op jit(solution)/shard_map/ppermute | solution.py:367
  31.0 8.6 %collective-permute-start.9 = (bf16[256,256]{1,0:T(8,128)(2,1)S(1)}, bf16[256,256]{1,0:T(8,128)(2,1)S(1)}, u32[]{:S(2)}, u32[]{:S(2)}) collective-permute-start(bf16[256,256]{1,0:T(8,128)(2,1)S(1)} %get-tuple-element.72), channel_id=1, source_target_pairs={{0,30},{2,4},{4,2},{6,8},{8,6},{10,12},{12,10},{14,16},{16,14},{18... | collective-permute-start | bytes 393224 | tf_op jit(solution)/shard_map/ppermute | solution.py:396
  39.6 1.3 %collective-permute-start.10 = (bf16[256,256]{1,0:T(8,128)(2,1)S(1)}, bf16[256,256]{1,0:T(8,128)(2,1)S(1)}, u32[]{:S(2)}, u32[]{:S(2)}) collective-permute-start(bf16[256,256]{1,0:T(8,128)(2,1)S(1)} %collective-permute-done.9.rows_ref), channel_id=1, source_target_pairs={{0,1},{1,0},{2,3},{3,2},{4,5},{5,4},{6,7},{7,6},{8,9},{9,8},{10,11... | collective-permute-start | bytes 393224 | tf_op jit(solution)/shard_map/ppermute | solution.py:367
  43.5 1.4 %collective-permute-start.11 = (bf16[256,256]{1,0:T(8,128)(2,1)S(1)}, bf16[256,256]{1,0:T(8,128)(2,1)S(1)}, u32[]{:S(2)}, u32[]{:S(2)}) collective-permute-start(bf16[256,256]{1,0:T(8,128)(2,1)S(1)} %get-tuple-element.78), channel_id=1, source_target_pairs={{0,1},{1,0},{2,3},{3,2},{4,5},{5,4},{6,7},{7,6},{8,9},{9,8},{10,11... | collective-permute-start | bytes 393224 | tf_op jit(solution)/shard_map/ppermute | solution.py:367

commit v12 on v11

--- a/solution.py
+++ b/solution.py
@@ -75,7 +75,7 @@
     return jax.ShapeDtypeStruct(shape, dtype)
 
 
-def call(kernel, outs, args, scratch=(), smem=(), stay=(), leave=(), aliases=None, flops=0, limit=24):
+def call(kernel, outs, args, scratch=(), smem=(), stay=(), leave=(), flops=0, limit=24):
     nbytes = sum(a.size * a.dtype.itemsize for a in args)
     return pl.pallas_call(
         kernel,
@@ -87,7 +87,6 @@
         if isinstance(outs, list)
         else IN_VMEM,
         scratch_shapes=scratch,
-        input_output_aliases=aliases or {},
         compiler_params=pltpu.CompilerParams(vmem_limit_bytes=limit << 20),
         cost_estimate=pl.CostEstimate(flops=flops, transcendentals=0, bytes_accessed=nbytes),
     )(*args)
@@ -301,23 +300,17 @@
     (give_ref if split else part_ref)[...] = sums[...].astype(BF16)
 
 
-def output_copies(edge_ref, hbm, sems, half):
-    rows = edge_ref.shape[0] // 2
-    blocks = [pl.ds(half * rows + start, ROWS) for start in range(0, rows, ROWS)]
-    return [
+def keep_kernel(recv_ref, msgs, edge_ref, keep_ref, hbm, sems):
+    blocks = [pl.ds(start, ROWS) for start in range(0, edge_ref.shape[0], ROWS)]
+    copies = [
         pltpu.make_async_copy(edge_ref.at[at, :], hbm.at[at, :], sems.at[k])
         for k, at in enumerate(blocks)
     ]
-
-
-def keep_kernel(recv_ref, msgs, edge_ref, keep_ref, hbm, sems):
-    copies = output_copies(edge_ref, hbm, sems, 0)
     for copy in copies:
         copy.start()
     node = lax.axis_index("edge") * TILE
     total = 0.0
-    for start in range(0, edge_ref.shape[0], ROWS):
-        at = pl.ds(start, ROWS)
+    for at in blocks:
         total = total + mm(receiver_hits(recv_ref, at, node, TILE), msgs[at, :])
     keep_ref[...] = total.astype(BF16)
     for copy in copies:
@@ -344,15 +337,10 @@
             ref[n * HALF : (n + 1) * HALF, :] = mm(hot[2 * n + k], nodes[n]).astype(BF16)
 
 
-def last_kernel(layer, nodes_ref, first, second, edge_ref, _, w1, b1, w2, gain, out, hbm, sems):
-    copies = output_copies(edge_ref, hbm, sems, 1)
-    for copy in copies:
-        copy.start()
+def last_kernel(layer, nodes_ref, first, second, w1, b1, w2, gain, out):
     core = lax.axis_index("edge")
     nodes = nodes_ref[dyn(core * TILE, TILE), :]
     out[...] = updated(layer, nodes, first[...], second[...], w1, b1, w2, gain)
-    for copy in copies:
-        copy.wait()
 
 
 def met(count, stride, odd):
@@ -476,23 +464,17 @@
         other = swapped(partial[0])
         weights = (node_w1, node_b1, node_w2, node_gain)
         if last:
-            sems = [pltpu.SemaphoreType.DMA((edges // ROWS // 2,))]
-            edge_out = shaped((edges, width), BF16)
-            keep, half_out = call(
+            keep, edge_out = call(
                 keep_kernel,
-                [shaped((nodes, width), BF16), edge_out],
+                [shaped((nodes, width), BF16), shaped((edges, width), BF16)],
                 (recv_at, partial[1], edge_rows),
-                scratch=sems,
+                scratch=[pltpu.SemaphoreType.DMA((edges // ROWS,))],
                 leave=(1,),
             )
-            out, edge_out = call(
+            out = call(
                 functools.partial(last_kernel, layer),
-                [shaped((nodes, width), BF16), edge_out],
-                (all_nodes, keep, other, edge_rows, *in_hbm([half_out]), *weights),
-                scratch=sems,
-                stay=(4,),
-                leave=(1,),
-                aliases={4: 1},
+                shaped((nodes, width), BF16),
+                (all_nodes, keep, other, *weights),
             )
         else:
             all_nodes, far_rows, near_rows = call(

time: 46.9 us -> 46.4 us (0.989)
  transfers between devices with their start and end apart: 12 -> 12, of which waited for: 8 -> 7; matrix products, arithmetic and copies ran while one was open for 0% -> 0% of each run, Pallas kernels for 30% -> 30%
where the time goes in v12:
time: 46.4 us; the launch traced here: 46.2 us
  Pallas kernels  21.8 us (47%)
  starting transfers between devices  14.7 us (32%)
  waiting for transfers between devices  8.25 us (18%)
  between operations  1.43 us (3%)
    pallas_call x15, Pallas kernels, call(): pl.pallas_call(kernel, out_shape=outs, in_specs=[IN_SMEM if k in smem els...  21.8 us
    ppermute x4, starting transfers between devices, sent_by_core(): return lax.ppermute(value, ('dom', 'edge'), pairs)  13.3 us
    ppermute x4, waiting for transfers between devices, sent_by_core(): return lax.ppermute(value, ('dom', 'edge'), pairs)  6.58 us
    ppermute x8, waiting for transfers between devices, swapped(): return lax.ppermute(value, 'edge', [(0, 1), (1, 0)])  1.68 us
    ppermute x8, starting transfers between devices, swapped(): return lax.ppermute(value, 'edge', [(0, 1), (1, 0)])  1.44 us
  transfers between devices with their start and end apart: 12, of which 7 were waited for; matrix products, arithmetic and copies ran while one was open for 0% of the time, Pallas kernels for 30%

profile of v12, /device:TPU:0, one launch (start us, length us, event | category | flops | bytes accessed | tf_op | source)
XLA Modules:
  0.0 46.2 jit_solution(695584101951667687)
XLA Ops:
  0.6 0.6 %collective-permute-start = (bf16[256,256]{1,0:T(8,128)(2,1)}, bf16[256,256]{1,0:T(8,128)(2,1)S(1)}, u32[]{:S(2)}, u32[]{:S(2)}) collective-permute-start(bf16[256,256]{1,0:T(8,128)(2,1)} %refs_0_.2), channel_id=1, source_target_pairs={{0,1},{1,0},{2,3},{3,2},{4,5},{5,4},{6,7},{7,6},{8,9},{9,8},{10,11... | collective-permute-start | bytes 393224 | tf_op jit(solution)/shard_map/ppermute | solution.py:355
  1.2 0.1 collective-permute-start.1
  1.3 1.2 %shard_map.149 = (bf16[256,256]{1,0:T(8,128)(2,1)S(1)}, s32[1,4,128]{2,1,0:T(4,128)S(1)}, s32[1,3072]{1,0:T(1,128)S(1)}, s32[1,3072]{1,0:T(1,128)S(1)}, f32[2,25...) custom-call(bf16[256,256]{1,0:T(8,128)(2,1)} %refs_0_.2, s32[1,4,128]{2,1,0:T(4,128)} %refs_1_.2, s32[1,3072]{1,0:T(1,128)} %bitcast.2, ...), custom_call_target="tpu_custom_call" | custom-call | bytes 946176 | tf_op jit(solution)/shard_map/pallas_call | solution.py:80
  2.5 0.1 collective-permute-done.1.list_peer
  2.6 0.0 collective-permute-done.peer_ref
  2.6 0.3 shard_map.151
  2.9 2.9 %collective-permute-start.2 = (bf16[256,256]{1,0:T(8,128)(2,1)S(1)}, bf16[256,256]{1,0:T(8,128)(2,1)S(1)}, u32[]{:S(2)}, u32[]{:S(2)}) collective-permute-start(bf16[256,256]{1,0:T(8,128)(2,1)S(1)} %get-tuple-element.48), channel_id=1, source_target_pairs={{0,2},{2,0},{4,6},{6,4},{8,10},{10,8},{12,14},{14,12},{16,18},{18,... | collective-permute-start | bytes 393224 | tf_op jit(solution)/shard_map/ppermute | solution.py:384
  5.8 2.6 %shard_map.150 = (f32[3072,256]{1,0:T(8,128)S(1)}, s16[2,3072,128]{2,1,0:T(8,128)(2,1)S(1)}, bf16[768,256]{1,0:T(8,128)(2,1)S(1)}, bf16[3072,256]{1,0:T(8,128)(2...) custom-call(s32[1,3072]{1,0:T(1,128)S(1)} %get-tuple-element.42.send, ...), custom_call_target="tpu_custom_call" | custom-call | flops 2013265920 | bytes 4096000 | tf_op jit(solution)/shard_map/pallas_call | solution.py:80
  8.4 0.3 collective-permute-done.2.rows_ref
  8.7 0.0 collective-permute-start.3
  8.7 6.0 %collective-permute-start.4 = (bf16[256,256]{1,0:T(8,128)(2,1)S(1)}, bf16[256,256]{1,0:T(8,128)(2,1)S(1)}, u32[]{:S(2)}, u32[]{:S(2)}) collective-permute-start(bf16[256,256]{1,0:T(8,128)(2,1)S(1)} %get-tuple-element.54), channel_id=1, source_target_pairs={{0,30},{2,4},{4,2},{6,8},{8,6},{10,12},{12,10},{14,16},{16,14},{18... | collective-permute-start | bytes 393224 | tf_op jit(solution)/shard_map/ppermute | solution.py:384
  14.7 1.5 %shard_map.152.pre_ref = f32[3072,256]{1,0:T(8,128)S(1)} custom-call(f32[3072,256]{1,0:T(8,128)S(1)} %get-tuple-element.50.pre_ref, s16[2,3072,128]{2,1,0:T(8,128)(2,1)S(1)} %get-tuple-element.51.cols, bf16[768,256]{1,0:T(8,128)(2,1)S(1)} %get-tuple-element.44.w1_ref, bf16[256,256]{1,0:T(8,128)(2,1)S(1)} %collective-permute-done.2.rows_ref, ...), custom_call_target="tpu_custom_call" | custom-call | flops 402653184 | bytes 6815744 | tf_op jit(solution)/shard_map/pallas_call | solution.py:80
  16.2 0.0 collective-permute-done.3.rows_ref
  16.2 0.9 %shard_map.153.pre_ref = f32[3072,256]{1,0:T(8,128)S(1)} custom-call(f32[3072,256]{1,0:T(8,128)S(1)} %shard_map.152.pre_ref, s16[2,3072,128]{2,1,0:T(8,128)(2,1)S(1)} %get-tuple-element.51.cols, bf16[768,256]{1,0:T(8,128)(2,1)S(1)} %get-tuple-element.44.w1_ref, bf16[256,256]{1,0:T(8,128)(2,1)S(1)} %collective-permute-done.3.rows_ref), custom_call_target="tpu_custom_call" | custom-call | flops 402653184 | bytes 5242880 | tf_op jit(solution)/shard_map/pallas_call | solution.py:80
  17.2 1.8 %collective-permute-done.4.rows_ref = bf16[256,256]{1,0:T(8,128)(2,1)S(1)} collective-permute-done((bf16[256,256]{1,0:T(8,128)(2,1)S(1)}, bf16[256,256]{1,0:T(8,128)(2,1)S(1)}, u32[]{:S(2)}, u32[]{:S(2)}) %collective-permute-start.4) | collective-permute-done | bytes 131104 | tf_op jit(solution)/shard_map/ppermute | solution.py:384
  19.0 0.0 collective-permute-start.5
  19.6 0.9 %shard_map.154.pre_ref = f32[3072,256]{1,0:T(8,128)S(1)} custom-call(f32[3072,256]{1,0:T(8,128)S(1)} %shard_map.153.pre_ref, s16[2,3072,128]{2,1,0:T(8,128)(2,1)S(1)} %get-tuple-element.51.cols, bf16[768,256]{1,0:T(8,128)(2,1)S(1)} %get-tuple-element.44.w1_ref, bf16[256,256]{1,0:T(8,128)(2,1)S(1)} %collective-permute-done.4.rows_ref), custom_call_target="tpu_custom_call" | custom-call | flops 402653184 | bytes 5242880 | tf_op jit(solution)/shard_map/pallas_call | solution.py:80
  20.6 0.0 collective-permute-done.5.peer
  20.6 2.6 %shard_map.155 = (bf16[3072,256]{1,0:T(8,128)(2,1)S(1)}, bf16[512,256]{1,0:T(8,128)(2,1)S(1)}) custom-call(s32[1,1]{1,0:T(1,128)S(6)} %copy.16.live_ref, f32[3072,256]{1,0:T(8,128)S(1)} %shard_map.154.pre_ref, s16[2,3072,128]{2,1,0:T(8,128)(2,1)S(1)} %get-tuple-element.51.cols, s32[1,3072]{1,0:T(1,128)S(1)} %get-tuple-element.43.recv_ref, ...), custom_call_target="tpu_custom_call" | custom-call | flops 2013265920 | bytes 7092228 | tf_op jit(solution)/shard_map/pallas_call | solution.py:80
  23.2 0.6 %collective-permute-start.6 = (bf16[512,256]{1,0:T(8,128)(2,1)S(1)}, bf16[512,256]{1,0:T(8,128)(2,1)S(1)}, u32[]{:S(2)}, u32[]{:S(2)}) collective-permute-start(bf16[512,256]{1,0:T(8,128)(2,1)S(1)} %get-tuple-element.59.first), channel_id=1, source_target_pairs={{0,1},{1,0},{2,3},{3,2},{4,5},{5,4},{6,7},{7,6},{8,9},{9,8},{10,11... | collective-permute-start | bytes 786440 | tf_op jit(solution)/shard_map/ppermute | solution.py:355
  23.8 1.2 %collective-permute-done.6.second = bf16[512,256]{1,0:T(8,128)(2,1)S(1)} collective-permute-done((bf16[512,256]{1,0:T(8,128)(2,1)S(1)}, bf16[512,256]{1,0:T(8,128)(2,1)S(1)}, u32[]{:S(2)}, u32[]{:S(2)}) %collective-permute-start.6) | collective-permute-done | bytes 262176 | tf_op jit(solution)/shard_map/ppermute | solution.py:355
  25.0 1.0 %shard_map.156 = (bf16[512,256]{1,0:T(8,128)(2,1)S(1)}, bf16[256,256]{1,0:T(8,128)(2,1)S(1)}, bf16[256,256]{1,0:T(8,128)(2,1)S(1)}) custom-call(bf16[256,256]{1,0:T(8,128)(2,1)S(1)} %get-tuple-element.41.own_ref, bf16[256,256]{1,0:T(8,128)(2,1)S(1)} %collective-permute-done.peer_ref, bf16[512,256]{1,0:T(8,128)(2,1)S(1)} %get-tuple-element.59.first, ...), custom_call_target="tpu_custom_call" | custom-call | bytes 1839104 | tf_op jit(solution)/shard_map/pallas_call | solution.py:80
  26.0 0.1 collective-permute-start.7
  26.1 2.8 %shard_map.157.pre_ref = f32[3072,256]{1,0:T(8,128)S(1)} custom-call(bf16[3072,256]{1,0:T(8,128)(2,1)S(1)} %get-tuple-element.66.edge_ref, s16[2,3072,128]{2,1,0:T(8,128)(2,1)S(1)} %get-tuple-element.51.cols, bf16[512,256]{1,0:T(8,128)(2,1)S(1)} %get-tuple-element.65.dom_ref.nodes_ref, bf16[768,256]{1,0:T(8,128)(2,1)S(1)} %get-tuple-element.67.w1_ref, ...), custom_call_target="tpu_custom_call" | custom-call | flops 2013265920 | bytes 3803136 | tf_op jit(solution)/shard_map/pallas_call | solution.py:80
  28.9 2.1 %collective-permute-done.7.rows_ref = bf16[256,256]{1,0:T(8,128)(2,1)S(1)} collective-permute-done((bf16[256,256]{1,0:T(8,128)(2,1)S(1)}, bf16[256,256]{1,0:T(8,128)(2,1)S(1)}, u32[]{:S(2)}, u32[]{:S(2)}) %collective-permute-start.7) | collective-permute-done | bytes 131104 | tf_op jit(solution)/shard_map/ppermute | solution.py:384
  31.0 0.0 collective-permute-start.8
  31.0 4.3 %collective-permute-start.9 = (bf16[256,256]{1,0:T(8,128)(2,1)S(1)}, bf16[256,256]{1,0:T(8,128)(2,1)S(1)}, u32[]{:S(2)}, u32[]{:S(2)}) collective-permute-start(bf16[256,256]{1,0:T(8,128)(2,1)S(1)} %get-tuple-element.72), channel_id=1, source_target_pairs={{0,30},{2,4},{4,2},{6,8},{8,6},{10,12},{12,10},{14,16},{16,14},{18... | collective-permute-start | bytes 393224 | tf_op jit(solution)/shard_map/ppermute | solution.py:384
  35.3 0.9 %shard_map.158.pre_ref = f32[3072,256]{1,0:T(8,128)S(1)} custom-call(f32[3072,256]{1,0:T(8,128)S(1)} %shard_map.157.pre_ref, s16[2,3072,128]{2,1,0:T(8,128)(2,1)S(1)} %get-tuple-element.51.cols, bf16[768,256]{1,0:T(8,128)(2,1)S(1)} %get-tuple-element.67.w1_ref, bf16[256,256]{1,0:T(8,128)(2,1)S(1)} %collective-permute-done.7.rows_ref), custom_call_target="tpu_custom_call" | custom-call | flops 402653184 | bytes 5242880 | tf_op jit(solution)/shard_map/pallas_call | solution.py:80
  36.3 0.0 collective-permute-done.8.rows_ref
  36.3 0.9 %shard_map.159.pre_ref = f32[3072,256]{1,0:T(8,128)S(1)} custom-call(f32[3072,256]{1,0:T(8,128)S(1)} %shard_map.158.pre_ref, s16[2,3072,128]{2,1,0:T(8,128)(2,1)S(1)} %get-tuple-element.51.cols, bf16[768,256]{1,0:T(8,128)(2,1)S(1)} %get-tuple-element.67.w1_ref, bf16[256,256]{1,0:T(8,128)(2,1)S(1)} %collective-permute-done.8.rows_ref), custom_call_target="tpu_custom_call" | custom-call | flops 402653184 | bytes 5242880 | tf_op jit(solution)/shard_map/pallas_call | solution.py:80
  37.2 2.4 %collective-permute-done.9.rows_ref = bf16[256,256]{1,0:T(8,128)(2,1)S(1)} collective-permute-done((bf16[256,256]{1,0:T(8,128)(2,1)S(1)}, bf16[256,256]{1,0:T(8,128)(2,1)S(1)}, u32[]{:S(2)}, u32[]{:S(2)}) %collective-permute-start.9) | collective-permute-done | bytes 131104 | tf_op jit(solution)/shard_map/ppermute | solution.py:384
  39.6 0.0 collective-permute-start.10
  39.6 0.9 %shard_map.160.pre_ref = f32[3072,256]{1,0:T(8,128)S(1)} custom-call(f32[3072,256]{1,0:T(8,128)S(1)} %shard_map.159.pre_ref, s16[2,3072,128]{2,1,0:T(8,128)(2,1)S(1)} %get-tuple-element.51.cols, bf16[768,256]{1,0:T(8,128)(2,1)S(1)} %get-tuple-element.67.w1_ref, bf16[256,256]{1,0:T(8,128)(2,1)S(1)} %collective-permute-done.9.rows_ref), custom_call_target="tpu_custom_call" | custom-call | flops 402653184 | bytes 5242880 | tf_op jit(solution)/shard_map/pallas_call | solution.py:80
  40.6 0.4 collective-permute-done.10.peer
  41.0 2.6 %shard_map.161 = (bf16[3072,256]{1,0:T(8,128)(2,1)S(1)}, bf16[256,256]{1,0:T(8,128)(2,1)S(1)}, bf16[3072,256]{1,0:T(8,128)(2,1)S(1)}) custom-call(s32[1,1]{1,0:T(1,128)S(6)} %copy.16.live_ref, f32[3072,256]{1,0:T(8,128)S(1)} %shard_map.160.pre_ref, s16[2,3072,128]{2,1,0:T(8,128)(2,1)S(1)} %get-tuple-element.51.cols, ...), custom_call_target="tpu_custom_call" | custom-call | flops 2013265920 | bytes 7092228 | tf_op jit(solution)/shard_map/pallas_call | solution.py:80
  43.6 0.2 collective-permute-start.11
  43.8 1.2 %shard_map.162 = (bf16[256,256]{1,0:T(8,128)(2,1)S(1)}, bf16[3072,256]{1,0:T(8,128)(2,1)}) custom-call(s32[1,3072]{1,0:T(1,128)S(1)} %get-tuple-element.43.recv_ref, bf16[3072,256]{1,0:T(8,128)(2,1)S(1)} %get-tuple-element.75.msgs, bf16[3072,256]{1,0:T(8,128)(2,1)S(1)} %get-tuple-element.76.edge_ref), custom_call_target="tpu_custom_call" | custom-call | bytes 3158016 | tf_op jit(solution)/shard_map/pallas_call | solution.py:80
  45.0 0.0 collective-permute-done.11.second
  45.0 1.2 %shard_map.163 = bf16[256,256]{1,0:T(8,128)(2,1)} custom-call(bf16[512,256]{1,0:T(8,128)(2,1)S(1)} %get-tuple-element.65.dom_ref.nodes_ref, bf16[256,256]{1,0:T(8,128)(2,1)S(1)} %get-tuple-element.77.first, bf16[256,256]{1,0:T(8,128)(2,1)S(1)} %collective-permute-done.11.second, bf16[2,512,256]{2,1,0:T(8,128)(2,1)S(1)} %get-tuple-element.61.w1, ...), custom_call_target="tpu_custom_call" | custom-call | bytes 1314816 | tf_op jit(solution)/shard_map/pallas_call | solution.py:80
Async XLA Ops:
  0.6 1.9 %collective-permute-start = (bf16[256,256]{1,0:T(8,128)(2,1)}, bf16[256,256]{1,0:T(8,128)(2,1)S(1)}, u32[]{:S(2)}, u32[]{:S(2)}) collective-permute-start(bf16[256,256]{1,0:T(8,128)(2,1)} %refs_0_.2), channel_id=1, source_target_pairs={{0,1},{1,0},{2,3},{3,2},{4,5},{5,4},{6,7},{7,6},{8,9},{9,8},{10,11... | collective-permute-start | bytes 393224 | tf_op jit(solution)/shard_map/ppermute | solution.py:355
  1.2 1.4 %collective-permute-start.1 = (s32[1,4,128]{2,1,0:T(4,128)}, s32[1,4,128]{2,1,0:T(4,128)S(1)}, u32[]{:S(2)}, u32[]{:S(2)}) collective-permute-start(s32[1,4,128]{2,1,0:T(4,128)} %refs_1_.2), channel_id=1, source_target_pairs={{0,1},{1,0},{2,3},{3,2},{4,5},{5,4},{6,7},{7,6},{8,9},{9,8},{10,11... | collective-permute-start | bytes 6152 | tf_op jit(solution)/shard_map/ppermute | solution.py:355
  2.9 5.8 %collective-permute-start.2 = (bf16[256,256]{1,0:T(8,128)(2,1)S(1)}, bf16[256,256]{1,0:T(8,128)(2,1)S(1)}, u32[]{:S(2)}, u32[]{:S(2)}) collective-permute-start(bf16[256,256]{1,0:T(8,128)(2,1)S(1)} %get-tuple-element.48), channel_id=1, source_target_pairs={{0,2},{2,0},{4,6},{6,4},{8,10},{10,8},{12,14},{14,12},{16,18},{18,... | collective-permute-start | bytes 393224 | tf_op jit(solution)/shard_map/ppermute | solution.py:384
  8.7 7.5 %collective-permute-start.3 = (bf16[256,256]{1,0:T(8,128)(2,1)S(1)}, bf16[256,256]{1,0:T(8,128)(2,1)S(1)}, u32[]{:S(2)}, u32[]{:S(2)}) collective-permute-start(bf16[256,256]{1,0:T(8,128)(2,1)S(1)} %collective-permute-done.2.rows_ref), channel_id=1, source_target_pairs={{0,1},{1,0},{2,3},{3,2},{4,5},{5,4},{6,7},{7,6},{8,9},{9,8},{10,11... | collective-permute-start | bytes 393224 | tf_op jit(solution)/shard_map/ppermute | solution.py:355
  8.7 10.3 %collective-permute-start.4 = (bf16[256,256]{1,0:T(8,128)(2,1)S(1)}, bf16[256,256]{1,0:T(8,128)(2,1)S(1)}, u32[]{:S(2)}, u32[]{:S(2)}) collective-permute-start(bf16[256,256]{1,0:T(8,128)(2,1)S(1)} %get-tuple-element.54), channel_id=1, source_target_pairs={{0,30},{2,4},{4,2},{6,8},{8,6},{10,12},{12,10},{14,16},{16,14},{18... | collective-permute-start | bytes 393224 | tf_op jit(solution)/shard_map/ppermute | solution.py:384
  19.0 1.6 %collective-permute-start.5 = (bf16[256,256]{1,0:T(8,128)(2,1)S(1)}, bf16[256,256]{1,0:T(8,128)(2,1)S(1)}, u32[]{:S(2)}, u32[]{:S(2)}) collective-permute-start(bf16[256,256]{1,0:T(8,128)(2,1)S(1)} %collective-permute-done.4.rows_ref), channel_id=1, source_target_pairs={{0,1},{1,0},{2,3},{3,2},{4,5},{5,4},{6,7},{7,6},{8,9},{9,8},{10,11... | collective-permute-start | bytes 393224 | tf_op jit(solution)/shard_map/ppermute | solution.py:355
  23.2 1.7 %collective-permute-start.6 = (bf16[512,256]{1,0:T(8,128)(2,1)S(1)}, bf16[512,256]{1,0:T(8,128)(2,1)S(1)}, u32[]{:S(2)}, u32[]{:S(2)}) collective-permute-start(bf16[512,256]{1,0:T(8,128)(2,1)S(1)} %get-tuple-element.59.first), channel_id=1, source_target_pairs={{0,1},{1,0},{2,3},{3,2},{4,5},{5,4},{6,7},{7,6},{8,9},{9,8},{10,11... | collective-permute-start | bytes 786440 | tf_op jit(solution)/shard_map/ppermute | solution.py:355
  26.0 5.0 %collective-permute-start.7 = (bf16[256,256]{1,0:T(8,128)(2,1)S(1)}, bf16[256,256]{1,0:T(8,128)(2,1)S(1)}, u32[]{:S(2)}, u32[]{:S(2)}) collective-permute-start(bf16[256,256]{1,0:T(8,128)(2,1)S(1)} %get-tuple-element.68), channel_id=1, source_target_pairs={{0,2},{2,0},{4,6},{6,4},{8,10},{10,8},{12,14},{14,12},{16,18},{18,... | collective-permute-start | bytes 393224 | tf_op jit(solution)/shard_map/ppermute | solution.py:384
  31.0 5.2 %collective-permute-start.8 = (bf16[256,256]{1,0:T(8,128)(2,1)S(1)}, bf16[256,256]{1,0:T(8,128)(2,1)S(1)}, u32[]{:S(2)}, u32[]{:S(2)}) collective-permute-start(bf16[256,256]{1,0:T(8,128)(2,1)S(1)} %collective-permute-done.7.rows_ref), channel_id=1, source_target_pairs={{0,1},{1,0},{2,3},{3,2},{4,5},{5,4},{6,7},{7,6},{8,9},{9,8},{10,11... | collective-permute-start | bytes 393224 | tf_op jit(solution)/shard_map/ppermute | solution.py:355
  31.0 8.6 %collective-permute-start.9 = (bf16[256,256]{1,0:T(8,128)(2,1)S(1)}, bf16[256,256]{1,0:T(8,128)(2,1)S(1)}, u32[]{:S(2)}, u32[]{:S(2)}) collective-permute-start(bf16[256,256]{1,0:T(8,128)(2,1)S(1)} %get-tuple-element.72), channel_id=1, source_target_pairs={{0,30},{2,4},{4,2},{6,8},{8,6},{10,12},{12,10},{14,16},{16,14},{18... | collective-permute-start | bytes 393224 | tf_op jit(solution)/shard_map/ppermute | solution.py:384
  39.6 1.3 %collective-permute-start.10 = (bf16[256,256]{1,0:T(8,128)(2,1)S(1)}, bf16[256,256]{1,0:T(8,128)(2,1)S(1)}, u32[]{:S(2)}, u32[]{:S(2)}) collective-permute-start(bf16[256,256]{1,0:T(8,128)(2,1)S(1)} %collective-permute-done.9.rows_ref), channel_id=1, source_target_pairs={{0,1},{1,0},{2,3},{3,2},{4,5},{5,4},{6,7},{7,6},{8,9},{9,8},{10,11... | collective-permute-start | bytes 393224 | tf_op jit(solution)/shard_map/ppermute | solution.py:355
  43.6 1.4 %collective-permute-start.11 = (bf16[256,256]{1,0:T(8,128)(2,1)S(1)}, bf16[256,256]{1,0:T(8,128)(2,1)S(1)}, u32[]{:S(2)}, u32[]{:S(2)}) collective-permute-start(bf16[256,256]{1,0:T(8,128)(2,1)S(1)} %get-tuple-element.78), channel_id=1, source_target_pairs={{0,1},{1,0},{2,3},{3,2},{4,5},{5,4},{6,7},{7,6},{8,9},{9,8},{10,11... | collective-permute-start | bytes 393224 | tf_op jit(solution)/shard_map/ppermute | solution.py:355

commit v13 on v12

--- a/solution.py
+++ b/solution.py
@@ -199,12 +199,12 @@
     copies = [pltpu.make_async_copy(*pair, sems.at[k]) for k, pair in enumerate(ends)]
     for copy in copies:
         copy.start()
-    blocks = [pl.ds(start, LOCAL_ROWS) for start in range(0, pre_ref.shape[0], LOCAL_ROWS)]
+    blocks = [pl.ds(start, ROWS) for start in range(0, pre_ref.shape[0], ROWS)]
     core = lax.axis_index("edge")
     parts = ((core * TILE, TILE, own_ref), ((1 - core) * TILE, TILE, peer_ref))
 
     def make(k):
-        for start in range(k * LOCAL_ROWS, (k + 1) * LOCAL_ROWS, HALF):
+        for start in range(k * ROWS, (k + 1) * ROWS, HALF):
             columns(stride, send_ref, recv_ref, cols, pl.ds(start, HALF))
 
     make(0)
@@ -234,17 +234,10 @@
     core = lax.axis_index("edge")
     tile = first + (1 - core if peer else core)
     table = mm(rows_ref[...], w1_ref[TILE : 2 * TILE, :]).astype(BF16)
-    half = pre_ref.shape[0] // 2
-
-    def step(k, carry):
-        at = dyn(k * half, half)
-        acc = pre_ref[at, :] + mm(hits(cols[0, at, :], tile, 1), table)
-        if len(refs) == 2:
-            acc = acc + mm(refs[0][at, :], w1_ref[0:TILE, :])
-        out_ref[at, :] = acc
-        return carry
-
-    lax.fori_loop(0, 2, step, 0)
+    acc = pre_ref[...] + mm(hits(cols[0], tile, 1), table)
+    if len(refs) == 2:
+        acc = acc + mm(refs[0][...], w1_ref[0:TILE, :])
+    out_ref[...] = acc
 
 
 def receiver_hits(recv_ref, at, node, nodes):

time: 46.4 us -> 46.2 us (level)
  Pallas kernels: 21.8 us -> 20.7 us
  waiting for transfers between devices: 8.25 us -> 9.26 us
    pallas_call x15, Pallas kernels: 21.8 us -> 20.7 us  [call(): pl.pallas_call(kernel, out_shape=outs, in_specs=[IN_SMEM if k in smem els...]
    ppermute x4, waiting for transfers between devices: 6.58 us -> 7.45 us  [sent_by_core(): return lax.ppermute(value, ('dom', 'edge'), pairs)]
  transfers between devices with their start and end apart: 12 -> 12, of which waited for: 7 -> 7; matrix products, arithmetic and copies ran while one was open for 0% -> 0% of each run, Pallas kernels for 30% -> 28%
where the time goes in v13:
time: 46.2 us; the launch traced here: 46.1 us
  Pallas kernels  20.7 us (45%)
  starting transfers between devices  14.7 us (32%)
  waiting for transfers between devices  9.26 us (20%)
  between operations  1.43 us (3%)
    pallas_call x15, Pallas kernels, call(): pl.pallas_call(kernel, out_shape=outs, in_specs=[IN_SMEM if k in smem els...  20.7 us
    ppermute x4, starting transfers between devices, sent_by_core(): return lax.ppermute(value, ('dom', 'edge'), pairs)  13.3 us
    ppermute x4, waiting for transfers between devices, sent_by_core(): return lax.ppermute(value, ('dom', 'edge'), pairs)  7.45 us
    ppermute x8, waiting for transfers between devices, swapped(): return lax.ppermute(value, 'edge', [(0, 1), (1, 0)])  1.82 us
    ppermute x8, starting transfers between devices, swapped(): return lax.ppermute(value, 'edge', [(0, 1), (1, 0)])  1.43 us
  transfers between devices with their start and end apart: 12, of which 7 were waited for; matrix products, arithmetic and copies ran while one was open for 0% of the time, Pallas kernels for 28%

profile of v13, /device:TPU:0, one launch (start us, length us, event | category | flops | bytes accessed | tf_op | source)
XLA Modules:
  0.0 46.1 jit_solution(6471602994630316097)
XLA Ops:
  0.6 0.6 %collective-permute-start = (bf16[256,256]{1,0:T(8,128)(2,1)}, bf16[256,256]{1,0:T(8,128)(2,1)S(1)}, u32[]{:S(2)}, u32[]{:S(2)}) collective-permute-start(bf16[256,256]{1,0:T(8,128)(2,1)} %refs_0_.2), channel_id=1, source_target_pairs={{0,1},{1,0},{2,3},{3,2},{4,5},{5,4},{6,7},{7,6},{8,9},{9,8},{10,11... | collective-permute-start | bytes 393224 | tf_op jit(solution)/shard_map/ppermute | solution.py:348
  1.2 0.1 collective-permute-start.1
  1.3 1.2 %shard_map.149 = (bf16[256,256]{1,0:T(8,128)(2,1)S(1)}, s32[1,4,128]{2,1,0:T(4,128)S(1)}, s32[1,3072]{1,0:T(1,128)S(1)}, s32[1,3072]{1,0:T(1,128)S(1)}, f32[2,25...) custom-call(bf16[256,256]{1,0:T(8,128)(2,1)} %refs_0_.2, s32[1,4,128]{2,1,0:T(4,128)} %refs_1_.2, s32[1,3072]{1,0:T(1,128)} %bitcast.2, ...), custom_call_target="tpu_custom_call" | custom-call | bytes 946176 | tf_op jit(solution)/shard_map/pallas_call | solution.py:80
  2.5 0.1 collective-permute-done.1.list_peer
  2.6 0.0 collective-permute-done.peer_ref
  2.6 0.3 shard_map.151
  2.9 2.9 %collective-permute-start.2 = (bf16[256,256]{1,0:T(8,128)(2,1)S(1)}, bf16[256,256]{1,0:T(8,128)(2,1)S(1)}, u32[]{:S(2)}, u32[]{:S(2)}) collective-permute-start(bf16[256,256]{1,0:T(8,128)(2,1)S(1)} %get-tuple-element.48), channel_id=1, source_target_pairs={{0,2},{2,0},{4,6},{6,4},{8,10},{10,8},{12,14},{14,12},{16,18},{18,... | collective-permute-start | bytes 393224 | tf_op jit(solution)/shard_map/ppermute | solution.py:377
  5.8 2.3 %shard_map.150 = (f32[3072,256]{1,0:T(8,128)S(1)}, s16[2,3072,128]{2,1,0:T(8,128)(2,1)S(1)}, bf16[768,256]{1,0:T(8,128)(2,1)S(1)}, bf16[3072,256]{1,0:T(8,128)(2...) custom-call(s32[1,3072]{1,0:T(1,128)S(1)} %get-tuple-element.42.send, ...), custom_call_target="tpu_custom_call" | custom-call | flops 2013265920 | bytes 4096000 | tf_op jit(solution)/shard_map/pallas_call | solution.py:80
  8.0 0.7 %collective-permute-done.2.rows_ref = bf16[256,256]{1,0:T(8,128)(2,1)S(1)} collective-permute-done((bf16[256,256]{1,0:T(8,128)(2,1)S(1)}, bf16[256,256]{1,0:T(8,128)(2,1)S(1)}, u32[]{:S(2)}, u32[]{:S(2)}) %collective-permute-start.2) | collective-permute-done | bytes 131104 | tf_op jit(solution)/shard_map/ppermute | solution.py:377
  8.7 0.0 collective-permute-start.3
  8.7 6.0 %collective-permute-start.4 = (bf16[256,256]{1,0:T(8,128)(2,1)S(1)}, bf16[256,256]{1,0:T(8,128)(2,1)S(1)}, u32[]{:S(2)}, u32[]{:S(2)}) collective-permute-start(bf16[256,256]{1,0:T(8,128)(2,1)S(1)} %get-tuple-element.54), channel_id=1, source_target_pairs={{0,30},{2,4},{4,2},{6,8},{8,6},{10,12},{12,10},{14,16},{16,14},{18... | collective-permute-start | bytes 393224 | tf_op jit(solution)/shard_map/ppermute | solution.py:377
  14.7 1.2 %shard_map.152.pre_ref = f32[3072,256]{1,0:T(8,128)S(1)} custom-call(f32[3072,256]{1,0:T(8,128)S(1)} %get-tuple-element.50.pre_ref, s16[2,3072,128]{2,1,0:T(8,128)(2,1)S(1)} %get-tuple-element.51.cols, bf16[768,256]{1,0:T(8,128)(2,1)S(1)} %get-tuple-element.44.w1_ref, bf16[256,256]{1,0:T(8,128)(2,1)S(1)} %collective-permute-done.2.rows_ref, ...), custom_call_target="tpu_custom_call" | custom-call | flops 402653184 | bytes 6815744 | tf_op jit(solution)/shard_map/pallas_call | solution.py:80
  16.0 0.0 collective-permute-done.3.rows_ref
  16.0 0.8 %shard_map.153.pre_ref = f32[3072,256]{1,0:T(8,128)S(1)} custom-call(f32[3072,256]{1,0:T(8,128)S(1)} %shard_map.152.pre_ref, s16[2,3072,128]{2,1,0:T(8,128)(2,1)S(1)} %get-tuple-element.51.cols, bf16[768,256]{1,0:T(8,128)(2,1)S(1)} %get-tuple-element.44.w1_ref, bf16[256,256]{1,0:T(8,128)(2,1)S(1)} %collective-permute-done.3.rows_ref), custom_call_target="tpu_custom_call" | custom-call | flops 402653184 | bytes 5242880 | tf_op jit(solution)/shard_map/pallas_call | solution.py:80
  16.8 2.2 %collective-permute-done.4.rows_ref = bf16[256,256]{1,0:T(8,128)(2,1)S(1)} collective-permute-done((bf16[256,256]{1,0:T(8,128)(2,1)S(1)}, bf16[256,256]{1,0:T(8,128)(2,1)S(1)}, u32[]{:S(2)}, u32[]{:S(2)}) %collective-permute-start.4) | collective-permute-done | bytes 131104 | tf_op jit(solution)/shard_map/ppermute | solution.py:377
  19.0 0.0 collective-permute-start.5
  19.6 0.8 %shard_map.154.pre_ref = f32[3072,256]{1,0:T(8,128)S(1)} custom-call(f32[3072,256]{1,0:T(8,128)S(1)} %shard_map.153.pre_ref, s16[2,3072,128]{2,1,0:T(8,128)(2,1)S(1)} %get-tuple-element.51.cols, bf16[768,256]{1,0:T(8,128)(2,1)S(1)} %get-tuple-element.44.w1_ref, bf16[256,256]{1,0:T(8,128)(2,1)S(1)} %collective-permute-done.4.rows_ref), custom_call_target="tpu_custom_call" | custom-call | flops 402653184 | bytes 5242880 | tf_op jit(solution)/shard_map/pallas_call | solution.py:80
  20.4 0.0 collective-permute-done.5.peer
  20.5 2.6 %shard_map.155 = (bf16[3072,256]{1,0:T(8,128)(2,1)S(1)}, bf16[512,256]{1,0:T(8,128)(2,1)S(1)}) custom-call(s32[1,1]{1,0:T(1,128)S(6)} %copy.16.live_ref, f32[3072,256]{1,0:T(8,128)S(1)} %shard_map.154.pre_ref, s16[2,3072,128]{2,1,0:T(8,128)(2,1)S(1)} %get-tuple-element.51.cols, s32[1,3072]{1,0:T(1,128)S(1)} %get-tuple-element.43.recv_ref, ...), custom_call_target="tpu_custom_call" | custom-call | flops 2013265920 | bytes 7092228 | tf_op jit(solution)/shard_map/pallas_call | solution.py:80
  23.1 0.6 %collective-permute-start.6 = (bf16[512,256]{1,0:T(8,128)(2,1)S(1)}, bf16[512,256]{1,0:T(8,128)(2,1)S(1)}, u32[]{:S(2)}, u32[]{:S(2)}) collective-permute-start(bf16[512,256]{1,0:T(8,128)(2,1)S(1)} %get-tuple-element.59.first), channel_id=1, source_target_pairs={{0,1},{1,0},{2,3},{3,2},{4,5},{5,4},{6,7},{7,6},{8,9},{9,8},{10,11... | collective-permute-start | bytes 786440 | tf_op jit(solution)/shard_map/ppermute | solution.py:348
  23.7 1.2 %collective-permute-done.6.second = bf16[512,256]{1,0:T(8,128)(2,1)S(1)} collective-permute-done((bf16[512,256]{1,0:T(8,128)(2,1)S(1)}, bf16[512,256]{1,0:T(8,128)(2,1)S(1)}, u32[]{:S(2)}, u32[]{:S(2)}) %collective-permute-start.6) | collective-permute-done | bytes 262176 | tf_op jit(solution)/shard_map/ppermute | solution.py:348
  24.8 1.0 %shard_map.156 = (bf16[512,256]{1,0:T(8,128)(2,1)S(1)}, bf16[256,256]{1,0:T(8,128)(2,1)S(1)}, bf16[256,256]{1,0:T(8,128)(2,1)S(1)}) custom-call(bf16[256,256]{1,0:T(8,128)(2,1)S(1)} %get-tuple-element.41.own_ref, bf16[256,256]{1,0:T(8,128)(2,1)S(1)} %collective-permute-done.peer_ref, bf16[512,256]{1,0:T(8,128)(2,1)S(1)} %get-tuple-element.59.first, ...), custom_call_target="tpu_custom_call" | custom-call | bytes 1839104 | tf_op jit(solution)/shard_map/pallas_call | solution.py:80
  25.9 0.1 collective-permute-start.7
  25.9 3.0 %shard_map.157.pre_ref = f32[3072,256]{1,0:T(8,128)S(1)} custom-call(bf16[3072,256]{1,0:T(8,128)(2,1)S(1)} %get-tuple-element.66.edge_ref, s16[2,3072,128]{2,1,0:T(8,128)(2,1)S(1)} %get-tuple-element.51.cols, bf16[512,256]{1,0:T(8,128)(2,1)S(1)} %get-tuple-element.65.dom_ref.nodes_ref, bf16[768,256]{1,0:T(8,128)(2,1)S(1)} %get-tuple-element.67.w1_ref, ...), custom_call_target="tpu_custom_call" | custom-call | flops 2013265920 | bytes 3803136 | tf_op jit(solution)/shard_map/pallas_call | solution.py:80
  29.0 1.9 %collective-permute-done.7.rows_ref = bf16[256,256]{1,0:T(8,128)(2,1)S(1)} collective-permute-done((bf16[256,256]{1,0:T(8,128)(2,1)S(1)}, bf16[256,256]{1,0:T(8,128)(2,1)S(1)}, u32[]{:S(2)}, u32[]{:S(2)}) %collective-permute-start.7) | collective-permute-done | bytes 131104 | tf_op jit(solution)/shard_map/ppermute | solution.py:377
  30.9 0.0 collective-permute-start.8
  30.9 4.3 %collective-permute-start.9 = (bf16[256,256]{1,0:T(8,128)(2,1)S(1)}, bf16[256,256]{1,0:T(8,128)(2,1)S(1)}, u32[]{:S(2)}, u32[]{:S(2)}) collective-permute-start(bf16[256,256]{1,0:T(8,128)(2,1)S(1)} %get-tuple-element.72), channel_id=1, source_target_pairs={{0,30},{2,4},{4,2},{6,8},{8,6},{10,12},{12,10},{14,16},{16,14},{18... | collective-permute-start | bytes 393224 | tf_op jit(solution)/shard_map/ppermute | solution.py:377
  35.2 0.8 %shard_map.158.pre_ref = f32[3072,256]{1,0:T(8,128)S(1)} custom-call(f32[3072,256]{1,0:T(8,128)S(1)} %shard_map.157.pre_ref, s16[2,3072,128]{2,1,0:T(8,128)(2,1)S(1)} %get-tuple-element.51.cols, bf16[768,256]{1,0:T(8,128)(2,1)S(1)} %get-tuple-element.67.w1_ref, bf16[256,256]{1,0:T(8,128)(2,1)S(1)} %collective-permute-done.7.rows_ref), custom_call_target="tpu_custom_call" | custom-call | flops 402653184 | bytes 5242880 | tf_op jit(solution)/shard_map/pallas_call | solution.py:80
  36.0 0.0 collective-permute-done.8.rows_ref
  36.0 0.8 %shard_map.159.pre_ref = f32[3072,256]{1,0:T(8,128)S(1)} custom-call(f32[3072,256]{1,0:T(8,128)S(1)} %shard_map.158.pre_ref, s16[2,3072,128]{2,1,0:T(8,128)(2,1)S(1)} %get-tuple-element.51.cols, bf16[768,256]{1,0:T(8,128)(2,1)S(1)} %get-tuple-element.67.w1_ref, bf16[256,256]{1,0:T(8,128)(2,1)S(1)} %collective-permute-done.8.rows_ref), custom_call_target="tpu_custom_call" | custom-call | flops 402653184 | bytes 5242880 | tf_op jit(solution)/shard_map/pallas_call | solution.py:80
  36.8 2.6 %collective-permute-done.9.rows_ref = bf16[256,256]{1,0:T(8,128)(2,1)S(1)} collective-permute-done((bf16[256,256]{1,0:T(8,128)(2,1)S(1)}, bf16[256,256]{1,0:T(8,128)(2,1)S(1)}, u32[]{:S(2)}, u32[]{:S(2)}) %collective-permute-start.9) | collective-permute-done | bytes 131104 | tf_op jit(solution)/shard_map/ppermute | solution.py:377
  39.5 0.0 collective-permute-start.10
  39.5 0.8 %shard_map.160.pre_ref = f32[3072,256]{1,0:T(8,128)S(1)} custom-call(f32[3072,256]{1,0:T(8,128)S(1)} %shard_map.159.pre_ref, s16[2,3072,128]{2,1,0:T(8,128)(2,1)S(1)} %get-tuple-element.51.cols, bf16[768,256]{1,0:T(8,128)(2,1)S(1)} %get-tuple-element.67.w1_ref, bf16[256,256]{1,0:T(8,128)(2,1)S(1)} %collective-permute-done.9.rows_ref), custom_call_target="tpu_custom_call" | custom-call | flops 402653184 | bytes 5242880 | tf_op jit(solution)/shard_map/pallas_call | solution.py:80
  40.3 0.5 %collective-permute-done.10.peer = bf16[256,256]{1,0:T(8,128)(2,1)S(1)} collective-permute-done((bf16[256,256]{1,0:T(8,128)(2,1)S(1)}, bf16[256,256]{1,0:T(8,128)(2,1)S(1)}, u32[]{:S(2)}, u32[]{:S(2)}) %collective-permute-start.10) | collective-permute-done | bytes 131104 | tf_op jit(solution)/shard_map/ppermute | solution.py:348
  40.8 2.6 %shard_map.161 = (bf16[3072,256]{1,0:T(8,128)(2,1)S(1)}, bf16[256,256]{1,0:T(8,128)(2,1)S(1)}, bf16[3072,256]{1,0:T(8,128)(2,1)S(1)}) custom-call(s32[1,1]{1,0:T(1,128)S(6)} %copy.16.live_ref, f32[3072,256]{1,0:T(8,128)S(1)} %shard_map.160.pre_ref, s16[2,3072,128]{2,1,0:T(8,128)(2,1)S(1)} %get-tuple-element.51.cols, ...), custom_call_target="tpu_custom_call" | custom-call | flops 2013265920 | bytes 7092228 | tf_op jit(solution)/shard_map/pallas_call | solution.py:80
  43.4 0.2 collective-permute-start.11
  43.6 1.2 %shard_map.162 = (bf16[256,256]{1,0:T(8,128)(2,1)S(1)}, bf16[3072,256]{1,0:T(8,128)(2,1)}) custom-call(s32[1,3072]{1,0:T(1,128)S(1)} %get-tuple-element.43.recv_ref, bf16[3072,256]{1,0:T(8,128)(2,1)S(1)} %get-tuple-element.75.msgs, bf16[3072,256]{1,0:T(8,128)(2,1)S(1)} %get-tuple-element.76.edge_ref), custom_call_target="tpu_custom_call" | custom-call | bytes 3158016 | tf_op jit(solution)/shard_map/pallas_call | solution.py:80
  44.8 0.0 collective-permute-done.11.second
  44.8 1.2 %shard_map.163 = bf16[256,256]{1,0:T(8,128)(2,1)} custom-call(bf16[512,256]{1,0:T(8,128)(2,1)S(1)} %get-tuple-element.65.dom_ref.nodes_ref, bf16[256,256]{1,0:T(8,128)(2,1)S(1)} %get-tuple-element.77.first, bf16[256,256]{1,0:T(8,128)(2,1)S(1)} %collective-permute-done.11.second, bf16[2,512,256]{2,1,0:T(8,128)(2,1)S(1)} %get-tuple-element.61.w1, ...), custom_call_target="tpu_custom_call" | custom-call | bytes 1314816 | tf_op jit(solution)/shard_map/pallas_call | solution.py:80
Async XLA Ops:
  0.6 1.9 %collective-permute-start = (bf16[256,256]{1,0:T(8,128)(2,1)}, bf16[256,256]{1,0:T(8,128)(2,1)S(1)}, u32[]{:S(2)}, u32[]{:S(2)}) collective-permute-start(bf16[256,256]{1,0:T(8,128)(2,1)} %refs_0_.2), channel_id=1, source_target_pairs={{0,1},{1,0},{2,3},{3,2},{4,5},{5,4},{6,7},{7,6},{8,9},{9,8},{10,11... | collective-permute-start | bytes 393224 | tf_op jit(solution)/shard_map/ppermute | solution.py:348
  1.2 1.4 %collective-permute-start.1 = (s32[1,4,128]{2,1,0:T(4,128)}, s32[1,4,128]{2,1,0:T(4,128)S(1)}, u32[]{:S(2)}, u32[]{:S(2)}) collective-permute-start(s32[1,4,128]{2,1,0:T(4,128)} %refs_1_.2), channel_id=1, source_target_pairs={{0,1},{1,0},{2,3},{3,2},{4,5},{5,4},{6,7},{7,6},{8,9},{9,8},{10,11... | collective-permute-start | bytes 6152 | tf_op jit(solution)/shard_map/ppermute | solution.py:348
  2.9 5.8 %collective-permute-start.2 = (bf16[256,256]{1,0:T(8,128)(2,1)S(1)}, bf16[256,256]{1,0:T(8,128)(2,1)S(1)}, u32[]{:S(2)}, u32[]{:S(2)}) collective-permute-start(bf16[256,256]{1,0:T(8,128)(2,1)S(1)} %get-tuple-element.48), channel_id=1, source_target_pairs={{0,2},{2,0},{4,6},{6,4},{8,10},{10,8},{12,14},{14,12},{16,18},{18,... | collective-permute-start | bytes 393224 | tf_op jit(solution)/shard_map/ppermute | solution.py:377
  8.7 7.3 %collective-permute-start.3 = (bf16[256,256]{1,0:T(8,128)(2,1)S(1)}, bf16[256,256]{1,0:T(8,128)(2,1)S(1)}, u32[]{:S(2)}, u32[]{:S(2)}) collective-permute-start(bf16[256,256]{1,0:T(8,128)(2,1)S(1)} %collective-permute-done.2.rows_ref), channel_id=1, source_target_pairs={{0,1},{1,0},{2,3},{3,2},{4,5},{5,4},{6,7},{7,6},{8,9},{9,8},{10,11... | collective-permute-start | bytes 393224 | tf_op jit(solution)/shard_map/ppermute | solution.py:348
  8.7 10.3 %collective-permute-start.4 = (bf16[256,256]{1,0:T(8,128)(2,1)S(1)}, bf16[256,256]{1,0:T(8,128)(2,1)S(1)}, u32[]{:S(2)}, u32[]{:S(2)}) collective-permute-start(bf16[256,256]{1,0:T(8,128)(2,1)S(1)} %get-tuple-element.54), channel_id=1, source_target_pairs={{0,30},{2,4},{4,2},{6,8},{8,6},{10,12},{12,10},{14,16},{16,14},{18... | collective-permute-start | bytes 393224 | tf_op jit(solution)/shard_map/ppermute | solution.py:377
  19.0 1.5 %collective-permute-start.5 = (bf16[256,256]{1,0:T(8,128)(2,1)S(1)}, bf16[256,256]{1,0:T(8,128)(2,1)S(1)}, u32[]{:S(2)}, u32[]{:S(2)}) collective-permute-start(bf16[256,256]{1,0:T(8,128)(2,1)S(1)} %collective-permute-done.4.rows_ref), channel_id=1, source_target_pairs={{0,1},{1,0},{2,3},{3,2},{4,5},{5,4},{6,7},{7,6},{8,9},{9,8},{10,11... | collective-permute-start | bytes 393224 | tf_op jit(solution)/shard_map/ppermute | solution.py:348
  23.1 1.7 %collective-permute-start.6 = (bf16[512,256]{1,0:T(8,128)(2,1)S(1)}, bf16[512,256]{1,0:T(8,128)(2,1)S(1)}, u32[]{:S(2)}, u32[]{:S(2)}) collective-permute-start(bf16[512,256]{1,0:T(8,128)(2,1)S(1)} %get-tuple-element.59.first), channel_id=1, source_target_pairs={{0,1},{1,0},{2,3},{3,2},{4,5},{5,4},{6,7},{7,6},{8,9},{9,8},{10,11... | collective-permute-start | bytes 786440 | tf_op jit(solution)/shard_map/ppermute | solution.py:348
  25.9 5.0 %collective-permute-start.7 = (bf16[256,256]{1,0:T(8,128)(2,1)S(1)}, bf16[256,256]{1,0:T(8,128)(2,1)S(1)}, u32[]{:S(2)}, u32[]{:S(2)}) collective-permute-start(bf16[256,256]{1,0:T(8,128)(2,1)S(1)} %get-tuple-element.68), channel_id=1, source_target_pairs={{0,2},{2,0},{4,6},{6,4},{8,10},{10,8},{12,14},{14,12},{16,18},{18,... | collective-permute-start | bytes 393224 | tf_op jit(solution)/shard_map/ppermute | solution.py:377
  30.9 5.1 %collective-permute-start.8 = (bf16[256,256]{1,0:T(8,128)(2,1)S(1)}, bf16[256,256]{1,0:T(8,128)(2,1)S(1)}, u32[]{:S(2)}, u32[]{:S(2)}) collective-permute-start(bf16[256,256]{1,0:T(8,128)(2,1)S(1)} %collective-permute-done.7.rows_ref), channel_id=1, source_target_pairs={{0,1},{1,0},{2,3},{3,2},{4,5},{5,4},{6,7},{7,6},{8,9},{9,8},{10,11... | collective-permute-start | bytes 393224 | tf_op jit(solution)/shard_map/ppermute | solution.py:348
  30.9 8.6 %collective-permute-start.9 = (bf16[256,256]{1,0:T(8,128)(2,1)S(1)}, bf16[256,256]{1,0:T(8,128)(2,1)S(1)}, u32[]{:S(2)}, u32[]{:S(2)}) collective-permute-start(bf16[256,256]{1,0:T(8,128)(2,1)S(1)} %get-tuple-element.72), channel_id=1, source_target_pairs={{0,30},{2,4},{4,2},{6,8},{8,6},{10,12},{12,10},{14,16},{16,14},{18... | collective-permute-start | bytes 393224 | tf_op jit(solution)/shard_map/ppermute | solution.py:377
  39.5 1.3 %collective-permute-start.10 = (bf16[256,256]{1,0:T(8,128)(2,1)S(1)}, bf16[256,256]{1,0:T(8,128)(2,1)S(1)}, u32[]{:S(2)}, u32[]{:S(2)}) collective-permute-start(bf16[256,256]{1,0:T(8,128)(2,1)S(1)} %collective-permute-done.9.rows_ref), channel_id=1, source_target_pairs={{0,1},{1,0},{2,3},{3,2},{4,5},{5,4},{6,7},{7,6},{8,9},{9,8},{10,11... | collective-permute-start | bytes 393224 | tf_op jit(solution)/shard_map/ppermute | solution.py:348
  43.4 1.4 %collective-permute-start.11 = (bf16[256,256]{1,0:T(8,128)(2,1)S(1)}, bf16[256,256]{1,0:T(8,128)(2,1)S(1)}, u32[]{:S(2)}, u32[]{:S(2)}) collective-permute-start(bf16[256,256]{1,0:T(8,128)(2,1)S(1)} %get-tuple-element.78), channel_id=1, source_target_pairs={{0,1},{1,0},{2,3},{3,2},{4,5},{5,4},{6,7},{7,6},{8,9},{9,8},{10,11... | collective-permute-start | bytes 393224 | tf_op jit(solution)/shard_map/ppermute | solution.py:348
